TPU v7x, 32 devices: a whole 2x2x4 slice. The times are simulated.
32 devices in a mesh: groups: 2 (over y), ctx: 4 (over z), chan: 4 (over x, core).
Axes of the slice: x: 2, y: 2, z: 4, core: 2. Of those that a mesh axis runs over, the one named last changes fastest.
Arguments:
- query_gate: float32 [4096, 1024], P(('groups', 'ctx'), 'chan'), parts along dimension 0, may hold values from -6 to 6
- key_gate: float32 [4096, 1024], P(('groups', 'ctx'), 'chan'), parts along dimension 0, may hold values from -6 to 6
- values: float32 [4096, 1024], P(('groups', 'ctx'), 'chan'), parts along dimension 0, may hold values from -6 to 6
- filter_taps: float32 [4096, 1024], P(None, 'chan'), may hold values from -0.125 to 0.125
- skip_gain: float32 [1024], P('chan'), may hold values from -1 to 1
- upstream: float32 [4096, 1024], P(('groups', 'ctx'), 'chan'), parts along dimension 0, may hold values from -6 to 6
Outputs:
- query_grad: float32 [4096, 1024], P(('groups', 'ctx'), 'chan'), parts along dimension 0
- key_grad: float32 [4096, 1024], P(('groups', 'ctx'), 'chan'), parts along dimension 0
- value_grad: float32 [4096, 1024], P(('groups', 'ctx'), 'chan'), parts along dimension 0
- filter_grad: float32 [8192, 1024], P(('groups', 'ctx'), 'chan'), parts along dimension 0
- skip_grad: float32 [2048], P(('groups', 'chan')), parts along dimension 0
There are 2 independent parts, one for each index of `groups`. A program takes and returns all parts, laid end to end along the dimension named above; an argument that names none is the same for every part. Nothing has to cross between parts.
All inputs are finite; a program needn't handle non-finite values.
Results may differ from a plain program's by a relative error of at most 0.0001.
Values sent between devices are 32-bit elements; how exact they have to be, the bound alone decides.
No kernel may reach another device: no remote copies, remote signals or barrier semaphores. Data moves between devices by JAX's collectives and lax.ppermute only.
A program may use at most 128 MiB of HBM per device.

v0:
```python
import math

import jax
import jax.numpy as jnp
from jax import lax
from jax.sharding import PartitionSpec as P


def matmul(left, right):
    return jnp.dot(left, right, preferred_element_type=jnp.float32, precision=lax.Precision.HIGHEST)


def forward_table(seg_len, count, offset):
    num_bins = seg_len + 1
    period = 2 * seg_len
    bin_index = lax.broadcasted_iota(jnp.int32, (num_bins, count), 0)
    pos_index = lax.broadcasted_iota(jnp.int32, (num_bins, count), 1) + offset
    angles = (bin_index * pos_index % period).astype(jnp.float32) * (2.0 * math.pi / period)
    return jnp.concatenate([jnp.cos(angles), -jnp.sin(angles)], axis=0)


def inverse_table(seg_len, count, offset):
    num_bins = seg_len + 1
    period = 2 * seg_len
    pos_index = lax.broadcasted_iota(jnp.int32, (count, num_bins), 0) + offset
    bin_index = lax.broadcasted_iota(jnp.int32, (count, num_bins), 1)
    angles = (bin_index * pos_index % period).astype(jnp.float32) * (2.0 * math.pi / period)
    weights = jnp.where((bin_index == 0) | (bin_index == seg_len), 1.0, 2.0) / period
    return jnp.concatenate([weights * jnp.cos(angles), -weights * jnp.sin(angles)], axis=1)


def times_spec(first, second):
    num_bins = first.shape[0] // 2
    real_a, imag_a = (first[:num_bins], first[num_bins:])
    real_b, imag_b = (second[:num_bins], second[num_bins:])
    return jnp.concatenate(
        [real_a * real_b - imag_a * imag_b, real_a * imag_b + imag_a * real_b], axis=0
    )


def conj_times(first, second):
    num_bins = first.shape[0] // 2
    real_a, imag_a = (first[:num_bins], first[num_bins:])
    real_b, imag_b = (second[:num_bins], second[num_bins:])
    return jnp.concatenate(
        [real_a * real_b + imag_a * imag_b, real_a * imag_b - imag_a * real_b], axis=0
    )


def pick(stack, index):
    return lax.dynamic_index_in_dim(stack, index, 0, keepdims=False)


def local(query_gate, key_gate, values, filter_taps, skip_gain, upstream):
    seg_len, width_dev = values.shape
    cycle_size = lax.axis_size("ctx")
    position = lax.axis_index("ctx")
    history = seg_len * cycle_size
    gated = key_gate * values
    mixed_grad = upstream * query_gate
    table_low = forward_table(seg_len, seg_len, 0)
    table_high = forward_table(seg_len, seg_len, seg_len)
    table_taps = forward_table(seg_len, 2 * seg_len, 0)
    back_low = inverse_table(seg_len, seg_len, 0)
    back_high = inverse_table(seg_len, seg_len, seg_len)
    back_full = inverse_table(seg_len, 2 * seg_len, 0)
    own_grad_spec = matmul(table_high, mixed_grad)
    spec_rows = 2 * (seg_len + 1)

    def taps_spec(lag_block):
        start_row = (lag_block - 1) * seg_len + history
        window = lax.dynamic_slice_in_dim(filter_taps, start_row, 2 * seg_len, 0)
        return matmul(table_taps, window)

    def visit(carry, gated_spec, grad_spec, source):
        acc_conv, acc_back, partial_value = carry
        lag_block = position - source
        acc_conv = acc_conv + times_spec(taps_spec(lag_block), gated_spec)
        acc_back = acc_back + conj_times(taps_spec(-lag_block), grad_spec)
        segment = matmul(back_full, conj_times(gated_spec, own_grad_spec))
        start_row = (lag_block - 1) * seg_len + history
        current = lax.dynamic_slice_in_dim(partial_value, start_row, 2 * seg_len, 0)
        partial_value = lax.dynamic_update_slice_in_dim(
            partial_value, current + segment, start_row, 0
        )
        return (acc_conv, acc_back, partial_value)

    initial = (
        jnp.zeros((spec_rows, width_dev), jnp.float32),
        jnp.zeros((spec_rows, width_dev), jnp.float32),
        jnp.zeros((2 * history, width_dev), jnp.float32),
    )
    own_gated_spec = matmul(table_low, gated)
    pieces = (
        lax.all_gather(own_gated_spec[None], "ctx", axis=0, tiled=True),
        lax.all_gather(own_grad_spec[None], "ctx", axis=0, tiled=True),
    )

    def advance(member, state):
        return visit(state, pick(pieces[0], member), pick(pieces[1], member), member)

    folded = lax.fori_loop(0, pieces[0].shape[0], advance, initial)
    acc_conv, acc_back, partial_value = folded
    filter_grad = lax.psum_scatter(partial_value, "ctx", scatter_dimension=0, tiled=True)
    conv = matmul(back_high, acc_conv)
    back = matmul(back_low, acc_back) + skip_gain[None, :] * mixed_grad
    query_grad = upstream * (conv + skip_gain[None, :] * gated)
    key_grad = back * values
    value_grad = back * key_gate
    skip_grad = lax.psum(jnp.sum(mixed_grad * gated, axis=0), "ctx")
    return (query_grad, key_grad, value_grad, filter_grad, skip_grad)


def solution(mesh):
    in_specs = (
        P(("groups", "ctx"), "chan"),
        P(("groups", "ctx"), "chan"),
        P(("groups", "ctx"), "chan"),
        P(None, "chan"),
        P("chan"),
        P(("groups", "ctx"), "chan"),
    )
    out_specs = (
        P(("groups", "ctx"), "chan"),
        P(("groups", "ctx"), "chan"),
        P(("groups", "ctx"), "chan"),
        P(("groups", "ctx"), "chan"),
        P(("groups", "chan")),
    )
    return jax.shard_map(local, mesh=mesh, in_specs=in_specs, out_specs=out_specs, check_vma=False)
```

profile of v0, /device:TPU:0, one launch (start us, length us, event | category | flops | bytes accessed | tf_op | source)
XLA Modules:
  0.0 386.0 jit_solution(120343839279487304)
XLA Ops:
  7.2 4.2 %sine_negate_fusion.2 = (f32[513,512]{1,0:T(8,128)S(1)}, f32[513,512]{1,0:T(8,128)S(1)}) fusion(), kind=kLoop, calls=%fused_computation.105 | loop fusion | flops 3939840 | bytes 2101248 | tf_op jit(solution)/shard_map/neg | solution.py:19
  11.4 2.9 convolution_bitcast_fusion.3
  14.7 4.2 %fusion.71 = (f32[513,512]{1,0:T(8,128)S(1)}, f32[513,512]{1,0:T(8,128)S(1)}) fusion(s32[512]{0:T(512)S(1)} %iota_add_fusion), kind=kLoop, calls=%fused_computation.112 | loop fusion | flops 3939840 | bytes 2103296 | tf_op jit(solution)/shard_map/cos | solution.py:19
  18.9 2.8 fusion.32
  21.8 1.8 reduce-scatter.2.cloned.1.call-start
  23.6 8.4 %sine_negate_fusion = (f32[513,1024]{1,0:T(8,128)S(1)}, f32[513,1024]{1,0:T(8,128)S(1)}) fusion(), kind=kLoop, calls=%fused_computation.54 | loop fusion | flops 7879680 | bytes 4202496 | tf_op jit(solution)/shard_map/neg | solution.py:19
  32.0 10.5 %sine_multiply_fusion = (f32[1024,513]{1,0:T(8,128)S(1)}, f32[1024,513]{1,0:T(8,128)S(1)}) fusion(f32[513]{0:T(1024)S(1)} %fusion.73, f32[513]{0:T(1024)S(1)} %select_multiply_fusion), kind=kLoop, calls=%fused_computation.38 | loop fusion | flops 8404992 | bytes 4206600 | tf_op jit(solution)/shard_map/mul | solution.py:29
  42.5 2.5 pad_maximum_fusion.1
  45.0 2.9 pad_maximum_fusion
  48.0 50.5 %all-gather.7.cloned.1.call-done = f32[4,1026,256]{2,1,0:T(8,128)} async-done(((f32[1,1026,256]{2,1,0:T(8,128)}), f32[4,1026,256]{2,1,0:T(8,128)}) %all-gather.7.cloned.1.call-update) | async-done | bytes 4202512 | tf_op jit(solution)/shard_map/all_gather | solution.py:95
  98.5 81.4 %all-gather.9.cloned.1.call-done = f32[4,1026,256]{2,1,0:T(8,128)} async-done(((f32[1,1026,256]{2,1,0:T(8,128)}), f32[4,1026,256]{2,1,0:T(8,128)}) %all-gather.9.cloned.1.call-update) | async-done | bytes 4202512 | tf_op jit(solution)/shard_map/all_gather | solution.py:96
  179.9 2.3 broadcast_in_dim.27.clone
  182.2 121.3 %while.21 = (s32[]{:T(128)}, f32[1026,256]{1,0:T(8,128)}, f32[1026,256]{1,0:T(8,128)}, f32[4096,256]{1,0:T(8,128)}, s32[]{:T(128)}, /*index=5*/f32[4096,256]{1,0...) while((s32[]{:T(128)}, f32[1026,256]{1,0:T(8,128)}, ...), condition=%wide.region_1.2_spmd.clone, body=%wide.region_0.1_spmd.clone.sunk | while | flops 9687015424 | bytes 64113172 | solution.py:102
  182.4 5.7 %convolution_bitcast_fusion.6 = f32[1026,256]{1,0:T(8,128)S(1)} fusion(f32[1026,1024]{1,0:T(8,128)} %get-tuple-element.519, f32[4096,256]{1,0:T(8,128)} %get-tuple-element.518, s32[]{:T(128)S(6)} %select_n.167), kind=kOutput, calls=%fused_computation.1.clone.1 | convolution fusion | flops 3227516928 | bytes 6326276 | tf_op jit(solution)/shard_map/while/body/eval_jaxpr/dot_general | solution.py:10
  188.1 1.6 multiply_add_fusion.5
  189.7 5.7 %convolution_bitcast_fusion.7 = f32[1026,256]{1,0:T(8,128)S(1)} fusion(f32[1026,1024]{1,0:T(8,128)} %get-tuple-element.519, f32[4096,256]{1,0:T(8,128)} %get-tuple-element.518, s32[]{:T(128)S(6)} %select_n.168), kind=kOutput, calls=%fused_computation.clone.1 | convolution fusion | flops 3227516928 | bytes 6326276 | tf_op jit(solution)/shard_map/while/body/eval_jaxpr/dot_general | solution.py:10
  195.4 1.6 multiply_add_fusion.6
  197.9 1.0 copy-done.3
  199.3 1.3 constant_dynamic-slice_fusion.2
  200.9 9.8 %fusion.98 = f32[1024,256]{0,1:T(8,128)S(1)} fusion(f32[1024,256]{0,1:T(8,128)S(1)} %copy.19, f32[1024,1026]{1,0:T(8,128)} %get-tuple-element.523, f32[513,256]{1,0:T(8,128)S(1)} %get-tuple-element.475, f32[513,256]{1,0:T(8,128)S(1)} %get-tuple-element.476), kind=kOutput, calls=%fused_computation.3.clone.1 | convolution fusion | flops 3228041728 | bytes 7350272 | tf_op jit(solution)/shard_map/while/body/eval_jaxpr/dot_general | solution.py:10
  211.1 1.1 constant_dynamic-update-slice_fusion.2
  212.7 5.7 %convolution_bitcast_fusion.6 = f32[1026,256]{1,0:T(8,128)S(1)} fusion(f32[1026,1024]{1,0:T(8,128)} %get-tuple-element.519, f32[4096,256]{1,0:T(8,128)} %get-tuple-element.518, s32[]{:T(128)S(6)} %select_n.167), kind=kOutput, calls=%fused_computation.1.clone.1 | convolution fusion | flops 3227516928 | bytes 6326276 | tf_op jit(solution)/shard_map/while/body/eval_jaxpr/dot_general | solution.py:10
  218.4 1.6 multiply_add_fusion.5
  220.0 5.7 %convolution_bitcast_fusion.7 = f32[1026,256]{1,0:T(8,128)S(1)} fusion(f32[1026,1024]{1,0:T(8,128)} %get-tuple-element.519, f32[4096,256]{1,0:T(8,128)} %get-tuple-element.518, s32[]{:T(128)S(6)} %select_n.168), kind=kOutput, calls=%fused_computation.clone.1 | convolution fusion | flops 3227516928 | bytes 6326276 | tf_op jit(solution)/shard_map/while/body/eval_jaxpr/dot_general | solution.py:10
  225.7 1.6 multiply_add_fusion.6
  228.2 1.0 copy-done.3
  229.5 1.3 constant_dynamic-slice_fusion.2
  231.1 9.8 %fusion.98 = f32[1024,256]{0,1:T(8,128)S(1)} fusion(f32[1024,256]{0,1:T(8,128)S(1)} %copy.19, f32[1024,1026]{1,0:T(8,128)} %get-tuple-element.523, f32[513,256]{1,0:T(8,128)S(1)} %get-tuple-element.475, f32[513,256]{1,0:T(8,128)S(1)} %get-tuple-element.476), kind=kOutput, calls=%fused_computation.3.clone.1 | convolution fusion | flops 3228041728 | bytes 7350272 | tf_op jit(solution)/shard_map/while/body/eval_jaxpr/dot_general | solution.py:10
  241.3 1.1 constant_dynamic-update-slice_fusion.2
  242.9 5.7 %convolution_bitcast_fusion.6 = f32[1026,256]{1,0:T(8,128)S(1)} fusion(f32[1026,1024]{1,0:T(8,128)} %get-tuple-element.519, f32[4096,256]{1,0:T(8,128)} %get-tuple-element.518, s32[]{:T(128)S(6)} %select_n.167), kind=kOutput, calls=%fused_computation.1.clone.1 | convolution fusion | flops 3227516928 | bytes 6326276 | tf_op jit(solution)/shard_map/while/body/eval_jaxpr/dot_general | solution.py:10
  248.6 1.6 multiply_add_fusion.5
  250.2 5.7 %convolution_bitcast_fusion.7 = f32[1026,256]{1,0:T(8,128)S(1)} fusion(f32[1026,1024]{1,0:T(8,128)} %get-tuple-element.519, f32[4096,256]{1,0:T(8,128)} %get-tuple-element.518, s32[]{:T(128)S(6)} %select_n.168), kind=kOutput, calls=%fused_computation.clone.1 | convolution fusion | flops 3227516928 | bytes 6326276 | tf_op jit(solution)/shard_map/while/body/eval_jaxpr/dot_general | solution.py:10
  256.0 1.6 multiply_add_fusion.6
  259.8 1.3 constant_dynamic-slice_fusion.2
  261.4 9.8 %fusion.98 = f32[1024,256]{0,1:T(8,128)S(1)} fusion(f32[1024,256]{0,1:T(8,128)S(1)} %copy.19, f32[1024,1026]{1,0:T(8,128)} %get-tuple-element.523, f32[513,256]{1,0:T(8,128)S(1)} %get-tuple-element.475, f32[513,256]{1,0:T(8,128)S(1)} %get-tuple-element.476), kind=kOutput, calls=%fused_computation.3.clone.1 | convolution fusion | flops 3228041728 | bytes 7350272 | tf_op jit(solution)/shard_map/while/body/eval_jaxpr/dot_general | solution.py:10
  271.6 1.0 constant_dynamic-update-slice_fusion.2
  273.2 5.7 %convolution_bitcast_fusion.6 = f32[1026,256]{1,0:T(8,128)S(1)} fusion(f32[1026,1024]{1,0:T(8,128)} %get-tuple-element.519, f32[4096,256]{1,0:T(8,128)} %get-tuple-element.518, s32[]{:T(128)S(6)} %select_n.167), kind=kOutput, calls=%fused_computation.1.clone.1 | convolution fusion | flops 3227516928 | bytes 6326276 | tf_op jit(solution)/shard_map/while/body/eval_jaxpr/dot_general | solution.py:10
  278.9 1.6 multiply_add_fusion.5
  280.5 5.7 %convolution_bitcast_fusion.7 = f32[1026,256]{1,0:T(8,128)S(1)} fusion(f32[1026,1024]{1,0:T(8,128)} %get-tuple-element.519, f32[4096,256]{1,0:T(8,128)} %get-tuple-element.518, s32[]{:T(128)S(6)} %select_n.168), kind=kOutput, calls=%fused_computation.clone.1 | convolution fusion | flops 3227516928 | bytes 6326276 | tf_op jit(solution)/shard_map/while/body/eval_jaxpr/dot_general | solution.py:10
  286.2 1.6 multiply_add_fusion.6
  290.0 1.3 constant_dynamic-slice_fusion.2
  291.7 9.8 %fusion.98 = f32[1024,256]{0,1:T(8,128)S(1)} fusion(f32[1024,256]{0,1:T(8,128)S(1)} %copy.19, f32[1024,1026]{1,0:T(8,128)} %get-tuple-element.523, f32[513,256]{1,0:T(8,128)S(1)} %get-tuple-element.475, f32[513,256]{1,0:T(8,128)S(1)} %get-tuple-element.476), kind=kOutput, calls=%fused_computation.3.clone.1 | convolution fusion | flops 3228041728 | bytes 7350272 | tf_op jit(solution)/shard_map/while/body/eval_jaxpr/dot_general | solution.py:10
  301.8 1.1 constant_dynamic-update-slice_fusion.2
  303.5 11.6 %sine_multiply_fusion.1 = (f32[512,513]{1,0:T(8,128)S(1)}, f32[512,513]{1,0:T(8,128)S(1)}, f32[512,513]{1,0:T(8,128)}, f32[512,513]{1,0:T(8,128)S(1)}) fusion(f32[513]{0:T(1024)S(1)} %fusion.73, s32[512]{0:T(512)S(1)} %iota_add_fusion, f32[513]{0:T(1024)S(1)} %select_multiply_fusion), kind=kLoop, calls=%fused_computation.83 | loop fusion | flops 8404992 | bytes 4208648 | tf_op jit(solution)/shard_map/mul | solution.py:29
  315.2 3.4 multiply_reduce_fusion
  318.6 9.7 %psum.7 = f32[256]{0:T(256)} all-reduce(f32[256]{0:T(256)S(1)} %get-tuple-element.376), channel_id=1, replica_groups=mesh['groups'=2,'ctx'=4,'chan'=4] {'ctx'}, use_global_device_ids=true, to_apply=%region_4.5 | all-reduce | flops 256 | bytes 2048 | tf_op jit(solution)/shard_map/psum | solution.py:110
  328.3 4.6 %fusion.54 = f32[512,256]{1,0:T(8,128)} fusion(f32[512,256]{1,0:T(8,128)S(1)} %copy-done.9, f32[1026,256]{1,0:T(8,128)S(1)} %copy-done.7, f32[512,513]{1,0:T(8,128)S(1)} %get-tuple-element.382, f32[512,513]{1,0:T(8,128)} %get-tuple-element.390, f32[256]{0:T(256)S(1)} %copy-done.16, f32[512,256]{1,0:T(8,128)S(1)} %copy-done.11, f32[512,256]{1,0:T(8,128)} %param.10), kind=kOutput, calls=%fused_computation.95 | convolution fusion | flops 1614808064 | bytes 5250048 | tf_op jit(solution)/shard_map/dot_general | solution.py:10
  333.0 46.2 %reduce-scatter.2.cloned.1.call-done = f32[1024,256]{1,0:T(8,128)} async-done(((f32[4096,256]{1,0:T(8,128)}), f32[1024,256]{1,0:T(8,128)}) %reduce-scatter.2.cloned.1.call-update) | async-done | bytes 1048592 | tf_op jit(solution)/shard_map/reduce_scatter | solution.py:104
  (84 shorter events, 12.1 us)
Async XLA Ops:
  7.2 4.3 %copy-start.10 = (f32[512,256]{1,0:T(8,128)S(1)}, f32[512,256]{1,0:T(8,128)}, u32[]{:S(2)}) copy-start(f32[512,256]{1,0:T(8,128)} %param.9) | copy-start | bytes 1572868
  7.2 4.3 %copy-start.12 = (f32[512,256]{1,0:T(8,128)S(1)}, f32[512,256]{1,0:T(8,128)}, u32[]{:S(2)}) copy-start(f32[512,256]{1,0:T(8,128)} %param.10) | copy-start | bytes 1572868
  7.2 91.3 %all-gather.7.cloned.1.call-start = ((), (), s32[]{:S(2)}) async-start(), calls=%async_computation.2 | async-start | bytes 5283840 | tf_op jit(solution)/shard_map/all_gather | solution.py:95
  14.3 4.6 %copy-start.8 = (f32[512,256]{1,0:T(8,128)S(1)}, f32[512,256]{1,0:T(8,128)}, u32[]{:S(2)}) copy-start(f32[512,256]{1,0:T(8,128)} %param.13) | copy-start | bytes 1572868
  14.3 4.6 %copy-start.14 = (f32[512,256]{1,0:T(8,128)S(1)}, f32[512,256]{1,0:T(8,128)}, u32[]{:S(2)}) copy-start(f32[512,256]{1,0:T(8,128)} %param.8) | copy-start | bytes 1572868
  14.3 165.6 %all-gather.9.cloned.1.call-start = ((), (), s32[]{:S(2)}) async-start(), calls=%async_computation.3 | async-start | bytes 5283840 | tf_op jit(solution)/shard_map/all_gather | solution.py:96
  21.8 357.4 %reduce-scatter.2.cloned.1.call-start = ((), (), s32[]{:S(2)}) async-start(), calls=%async_computation.1 | async-start | bytes 5242880 | tf_op jit(solution)/shard_map/reduce_scatter | solution.py:104
  47.9 134.2 %copy-start = (f32[1026,256]{1,0:T(8,128)S(1)}, f32[1026,256]{1,0:T(8,128)}, u32[]{:S(2)}) copy-start(f32[1026,256]{1,0:T(8,128)} %fusion.32) | copy-start | bytes 3151876
  195.4 1.6 copy-start.2
  195.4 1.9 copy-start.5
  197.9 1.0 copy-start.3
  197.9 1.3 copy-start.6
  211.1 1.6 copy-start.1
  225.7 1.6 copy-start.2
  225.7 1.9 copy-start.5
  228.2 1.0 copy-start.3
  228.2 1.3 copy-start.6
  241.3 1.6 copy-start.1
  255.9 1.6 copy-start.2
  255.9 1.9 copy-start.5
  258.4 1.0 copy-start.3
  258.4 1.3 copy-start.6
  271.6 1.6 copy-start.1
  286.2 1.6 copy-start.2
  286.2 1.9 copy-start.5
  288.7 1.0 copy-start.3
  288.7 1.3 copy-start.6
  301.8 1.6 copy-start.1
  303.5 11.7 %copy-start.4 = (f32[1026,256]{1,0:T(8,128)S(1)}, f32[1026,256]{1,0:T(8,128)}, u32[]{:S(2)}) copy-start(f32[1026,256]{1,0:T(8,128)} %get-tuple-element.538) | copy-start | bytes 3151876
  303.5 11.7 %copy-start.9 = (f32[512,256]{1,0:T(8,128)S(1)}, f32[512,256]{1,0:T(8,128)}, u32[]{:S(2)}) copy-start(f32[512,256]{1,0:T(8,128)} %param.13) | copy-start | bytes 1572868
  303.5 11.7 %copy-start.11 = (f32[512,256]{1,0:T(8,128)S(1)}, f32[512,256]{1,0:T(8,128)}, u32[]{:S(2)}) copy-start(f32[512,256]{1,0:T(8,128)} %param.9) | copy-start | bytes 1572868
  303.5 11.7 %copy-start.13 = (f32[512,256]{1,0:T(8,128)S(1)}, f32[512,256]{1,0:T(8,128)}, u32[]{:S(2)}) copy-start(f32[512,256]{1,0:T(8,128)} %param.10) | copy-start | bytes 1572868
  303.5 11.7 %copy-start.15 = (f32[512,256]{1,0:T(8,128)S(1)}, f32[512,256]{1,0:T(8,128)}, u32[]{:S(2)}) copy-start(f32[512,256]{1,0:T(8,128)} %param.8) | copy-start | bytes 1572868
  303.5 11.7 %copy-start.16 = (f32[256]{0:T(256)S(1)}, f32[256]{0:T(256)}, u32[]{:S(2)}) copy-start(f32[256]{0:T(256)} %param.12) | copy-start | bytes 3076
  315.2 13.1 %copy-start.7 = (f32[1026,256]{1,0:T(8,128)S(1)}, f32[1026,256]{1,0:T(8,128)}, u32[]{:S(2)}) copy-start(f32[1026,256]{1,0:T(8,128)} %get-tuple-element.537) | copy-start | bytes 3151876
Sparse Core Ops, SparseCore 0:
  14.4 83.9 all-gather.6
  100.0 79.8 all-gather.8
  303.6 75.5 reduce-scatter.1
where the time goes:
time: 392 us; the launch traced here: 386 us
  waiting for transfers between devices  178 us (45%)
  matrix products  98.5 us (25%)
  other arithmetic  59.7 us (15%)
  local copies, waits for them, and re-layouts  22.8 us (6%)
  between operations  14.2 us (4%)
  blocking collectives  9.74 us (2%)
    dot_general x16, matrix products, matmul(): jnp.dot(left, right, preferred_element_type=jnp.float32, precision=lax.Pr...  98.5 us
    all_gather x1, waiting for transfers between devices, local(): lax.all_gather(own_grad_spec[None], 'ctx', axis=0, tiled=True)  81.4 us
    all_gather x1, waiting for transfers between devices, local(): lax.all_gather(own_gated_spec[None], 'ctx', axis=0, tiled=True)  50.5 us
    reduce_scatter x1, waiting for transfers between devices, local(): lax.psum_scatter(partial_value, 'ctx', scatter_dimension=0, tiled=True)  46.2 us
    mul x2, other arithmetic, inverse_table(): -weights * jnp.sin(angles)  22.2 us
    add x8, other arithmetic, conj_times(): real_a * real_b + imag_a * imag_b  12.8 us
    neg x2, other arithmetic, forward_table(): return jnp.concatenate([jnp.cos(angles), -jnp.sin(angles)], axis=0)  12.5 us
    psum x1, blocking collectives, local(): skip_grad = lax.psum(jnp.sum(mixed_grad * gated, axis=0), 'ctx')  9.74 us
  transfers between devices with their start and end apart: 3, of which 3 were waited for; matrix products, arithmetic and copies ran while one was open for 13% of the time, Pallas kernels for 0%

commit v1 on v0

--- a/solution.py
+++ b/solution.py
@@ -1,9 +1,407 @@
+import functools
 import math
 
 import jax
 import jax.numpy as jnp
+import ml_dtypes
+import numpy as np
 from jax import lax
+from jax.experimental import pallas as pl
+from jax.experimental.pallas import tpu as pltpu
 from jax.sharding import PartitionSpec as P
+
+COS1, SIN1, HALF = math.cos(math.pi / 8), math.sin(math.pi / 8), math.sqrt(0.5)
+
+
+def split_np(table):
+    high = table.astype(ml_dtypes.bfloat16)
+    low = (table - high.astype(np.float64)).astype(ml_dtypes.bfloat16)
+    return np.stack([high, low])
+
+
+def tables(seg):
+    sub = seg // 4
+    bins, pos = np.arange(sub)[:, None], np.arange(sub)[None, :]
+    forward = []
+    for group in range(4):
+        angle = 2 * np.pi * pos * (8 * bins + group + 0.5) / (2 * seg)
+        cos, sin = np.cos(angle), np.sin(angle)
+        forward.append(np.block([[cos, -sin], [-sin, -cos]]))
+    forward = np.stack(forward)
+    inverse = forward.transpose(0, 2, 1) / seg
+    return split_np(forward), split_np(inverse)
+
+
+def split(x):
+    high = x.astype(jnp.bfloat16)
+    return high, (x - high.astype(jnp.float32)).astype(jnp.bfloat16)
+
+
+def dot3(table_ref, group, high, low):
+    t_high, t_low = table_ref[0, group], table_ref[1, group]
+    dot = functools.partial(jnp.dot, preferred_element_type=jnp.float32)
+    return dot(t_high, high) + dot(t_high, low) + dot(t_low, high)
+
+
+def spread(x):
+    sub = x.shape[0] // 4
+    x0, x1, x2, x3 = (x[i * sub : (i + 1) * sub] for i in range(4))
+    u, p, s, q, t = HALF * x2, COS1 * x1, SIN1 * x1, COS1 * x3, SIN1 * x3
+    a, b, pt, sq, pmt, spq = x0 + u, x0 - u, p + t, s - q, p - t, s + q
+    pairs = ((a + pt, spq + u), (b + sq, pmt + u), (b - sq, pmt - u), (a - pt, spq - u))
+    return [jnp.concatenate(pair, axis=0) for pair in pairs]
+
+
+def gather_quarters(re, im):
+    e03, d03, e12, d12 = re[0] + re[3], re[0] - re[3], re[1] + re[2], re[1] - re[2]
+    f03, g03, f12, g12 = im[0] + im[3], im[0] - im[3], im[1] + im[2], im[1] - im[2]
+    return (
+        e03 + e12,
+        COS1 * (d03 + f12) + SIN1 * (d12 + f03),
+        HALF * (e03 - e12 + g03 + g12),
+        SIN1 * (d03 - f12) + COS1 * (f03 - d12),
+    )
+
+
+def transform(x, table_ref, store):
+    for group, part in enumerate(spread(x)):
+        store(group, dot3(table_ref, group, *split(part)))
+
+
+def dft_kernel(table_ref, x_ref, out_ref):
+    rows = out_ref.shape[1] // 4
+
+    def store(group, value):
+        out_ref[0, group * rows : (group + 1) * rows, :] = value
+
+    transform(x_ref[...], table_ref, store)
+
+
+def cost(flops, nbytes):
+    return pl.CostEstimate(flops=int(flops), bytes_accessed=int(nbytes), transcendentals=0)
+
+
+VMEM_LIMIT = 48 << 20
+
+
+def params():
+    return pltpu.CompilerParams(vmem_limit_bytes=VMEM_LIMIT)
+
+
+def whole_spec(shape):
+    return pl.BlockSpec(shape, lambda *_: (0,) * len(shape))
+
+
+def dft(table, x, seg):
+    width = x.shape[1]
+    blocks = x.shape[0] // seg
+    return pl.pallas_call(
+        dft_kernel,
+        grid=(blocks,),
+        in_specs=[whole_spec(table.shape), pl.BlockSpec((seg, width), lambda i: (i, 0))],
+        out_specs=pl.BlockSpec((1, 2 * seg, width), lambda i: (i, 0, 0)),
+        out_shape=jax.ShapeDtypeStruct((blocks, 2 * seg, width), jnp.float32),
+        compiler_params=params(),
+        cost_estimate=cost(blocks * 3 * seg * seg * width * 2, blocks * 12 * seg * width),
+        name="dft",
+    )(table, x)
+
+
+def taps_kernel(table_ref, x_ref, out_ref, last_ref):
+    step = pl.program_id(0)
+    rows = out_ref.shape[1] // 4
+    sub = rows // 2
+
+    def store(group, value):
+        base = group * rows
+        sign = 1.0 if group % 2 == 0 else -1.0
+        re, im = slice(base, base + sub), slice(base + sub, base + rows)
+        out_ref[0, re, :] = value[:sub] - sign * last_ref[im, :]
+        out_ref[0, im, :] = value[sub:] + sign * last_ref[re, :]
+        last_ref[base : base + rows, :] = value
+
+    @pl.when(step == 0)
+    def _():
+        last_ref[...] = jnp.zeros_like(last_ref)
+
+    transform(x_ref[...], table_ref, store)
+
+
+def taps_spectra(table, taps, seg):
+    width = taps.shape[1]
+    blocks = taps.shape[0] // seg
+    return pl.pallas_call(
+        taps_kernel,
+        grid=(blocks,),
+        in_specs=[whole_spec(table.shape), pl.BlockSpec((seg, width), lambda i: (i, 0))],
+        out_specs=pl.BlockSpec((1, 2 * seg, width), lambda i: (jnp.maximum(i - 1, 0), 0, 0)),
+        out_shape=jax.ShapeDtypeStruct((blocks - 1, 2 * seg, width), jnp.float32),
+        scratch_shapes=[pltpu.VMEM((2 * seg, width), jnp.float32)],
+        compiler_params=params(),
+        cost_estimate=cost(blocks * 3 * seg * seg * width * 2, blocks * 12 * seg * width),
+        name="taps",
+    )(table, taps)
+
+
+def conj_mul(a, b):
+    return a[0] * b[0] + a[1] * b[1], a[0] * b[1] - a[1] * b[0]
+
+
+def mul(a, b):
+    return a[0] * b[0] - a[1] * b[1], a[0] * b[1] + a[1] * b[0]
+
+
+def add(a, b):
+    return a[0] + b[0], a[1] + b[1]
+
+
+def partial_kernel(pos_ref, table_ref, inverse_ref, win_near, win_far, near_ref, x_ref, far_ref, out_ref, z_ref):
+    rows = far_ref.shape[0] // 4
+    sub = rows // 2
+    for group, part in enumerate(spread(x_ref[...])):
+        base = group * rows
+        far = dot3(table_ref, group, *split(part))
+        far_ref[base : base + rows, :] = far
+        re, im = slice(base, base + sub), slice(base + sub, base + rows)
+        near = (near_ref[0, re, :], near_ref[0, im, :])
+        total = add(
+            conj_mul((win_near[0, re, :], win_near[0, im, :]), near),
+            conj_mul((win_far[0, re, :], win_far[0, im, :]), (far[:sub], far[sub:])),
+        )
+        z_ref[group] = dot3(inverse_ref, group, *split(jnp.concatenate(total, axis=0)))
+    quarters = gather_quarters([z_ref[g, :sub] for g in range(4)], [z_ref[g, sub:] for g in range(4)])
+    for i, quarter in enumerate(quarters):
+        out_ref[i * sub : (i + 1) * sub, :] = quarter
+
+
+def back_partial(pos, table, inverse, windows, near, x, seg):
+    width = x.shape[1]
+    n = (windows.shape[0] + 1) // 2
+    block = (1, 2 * seg, width)
+
+    def window(distance):
+        return pl.BlockSpec(block, lambda i, pos: (jnp.where(pos[0] == 1, n - 1 + distance, n - 1 - distance), 0, 0))
+
+    return pl.pallas_call(
+        partial_kernel,
+        grid_spec=pltpu.PrefetchScalarGridSpec(
+            num_scalar_prefetch=1,
+            grid=(1,),
+            in_specs=[
+                whole_spec(table.shape),
+                whole_spec(inverse.shape),
+                window(2),
+                window(3),
+                pl.BlockSpec(block, lambda i, pos: (jnp.where(pos[0] == 1, 3, 1), 0, 0)),
+                whole_spec((seg, width)),
+            ],
+            out_specs=[whole_spec((2 * seg, width)), whole_spec((seg, width))],
+            scratch_shapes=[pltpu.VMEM((4, seg // 2, width), jnp.float32)],
+        ),
+        out_shape=[
+            jax.ShapeDtypeStruct((2 * seg, width), jnp.float32),
+            jax.ShapeDtypeStruct((seg, width), jnp.float32),
+        ],
+        compiler_params=params(),
+        cost_estimate=cost(6 * seg * seg * width * 2, 24 * seg * width),
+        name="partial",
+    )(pos, table, inverse, windows, windows, near, x)
+
+
+OWN, LEFT, RIGHT, TWO, THREE = range(5)
+PAIRS = (
+    ((), ((OWN, THREE),), ((OWN, TWO), (RIGHT, THREE))),
+    (
+        ((LEFT, RIGHT), (OWN, TWO)),
+        ((LEFT, OWN), (OWN, RIGHT), (RIGHT, TWO)),
+        ((LEFT, LEFT), (OWN, OWN), (RIGHT, RIGHT), (TWO, TWO)),
+    ),
+    (
+        ((TWO, TWO), (LEFT, LEFT), (OWN, OWN), (RIGHT, RIGHT)),
+        ((LEFT, TWO), (OWN, LEFT), (RIGHT, OWN)),
+        ((OWN, TWO), (RIGHT, LEFT)),
+    ),
+    (((LEFT, THREE), (OWN, TWO)), ((OWN, THREE),), ()),
+)
+
+
+def final_kernel(
+    pos_ref, inverse_ref, win_ref, own_ref, near_ref, two_g, two_m, three_g, gm_ref, skip_ref, up_ref,
+    query_out, filter_out, back_out, x_high, x_low, z_ref,
+):
+    group = pl.program_id(0)
+    pos = pos_ref[0]
+    rows = own_ref.shape[1]
+    sub = rows // 2
+    width = own_ref.shape[2]
+    seg = 4 * sub
+    mid = win_ref.shape[0] // 2
+    sign = jnp.where(group % 2 == 0, 1.0, -1.0)
+    step = 8
+    two_off = jnp.where(pos < 2, -2, 2)
+    three_off = jnp.where(pos == 0, -3, 3)
+
+    def put(slot, tile, value):
+        for half in range(2):
+            high, low = split(value[half])
+            at = pl.ds(pl.multiple_of(half * sub + tile * step * 2, 16), 2 * step)
+            x_high[at, slot * width : (slot + 1) * width] = high
+            x_low[at, slot * width : (slot + 1) * width] = low
+
+    def tiles(tile):
+        re = pl.ds(pl.multiple_of(tile * step * 2, 16), 2 * step)
+        im = pl.ds(pl.multiple_of(sub + tile * step * 2, 16), 2 * step)
+
+        def read(ref, *lead):
+            return ref[(*lead, re, slice(None))], ref[(*lead, im, slice(None))]
+
+        gated = (
+            lambda: read(own_ref, 0), lambda: read(near_ref, 0), lambda: read(near_ref, 2),
+            lambda: read(two_g, 0), lambda: read(three_g, 0),
+        )
+        mixed = (lambda: read(own_ref, 1), lambda: read(near_ref, 1), lambda: read(near_ref, 3), lambda: read(two_m))
+        return read, gated, mixed
+
+    def sums(tile, _):
+        read, gated, mixed = tiles(tile)
+        conv = mul(read(win_ref, mid), gated[OWN]())
+        conv = add(conv, mul(read(win_ref, mid + 1), gated[LEFT]()))
+        conv = add(conv, mul(read(win_ref, mid - 1), gated[RIGHT]()))
+        conv = add(conv, mul(read(win_ref, mid + two_off), gated[TWO]()))
+        conv = add(conv, mul(read(win_ref, mid + three_off), gated[THREE]()))
+        put(0, tile, conv)
+        back = conj_mul(read(win_ref, mid), mixed[OWN]())
+        back = add(back, conj_mul(read(win_ref, mid - 1), mixed[LEFT]()))
+        back = add(back, conj_mul(read(win_ref, mid + 1), mixed[RIGHT]()))
+        back = add(back, conj_mul(read(win_ref, mid - two_off), mixed[TWO]()))
+        put(1, tile, back)
+        return _
+
+    count = sub // (2 * step)
+    lax.fori_loop(0, count, sums, 0)
+
+    for where, distances in enumerate(PAIRS):
+
+        @pl.when(pos == where)
+        def _():
+            def lags(tile, _):
+                read, gated, mixed = tiles(tile)
+                total = []
+                for pairs in distances:
+                    value = None
+                    for m, g in pairs:
+                        term = conj_mul(gated[g](), mixed[m]())
+                        value = term if value is None else add(value, term)
+                    total.append(value)
+                for slot in range(2):
+                    low, high = total[slot], total[slot + 1]
+                    if high is None:
+                        value = low
+                    else:
+                        turned = (sign * high[1], -sign * high[0])
+                        value = turned if low is None else add(low, turned)
+                    put(2 + slot, tile, value)
+                return _
+
+            lax.fori_loop(0, count, lags, 0)
+
+    dot = functools.partial(jnp.dot, preferred_element_type=jnp.float32)
+    t_high, t_low = inverse_ref[0, 0], inverse_ref[1, 0]
+    for slot in range(4):
+        cols = slice(slot * width, (slot + 1) * width)
+        z_ref[group, :, cols] = (
+            dot(t_high, x_high[:, cols]) + dot(t_high, x_low[:, cols]) + dot(t_low, x_high[:, cols])
+        )
+
+    @pl.when(group == 3)
+    def _():
+        for slot in range(4):
+            cols = slice(slot * width, (slot + 1) * width)
+            quarters = gather_quarters(
+                [z_ref[g, :sub, cols] for g in range(4)], [z_ref[g, sub:, cols] for g in range(4)]
+            )
+            for i, quarter in enumerate(quarters):
+                at = slice(i * sub, (i + 1) * sub)
+                if slot == 0:
+                    query_out[at, :] = up_ref[at, :] * (quarter + skip_ref[...] * gm_ref[at, :])
+                elif slot == 1:
+                    back_out[at, :] = quarter + skip_ref[...] * gm_ref[seg + i * sub : seg + (i + 1) * sub, :]
+                else:
+                    base = (slot - 2) * seg + i * sub
+                    filter_out[base : base + sub, :] = quarter
+
+
+def final(pos, inverse, windows, own, near, two_g, two_m, three_g, gm, skip, upstream, seg):
+    width = gm.shape[1]
+    rows = seg // 2
+
+    def groups(lead):
+        return pl.BlockSpec((lead, rows, width), lambda i, pos: (0, i, 0))
+
+    return pl.pallas_call(
+        final_kernel,
+        grid_spec=pltpu.PrefetchScalarGridSpec(
+            num_scalar_prefetch=1,
+            grid=(4,),
+            in_specs=[
+                pl.BlockSpec((2, 1, rows, rows), lambda i, pos: (0, i, 0, 0)),
+                groups(windows.shape[0]),
+                groups(2),
+                groups(4),
+                groups(1),
+                pl.BlockSpec((rows, width), lambda i, pos: (i, 0)),
+                groups(1),
+                whole_spec((2 * seg, width)),
+                whole_spec((1, width)),
+                whole_spec((seg, width)),
+            ],
+            out_specs=[whole_spec((seg, width)), whole_spec((2 * seg, width)), whole_spec((seg, width))],
+            scratch_shapes=[
+                pltpu.VMEM((rows, 4 * width), jnp.bfloat16),
+                pltpu.VMEM((rows, 4 * width), jnp.bfloat16),
+                pltpu.VMEM((4, rows, 4 * width), jnp.float32),
+            ],
+        ),
+        out_shape=[
+            jax.ShapeDtypeStruct((seg, width), jnp.float32),
+            jax.ShapeDtypeStruct((2 * seg, width), jnp.float32),
+            jax.ShapeDtypeStruct((seg, width), jnp.float32),
+        ],
+        compiler_params=params(),
+        cost_estimate=cost(12 * seg * seg * width * 2, 150 * seg * width),
+        name="final",
+    )(pos, inverse, windows, own, near, two_g, two_m, three_g, gm, skip, upstream)
+
+
+def local_line(query_gate, key_gate, values, filter_taps, skip_gain, upstream):
+    seg, width = values.shape
+    forward_np, inverse_np = tables(seg)
+    table, inverse = jnp.asarray(forward_np), jnp.asarray(inverse_np)
+    position = lax.axis_index("ctx")
+    pos = position.astype(jnp.int32).reshape(1)
+    gm = jnp.concatenate([key_gate * values, upstream * query_gate], axis=0)
+    skip_grad = lax.psum(jnp.sum(gm[:seg] * gm[seg:], axis=0), "ctx")
+    from_left = lax.ppermute(gm, "ctx", [(0, 1), (1, 2), (2, 3)])
+    from_right = lax.ppermute(gm, "ctx", [(1, 0), (2, 1), (3, 2)])
+    windows = taps_spectra(table, filter_taps, seg)
+    own = dft(table, gm, seg)
+    two_g = lax.ppermute(from_left[:seg], "ctx", [(1, 2), (2, 3)]) + lax.ppermute(
+        from_right[:seg], "ctx", [(2, 1), (1, 0)]
+    )
+    far_m = jnp.where(position == 1, from_left[seg:], from_right[seg:])
+    near = dft(table, jnp.concatenate([from_left, from_right], axis=0), seg)
+    far_m, two_g = lax.optimization_barrier((far_m, two_g))
+    three_g = lax.ppermute(two_g, "ctx", [(1, 0), (2, 3)])
+    two_m = lax.ppermute(far_m, "ctx", [(1, 2), (2, 1)])
+    two_g = dft(table, two_g, seg)
+    two_m, partial = back_partial(pos, table, inverse, windows, near, two_m, seg)
+    partial = lax.ppermute(partial, "ctx", [(1, 0), (2, 3)])
+    three_g = dft(table, three_g, seg)
+    query_grad, filter_grad, back = final(
+        pos, inverse, windows, own, near, two_g, two_m, three_g, gm, skip_gain[None, :], upstream, seg
+    )
+    back = back + partial
+    return (query_grad, back * values, back * key_gate, filter_grad, skip_grad)
 
 
 def matmul(left, right):
@@ -127,4 +525,5 @@
         P(("groups", "ctx"), "chan"),
         P(("groups", "chan")),
     )
-    return jax.shard_map(local, mesh=mesh, in_specs=in_specs, out_specs=out_specs, check_vma=False)
+    body = local_line if mesh.shape["ctx"] == 4 else local
+    return jax.shard_map(body, mesh=mesh, in_specs=in_specs, out_specs=out_specs, check_vma=False)

time: 392 us -> 112 us (0.29); the launches traced: 386 us -> 111 us
  waiting for transfers between devices: 178 us -> 34.9 us
  matrix products: 98.5 us -> 0 us
  other arithmetic: 59.7 us -> 7.48 us
  Pallas kernels: 0 us -> 31.4 us
  local copies, waits for them, and re-layouts: 22.8 us -> 2.45 us
  between operations: 14.2 us -> 0.83 us
  starting transfers between devices: 2.14 us -> 13.3 us
  blocking collectives: 9.74 us -> 20.8 us
    all_gather x2 -> x0, waiting for transfers between devices: 132 us -> none  [the longest x1 81.4 us: local(): lax.all_gather(own_grad_spec[None], 'ctx', axis=0, tiled=True)]
    dot_general x16 -> x0, matrix products: 98.5 us -> none  [matmul(): jnp.dot(left, right, preferred_element_type=jnp.float32, precision=lax.Pr...]
    reduce_scatter x1 -> x0, waiting for transfers between devices: 46.2 us -> none  [local(): lax.psum_scatter(partial_value, 'ctx', scatter_dimension=0, tiled=True)]
    ppermute x0 -> x7, waiting for transfers between devices: none -> 34.9 us  [the longest x1 20.2 us: local_line(): from_right = lax.ppermute(gm, 'ctx', [(1, 0), (2, 1), (3, 2)])]
    pallas_call x0 -> x7, Pallas kernels: none -> 31.4 us  [the longest x1 10.2 us: final(): pl.pallas_call(final_kernel, grid_spec=pltpu.PrefetchScalarGridSpec(num_s...]
    mul x2 -> x1, other arithmetic: 22.2 us -> 2.14 us  [local_line(): return (query_grad, back * values, back * key_gate, filter_grad, skip_grad)]
    add x13 -> x1, other arithmetic: 15.3 us -> 0.86 us  [local_line(): lax.ppermute(from_left[:seg], 'ctx', [(1, 2), (2, 3)])]
    ppermute x0 -> x7, starting transfers between devices: none -> 13.3 us  [the longest x1 6.6 us: local_line(): from_left = lax.ppermute(gm, 'ctx', [(0, 1), (1, 2), (2, 3)])]
  transfers between devices with their start and end apart: 3 -> 7, of which waited for: 3 -> 3; matrix products, arithmetic and copies ran while one was open for 13% -> 1% of each run, Pallas kernels for 0% -> 28%
where the time goes in v1:
time: 112 us; the launch traced here: 111 us
  waiting for transfers between devices  34.9 us (31%)
  Pallas kernels  31.4 us (28%)
  blocking collectives  20.8 us (19%)
  starting transfers between devices  13.3 us (12%)
  other arithmetic  7.48 us (7%)
  local copies, waits for them, and re-layouts  2.45 us (2%)
    psum x1, blocking collectives, local_line(): skip_grad = lax.psum(jnp.sum(gm[:seg] * gm[seg:], axis=0), 'ctx')  20.8 us
    ppermute x1, waiting for transfers between devices, local_line(): from_right = lax.ppermute(gm, 'ctx', [(1, 0), (2, 1), (3, 2)])  20.2 us
    ppermute x1, waiting for transfers between devices, local_line(): lax.ppermute(from_right[:seg], 'ctx', [(2, 1), (1, 0)])  13.5 us
    pallas_call x1, Pallas kernels, final(): pl.pallas_call(final_kernel, grid_spec=pltpu.PrefetchScalarGridSpec(num_s...  10.2 us
    pallas_call x4, Pallas kernels, dft(): pl.pallas_call(dft_kernel, grid=(blocks,), in_specs=[whole_spec(table.sha...  9.27 us
    pallas_call x1, Pallas kernels, taps_spectra(): pl.pallas_call(taps_kernel, grid=(blocks,), in_specs=[whole_spec(table.sh...  7.64 us
    ppermute x1, starting transfers between devices, local_line(): from_left = lax.ppermute(gm, 'ctx', [(0, 1), (1, 2), (2, 3)])  6.6 us
    pallas_call x1, Pallas kernels, back_partial(): pl.pallas_call(partial_kernel, grid_spec=pltpu.PrefetchScalarGridSpec(num...  4.2 us
  transfers between devices with their start and end apart: 7, of which 3 were waited for; matrix products, arithmetic and copies ran while one was open for 1% of the time, Pallas kernels for 28%

profile of v1, /device:TPU:0, one launch (start us, length us, event | category | flops | bytes accessed | tf_op | source)
XLA Modules:
  0.0 111.1 jit_solution(14595562089938505952)
XLA Ops:
  0.6 1.7 %multiply_reduce_fusion = (f32[256]{0:T(256)S(1)}, f32[512,256]{1,0:T(8,128)S(1)}, f32[512,256]{1,0:T(8,128)S(1)}) fusion(f32[512,256]{1,0:T(8,128)} %param.9, f32[512,256]{1,0:T(8,128)} %param.10, f32[512,256]{1,0:T(8,128)} %up_ref.1, f32[512,256]{1,0:T(8,128)} %param.8), kind=kLoop, calls=%fused_computation.3 | loop fusion | flops 524032 | bytes 3146752 | tf_op jit(solution)/shard_map/reduce_sum | solution.py:383
  2.3 0.1 pad_maximum_fusion.1.x_ref.gm_ref
  2.4 0.0 copy-start.1
  2.4 1.3 %collective-permute-start.1 = (f32[1024,256]{1,0:T(8,128)S(1)}, f32[1024,256]{1,0:T(8,128)S(1)}, u32[]{:S(2)}, u32[]{:S(2)}) collective-permute-start(f32[1024,256]{1,0:T(8,128)S(1)} %pad_maximum_fusion.1.x_ref.gm_ref), channel_id=1, source_target_pairs={{4,0},{8,4},{12,8},{5,1},{9,5},{13,9},{6,2},{10,6},{14,10},{7,3},{... | collective-permute-start | bytes 3145736 | tf_op jit(solution)/shard_map/ppermute | solution.py:385
  3.7 6.6 %collective-permute-start = (f32[1024,256]{1,0:T(8,128)S(1)}, f32[1024,256]{1,0:T(8,128)}, u32[]{:S(2)}, u32[]{:S(2)}) collective-permute-start(f32[1024,256]{1,0:T(8,128)S(1)} %pad_maximum_fusion.1.x_ref.gm_ref), channel_id=1, source_target_pairs={{0,4},{4,8},{8,12},{1,5},{5,9},{9,13},{2,6},{6,10},{10,14},{3,7},{... | collective-permute-start | bytes 3145736 | tf_op jit(solution)/shard_map/ppermute | solution.py:384
  10.3 0.0 copy-start
  10.3 0.0 copy-start.3
  10.3 20.2 %collective-permute-done.1 = f32[1024,256]{1,0:T(8,128)S(1)} collective-permute-done((f32[1024,256]{1,0:T(8,128)S(1)}, f32[1024,256]{1,0:T(8,128)S(1)}, u32[]{:S(2)}, u32[]{:S(2)}) %collective-permute-start.1) | collective-permute-done | bytes 1048608 | tf_op jit(solution)/shard_map/ppermute | solution.py:385
  30.5 1.2 %collective-permute-done = f32[1024,256]{1,0:T(8,128)} collective-permute-done((f32[1024,256]{1,0:T(8,128)S(1)}, f32[1024,256]{1,0:T(8,128)}, u32[]{:S(2)}, u32[]{:S(2)}) %collective-permute-start) | collective-permute-done | bytes 1048608 | tf_op jit(solution)/shard_map/ppermute | solution.py:384
  31.7 1.4 %fusion = (f32[512,256]{1,0:T(8,128)S(1)}, f32[512,256]{1,0:T(8,128)S(1)}, f32[512,256]{1,0:T(8,128)S(1)}) fusion(f32[1024,256]{1,0:T(8,128)S(1)} %collective-permute-done.1, f32[1024,256]{1,0:T(8,128)} %collective-permute-done, pred[]{:T(512)S(6)} %eq.3), kind=kLoop, calls=%fused_computation.6 | loop fusion | flops 131072 | bytes 3670017 | tf_op jit(solution)/shard_map/slice | solution.py:389
  33.0 1.3 %collective-permute-start.3 = (f32[512,256]{1,0:T(8,128)S(1)}, f32[512,256]{1,0:T(8,128)S(1)}, u32[]{:S(2)}, u32[]{:S(2)}) collective-permute-start(f32[512,256]{1,0:T(8,128)S(1)} %get-tuple-element.24), channel_id=1, source_target_pairs={{8,4},{4,0},{9,5},{5,1},{10,6},{6,2},{11,7},{7,3},{24,20},{20,16},... | collective-permute-start | bytes 1572872 | tf_op jit(solution)/shard_map/ppermute | solution.py:388
  34.3 0.7 collective-permute-start.2
  35.0 13.5 %collective-permute-done.3 = f32[512,256]{1,0:T(8,128)S(1)} collective-permute-done((f32[512,256]{1,0:T(8,128)S(1)}, f32[512,256]{1,0:T(8,128)S(1)}, u32[]{:S(2)}, u32[]{:S(2)}) %collective-permute-start.3) | collective-permute-done | bytes 524320 | tf_op jit(solution)/shard_map/ppermute | solution.py:388
  48.6 0.0 collective-permute-done.2
  48.6 0.9 add.8.x_ref
  49.4 0.7 collective-permute-start.4
  50.1 0.0 copy-done
  50.1 0.0 copy-done.3
  50.1 7.6 %taps.1.win_near.win_far.win_ref = f32[7,1024,256]{2,1,0:T(8,128)} custom-call(bf16[2,4,256,256]{3,2,1,0:T(8,128)(2,1)S(1)} %copy-done, f32[4096,256]{1,0:T(8,128)S(1)} %copy-done.3), custom_call_target="tpu_custom_call" | custom-call | flops 3221225472 | bytes 12582912 | tf_op jit(solution)/shard_map/taps/pallas_call | solution.py:133
  57.8 1.4 %pad_maximum_fusion.x_ref = f32[2048,256]{1,0:T(8,128)S(1)} fusion(f32[1024,256]{1,0:T(8,128)S(1)} %collective-permute-done.1, f32[1024,256]{1,0:T(8,128)} %collective-permute-done), kind=kLoop, calls=%fused_computation | loop fusion | flops 524288 | bytes 4194304 | tf_op jit(solution)/shard_map/concatenate | solution.py:392
  59.1 0.0 copy-start.4
  59.2 1.4 %collective-permute-start.5 = (f32[512,256]{1,0:T(8,128)}, f32[512,256]{1,0:T(8,128)}, u32[]{:S(2)}, u32[]{:S(2)}) collective-permute-start(f32[512,256]{1,0:T(8,128)} %add.8.x_ref), channel_id=1, source_target_pairs={{4,0},{8,12},{5,1},{9,13},{6,2},{10,14},{7,3},{11,15},{20,16},{24,... | collective-permute-start | bytes 1572872 | tf_op jit(solution)/shard_map/ppermute | solution.py:394
  60.6 4.2 %dft.5.near_ref = f32[4,1024,256]{2,1,0:T(8,128)} custom-call(bf16[2,4,256,256]{3,2,1,0:T(8,128)(2,1)S(1)} %copy-done, f32[2048,256]{1,0:T(8,128)S(1)} %pad_maximum_fusion.x_ref), custom_call_target="tpu_custom_call" | custom-call | flops 1610612736 | bytes 6291456 | tf_op jit(solution)/shard_map/dft/pallas_call | solution.py:98
  64.8 0.0 collective-permute-done.4.x_ref
  64.8 0.0 copy-done.4
  64.8 4.2 %partial.1 = (f32[1024,256]{1,0:T(8,128)S(1)}, f32[512,256]{1,0:T(8,128)}) custom-call(s32[1]{0:T(128)} %bitcast.pos_ref, bf16[2,4,256,256]{3,2,1,0:T(8,128)(2,1)S(1)} %copy-done, bf16[2,4,256,256]{3,2,1,0:T(8,128)(2,1)S(1)} %copy-done.4, f32[7,1024,256]{2,1,0:T(8,128)} %taps.1.win_near.win_far.win_ref, f32[7,1024,256]{2,1,0:T(8,128)} %taps.1.win_near.win_far.win_ref, ...), custom_call_target="tpu_custom_call" | custom-call | flops 805306368 | bytes 3145728 | tf_op jit(solution)/shard_map/partial/pallas_call | solution.py:185
  69.0 0.0 copy-start.6
  69.0 1.0 copy-done.6
  70.0 1.3 %collective-permute-start.6 = (f32[512,256]{1,0:T(8,128)}, f32[512,256]{1,0:T(8,128)}, u32[]{:S(2)}, u32[]{:S(2)}) collective-permute-start(f32[512,256]{1,0:T(8,128)} %get-tuple-element.17), channel_id=1, source_target_pairs={{4,0},{8,12},{5,1},{9,13},{6,2},{10,14},{7,3},{11,15},{20,16},{24,... | collective-permute-start | bytes 1572872 | tf_op jit(solution)/shard_map/ppermute | solution.py:398
  71.3 20.8 %psum.7 = f32[256]{0:T(256)} all-reduce(f32[256]{0:T(256)S(1)} %get-tuple-element.19), channel_id=1, replica_groups=mesh['groups'=2,'ctx'=4,'chan'=4] {'ctx'}, use_global_device_ids=true, to_apply=%region_1.0 | all-reduce | flops 256 | bytes 2048 | tf_op jit(solution)/shard_map/psum | solution.py:383
  92.1 0.0 copy-done.1
  92.1 1.4 %dft.4.own_ref = f32[2,1024,256]{2,1,0:T(8,128)S(1)} custom-call(bf16[2,4,256,256]{3,2,1,0:T(8,128)(2,1)S(1)} %copy-done, f32[1024,256]{1,0:T(8,128)S(1)} %pad_maximum_fusion.1.x_ref.gm_ref), custom_call_target="tpu_custom_call" | custom-call | flops 805306368 | bytes 3145728 | tf_op jit(solution)/shard_map/dft/pallas_call | solution.py:98
  93.6 0.0 copy-start.2
  93.6 1.4 %copy-done.2 = f32[2,1024,256]{2,1,0:T(8,128)} copy-done((f32[2,1024,256]{2,1,0:T(8,128)}, f32[2,1024,256]{2,1,0:T(8,128)S(1)}, u32[]{:S(2)}) %copy-start.2) | copy-done | bytes 2097176
  95.0 0.0 copy-start.5
  95.0 1.9 %dft.6.two_g = f32[1,1024,256]{2,1,0:T(8,128)S(1)} custom-call(bf16[2,4,256,256]{3,2,1,0:T(8,128)(2,1)S(1)} %copy-done, f32[512,256]{1,0:T(8,128)} %add.8.x_ref), custom_call_target="tpu_custom_call" | custom-call | flops 402653184 | bytes 1572864 | tf_op jit(solution)/shard_map/dft/pallas_call | solution.py:98
  96.9 0.0 collective-permute-done.5.x_ref
  96.9 1.8 %dft.7.three_g = f32[1,1024,256]{2,1,0:T(8,128)S(1)} custom-call(bf16[2,4,256,256]{3,2,1,0:T(8,128)(2,1)S(1)} %copy-done, f32[512,256]{1,0:T(8,128)} %collective-permute-done.5.x_ref), custom_call_target="tpu_custom_call" | custom-call | flops 402653184 | bytes 1572864 | tf_op jit(solution)/shard_map/dft/pallas_call | solution.py:98
  98.6 0.0 copy-done.5
  98.7 0.0 copy-done.7
  98.7 0.0 copy-done.8
  98.7 0.0 copy-start.9
  98.7 0.0 copy-start.10
  98.7 10.2 %final.1 = (f32[512,256]{1,0:T(8,128)}, f32[1024,256]{1,0:T(8,128)}, f32[512,256]{1,0:T(8,128)S(1)}) custom-call(s32[1]{0:T(128)} %bitcast.pos_ref, bf16[2,4,256,256]{3,2,1,0:T(8,128)(2,1)S(1)} %copy-done.4, f32[7,1024,256]{2,1,0:T(8,128)} %taps.1.win_near.win_far.win_ref, f32[2,1024,256]{2,1,0:T(8,128)} %copy-done.2, f32[4,1024,256]{2,1,0:T(8,128)} %dft.5.near_ref, ...), custom_call_target="tpu_custom_call" | custom-call | flops 1610612736 | bytes 19660800 | tf_op jit(solution)/shard_map/final/pallas_call | solution.py:341
  108.9 0.0 collective-permute-done.6
  108.9 0.0 copy-done.9
  108.9 0.0 copy-done.10
  109.0 2.1 %add_multiply_fusion = (f32[512,256]{1,0:T(8,128)}, f32[512,256]{1,0:T(8,128)}) fusion(f32[512,256]{1,0:T(8,128)S(1)} %copy-done.9, f32[512,256]{1,0:T(8,128)S(1)} %get-tuple-element.16, f32[512,256]{1,0:T(8,128)} %collective-permute-done.6, f32[512,256]{1,0:T(8,128)S(1)} %copy-done.10), kind=kLoop, calls=%fused_computation.4 | loop fusion | flops 393216 | bytes 3145728 | tf_op jit(solution)/shard_map/mul | solution.py:404
  (2 shorter events, 0.0 us)
Async XLA Ops:
  2.4 89.7 %copy-start.1 = (f32[1024,256]{1,0:T(8,128)}, f32[1024,256]{1,0:T(8,128)S(1)}, u32[]{:S(2)}) copy-start(f32[1024,256]{1,0:T(8,128)S(1)} %pad_maximum_fusion.1.x_ref.gm_ref) | copy-start | bytes 3145732
  2.4 28.1 %collective-permute-start.1 = (f32[1024,256]{1,0:T(8,128)S(1)}, f32[1024,256]{1,0:T(8,128)S(1)}, u32[]{:S(2)}, u32[]{:S(2)}) collective-permute-start(f32[1024,256]{1,0:T(8,128)S(1)} %pad_maximum_fusion.1.x_ref.gm_ref), channel_id=1, source_target_pairs={{4,0},{8,4},{12,8},{5,1},{9,5},{13,9},{6,2},{10,6},{14,10},{7,3},{... | collective-permute-start | bytes 3145736 | tf_op jit(solution)/shard_map/ppermute | solution.py:385
  3.7 28.0 %collective-permute-start = (f32[1024,256]{1,0:T(8,128)S(1)}, f32[1024,256]{1,0:T(8,128)}, u32[]{:S(2)}, u32[]{:S(2)}) collective-permute-start(f32[1024,256]{1,0:T(8,128)S(1)} %pad_maximum_fusion.1.x_ref.gm_ref), channel_id=1, source_target_pairs={{0,4},{4,8},{8,12},{1,5},{5,9},{9,13},{2,6},{6,10},{10,14},{3,7},{... | collective-permute-start | bytes 3145736 | tf_op jit(solution)/shard_map/ppermute | solution.py:384
  10.3 39.8 %copy-start = (bf16[2,4,256,256]{3,2,1,0:T(8,128)(2,1)S(1)}, bf16[2,4,256,256]{3,2,1,0:T(8,128)(2,1)}, u32[]{:S(2)}) copy-start(bf16[2,4,256,256]{3,2,1,0:T(8,128)(2,1)} %constant.13.clone.table_ref) | copy-start | bytes 3145732
  10.3 39.8 %copy-start.3 = (f32[4096,256]{1,0:T(8,128)S(1)}, f32[4096,256]{1,0:T(8,128)}, u32[]{:S(2)}) copy-start(f32[4096,256]{1,0:T(8,128)} %x_ref.1) | copy-start | bytes 12582916
  33.0 15.5 %collective-permute-start.3 = (f32[512,256]{1,0:T(8,128)S(1)}, f32[512,256]{1,0:T(8,128)S(1)}, u32[]{:S(2)}, u32[]{:S(2)}) collective-permute-start(f32[512,256]{1,0:T(8,128)S(1)} %get-tuple-element.24), channel_id=1, source_target_pairs={{8,4},{4,0},{9,5},{5,1},{10,6},{6,2},{11,7},{7,3},{24,20},{20,16},... | collective-permute-start | bytes 1572872 | tf_op jit(solution)/shard_map/ppermute | solution.py:388
  34.3 14.2 %collective-permute-start.2 = (f32[512,256]{1,0:T(8,128)S(1)}, f32[512,256]{1,0:T(8,128)S(1)}, u32[]{:S(2)}, u32[]{:S(2)}) collective-permute-start(f32[512,256]{1,0:T(8,128)S(1)} %get-tuple-element.26), channel_id=1, source_target_pairs={{4,8},{8,12},{5,9},{9,13},{6,10},{10,14},{7,11},{11,15},{20,24},{2... | collective-permute-start | bytes 1572872 | tf_op jit(solution)/shard_map/ppermute | solution.py:388
  49.4 15.4 %collective-permute-start.4 = (f32[512,256]{1,0:T(8,128)S(1)}, f32[512,256]{1,0:T(8,128)S(1)}, u32[]{:S(2)}, u32[]{:S(2)}) collective-permute-start(f32[512,256]{1,0:T(8,128)S(1)} %get-tuple-element.13), channel_id=1, source_target_pairs={{4,8},{8,4},{5,9},{9,5},{6,10},{10,6},{7,11},{11,7},{20,24},{24,20... | collective-permute-start | bytes 1572872 | tf_op jit(solution)/shard_map/ppermute | solution.py:395
  59.1 5.7 %copy-start.4 = (bf16[2,4,256,256]{3,2,1,0:T(8,128)(2,1)S(1)}, bf16[2,4,256,256]{3,2,1,0:T(8,128)(2,1)}, u32[]{:S(2)}) copy-start(bf16[2,4,256,256]{3,2,1,0:T(8,128)(2,1)} %constant.14.clone.inverse_ref) | copy-start | bytes 3145732
  59.2 37.7 %collective-permute-start.5 = (f32[512,256]{1,0:T(8,128)}, f32[512,256]{1,0:T(8,128)}, u32[]{:S(2)}, u32[]{:S(2)}) collective-permute-start(f32[512,256]{1,0:T(8,128)} %add.8.x_ref), channel_id=1, source_target_pairs={{4,0},{8,12},{5,1},{9,13},{6,2},{10,14},{7,3},{11,15},{20,16},{24,... | collective-permute-start | bytes 1572872 | tf_op jit(solution)/shard_map/ppermute | solution.py:394
  69.0 1.0 copy-start.6
  70.0 39.0 %collective-permute-start.6 = (f32[512,256]{1,0:T(8,128)}, f32[512,256]{1,0:T(8,128)}, u32[]{:S(2)}, u32[]{:S(2)}) collective-permute-start(f32[512,256]{1,0:T(8,128)} %get-tuple-element.17), channel_id=1, source_target_pairs={{4,0},{8,12},{5,1},{9,13},{6,2},{10,14},{7,3},{11,15},{20,16},{24,... | collective-permute-start | bytes 1572872 | tf_op jit(solution)/shard_map/ppermute | solution.py:398
  93.6 1.4 %copy-start.2 = (f32[2,1024,256]{2,1,0:T(8,128)}, f32[2,1024,256]{2,1,0:T(8,128)S(1)}, u32[]{:S(2)}) copy-start(f32[2,1024,256]{2,1,0:T(8,128)S(1)} %dft.4.own_ref) | copy-start | bytes 6291460
  95.0 3.7 %copy-start.5 = (f32[512,256]{1,0:T(8,128)S(1)}, f32[512,256]{1,0:T(8,128)}, u32[]{:S(2)}) copy-start(f32[512,256]{1,0:T(8,128)} %up_ref.1) | copy-start | bytes 1572868
  95.0 3.7 %copy-start.7 = (f32[1024,256]{1,0:T(8,128)S(1)}, f32[1024,256]{1,0:T(8,128)}, u32[]{:S(2)}) copy-start(f32[1024,256]{1,0:T(8,128)} %copy-done.6) | copy-start | bytes 3145732
  95.0 3.7 %copy-start.8 = (f32[256]{0:T(256)S(1)}, f32[256]{0:T(256)}, u32[]{:S(2)}) copy-start(f32[256]{0:T(256)} %param.12) | copy-start | bytes 3076
  98.7 10.3 %copy-start.9 = (f32[512,256]{1,0:T(8,128)S(1)}, f32[512,256]{1,0:T(8,128)}, u32[]{:S(2)}) copy-start(f32[512,256]{1,0:T(8,128)} %param.9) | copy-start | bytes 1572868
  98.7 10.3 %copy-start.10 = (f32[512,256]{1,0:T(8,128)S(1)}, f32[512,256]{1,0:T(8,128)}, u32[]{:S(2)}) copy-start(f32[512,256]{1,0:T(8,128)} %param.10) | copy-start | bytes 1572868

commit v2 on v1

--- a/solution.py
+++ b/solution.py
@@ -68,43 +68,90 @@
         store(group, dot3(table_ref, group, *split(part)))
 
 
-def dft_kernel(table_ref, x_ref, out_ref):
-    rows = out_ref.shape[1] // 4
-
-    def store(group, value):
-        out_ref[0, group * rows : (group + 1) * rows, :] = value
-
-    transform(x_ref[...], table_ref, store)
-
-
 def cost(flops, nbytes):
     return pl.CostEstimate(flops=int(flops), bytes_accessed=int(nbytes), transcendentals=0)
 
 
-VMEM_LIMIT = 48 << 20
-
-
-def params():
-    return pltpu.CompilerParams(vmem_limit_bytes=VMEM_LIMIT)
+def params(mib):
+    return pltpu.CompilerParams(vmem_limit_bytes=mib << 20)
 
 
 def whole_spec(shape):
     return pl.BlockSpec(shape, lambda *_: (0,) * len(shape))
 
 
-def dft(table, x, seg):
-    width = x.shape[1]
-    blocks = x.shape[0] // seg
+def f32(*shape):
+    return jax.ShapeDtypeStruct(shape, jnp.float32)
+
+
+def prepare_kernel(query_ref, key_ref, values_ref, up_ref, gated_ref, *rest):
+    mixed_refs, sum_ref = rest[:-1], rest[-1]
+    step = pl.program_id(0)
+    rows, width = key_ref.shape
+    half = width // len(mixed_refs)
+    gated = key_ref[...] * values_ref[...]
+    mixed = up_ref[...] * query_ref[...]
+    gated_ref[pl.ds(pl.multiple_of(step * rows, rows), rows), :] = gated
+    for i, ref in enumerate(mixed_refs):
+        ref[...] = mixed[:, i * half : (i + 1) * half]
+    part = jnp.sum((gated * mixed).reshape(rows // 8, 8, width), axis=0)
+
+    @pl.when(step == 0)
+    def _():
+        sum_ref[...] = part
+
+    @pl.when(step > 0)
+    def _():
+        sum_ref[...] += part
+
+    @pl.when(step == pl.num_programs(0) - 1)
+    def _():
+        seg = gated_ref.shape[0] - 8
+        gated_ref[seg:, :] = sum_ref[...]
+
+
+def prepare(query_gate, key_gate, values, upstream, halves):
+    seg, width = values.shape
+    steps = 4
+    rows = seg // steps
+    block = pl.BlockSpec((rows, width), lambda i: (i, 0))
+    half = pl.BlockSpec((rows, width // halves), lambda i: (i, 0))
+    return pl.pallas_call(
+        prepare_kernel,
+        grid=(steps,),
+        in_specs=[block] * 4,
+        out_specs=[whole_spec((seg + 8, width))] + [half] * halves,
+        out_shape=[f32(seg + 8, width)] + [f32(seg, width // halves)] * halves,
+        scratch_shapes=[pltpu.VMEM((8, width), jnp.float32)],
+        compiler_params=params(8),
+        cost_estimate=cost(4 * seg * width, 24 * seg * width),
+        name="prepare",
+    )(query_gate, key_gate, values, upstream)
+
+
+def dft_kernel(table_ref, *refs):
+    *x_refs, out_ref = refs
+    rows = out_ref.shape[0] // 4
+
+    def store(group, value):
+        out_ref[group * rows : (group + 1) * rows, :] = value
+
+    parts = [ref[...] for ref in x_refs]
+    transform(parts[0] if len(parts) == 1 else jnp.concatenate(parts, axis=1), table_ref, store)
+
+
+def dft(table, seg, *xs):
+    width = sum(x.shape[1] for x in xs)
     return pl.pallas_call(
         dft_kernel,
-        grid=(blocks,),
-        in_specs=[whole_spec(table.shape), pl.BlockSpec((seg, width), lambda i: (i, 0))],
-        out_specs=pl.BlockSpec((1, 2 * seg, width), lambda i: (i, 0, 0)),
-        out_shape=jax.ShapeDtypeStruct((blocks, 2 * seg, width), jnp.float32),
-        compiler_params=params(),
-        cost_estimate=cost(blocks * 3 * seg * seg * width * 2, blocks * 12 * seg * width),
+        grid=(1,),
+        in_specs=[whole_spec(table.shape)] + [whole_spec((seg, x.shape[1])) for x in xs],
+        out_specs=whole_spec((2 * seg, width)),
+        out_shape=f32(2 * seg, width),
+        compiler_params=params(12),
+        cost_estimate=cost(3 * seg * seg * width * 2, 12 * seg * width),
         name="dft",
-    )(table, x)
+    )(table, *xs)
 
 
 def taps_kernel(table_ref, x_ref, out_ref, last_ref):
@@ -137,7 +184,7 @@
         out_specs=pl.BlockSpec((1, 2 * seg, width), lambda i: (jnp.maximum(i - 1, 0), 0, 0)),
         out_shape=jax.ShapeDtypeStruct((blocks - 1, 2 * seg, width), jnp.float32),
         scratch_shapes=[pltpu.VMEM((2 * seg, width), jnp.float32)],
-        compiler_params=params(),
+        compiler_params=params(14),
         cost_estimate=cost(blocks * 3 * seg * seg * width * 2, blocks * 12 * seg * width),
         name="taps",
     )(table, taps)
@@ -155,15 +202,18 @@
     return a[0] + b[0], a[1] + b[1]
 
 
-def partial_kernel(pos_ref, table_ref, inverse_ref, win_near, win_far, near_ref, x_ref, far_ref, out_ref, z_ref):
+def partial_kernel(
+    pos_ref, table_ref, inverse_ref, win_near, win_far, left_ref, right_ref, x_ref, far_ref, out_ref, z_ref
+):
     rows = far_ref.shape[0] // 4
     sub = rows // 2
+    is_left = pos_ref[0] != 1
     for group, part in enumerate(spread(x_ref[...])):
         base = group * rows
         far = dot3(table_ref, group, *split(part))
         far_ref[base : base + rows, :] = far
         re, im = slice(base, base + sub), slice(base + sub, base + rows)
-        near = (near_ref[0, re, :], near_ref[0, im, :])
+        near = tuple(jnp.where(is_left, left_ref[at, :], right_ref[at, :]) for at in (re, im))
         total = add(
             conj_mul((win_near[0, re, :], win_near[0, im, :]), near),
             conj_mul((win_far[0, re, :], win_far[0, im, :]), (far[:sub], far[sub:])),
@@ -174,14 +224,17 @@
         out_ref[i * sub : (i + 1) * sub, :] = quarter
 
 
-def back_partial(pos, table, inverse, windows, near, x, seg):
+def back_partial(pos, table, inverse, windows, left, right, x, half, seg):
     width = x.shape[1]
     n = (windows.shape[0] + 1) // 2
-    block = (1, 2 * seg, width)
 
     def window(distance):
-        return pl.BlockSpec(block, lambda i, pos: (jnp.where(pos[0] == 1, n - 1 + distance, n - 1 - distance), 0, 0))
-
+        return pl.BlockSpec(
+            (1, 2 * seg, width),
+            lambda i, pos: (jnp.where(pos[0] == 1, n - 1 + distance, n - 1 - distance), 0, half),
+        )
+
+    near = pl.BlockSpec((2 * seg, width), lambda i, pos: (0, half))
     return pl.pallas_call(
         partial_kernel,
         grid_spec=pltpu.PrefetchScalarGridSpec(
@@ -192,20 +245,18 @@
                 whole_spec(inverse.shape),
                 window(2),
                 window(3),
-                pl.BlockSpec(block, lambda i, pos: (jnp.where(pos[0] == 1, 3, 1), 0, 0)),
+                near,
+                near,
                 whole_spec((seg, width)),
             ],
             out_specs=[whole_spec((2 * seg, width)), whole_spec((seg, width))],
             scratch_shapes=[pltpu.VMEM((4, seg // 2, width), jnp.float32)],
         ),
-        out_shape=[
-            jax.ShapeDtypeStruct((2 * seg, width), jnp.float32),
-            jax.ShapeDtypeStruct((seg, width), jnp.float32),
-        ],
-        compiler_params=params(),
+        out_shape=[f32(2 * seg, width), f32(seg, width)],
+        compiler_params=params(20),
         cost_estimate=cost(6 * seg * seg * width * 2, 24 * seg * width),
         name="partial",
-    )(pos, table, inverse, windows, windows, near, x)
+    )(pos, table, inverse, windows, windows, left, right, x)
 
 
 OWN, LEFT, RIGHT, TWO, THREE = range(5)
@@ -225,85 +276,160 @@
 )
 
 
-def final_kernel(
-    pos_ref, inverse_ref, win_ref, own_ref, near_ref, two_g, two_m, three_g, gm_ref, skip_ref, up_ref,
-    query_out, filter_out, back_out, x_high, x_low, z_ref,
+def is_late(pair):
+    return pair[0] == TWO or pair[1] == THREE
+
+
+def pair_sums(distances, gated, mixed, sign, late):
+    total = []
+    for pairs in distances:
+        value = None
+        for m, g in pairs:
+            if is_late((m, g)) == late:
+                term = conj_mul(gated[g](), mixed[m]())
+                value = term if value is None else add(value, term)
+        total.append(value)
+    out = []
+    for low, high in zip(total[:2], total[1:]):
+        if high is not None:
+            turned = (sign * high[1], -sign * high[0])
+            low = turned if low is None else add(low, turned)
+        out.append(low)
+    return out
+
+
+TILE = 16
+
+
+def tile_reader(tile, sub):
+    re = pl.ds(pl.multiple_of(tile * TILE, TILE), TILE)
+    im = pl.ds(pl.multiple_of(sub + tile * TILE, TILE), TILE)
+
+    def read(ref, *lead):
+        return ref[(*lead, re, slice(None))], ref[(*lead, im, slice(None))]
+
+    return re, im, read
+
+
+def group_sign():
+    return jnp.where(pl.program_id(0) % 2 == 0, 1.0, -1.0)
+
+
+def early_kernel(
+    pos_ref, win_own, win_left, win_right, win_two, own_g, left_g, right_g, two_g, own_m, left_m, right_m, out_ref
 ):
-    group = pl.program_id(0)
-    pos = pos_ref[0]
-    rows = own_ref.shape[1]
+    pos, sign = pos_ref[0], group_sign()
+    rows = own_g.shape[0]
     sub = rows // 2
-    width = own_ref.shape[2]
-    seg = 4 * sub
-    mid = win_ref.shape[0] // 2
-    sign = jnp.where(group % 2 == 0, 1.0, -1.0)
-    step = 8
-    two_off = jnp.where(pos < 2, -2, 2)
-    three_off = jnp.where(pos == 0, -3, 3)
-
-    def put(slot, tile, value):
-        for half in range(2):
-            high, low = split(value[half])
-            at = pl.ds(pl.multiple_of(half * sub + tile * step * 2, 16), 2 * step)
-            x_high[at, slot * width : (slot + 1) * width] = high
-            x_low[at, slot * width : (slot + 1) * width] = low
-
-    def tiles(tile):
-        re = pl.ds(pl.multiple_of(tile * step * 2, 16), 2 * step)
-        im = pl.ds(pl.multiple_of(sub + tile * step * 2, 16), 2 * step)
-
-        def read(ref, *lead):
-            return ref[(*lead, re, slice(None))], ref[(*lead, im, slice(None))]
-
-        gated = (
-            lambda: read(own_ref, 0), lambda: read(near_ref, 0), lambda: read(near_ref, 2),
-            lambda: read(two_g, 0), lambda: read(three_g, 0),
-        )
-        mixed = (lambda: read(own_ref, 1), lambda: read(near_ref, 1), lambda: read(near_ref, 3), lambda: read(two_m))
-        return read, gated, mixed
+    count = sub // TILE
+
+    def put(at, slot, value):
+        re, im = at
+        out_ref[slot, re, :] = value[0]
+        out_ref[slot, im, :] = value[1]
 
     def sums(tile, _):
-        read, gated, mixed = tiles(tile)
-        conv = mul(read(win_ref, mid), gated[OWN]())
-        conv = add(conv, mul(read(win_ref, mid + 1), gated[LEFT]()))
-        conv = add(conv, mul(read(win_ref, mid - 1), gated[RIGHT]()))
-        conv = add(conv, mul(read(win_ref, mid + two_off), gated[TWO]()))
-        conv = add(conv, mul(read(win_ref, mid + three_off), gated[THREE]()))
-        put(0, tile, conv)
-        back = conj_mul(read(win_ref, mid), mixed[OWN]())
-        back = add(back, conj_mul(read(win_ref, mid - 1), mixed[LEFT]()))
-        back = add(back, conj_mul(read(win_ref, mid + 1), mixed[RIGHT]()))
-        back = add(back, conj_mul(read(win_ref, mid - two_off), mixed[TWO]()))
-        put(1, tile, back)
+        re, im, read = tile_reader(tile, sub)
+        own, left, right = read(win_own, 0), read(win_left, 0), read(win_right, 0)
+        conv = add(mul(own, read(own_g)), mul(left, read(left_g)))
+        conv = add(conv, add(mul(right, read(right_g)), mul(read(win_two, 0), read(two_g))))
+        put((re, im), 0, conv)
+        back = add(conj_mul(own, read(own_m)), conj_mul(right, read(left_m)))
+        put((re, im), 1, add(back, conj_mul(left, read(right_m))))
         return _
 
-    count = sub // (2 * step)
     lax.fori_loop(0, count, sums, 0)
-
     for where, distances in enumerate(PAIRS):
 
         @pl.when(pos == where)
         def _():
             def lags(tile, _):
-                read, gated, mixed = tiles(tile)
-                total = []
-                for pairs in distances:
-                    value = None
-                    for m, g in pairs:
-                        term = conj_mul(gated[g](), mixed[m]())
-                        value = term if value is None else add(value, term)
-                    total.append(value)
-                for slot in range(2):
-                    low, high = total[slot], total[slot + 1]
-                    if high is None:
-                        value = low
-                    else:
-                        turned = (sign * high[1], -sign * high[0])
-                        value = turned if low is None else add(low, turned)
-                    put(2 + slot, tile, value)
+                re, im, read = tile_reader(tile, sub)
+                gated = [functools.partial(read, ref) for ref in (own_g, left_g, right_g, two_g)]
+                mixed = [functools.partial(read, ref) for ref in (own_m, left_m, right_m)]
+                for slot, value in enumerate(pair_sums(distances, gated, mixed, sign, False)):
+                    if value is None:
+                        value = (jnp.zeros_like(own_g[re, :]),) * 2
+                    put((re, im), 2 + slot, value)
                 return _
 
             lax.fori_loop(0, count, lags, 0)
+
+
+def early(pos, windows, gated, mixed, seg):
+    width = gated[0].shape[1]
+    rows = seg // 2
+    mid = windows.shape[0] // 2
+
+    def window(index):
+        return pl.BlockSpec((1, rows, width), lambda i, pos: (index(pos[0]), i, 0))
+
+    group = pl.BlockSpec((rows, width), lambda i, pos: (i, 0))
+    return pl.pallas_call(
+        early_kernel,
+        grid_spec=pltpu.PrefetchScalarGridSpec(
+            num_scalar_prefetch=1,
+            grid=(4,),
+            in_specs=[
+                window(lambda p: mid),
+                window(lambda p: mid + 1),
+                window(lambda p: mid - 1),
+                window(lambda p: jnp.where(p < 2, mid - 2, mid + 2)),
+            ]
+            + [group] * 7,
+            out_specs=pl.BlockSpec((4, rows, width), lambda i, pos: (0, i, 0)),
+        ),
+        out_shape=f32(4, 2 * seg, width),
+        compiler_params=params(14),
+        cost_estimate=cost(200 * seg * width, 120 * seg * width),
+        name="early",
+    )(pos, *[windows] * 4, *gated, *mixed)
+
+
+def late_kernel(
+    pos_ref, inverse_ref, acc_ref, win_ref, three_g, two_g, own_m, left_m, right_m, *rest
+):
+    two_m, (gated_ref, mixed, strips), (skip_ref, up_ref, query_out, filter_out, back_out, skip_out) = (
+        rest[:2], (rest[2], rest[3:5], rest[5:10]), rest[10:16])
+    x_high, x_low, z_ref = rest[16:]
+    group = pl.program_id(0)
+    pos, sign = pos_ref[0], group_sign()
+    rows, width = own_m.shape
+    half = width // 2
+    sub = rows // 2
+
+    def put(at, slot, value):
+        for rows_at, part in zip(at, value):
+            high, low = split(part)
+            x_high[rows_at, slot * width : (slot + 1) * width] = high
+            x_low[rows_at, slot * width : (slot + 1) * width] = low
+
+    for where, distances in enumerate(PAIRS):
+
+        @pl.when(pos == where)
+        def _():
+            def lags(tile, _):
+                re, im, read = tile_reader(tile, sub)
+
+                def read_two():
+                    parts = [read(ref) for ref in two_m]
+                    return tuple(jnp.concatenate([p[i] for p in parts], axis=1) for i in range(2))
+
+                gated = [None, None, None, functools.partial(read, two_g), functools.partial(read, three_g)]
+                mixed = [functools.partial(read, ref) for ref in (own_m, left_m, right_m)] + [read_two]
+                total = [read(acc_ref, slot) for slot in range(4)]
+                if where in (0, 3):
+                    total[0] = add(total[0], mul(read(win_ref, 0), gated[THREE]()))
+                else:
+                    total[1] = add(total[1], conj_mul(read(win_ref, 0), mixed[TWO]()))
+                for slot, value in enumerate(pair_sums(distances, gated, mixed, sign, True)):
+                    if value is not None:
+                        total[2 + slot] = add(total[2 + slot], value)
+                for slot, value in enumerate(total):
+                    put((re, im), slot, value)
+                return _
+
+            lax.fori_loop(0, sub // TILE, lags, 0)
 
     dot = functools.partial(jnp.dot, preferred_element_type=jnp.float32)
     t_high, t_low = inverse_ref[0, 0], inverse_ref[1, 0]
@@ -315,6 +441,7 @@
 
     @pl.when(group == 3)
     def _():
+        seg = 4 * sub
         for slot in range(4):
             cols = slice(slot * width, (slot + 1) * width)
             quarters = gather_quarters(
@@ -323,54 +450,83 @@
             for i, quarter in enumerate(quarters):
                 at = slice(i * sub, (i + 1) * sub)
                 if slot == 0:
-                    query_out[at, :] = up_ref[at, :] * (quarter + skip_ref[...] * gm_ref[at, :])
+                    query_out[at, :] = up_ref[at, :] * (quarter + skip_ref[...] * gated_ref[at, :])
                 elif slot == 1:
-                    back_out[at, :] = quarter + skip_ref[...] * gm_ref[seg + i * sub : seg + (i + 1) * sub, :]
+                    for h in range(2):
+                        lanes = slice(h * half, (h + 1) * half)
+                        back_out[at, lanes] = quarter[:, lanes] + skip_ref[:, lanes] * mixed[h][at, :]
                 else:
                     base = (slot - 2) * seg + i * sub
                     filter_out[base : base + sub, :] = quarter
-
-
-def final(pos, inverse, windows, own, near, two_g, two_m, three_g, gm, skip, upstream, seg):
-    width = gm.shape[1]
+        sources = (pos, pos - 1, pos + 1, jnp.where(pos < 2, pos + 2, pos - 2), 3 - pos)
+        total = jnp.zeros((8, width), jnp.float32)
+        for block in range(4):
+            value = jnp.zeros((8, width), jnp.float32)
+            for where, (ref, source) in enumerate(zip(strips, sources)):
+                hit = source == block
+                if where == THREE:
+                    hit = jnp.logical_and(hit, jnp.logical_or(pos == 0, pos == 3))
+                value = value + jnp.where(hit, ref[...], 0.0)
+            total = total + value
+        skip_out[...] = jnp.sum(total, axis=0, keepdims=True)
+
+
+def late(pos, inverse, acc, windows, three_g, two_g, own_m, left_m, right_m, two_m, blocks, mixed, skip, upstream):
+    seg, width = upstream.shape
     rows = seg // 2
-
-    def groups(lead):
-        return pl.BlockSpec((lead, rows, width), lambda i, pos: (0, i, 0))
-
+    mid = windows.shape[0] // 2
+
+    def win_at(i, pos):
+        p = pos[0]
+        ends = jnp.where(p == 0, mid - 3, mid + 3)
+        return jnp.where(p == 1, mid + 2, jnp.where(p == 2, mid - 2, ends)), i, 0
+
+    group = pl.BlockSpec((rows, width), lambda i, pos: (i, 0))
+    group_half = pl.BlockSpec((rows, width // 2), lambda i, pos: (i, 0))
+    strip = pl.BlockSpec((8, width), lambda i, pos: (seg // 8, 0))
     return pl.pallas_call(
-        final_kernel,
+        late_kernel,
         grid_spec=pltpu.PrefetchScalarGridSpec(
             num_scalar_prefetch=1,
             grid=(4,),
             in_specs=[
                 pl.BlockSpec((2, 1, rows, rows), lambda i, pos: (0, i, 0, 0)),
-                groups(windows.shape[0]),
-                groups(2),
-                groups(4),
-                groups(1),
-                pl.BlockSpec((rows, width), lambda i, pos: (i, 0)),
-                groups(1),
-                whole_spec((2 * seg, width)),
+                pl.BlockSpec((4, rows, width), lambda i, pos: (0, i, 0)),
+                pl.BlockSpec((1, rows, width), win_at),
+                *[group] * 5,
+                *[group_half] * 2,
+                whole_spec((seg, width)),
+                *[whole_spec((seg, width // 2))] * 2,
+                *[strip] * 5,
                 whole_spec((1, width)),
                 whole_spec((seg, width)),
             ],
-            out_specs=[whole_spec((seg, width)), whole_spec((2 * seg, width)), whole_spec((seg, width))],
+            out_specs=[
+                whole_spec((seg, width)), whole_spec((2 * seg, width)), whole_spec((seg, width)), whole_spec((1, width)),
+            ],
             scratch_shapes=[
                 pltpu.VMEM((rows, 4 * width), jnp.bfloat16),
                 pltpu.VMEM((rows, 4 * width), jnp.bfloat16),
                 pltpu.VMEM((4, rows, 4 * width), jnp.float32),
             ],
         ),
-        out_shape=[
-            jax.ShapeDtypeStruct((seg, width), jnp.float32),
-            jax.ShapeDtypeStruct((2 * seg, width), jnp.float32),
-            jax.ShapeDtypeStruct((seg, width), jnp.float32),
-        ],
-        compiler_params=params(),
-        cost_estimate=cost(12 * seg * seg * width * 2, 150 * seg * width),
-        name="final",
-    )(pos, inverse, windows, own, near, two_g, two_m, three_g, gm, skip, upstream)
+        out_shape=[f32(seg, width), f32(2 * seg, width), f32(seg, width), f32(1, width)],
+        compiler_params=params(32),
+        cost_estimate=cost(12 * seg * seg * width * 2, 100 * seg * width),
+        name="late",
+    )(pos, inverse, acc, windows, three_g, two_g, own_m, left_m, right_m, *two_m, blocks[0], *mixed, *blocks, skip, upstream)
+
+
+def send(x, *pairs):
+    return lax.ppermute(x, "ctx", list(pairs))
+
+
+def to_right(x):
+    return send(x, (0, 1), (1, 2), (2, 3))
+
+
+def to_left(x):
+    return send(x, (1, 0), (2, 1), (3, 2))
 
 
 def local_line(query_gate, key_gate, values, filter_taps, skip_gain, upstream):
@@ -379,29 +535,45 @@
     table, inverse = jnp.asarray(forward_np), jnp.asarray(inverse_np)
     position = lax.axis_index("ctx")
     pos = position.astype(jnp.int32).reshape(1)
-    gm = jnp.concatenate([key_gate * values, upstream * query_gate], axis=0)
-    skip_grad = lax.psum(jnp.sum(gm[:seg] * gm[seg:], axis=0), "ctx")
-    from_left = lax.ppermute(gm, "ctx", [(0, 1), (1, 2), (2, 3)])
-    from_right = lax.ppermute(gm, "ctx", [(1, 0), (2, 1), (3, 2)])
+    after = lax.optimization_barrier
+
+    gated, *mixed = prepare(query_gate, key_gate, values, upstream, 2)
+    left, right = to_right(gated), to_left(gated)
+    left_m0, right_m0 = to_right(mixed[0]), to_left(mixed[0])
     windows = taps_spectra(table, filter_taps, seg)
-    own = dft(table, gm, seg)
-    two_g = lax.ppermute(from_left[:seg], "ctx", [(1, 2), (2, 3)]) + lax.ppermute(
-        from_right[:seg], "ctx", [(2, 1), (1, 0)]
+    own_g, own_m = dft(table, seg, gated), dft(table, seg, *mixed)
+    left, right, windows, own_g, own_m = after((left, right, windows, own_g, own_m))
+
+    two_l, two_r = send(left, (1, 2), (2, 3)), send(right, (2, 1), (1, 0))
+    left_g, right_g = dft(table, seg, left), dft(table, seg, right)
+    left_m0, right_m0, mixed_1, left_g, right_g = after((left_m0, right_m0, mixed[1], left_g, right_g))
+    left_m1, right_m1 = to_right(mixed_1), to_left(mixed_1)
+    far_0 = jnp.where(position == 1, left_m0, right_m0)
+    two_l, two_r, far_0 = after((two_l, two_r, far_0))
+    two = two_l + two_r
+    three = send(two, (1, 0), (2, 3))
+    two_m0 = send(far_0, (1, 2), (2, 1))
+    two_g = dft(table, seg, two)
+
+    left_m1, right_m1, two_g = after((left_m1, right_m1, two_g))
+    far_1 = jnp.where(position == 1, left_m1, right_m1)
+    two_m1 = send(far_1, (1, 2), (2, 1))
+    left_m, right_m = dft(table, seg, left_m0, left_m1), dft(table, seg, right_m0, right_m1)
+    acc = early(pos, windows, (own_g, left_g, right_g, two_g), (own_m, left_m, right_m), seg)
+    two_m0, left_m, right_m = after((two_m0, left_m, right_m))
+    spec_0, partial_0 = back_partial(pos, table, inverse, windows, left_m, right_m, two_m0, 0, seg)
+    two_m1, partial_0 = after((two_m1, partial_0))
+    partial_0 = send(partial_0, (1, 0), (2, 3))
+    spec_1, partial_1 = back_partial(pos, table, inverse, windows, left_m, right_m, two_m1, 1, seg)
+    partial_1 = send(partial_1, (1, 0), (2, 3))
+    three_g = dft(table, seg, three)
+    query_grad, filter_grad, back, skip_grad = late(
+        pos, inverse, acc, windows, three_g, two_g, own_m, left_m, right_m, (spec_0, spec_1),
+        (gated, left, right, two, three), mixed, skip_gain[None, :], upstream,
     )
-    far_m = jnp.where(position == 1, from_left[seg:], from_right[seg:])
-    near = dft(table, jnp.concatenate([from_left, from_right], axis=0), seg)
-    far_m, two_g = lax.optimization_barrier((far_m, two_g))
-    three_g = lax.ppermute(two_g, "ctx", [(1, 0), (2, 3)])
-    two_m = lax.ppermute(far_m, "ctx", [(1, 2), (2, 1)])
-    two_g = dft(table, two_g, seg)
-    two_m, partial = back_partial(pos, table, inverse, windows, near, two_m, seg)
-    partial = lax.ppermute(partial, "ctx", [(1, 0), (2, 3)])
-    three_g = dft(table, three_g, seg)
-    query_grad, filter_grad, back = final(
-        pos, inverse, windows, own, near, two_g, two_m, three_g, gm, skip_gain[None, :], upstream, seg
-    )
-    back = back + partial
-    return (query_grad, back * values, back * key_gate, filter_grad, skip_grad)
+    partial_0, partial_1, back = after((partial_0, partial_1, back))
+    back = back + jnp.concatenate([partial_0, partial_1], axis=1)
+    return (query_grad, back * values, back * key_gate, filter_grad, skip_grad[0])
 
 
 def matmul(left, right):

time: 112 us -> 89.3 us (0.80)
  the two profiles are of different devices: /device:TPU:0 before, /device:TPU:12 now
where the time goes in v2:
time: 89.3 us; the launch traced here: 88.5 us
  starting transfers between devices  34.9 us (39%)
  Pallas kernels  28.3 us (32%)
  waiting for transfers between devices  11.3 us (13%)
  local copies, waits for them, and re-layouts  9.54 us (11%)
  other arithmetic  3.4 us (4%)
  between operations  1.1 us (1%)
    ppermute x13, starting transfers between devices, send(): return lax.ppermute(x, 'ctx', list(pairs))  34.9 us
    ppermute x13, waiting for transfers between devices, send(): return lax.ppermute(x, 'ctx', list(pairs))  11.3 us
    unnamed x38, local copies, waits for them, and re-layouts  9.54 us
    pallas_call x8, Pallas kernels, dft(): pl.pallas_call(dft_kernel, grid=(1,), in_specs=[whole_spec(table.shape)]...  8.8 us
    pallas_call x1, Pallas kernels, late(): pl.pallas_call(late_kernel, grid_spec=pltpu.PrefetchScalarGridSpec(num_sc...  6.77 us
    pallas_call x1, Pallas kernels, taps_spectra(): pl.pallas_call(taps_kernel, grid=(blocks,), in_specs=[whole_spec(table.sh...  5.93 us
    pallas_call x2, Pallas kernels, back_partial(): pl.pallas_call(partial_kernel, grid_spec=pltpu.PrefetchScalarGridSpec(num...  3.34 us
    pallas_call x1, Pallas kernels, early(): pl.pallas_call(early_kernel, grid_spec=pltpu.PrefetchScalarGridSpec(num_s...  3.23 us
  transfers between devices with their start and end apart: 13, of which 5 were waited for; matrix products, arithmetic and copies ran while one was open for 3% of the time, Pallas kernels for 32%

profile of v2, /device:TPU:12, one launch (start us, length us, event | category | flops | bytes accessed | tf_op | source)
XLA Modules:
  0.0 88.5 jit_solution(4969975571528766553)
XLA Ops:
  0.6 0.0 copy-start.2
  0.6 0.0 copy-start.7
  0.7 1.1 %copy-done.7 = f32[512,256]{1,0:T(8,128)S(1)} copy-done((f32[512,256]{1,0:T(8,128)S(1)}, f32[512,256]{1,0:T(8,128)}, u32[]{:S(2)}) %copy-start.7) | copy-done | bytes 524312
  1.8 1.0 %copy-done.9 = f32[512,256]{1,0:T(8,128)S(1)} copy-done((f32[512,256]{1,0:T(8,128)S(1)}, f32[512,256]{1,0:T(8,128)}, u32[]{:S(2)}) %copy-start.9) | copy-done | bytes 524312
  2.8 1.0 %copy-done.11 = f32[512,256]{1,0:T(8,128)S(1)} copy-done((f32[512,256]{1,0:T(8,128)S(1)}, f32[512,256]{1,0:T(8,128)}, u32[]{:S(2)}) %copy-start.11) | copy-done | bytes 524312
  3.9 1.0 %copy-done.15 = f32[512,256]{1,0:T(8,128)S(1)} copy-done((f32[512,256]{1,0:T(8,128)S(1)}, f32[512,256]{1,0:T(8,128)}, u32[]{:S(2)}) %copy-start.15) | copy-done | bytes 524312
  4.9 0.2 prepare.1
  5.1 0.0 copy-start.13
  5.2 3.5 %collective-permute-start = (f32[520,256]{1,0:T(8,128)S(1)}, f32[520,256]{1,0:T(8,128)S(1)}, u32[]{:S(2)}, u32[]{:S(2)}) collective-permute-start(f32[520,256]{1,0:T(8,128)S(1)} %get-tuple-element.40.refs_0_.rest_2_.rest_5_), channel_id=1, source_target_pairs={{0,4},{4,8},{8,12},{1,5},{5,9},{9,13},{2,6},{6,10},{10,14},{3,7},{... | collective-permute-start | bytes 1597448 | tf_op jit(solution)/shard_map/ppermute | solution.py:521
  8.6 2.4 %collective-permute-start.1 = (f32[520,256]{1,0:T(8,128)S(1)}, f32[520,256]{1,0:T(8,128)}, u32[]{:S(2)}, u32[]{:S(2)}) collective-permute-start(f32[520,256]{1,0:T(8,128)S(1)} %get-tuple-element.40.refs_0_.rest_2_.rest_5_), channel_id=1, source_target_pairs={{4,0},{8,4},{12,8},{5,1},{9,5},{13,9},{6,2},{10,6},{14,10},{7,3},{... | collective-permute-start | bytes 1597448 | tf_op jit(solution)/shard_map/ppermute | solution.py:521
  11.0 0.0 copy-start.1
  11.1 1.2 %copy-done.1 = bf16[2,4,256,256]{3,2,1,0:T(8,128)(2,1)S(1)} copy-done((bf16[2,4,256,256]{3,2,1,0:T(8,128)(2,1)S(1)}, bf16[2,4,256,256]{3,2,1,0:T(8,128)(2,1)}, u32[]{:S(2)}) %copy-start.1) | copy-done | bytes 1048600
  12.3 0.7 dft.8.own_g
  13.0 1.0 %copy-done.5 = f32[1024,256]{1,0:T(8,128)} copy-done((f32[1024,256]{1,0:T(8,128)}, f32[1024,256]{1,0:T(8,128)S(1)}, u32[]{:S(2)}) %copy-start.5) | copy-done | bytes 1048600
  14.0 0.7 dft.9.own_m
  14.7 0.1 copy-done.4
  14.8 5.9 %taps.1.win_own.win_left.win_right.win_two.win_near.win_far.win_ref = f32[7,1024,256]{2,1,0:T(8,128)S(1)} custom-call(bf16[2,4,256,256]{3,2,1,0:T(8,128)(2,1)S(1)} %copy-done.2, f32[4096,256]{1,0:T(8,128)S(1)} %copy-done.4), custom_call_target="tpu_custom_call" | custom-call | flops 3221225472 | bytes 12582912 | tf_op jit(solution)/shard_map/taps/pallas_call | solution.py:180
  20.8 2.9 %copy-done = f32[7,1024,256]{2,1,0:T(8,128)} copy-done((f32[7,1024,256]{2,1,0:T(8,128)}, f32[7,1024,256]{2,1,0:T(8,128)S(1)}, u32[]{:S(2)}) %copy-start) | copy-done | bytes 7340056
  23.7 0.5 collective-permute-done.1.refs_0_.rest_7_
  24.2 4.3 %collective-permute-start.6 = (f32[520,256]{1,0:T(8,128)S(1)}, f32[520,256]{1,0:T(8,128)}, u32[]{:S(2)}, u32[]{:S(2)}) collective-permute-start(f32[520,256]{1,0:T(8,128)S(1)} %collective-permute-done.refs_0_.rest_6_), channel_id=1, source_target_pairs={{4,8},{8,12},{5,9},{9,13},{6,10},{10,14},{7,11},{11,15},{20,24},{2... | collective-permute-start | bytes 1597448 | tf_op jit(solution)/shard_map/ppermute | solution.py:521
  28.5 1.9 %collective-permute-start.7 = (f32[520,256]{1,0:T(8,128)}, f32[520,256]{1,0:T(8,128)}, u32[]{:S(2)}, u32[]{:S(2)}) collective-permute-start(f32[520,256]{1,0:T(8,128)} %collective-permute-done.1.refs_0_.rest_7_), channel_id=1, source_target_pairs={{8,4},{4,0},{9,5},{5,1},{10,6},{6,2},{11,7},{7,3},{24,20},{20,16},... | collective-permute-start | bytes 1597448 | tf_op jit(solution)/shard_map/ppermute | solution.py:521
  30.4 4.8 %collective-permute-start.2 = (f32[512,128]{1,0:T(8,128)S(1)}, f32[512,128]{1,0:T(8,128)}, u32[]{:S(2)}, u32[]{:S(2)}) collective-permute-start(f32[512,128]{1,0:T(8,128)S(1)} %get-tuple-element.41.refs_0_.rest_3_), channel_id=1, source_target_pairs={{0,4},{4,8},{8,12},{1,5},{5,9},{9,13},{2,6},{6,10},{10,14},{3,7},{... | collective-permute-start | bytes 786440 | tf_op jit(solution)/shard_map/ppermute | solution.py:521
  35.2 1.9 %collective-permute-start.3 = (f32[512,128]{1,0:T(8,128)S(1)}, f32[512,128]{1,0:T(8,128)}, u32[]{:S(2)}, u32[]{:S(2)}) collective-permute-start(f32[512,128]{1,0:T(8,128)S(1)} %get-tuple-element.41.refs_0_.rest_3_), channel_id=1, source_target_pairs={{4,0},{8,4},{12,8},{5,1},{9,5},{13,9},{6,2},{10,6},{14,10},{7,3},{... | collective-permute-start | bytes 786440 | tf_op jit(solution)/shard_map/ppermute | solution.py:521
  37.1 0.7 dft.10.left_g
  37.9 1.9 %dft.11.right_g = f32[1024,256]{1,0:T(8,128)S(1)} custom-call(bf16[2,4,256,256]{3,2,1,0:T(8,128)(2,1)S(1)} %copy-done.2, f32[520,256]{1,0:T(8,128)} %collective-permute-done.1.refs_0_.rest_7_), custom_call_target="tpu_custom_call" | custom-call | flops 402653184 | bytes 1572864 | tf_op jit(solution)/shard_map/dft/pallas_call | solution.py:145
  39.8 3.8 %collective-permute-done.2.refs_0_ = f32[512,128]{1,0:T(8,128)} collective-permute-done((f32[512,128]{1,0:T(8,128)S(1)}, f32[512,128]{1,0:T(8,128)}, u32[]{:S(2)}, u32[]{:S(2)}) %collective-permute-start.2) | collective-permute-done | bytes 262176 | tf_op jit(solution)/shard_map/ppermute | solution.py:521
  43.5 5.3 %collective-permute-done.3.refs_0_ = f32[512,128]{1,0:T(8,128)} collective-permute-done((f32[512,128]{1,0:T(8,128)S(1)}, f32[512,128]{1,0:T(8,128)}, u32[]{:S(2)}, u32[]{:S(2)}) %collective-permute-start.3) | collective-permute-done | bytes 262176 | tf_op jit(solution)/shard_map/ppermute | solution.py:521
  48.8 1.9 %collective-permute-start.4 = (f32[512,128]{1,0:T(8,128)S(1)}, f32[512,128]{1,0:T(8,128)S(1)}, u32[]{:S(2)}, u32[]{:S(2)}) collective-permute-start(f32[512,128]{1,0:T(8,128)S(1)} %copy-done.14), channel_id=1, source_target_pairs={{0,4},{4,8},{8,12},{1,5},{5,9},{9,13},{2,6},{6,10},{10,14},{3,7},{... | collective-permute-start | bytes 786440 | tf_op jit(solution)/shard_map/ppermute | solution.py:521
  50.7 3.9 %collective-permute-start.5 = (f32[512,128]{1,0:T(8,128)S(1)}, f32[512,128]{1,0:T(8,128)S(1)}, u32[]{:S(2)}, u32[]{:S(2)}) collective-permute-start(f32[512,128]{1,0:T(8,128)S(1)} %copy-done.14), channel_id=1, source_target_pairs={{4,0},{8,4},{12,8},{5,1},{9,5},{13,9},{6,2},{10,6},{14,10},{7,3},{... | collective-permute-start | bytes 786440 | tf_op jit(solution)/shard_map/ppermute | solution.py:521
  54.7 1.0 %broadcast_select_fusion.1 = f32[512,128]{1,0:T(8,128)S(1)} fusion(f32[512,128]{1,0:T(8,128)} %collective-permute-done.2.refs_0_, f32[512,128]{1,0:T(8,128)} %collective-permute-done.3.refs_0_, pred[]{:T(512)S(6)} %eq.4), kind=kLoop, calls=%fused_computation.4 | loop fusion | flops 65536 | bytes 786433 | tf_op jit(solution)/shard_map/jit(_where)/select_n | solution.py:551
  55.7 1.3 %add.6.refs_0_.rest_8_ = f32[520,256]{1,0:T(8,128)S(1)} add(f32[520,256]{1,0:T(8,128)} %collective-permute-done.6, f32[520,256]{1,0:T(8,128)} %collective-permute-done.7) | non-fusion elementwise | flops 133120 | bytes 1597440 | tf_op jit(solution)/shard_map/add | solution.py:553
  57.0 0.0 copy-start.3
  57.0 1.7 %collective-permute-start.8 = (f32[520,256]{1,0:T(8,128)S(1)}, f32[520,256]{1,0:T(8,128)S(1)}, u32[]{:S(2)}, u32[]{:S(2)}) collective-permute-start(f32[520,256]{1,0:T(8,128)S(1)} %add.6.refs_0_.rest_8_), channel_id=1, source_target_pairs={{4,0},{8,12},{5,1},{9,13},{6,2},{10,14},{7,3},{11,15},{20,16},{24,... | collective-permute-start | bytes 1597448 | tf_op jit(solution)/shard_map/ppermute | solution.py:521
  58.7 0.7 dft.12.two_g
  59.4 1.6 %collective-permute-done.5.refs_1_ = f32[512,128]{1,0:T(8,128)S(1)} collective-permute-done((f32[512,128]{1,0:T(8,128)S(1)}, f32[512,128]{1,0:T(8,128)S(1)}, u32[]{:S(2)}, u32[]{:S(2)}) %collective-permute-start.5) | collective-permute-done | bytes 262176 | tf_op jit(solution)/shard_map/ppermute | solution.py:521
  61.0 1.9 %collective-permute-start.9 = (f32[512,128]{1,0:T(8,128)S(1)}, f32[512,128]{1,0:T(8,128)S(1)}, u32[]{:S(2)}, u32[]{:S(2)}) collective-permute-start(f32[512,128]{1,0:T(8,128)S(1)} %broadcast_select_fusion.1), channel_id=1, source_target_pairs={{4,8},{8,4},{5,9},{9,5},{6,10},{10,6},{7,11},{11,7},{20,24},{24,20... | collective-permute-start | bytes 786440 | tf_op jit(solution)/shard_map/ppermute | solution.py:521
  63.0 3.9 %collective-permute-start.10 = (f32[512,128]{1,0:T(8,128)S(1)}, f32[512,128]{1,0:T(8,128)S(1)}, u32[]{:S(2)}, u32[]{:S(2)}) collective-permute-start(f32[512,128]{1,0:T(8,128)S(1)} %broadcast_select_fusion), channel_id=1, source_target_pairs={{4,8},{8,4},{5,9},{9,5},{6,10},{10,6},{7,11},{11,7},{20,24},{24,20... | collective-permute-start | bytes 786440 | tf_op jit(solution)/shard_map/ppermute | solution.py:521
  66.9 1.7 %dft.14.right_m.right_ref = f32[1024,256]{1,0:T(8,128)S(1)} custom-call(bf16[2,4,256,256]{3,2,1,0:T(8,128)(2,1)S(1)} %copy-done.2, f32[512,128]{1,0:T(8,128)} %collective-permute-done.3.refs_0_, f32[512,128]{1,0:T(8,128)S(1)} %collective-permute-done.5.refs_1_), custom_call_target="tpu_custom_call" | custom-call | flops 402653184 | bytes 1572864 | tf_op jit(solution)/shard_map/dft/pallas_call | solution.py:145
  68.6 1.7 %dft.13.left_m.left_ref = f32[1024,256]{1,0:T(8,128)S(1)} custom-call(bf16[2,4,256,256]{3,2,1,0:T(8,128)(2,1)S(1)} %copy-done.2, f32[512,128]{1,0:T(8,128)} %collective-permute-done.2.refs_0_, f32[512,128]{1,0:T(8,128)S(1)} %collective-permute-done.4.refs_1_), custom_call_target="tpu_custom_call" | custom-call | flops 402653184 | bytes 1572864 | tf_op jit(solution)/shard_map/dft/pallas_call | solution.py:145
  70.3 1.7 %partial.2 = (f32[1024,128]{1,0:T(8,128)S(1)}, f32[512,128]{1,0:T(8,128)S(1)}) custom-call(s32[1]{0:T(128)} %bitcast.pos_ref, bf16[2,4,256,256]{3,2,1,0:T(8,128)(2,1)S(1)} %copy-done.2, bf16[2,4,256,256]{3,2,1,0:T(8,128)(2,1)S(1)} %copy-done.3, f32[7,1024,256]{2,1,0:T(8,128)S(1)} %bitcast.4, f32[7,1024,256]{2,1,0:T(8,128)S(1)} %bitcast.4, ...), custom_call_target="tpu_custom_call" | custom-call | flops 402653184 | bytes 1572864 | tf_op jit(solution)/shard_map/partial/pallas_call | solution.py:238
  72.0 0.1 collective-permute-done.10.x_ref
  72.1 1.7 %partial.3 = (f32[1024,128]{1,0:T(8,128)S(1)}, f32[512,128]{1,0:T(8,128)S(1)}) custom-call(s32[1]{0:T(128)} %bitcast.pos_ref, bf16[2,4,256,256]{3,2,1,0:T(8,128)(2,1)S(1)} %copy-done.2, bf16[2,4,256,256]{3,2,1,0:T(8,128)(2,1)S(1)} %copy-done.3, f32[7,1024,256]{2,1,0:T(8,128)S(1)} %bitcast.4, f32[7,1024,256]{2,1,0:T(8,128)S(1)} %bitcast.4, ...), custom_call_target="tpu_custom_call" | custom-call | flops 402653184 | bytes 1572864 | tf_op jit(solution)/shard_map/partial/pallas_call | solution.py:238
  73.8 1.4 %collective-permute-start.12 = (f32[512,128]{1,0:T(8,128)S(1)}, f32[512,128]{1,0:T(8,128)S(1)}, u32[]{:S(2)}, u32[]{:S(2)}) collective-permute-start(f32[512,128]{1,0:T(8,128)S(1)} %get-tuple-element.68), channel_id=1, source_target_pairs={{4,0},{8,12},{5,1},{9,13},{6,2},{10,14},{7,3},{11,15},{20,16},{24,... | collective-permute-start | bytes 786440 | tf_op jit(solution)/shard_map/ppermute | solution.py:521
  75.3 1.3 %collective-permute-start.11 = (f32[512,128]{1,0:T(8,128)S(1)}, f32[512,128]{1,0:T(8,128)S(1)}, u32[]{:S(2)}, u32[]{:S(2)}) collective-permute-start(f32[512,128]{1,0:T(8,128)S(1)} %get-tuple-element.67), channel_id=1, source_target_pairs={{4,0},{8,12},{5,1},{9,13},{6,2},{10,14},{7,3},{11,15},{20,16},{24,... | collective-permute-start | bytes 786440 | tf_op jit(solution)/shard_map/ppermute | solution.py:521
  76.6 3.2 %early.1.acc_ref = f32[4,1024,256]{2,1,0:T(8,128)S(1)} custom-call(s32[1]{0:T(128)} %bitcast.pos_ref, f32[7,1024,256]{2,1,0:T(8,128)S(1)} %bitcast.4, f32[7,1024,256]{2,1,0:T(8,128)S(1)} %bitcast.4, f32[7,1024,256]{2,1,0:T(8,128)S(1)} %bitcast.4, f32[7,1024,256]{2,1,0:T(8,128)S(1)} %bitcast.4, f32[1024,256]{1,0:T(8,128)S(1)} %copy-done.6, ...), custom_call_target="tpu_custom_call" | custom-call | flops 26214400 | bytes 15728640 | tf_op jit(solution)/shard_map/early/pallas_call | solution.py:368
  79.9 0.7 dft.15.three_g
  80.6 6.8 %late.1 = (f32[512,256]{1,0:T(8,128)}, f32[1024,256]{1,0:T(8,128)}, f32[512,256]{1,0:T(8,128)S(1)}, f32[1,256]{1,0:T(1,128)}) custom-call(s32[1]{0:T(128)} %bitcast.pos_ref, bf16[2,4,256,256]{3,2,1,0:T(8,128)(2,1)S(1)} %copy-done.3, f32[4,1024,256]{2,1,0:T(8,128)S(1)} %early.1.acc_ref, f32[7,1024,256]{2,1,0:T(8,128)} %copy-done, ...), custom_call_target="tpu_custom_call" | custom-call | flops 1610612736 | bytes 13107200 | tf_op jit(solution)/shard_map/late/pallas_call | solution.py:487
  87.4 1.1 %fusion = (f32[512,256]{1,0:T(8,128)}, f32[512,256]{1,0:T(8,128)}) fusion(f32[512,256]{1,0:T(8,128)S(1)} %copy-done.10, f32[512,256]{1,0:T(8,128)S(1)} %get-tuple-element.70, f32[512,128]{1,0:T(8,128)S(1)} %collective-permute-done.12, f32[512,128]{1,0:T(8,128)S(1)} %collective-permute-done.11, f32[512,256]{1,0:T(8,128)S(1)} %copy-done.12), kind=kLoop, calls=%fused_computation.1 | loop fusion | flops 524288 | bytes 3145728 | tf_op jit(solution)/shard_map/mul | solution.py:576
  (35 shorter events, 0.1 us)
Async XLA Ops:
  0.6 14.1 %copy-start.2 = (bf16[2,4,256,256]{3,2,1,0:T(8,128)(2,1)S(1)}, bf16[2,4,256,256]{3,2,1,0:T(8,128)(2,1)}, u32[]{:S(2)}) copy-start(bf16[2,4,256,256]{3,2,1,0:T(8,128)(2,1)} %constant.11.clone.table_ref) | copy-start | bytes 3145732
  0.6 1.1 %copy-start.7 = (f32[512,256]{1,0:T(8,128)S(1)}, f32[512,256]{1,0:T(8,128)}, u32[]{:S(2)}) copy-start(f32[512,256]{1,0:T(8,128)} %rest_11_.1) | copy-start | bytes 1572868
  1.8 1.0 %copy-start.9 = (f32[512,256]{1,0:T(8,128)S(1)}, f32[512,256]{1,0:T(8,128)}, u32[]{:S(2)}) copy-start(f32[512,256]{1,0:T(8,128)} %key_ref.1) | copy-start | bytes 1572868
  2.8 1.0 %copy-start.11 = (f32[512,256]{1,0:T(8,128)S(1)}, f32[512,256]{1,0:T(8,128)}, u32[]{:S(2)}) copy-start(f32[512,256]{1,0:T(8,128)} %values_ref.1) | copy-start | bytes 1572868
  3.9 1.0 %copy-start.15 = (f32[512,256]{1,0:T(8,128)S(1)}, f32[512,256]{1,0:T(8,128)}, u32[]{:S(2)}) copy-start(f32[512,256]{1,0:T(8,128)} %query_ref.1) | copy-start | bytes 1572868
  5.1 8.8 %copy-start.13 = (f32[512,128]{1,0:T(8,128)}, f32[512,128]{1,0:T(8,128)S(1)}, u32[]{:S(2)}) copy-start(f32[512,128]{1,0:T(8,128)S(1)} %get-tuple-element.49.refs_1_.rest_4_) | copy-start | bytes 786436
  5.2 18.5 %collective-permute-start = (f32[520,256]{1,0:T(8,128)S(1)}, f32[520,256]{1,0:T(8,128)S(1)}, u32[]{:S(2)}, u32[]{:S(2)}) collective-permute-start(f32[520,256]{1,0:T(8,128)S(1)} %get-tuple-element.40.refs_0_.rest_2_.rest_5_), channel_id=1, source_target_pairs={{0,4},{4,8},{8,12},{1,5},{5,9},{9,13},{2,6},{6,10},{10,14},{3,7},{... | collective-permute-start | bytes 1597448 | tf_op jit(solution)/shard_map/ppermute | solution.py:521
  8.6 15.6 %collective-permute-start.1 = (f32[520,256]{1,0:T(8,128)S(1)}, f32[520,256]{1,0:T(8,128)}, u32[]{:S(2)}, u32[]{:S(2)}) collective-permute-start(f32[520,256]{1,0:T(8,128)S(1)} %get-tuple-element.40.refs_0_.rest_2_.rest_5_), channel_id=1, source_target_pairs={{4,0},{8,4},{12,8},{5,1},{9,5},{13,9},{6,2},{10,6},{14,10},{7,3},{... | collective-permute-start | bytes 1597448 | tf_op jit(solution)/shard_map/ppermute | solution.py:521
  11.0 1.2 %copy-start.1 = (bf16[2,4,256,256]{3,2,1,0:T(8,128)(2,1)S(1)}, bf16[2,4,256,256]{3,2,1,0:T(8,128)(2,1)}, u32[]{:S(2)}) copy-start(bf16[2,4,256,256]{3,2,1,0:T(8,128)(2,1)} %constant.11.clone.table_ref) | copy-start | bytes 3145732
  12.3 2.6 %copy-start.4 = (f32[4096,256]{1,0:T(8,128)S(1)}, f32[4096,256]{1,0:T(8,128)}, u32[]{:S(2)}) copy-start(f32[4096,256]{1,0:T(8,128)} %x_ref.1) | copy-start | bytes 12582916
  13.0 1.0 %copy-start.5 = (f32[1024,256]{1,0:T(8,128)}, f32[1024,256]{1,0:T(8,128)S(1)}, u32[]{:S(2)}) copy-start(f32[1024,256]{1,0:T(8,128)S(1)} %dft.8.own_g) | copy-start | bytes 3145732
  20.8 2.9 %copy-start = (f32[7,1024,256]{2,1,0:T(8,128)}, f32[7,1024,256]{2,1,0:T(8,128)S(1)}, u32[]{:S(2)}) copy-start(f32[7,1024,256]{2,1,0:T(8,128)S(1)} %taps.1.win_own.win_left.win_right.win_two.win_near.win_far.win_ref) | copy-start | bytes 22020100
  24.2 31.5 %collective-permute-start.6 = (f32[520,256]{1,0:T(8,128)S(1)}, f32[520,256]{1,0:T(8,128)}, u32[]{:S(2)}, u32[]{:S(2)}) collective-permute-start(f32[520,256]{1,0:T(8,128)S(1)} %collective-permute-done.refs_0_.rest_6_), channel_id=1, source_target_pairs={{4,8},{8,12},{5,9},{9,13},{6,10},{10,14},{7,11},{11,15},{20,24},{2... | collective-permute-start | bytes 1597448 | tf_op jit(solution)/shard_map/ppermute | solution.py:521
  28.5 27.2 %collective-permute-start.7 = (f32[520,256]{1,0:T(8,128)}, f32[520,256]{1,0:T(8,128)}, u32[]{:S(2)}, u32[]{:S(2)}) collective-permute-start(f32[520,256]{1,0:T(8,128)} %collective-permute-done.1.refs_0_.rest_7_), channel_id=1, source_target_pairs={{8,4},{4,0},{9,5},{5,1},{10,6},{6,2},{11,7},{7,3},{24,20},{20,16},... | collective-permute-start | bytes 1597448 | tf_op jit(solution)/shard_map/ppermute | solution.py:521
  30.4 13.1 %collective-permute-start.2 = (f32[512,128]{1,0:T(8,128)S(1)}, f32[512,128]{1,0:T(8,128)}, u32[]{:S(2)}, u32[]{:S(2)}) collective-permute-start(f32[512,128]{1,0:T(8,128)S(1)} %get-tuple-element.41.refs_0_.rest_3_), channel_id=1, source_target_pairs={{0,4},{4,8},{8,12},{1,5},{5,9},{9,13},{2,6},{6,10},{10,14},{3,7},{... | collective-permute-start | bytes 786440 | tf_op jit(solution)/shard_map/ppermute | solution.py:521
  35.2 13.6 %collective-permute-start.3 = (f32[512,128]{1,0:T(8,128)S(1)}, f32[512,128]{1,0:T(8,128)}, u32[]{:S(2)}, u32[]{:S(2)}) collective-permute-start(f32[512,128]{1,0:T(8,128)S(1)} %get-tuple-element.41.refs_0_.rest_3_), channel_id=1, source_target_pairs={{4,0},{8,4},{12,8},{5,1},{9,5},{13,9},{6,2},{10,6},{14,10},{7,3},{... | collective-permute-start | bytes 786440 | tf_op jit(solution)/shard_map/ppermute | solution.py:521
  37.1 11.7 %copy-start.14 = (f32[512,128]{1,0:T(8,128)S(1)}, f32[512,128]{1,0:T(8,128)}, u32[]{:S(2)}) copy-start(f32[512,128]{1,0:T(8,128)} %copy-done.13) | copy-start | bytes 786436
  37.9 32.4 %slice-start = ((s8[7340032]{0:T(1024)(128)(4,1)}), s8[4194304]{0:T(1024)(128)(4,1)S(1)}, s32[]{:S(2)}) async-start(s8[7340032]{0:T(1024)(128)(4,1)} %bitcast.3), calls=%async_computation | async-start | bytes 8388608
  48.8 10.6 %collective-permute-start.4 = (f32[512,128]{1,0:T(8,128)S(1)}, f32[512,128]{1,0:T(8,128)S(1)}, u32[]{:S(2)}, u32[]{:S(2)}) collective-permute-start(f32[512,128]{1,0:T(8,128)S(1)} %copy-done.14), channel_id=1, source_target_pairs={{0,4},{4,8},{8,12},{1,5},{5,9},{9,13},{2,6},{6,10},{10,14},{3,7},{... | collective-permute-start | bytes 786440 | tf_op jit(solution)/shard_map/ppermute | solution.py:521
  50.7 10.3 %collective-permute-start.5 = (f32[512,128]{1,0:T(8,128)S(1)}, f32[512,128]{1,0:T(8,128)S(1)}, u32[]{:S(2)}, u32[]{:S(2)}) collective-permute-start(f32[512,128]{1,0:T(8,128)S(1)} %copy-done.14), channel_id=1, source_target_pairs={{4,0},{8,4},{12,8},{5,1},{9,5},{13,9},{6,2},{10,6},{14,10},{7,3},{... | collective-permute-start | bytes 786440 | tf_op jit(solution)/shard_map/ppermute | solution.py:521
  57.0 13.3 %slice-start.1 = ((s8[7340032]{0:T(1024)(128)(4,1)}), s8[3145728]{0:T(1024)(128)(4,1)S(1)}, s32[]{:S(2)}) async-start(s8[7340032]{0:T(1024)(128)(4,1)} %bitcast.3), calls=%async_computation.1 | async-start | bytes 6291456
  57.0 13.3 %copy-start.3 = (bf16[2,4,256,256]{3,2,1,0:T(8,128)(2,1)S(1)}, bf16[2,4,256,256]{3,2,1,0:T(8,128)(2,1)}, u32[]{:S(2)}) copy-start(bf16[2,4,256,256]{3,2,1,0:T(8,128)(2,1)} %constant.12.clone.inverse_ref) | copy-start | bytes 3145732
  57.0 22.9 %collective-permute-start.8 = (f32[520,256]{1,0:T(8,128)S(1)}, f32[520,256]{1,0:T(8,128)S(1)}, u32[]{:S(2)}, u32[]{:S(2)}) collective-permute-start(f32[520,256]{1,0:T(8,128)S(1)} %add.6.refs_0_.rest_8_), channel_id=1, source_target_pairs={{4,0},{8,12},{5,1},{9,13},{6,2},{10,14},{7,3},{11,15},{20,16},{24,... | collective-permute-start | bytes 1597448 | tf_op jit(solution)/shard_map/ppermute | solution.py:521
  61.0 9.2 %collective-permute-start.9 = (f32[512,128]{1,0:T(8,128)S(1)}, f32[512,128]{1,0:T(8,128)S(1)}, u32[]{:S(2)}, u32[]{:S(2)}) collective-permute-start(f32[512,128]{1,0:T(8,128)S(1)} %broadcast_select_fusion.1), channel_id=1, source_target_pairs={{4,8},{8,4},{5,9},{9,5},{6,10},{10,6},{7,11},{11,7},{20,24},{24,20... | collective-permute-start | bytes 786440 | tf_op jit(solution)/shard_map/ppermute | solution.py:521
  63.0 9.1 %collective-permute-start.10 = (f32[512,128]{1,0:T(8,128)S(1)}, f32[512,128]{1,0:T(8,128)S(1)}, u32[]{:S(2)}, u32[]{:S(2)}) collective-permute-start(f32[512,128]{1,0:T(8,128)S(1)} %broadcast_select_fusion), channel_id=1, source_target_pairs={{4,8},{8,4},{5,9},{9,5},{6,10},{10,6},{7,11},{11,7},{20,24},{24,20... | collective-permute-start | bytes 786440 | tf_op jit(solution)/shard_map/ppermute | solution.py:521
  72.1 4.5 %copy-start.6 = (f32[1024,256]{1,0:T(8,128)S(1)}, f32[1024,256]{1,0:T(8,128)}, u32[]{:S(2)}) copy-start(f32[1024,256]{1,0:T(8,128)} %copy-done.5) | copy-start | bytes 3145732
  73.8 6.8 %copy-start.8 = (f32[512,256]{1,0:T(8,128)S(1)}, f32[512,256]{1,0:T(8,128)}, u32[]{:S(2)}) copy-start(f32[512,256]{1,0:T(8,128)} %rest_11_.1) | copy-start | bytes 1572868
  73.8 6.8 %copy-start.16 = (f32[256]{0:T(256)S(1)}, f32[256]{0:T(256)}, u32[]{:S(2)}) copy-start(f32[256]{0:T(256)} %param.12) | copy-start | bytes 3076
  73.8 13.6 %collective-permute-start.12 = (f32[512,128]{1,0:T(8,128)S(1)}, f32[512,128]{1,0:T(8,128)S(1)}, u32[]{:S(2)}, u32[]{:S(2)}) collective-permute-start(f32[512,128]{1,0:T(8,128)S(1)} %get-tuple-element.68), channel_id=1, source_target_pairs={{4,0},{8,12},{5,1},{9,13},{6,2},{10,14},{7,3},{11,15},{20,16},{24,... | collective-permute-start | bytes 786440 | tf_op jit(solution)/shard_map/ppermute | solution.py:521
  75.3 12.1 %collective-permute-start.11 = (f32[512,128]{1,0:T(8,128)S(1)}, f32[512,128]{1,0:T(8,128)S(1)}, u32[]{:S(2)}, u32[]{:S(2)}) collective-permute-start(f32[512,128]{1,0:T(8,128)S(1)} %get-tuple-element.67), channel_id=1, source_target_pairs={{4,0},{8,12},{5,1},{9,13},{6,2},{10,14},{7,3},{11,15},{20,16},{24,... | collective-permute-start | bytes 786440 | tf_op jit(solution)/shard_map/ppermute | solution.py:521
  80.6 6.8 %copy-start.10 = (f32[512,256]{1,0:T(8,128)S(1)}, f32[512,256]{1,0:T(8,128)}, u32[]{:S(2)}) copy-start(f32[512,256]{1,0:T(8,128)} %key_ref.1) | copy-start | bytes 1572868
  80.6 6.8 %copy-start.12 = (f32[512,256]{1,0:T(8,128)S(1)}, f32[512,256]{1,0:T(8,128)}, u32[]{:S(2)}) copy-start(f32[512,256]{1,0:T(8,128)} %values_ref.1) | copy-start | bytes 1572868

commit v3 on v2

--- a/solution.py
+++ b/solution.py
@@ -84,16 +84,13 @@
     return jax.ShapeDtypeStruct(shape, jnp.float32)
 
 
-def prepare_kernel(query_ref, key_ref, values_ref, up_ref, gated_ref, *rest):
-    mixed_refs, sum_ref = rest[:-1], rest[-1]
+def prepare_kernel(query_ref, key_ref, values_ref, up_ref, gated_ref, mixed_ref, sum_ref):
     step = pl.program_id(0)
     rows, width = key_ref.shape
-    half = width // len(mixed_refs)
     gated = key_ref[...] * values_ref[...]
     mixed = up_ref[...] * query_ref[...]
     gated_ref[pl.ds(pl.multiple_of(step * rows, rows), rows), :] = gated
-    for i, ref in enumerate(mixed_refs):
-        ref[...] = mixed[:, i * half : (i + 1) * half]
+    mixed_ref[...] = mixed
     part = jnp.sum((gated * mixed).reshape(rows // 8, 8, width), axis=0)
 
     @pl.when(step == 0)
@@ -110,20 +107,19 @@
         gated_ref[seg:, :] = sum_ref[...]
 
 
-def prepare(query_gate, key_gate, values, upstream, halves):
+def prepare(query_gate, key_gate, values, upstream):
     seg, width = values.shape
     steps = 4
     rows = seg // steps
     block = pl.BlockSpec((rows, width), lambda i: (i, 0))
-    half = pl.BlockSpec((rows, width // halves), lambda i: (i, 0))
     return pl.pallas_call(
         prepare_kernel,
         grid=(steps,),
         in_specs=[block] * 4,
-        out_specs=[whole_spec((seg + 8, width))] + [half] * halves,
-        out_shape=[f32(seg + 8, width)] + [f32(seg, width // halves)] * halves,
+        out_specs=[whole_spec((seg + 8, width)), block],
+        out_shape=[f32(seg + 8, width), f32(seg, width)],
         scratch_shapes=[pltpu.VMEM((8, width), jnp.float32)],
-        compiler_params=params(8),
+        compiler_params=params(56),
         cost_estimate=cost(4 * seg * width, 24 * seg * width),
         name="prepare",
     )(query_gate, key_gate, values, upstream)
@@ -389,9 +385,8 @@
 def late_kernel(
     pos_ref, inverse_ref, acc_ref, win_ref, three_g, two_g, own_m, left_m, right_m, *rest
 ):
-    two_m, (gated_ref, mixed, strips), (skip_ref, up_ref, query_out, filter_out, back_out, skip_out) = (
-        rest[:2], (rest[2], rest[3:5], rest[5:10]), rest[10:16])
-    x_high, x_low, z_ref = rest[16:]
+    two_m, (gated_ref, mixed_ref, partial_ref), strips = rest[:2], rest[2:5], rest[5:10]
+    skip_ref, up_ref, query_out, filter_out, back_out, skip_out, x_high, x_low, z_ref = rest[10:]
     group = pl.program_id(0)
     pos, sign = pos_ref[0], group_sign()
     rows, width = own_m.shape
@@ -452,9 +447,9 @@
                 if slot == 0:
                     query_out[at, :] = up_ref[at, :] * (quarter + skip_ref[...] * gated_ref[at, :])
                 elif slot == 1:
-                    for h in range(2):
-                        lanes = slice(h * half, (h + 1) * half)
-                        back_out[at, lanes] = quarter[:, lanes] + skip_ref[:, lanes] * mixed[h][at, :]
+                    back = quarter + skip_ref[...] * mixed_ref[at, :]
+                    back_out[at, :half] = back[:, :half] + partial_ref[at, :]
+                    back_out[at, half:] = back[:, half:]
                 else:
                     base = (slot - 2) * seg + i * sub
                     filter_out[base : base + sub, :] = quarter
@@ -471,7 +466,7 @@
         skip_out[...] = jnp.sum(total, axis=0, keepdims=True)
 
 
-def late(pos, inverse, acc, windows, three_g, two_g, own_m, left_m, right_m, two_m, blocks, mixed, skip, upstream):
+def late(pos, inverse, acc, windows, three_g, two_g, own_m, left_m, right_m, two_m, blocks, mixed, partial, skip, upstream):
     seg, width = upstream.shape
     rows = seg // 2
     mid = windows.shape[0] // 2
@@ -496,7 +491,8 @@
                 *[group] * 5,
                 *[group_half] * 2,
                 whole_spec((seg, width)),
-                *[whole_spec((seg, width // 2))] * 2,
+                whole_spec((seg, width)),
+                whole_spec((seg, width // 2)),
                 *[strip] * 5,
                 whole_spec((1, width)),
                 whole_spec((seg, width)),
@@ -511,10 +507,10 @@
             ],
         ),
         out_shape=[f32(seg, width), f32(2 * seg, width), f32(seg, width), f32(1, width)],
-        compiler_params=params(32),
+        compiler_params=params(20),
         cost_estimate=cost(12 * seg * seg * width * 2, 100 * seg * width),
         name="late",
-    )(pos, inverse, acc, windows, three_g, two_g, own_m, left_m, right_m, *two_m, blocks[0], *mixed, *blocks, skip, upstream)
+    )(pos, inverse, acc, windows, three_g, two_g, own_m, left_m, right_m, *two_m, blocks[0], mixed, partial, *blocks, skip, upstream)
 
 
 def send(x, *pairs):
@@ -533,34 +529,33 @@
     seg, width = values.shape
     forward_np, inverse_np = tables(seg)
     table, inverse = jnp.asarray(forward_np), jnp.asarray(inverse_np)
+    half = width // 2
     position = lax.axis_index("ctx")
     pos = position.astype(jnp.int32).reshape(1)
     after = lax.optimization_barrier
 
-    gated, *mixed = prepare(query_gate, key_gate, values, upstream, 2)
+    gated, mixed = prepare(query_gate, key_gate, values, upstream)
     left, right = to_right(gated), to_left(gated)
-    left_m0, right_m0 = to_right(mixed[0]), to_left(mixed[0])
+    left_x, right_x = to_right(mixed), to_left(mixed)
     windows = taps_spectra(table, filter_taps, seg)
-    own_g, own_m = dft(table, seg, gated), dft(table, seg, *mixed)
-    left, right, windows, own_g, own_m = after((left, right, windows, own_g, own_m))
+    own_g = dft(table, seg, gated)
+    left, right, windows, own_g = after((left, right, windows, own_g))
 
     two_l, two_r = send(left, (1, 2), (2, 3)), send(right, (2, 1), (1, 0))
-    left_g, right_g = dft(table, seg, left), dft(table, seg, right)
-    left_m0, right_m0, mixed_1, left_g, right_g = after((left_m0, right_m0, mixed[1], left_g, right_g))
-    left_m1, right_m1 = to_right(mixed_1), to_left(mixed_1)
-    far_0 = jnp.where(position == 1, left_m0, right_m0)
-    two_l, two_r, far_0 = after((two_l, two_r, far_0))
+    own_m, left_g, right_g = dft(table, seg, mixed), dft(table, seg, left), dft(table, seg, right)
+    left_x, right_x, own_m, left_g, right_g = after((left_x, right_x, own_m, left_g, right_g))
+
+    far = [jnp.where(position == 1, left_x[:, at], right_x[:, at]) for at in (slice(half), slice(half, None))]
+    two_m0, two_m1 = [send(x, (1, 2), (2, 1)) for x in far]
+    left_m, right_m = dft(table, seg, left_x), dft(table, seg, right_x)
+    two_l, two_r, left_m, right_m = after((two_l, two_r, left_m, right_m))
+
     two = two_l + two_r
     three = send(two, (1, 0), (2, 3))
-    two_m0 = send(far_0, (1, 2), (2, 1))
     two_g = dft(table, seg, two)
-
-    left_m1, right_m1, two_g = after((left_m1, right_m1, two_g))
-    far_1 = jnp.where(position == 1, left_m1, right_m1)
-    two_m1 = send(far_1, (1, 2), (2, 1))
-    left_m, right_m = dft(table, seg, left_m0, left_m1), dft(table, seg, right_m0, right_m1)
     acc = early(pos, windows, (own_g, left_g, right_g, two_g), (own_m, left_m, right_m), seg)
-    two_m0, left_m, right_m = after((two_m0, left_m, right_m))
+    two_m0, acc = after((two_m0, acc))
+
     spec_0, partial_0 = back_partial(pos, table, inverse, windows, left_m, right_m, two_m0, 0, seg)
     two_m1, partial_0 = after((two_m1, partial_0))
     partial_0 = send(partial_0, (1, 0), (2, 3))
@@ -569,10 +564,10 @@
     three_g = dft(table, seg, three)
     query_grad, filter_grad, back, skip_grad = late(
         pos, inverse, acc, windows, three_g, two_g, own_m, left_m, right_m, (spec_0, spec_1),
-        (gated, left, right, two, three), mixed, skip_gain[None, :], upstream,
-    )
-    partial_0, partial_1, back = after((partial_0, partial_1, back))
-    back = back + jnp.concatenate([partial_0, partial_1], axis=1)
+        (gated, left, right, two, three), mixed, partial_0, skip_gain[None, :], upstream,
+    )
+    back, partial_1 = after((back, partial_1))
+    back = jnp.concatenate([back[:, :half], back[:, half:] + partial_1], axis=1)
     return (query_grad, back * values, back * key_gate, filter_grad, skip_grad[0])
 
 

time: 89.3 us -> 85.7 us (0.960)
  the two profiles are of different devices: /device:TPU:12 before, /device:TPU:0 now
where the time goes in v3:
time: 85.7 us; the launch traced here: 85.1 us
  Pallas kernels  31.3 us (37%)
  starting transfers between devices  22.4 us (26%)
  waiting for transfers between devices  19.3 us (23%)
  local copies, waits for them, and re-layouts  7.41 us (9%)
  other arithmetic  3.62 us (4%)
  between operations  1 us (1%)
    ppermute x11, starting transfers between devices, send(): return lax.ppermute(x, 'ctx', list(pairs))  22.4 us
    ppermute x11, waiting for transfers between devices, send(): return lax.ppermute(x, 'ctx', list(pairs))  19.3 us
    pallas_call x8, Pallas kernels, dft(): pl.pallas_call(dft_kernel, grid=(1,), in_specs=[whole_spec(table.shape)]...  9.33 us
    unnamed x28, local copies, waits for them, and re-layouts  7.41 us
    pallas_call x1, Pallas kernels, late(): pl.pallas_call(late_kernel, grid_spec=pltpu.PrefetchScalarGridSpec(num_sc...  6.78 us
    pallas_call x1, Pallas kernels, taps_spectra(): pl.pallas_call(taps_kernel, grid=(blocks,), in_specs=[whole_spec(table.sh...  5.93 us
    pallas_call x1, Pallas kernels, prepare(): pl.pallas_call(prepare_kernel, grid=(steps,), in_specs=[block] * 4, out_s...  3.74 us
    pallas_call x2, Pallas kernels, back_partial(): pl.pallas_call(partial_kernel, grid_spec=pltpu.PrefetchScalarGridSpec(num...  3.34 us
  transfers between devices with their start and end apart: 11, of which 3 were waited for; matrix products, arithmetic and copies ran while one was open for 1% of the time, Pallas kernels for 32%

profile of v3, /device:TPU:0, one launch (start us, length us, event | category | flops | bytes accessed | tf_op | source)
XLA Modules:
  0.0 85.1 jit_solution(10377977941148694388)
XLA Ops:
  0.6 3.7 %prepare.1 = (f32[520,256]{1,0:T(8,128)}, f32[512,256]{1,0:T(8,128)}) custom-call(f32[512,256]{1,0:T(8,128)} %query_ref.1, f32[512,256]{1,0:T(8,128)} %key_ref.1, f32[512,256]{1,0:T(8,128)} %values_ref.1, f32[512,256]{1,0:T(8,128)} %rest_11_.1), custom_call_target="tpu_custom_call" | custom-call | flops 524288 | bytes 3145728 | tf_op jit(solution)/shard_map/prepare/pallas_call | solution.py:115
  4.4 1.3 %collective-permute-start.3 = (f32[520,256]{1,0:T(8,128)}, f32[520,256]{1,0:T(8,128)S(1)}, u32[]{:S(2)}, u32[]{:S(2)}) collective-permute-start(f32[520,256]{1,0:T(8,128)} %get-tuple-element.35.refs_0_.rest_2_.rest_5_), channel_id=1, source_target_pairs={{4,0},{8,4},{12,8},{5,1},{9,5},{13,9},{6,2},{10,6},{14,10},{7,3},{... | collective-permute-start | bytes 1597448 | tf_op jit(solution)/shard_map/ppermute | solution.py:517
  5.7 6.4 %collective-permute-start.2 = (f32[520,256]{1,0:T(8,128)}, f32[520,256]{1,0:T(8,128)}, u32[]{:S(2)}, u32[]{:S(2)}) collective-permute-start(f32[520,256]{1,0:T(8,128)} %get-tuple-element.35.refs_0_.rest_2_.rest_5_), channel_id=1, source_target_pairs={{0,4},{4,8},{8,12},{1,5},{5,9},{9,13},{2,6},{6,10},{10,14},{3,7},{... | collective-permute-start | bytes 1597448 | tf_op jit(solution)/shard_map/ppermute | solution.py:517
  12.0 1.3 %collective-permute-start.1 = (f32[512,256]{1,0:T(8,128)}, f32[512,256]{1,0:T(8,128)}, u32[]{:S(2)}, u32[]{:S(2)}) collective-permute-start(f32[512,256]{1,0:T(8,128)} %get-tuple-element.34.refs_0_.rest_3_), channel_id=1, source_target_pairs={{4,0},{8,4},{12,8},{5,1},{9,5},{13,9},{6,2},{10,6},{14,10},{7,3},{... | collective-permute-start | bytes 1572872 | tf_op jit(solution)/shard_map/ppermute | solution.py:517
  13.3 5.4 %collective-permute-start = (f32[512,256]{1,0:T(8,128)}, f32[512,256]{1,0:T(8,128)}, u32[]{:S(2)}, u32[]{:S(2)}) collective-permute-start(f32[512,256]{1,0:T(8,128)} %get-tuple-element.34.refs_0_.rest_3_), channel_id=1, source_target_pairs={{0,4},{4,8},{8,12},{1,5},{5,9},{9,13},{2,6},{6,10},{10,14},{3,7},{... | collective-permute-start | bytes 1572872 | tf_op jit(solution)/shard_map/ppermute | solution.py:517
  18.7 1.2 %copy-done.1 = bf16[2,4,256,256]{3,2,1,0:T(8,128)(2,1)S(1)} copy-done((bf16[2,4,256,256]{3,2,1,0:T(8,128)(2,1)S(1)}, bf16[2,4,256,256]{3,2,1,0:T(8,128)(2,1)}, u32[]{:S(2)}) %copy-start.1) | copy-done | bytes 1048600
  19.9 2.2 %copy-done.5 = f32[4096,256]{1,0:T(8,128)S(1)} copy-done((f32[4096,256]{1,0:T(8,128)S(1)}, f32[4096,256]{1,0:T(8,128)}, u32[]{:S(2)}) %copy-start.5) | copy-done | bytes 4194328
  22.1 5.9 %taps.1.win_own.win_left.win_right.win_two.win_near.win_far.win_ref = f32[7,1024,256]{2,1,0:T(8,128)S(1)} custom-call(bf16[2,4,256,256]{3,2,1,0:T(8,128)(2,1)S(1)} %copy-done.1, f32[4096,256]{1,0:T(8,128)S(1)} %copy-done.5), custom_call_target="tpu_custom_call" | custom-call | flops 3221225472 | bytes 12582912 | tf_op jit(solution)/shard_map/taps/pallas_call | solution.py:176
  28.1 2.9 %copy-done = f32[7,1024,256]{2,1,0:T(8,128)} copy-done((f32[7,1024,256]{2,1,0:T(8,128)}, f32[7,1024,256]{2,1,0:T(8,128)S(1)}, u32[]{:S(2)}) %copy-start) | copy-done | bytes 7340056
  31.0 0.7 dft.9.own_g
  31.7 0.0 collective-permute-done.2.refs_0_.rest_6_
  31.7 1.5 %collective-permute-start.5 = (f32[520,256]{1,0:T(8,128)}, f32[520,256]{1,0:T(8,128)}, u32[]{:S(2)}, u32[]{:S(2)}) collective-permute-start(f32[520,256]{1,0:T(8,128)} %collective-permute-done.2.refs_0_.rest_6_), channel_id=1, source_target_pairs={{4,8},{8,12},{5,9},{9,13},{6,10},{10,14},{7,11},{11,15},{20,24},{2... | collective-permute-start | bytes 1597448 | tf_op jit(solution)/shard_map/ppermute | solution.py:517
  33.2 1.3 %collective-permute-start.6 = (f32[520,256]{1,0:T(8,128)S(1)}, f32[520,256]{1,0:T(8,128)}, u32[]{:S(2)}, u32[]{:S(2)}) collective-permute-start(f32[520,256]{1,0:T(8,128)S(1)} %collective-permute-done.3.refs_0_.rest_7_), channel_id=1, source_target_pairs={{8,4},{4,0},{9,5},{5,1},{10,6},{6,2},{11,7},{7,3},{24,20},{20,16},... | collective-permute-start | bytes 1597448 | tf_op jit(solution)/shard_map/ppermute | solution.py:517
  34.5 0.0 copy-start.6
  34.5 1.0 %copy-done.6 = f32[512,256]{1,0:T(8,128)S(1)} copy-done((f32[512,256]{1,0:T(8,128)S(1)}, f32[512,256]{1,0:T(8,128)}, u32[]{:S(2)}) %copy-start.6) | copy-done | bytes 524312
  35.5 0.7 dft.8.own_m
  36.3 1.8 %dft.10.left_g = f32[1024,256]{1,0:T(8,128)S(1)} custom-call(bf16[2,4,256,256]{3,2,1,0:T(8,128)(2,1)S(1)} %copy-done.2, f32[520,256]{1,0:T(8,128)} %collective-permute-done.2.refs_0_.rest_6_), custom_call_target="tpu_custom_call" | custom-call | flops 402653184 | bytes 1572864 | tf_op jit(solution)/shard_map/dft/pallas_call | solution.py:141
  38.0 0.0 slice-start
  38.0 0.7 dft.11.right_g
  38.7 0.0 collective-permute-done.1.refs_0_
  38.8 2.1 %dft.12.left_m.left_ref = f32[1024,256]{1,0:T(8,128)S(1)} custom-call(bf16[2,4,256,256]{3,2,1,0:T(8,128)(2,1)S(1)} %copy-done.2, f32[512,256]{1,0:T(8,128)} %collective-permute-done.refs_0_), custom_call_target="tpu_custom_call" | custom-call | flops 402653184 | bytes 1572864 | tf_op jit(solution)/shard_map/dft/pallas_call | solution.py:141
  40.9 0.0 slice-start.1
  40.9 1.9 %dft.13.right_m.right_ref = f32[1024,256]{1,0:T(8,128)S(1)} custom-call(bf16[2,4,256,256]{3,2,1,0:T(8,128)(2,1)S(1)} %copy-done.2, f32[512,256]{1,0:T(8,128)} %collective-permute-done.1.refs_0_), custom_call_target="tpu_custom_call" | custom-call | flops 402653184 | bytes 1572864 | tf_op jit(solution)/shard_map/dft/pallas_call | solution.py:141
  42.8 7.1 %collective-permute-done.6 = f32[520,256]{1,0:T(8,128)} collective-permute-done((f32[520,256]{1,0:T(8,128)S(1)}, f32[520,256]{1,0:T(8,128)}, u32[]{:S(2)}, u32[]{:S(2)}) %collective-permute-start.6) | collective-permute-done | bytes 532512 | tf_op jit(solution)/shard_map/ppermute | solution.py:517
  50.0 1.3 %add.6.refs_0_.rest_8_ = f32[520,256]{1,0:T(8,128)S(1)} add(f32[520,256]{1,0:T(8,128)} %collective-permute-done.5, f32[520,256]{1,0:T(8,128)} %collective-permute-done.6) | non-fusion elementwise | flops 133120 | bytes 1597440 | tf_op jit(solution)/shard_map/add | solution.py:553
  51.2 1.3 %collective-permute-start.7 = (f32[520,256]{1,0:T(8,128)S(1)}, f32[520,256]{1,0:T(8,128)S(1)}, u32[]{:S(2)}, u32[]{:S(2)}) collective-permute-start(f32[520,256]{1,0:T(8,128)S(1)} %add.6.refs_0_.rest_8_), channel_id=1, source_target_pairs={{4,0},{8,12},{5,1},{9,13},{6,2},{10,14},{7,3},{11,15},{20,16},{24,... | collective-permute-start | bytes 1597448 | tf_op jit(solution)/shard_map/ppermute | solution.py:517
  52.5 1.2 %slice_select_fusion = (f32[512,128]{1,0:T(8,128)S(1)}, f32[512,128]{1,0:T(8,128)S(1)}) fusion(f32[512,256]{1,0:T(8,128)} %collective-permute-done.1.refs_0_, f32[512,256]{1,0:T(8,128)} %collective-permute-done.refs_0_, pred[]{:T(512)S(6)} %eq.4), kind=kLoop, calls=%fused_computation.4 | loop fusion | flops 131072 | bytes 1572865 | tf_op jit(solution)/shard_map/jit(_where)/select_n | solution.py:548
  53.8 0.7 collective-permute-start.4
  54.5 0.7 collective-permute-start.8
  55.2 0.7 dft.14.two_g
  55.9 0.0 copy-start.3
  55.9 2.2 %early.1.acc_ref = f32[4,1024,256]{2,1,0:T(8,128)S(1)} custom-call(s32[1]{0:T(128)} %bitcast.pos_ref, f32[7,1024,256]{2,1,0:T(8,128)S(1)} %bitcast.4, f32[7,1024,256]{2,1,0:T(8,128)S(1)} %bitcast.4, f32[7,1024,256]{2,1,0:T(8,128)S(1)} %bitcast.4, f32[7,1024,256]{2,1,0:T(8,128)S(1)} %bitcast.4, f32[1024,256]{1,0:T(8,128)S(1)} %dft.9.own_g, ...), custom_call_target="tpu_custom_call" | custom-call | flops 26214400 | bytes 15728640 | tf_op jit(solution)/shard_map/early/pallas_call | solution.py:364
  58.1 0.0 collective-permute-done.4.x_ref
  58.1 1.7 %partial.2 = (f32[1024,128]{1,0:T(8,128)S(1)}, f32[512,128]{1,0:T(8,128)S(1)}) custom-call(s32[1]{0:T(128)} %bitcast.pos_ref, bf16[2,4,256,256]{3,2,1,0:T(8,128)(2,1)S(1)} %copy-done.2, bf16[2,4,256,256]{3,2,1,0:T(8,128)(2,1)S(1)} %copy-done.3, f32[7,1024,256]{2,1,0:T(8,128)S(1)} %bitcast.4, f32[7,1024,256]{2,1,0:T(8,128)S(1)} %bitcast.4, ...), custom_call_target="tpu_custom_call" | custom-call | flops 402653184 | bytes 1572864 | tf_op jit(solution)/shard_map/partial/pallas_call | solution.py:234
  59.8 0.0 copy-start.7
  59.8 0.0 copy-start.8
  59.8 0.0 copy-start.9
  59.8 1.4 %collective-permute-start.9 = (f32[512,128]{1,0:T(8,128)S(1)}, f32[512,128]{1,0:T(8,128)S(1)}, u32[]{:S(2)}, u32[]{:S(2)}) collective-permute-start(f32[512,128]{1,0:T(8,128)S(1)} %get-tuple-element.55), channel_id=1, source_target_pairs={{4,0},{8,12},{5,1},{9,13},{6,2},{10,14},{7,3},{11,15},{20,16},{24,... | collective-permute-start | bytes 786440 | tf_op jit(solution)/shard_map/ppermute | solution.py:517
  61.3 1.7 %partial.3 = (f32[1024,128]{1,0:T(8,128)S(1)}, f32[512,128]{1,0:T(8,128)S(1)}) custom-call(s32[1]{0:T(128)} %bitcast.pos_ref, bf16[2,4,256,256]{3,2,1,0:T(8,128)(2,1)S(1)} %copy-done.2, bf16[2,4,256,256]{3,2,1,0:T(8,128)(2,1)S(1)} %copy-done.3, f32[7,1024,256]{2,1,0:T(8,128)S(1)} %bitcast.4, f32[7,1024,256]{2,1,0:T(8,128)S(1)} %bitcast.4, ...), custom_call_target="tpu_custom_call" | custom-call | flops 402653184 | bytes 1572864 | tf_op jit(solution)/shard_map/partial/pallas_call | solution.py:234
  63.0 1.3 %collective-permute-start.10 = (f32[512,128]{1,0:T(8,128)S(1)}, f32[512,128]{1,0:T(8,128)S(1)}, u32[]{:S(2)}, u32[]{:S(2)}) collective-permute-start(f32[512,128]{1,0:T(8,128)S(1)} %get-tuple-element.58), channel_id=1, source_target_pairs={{4,0},{8,12},{5,1},{9,13},{6,2},{10,14},{7,3},{11,15},{20,16},{24,... | collective-permute-start | bytes 786440 | tf_op jit(solution)/shard_map/ppermute | solution.py:517
  64.3 0.7 collective-permute-done.7.refs_0_.rest_9_
  64.9 0.7 dft.15.three_g
  65.6 11.5 %collective-permute-done.9.rest_4_ = f32[512,128]{1,0:T(8,128)S(1)} collective-permute-done((f32[512,128]{1,0:T(8,128)S(1)}, f32[512,128]{1,0:T(8,128)S(1)}, u32[]{:S(2)}, u32[]{:S(2)}) %collective-permute-start.9) | collective-permute-done | bytes 262176 | tf_op jit(solution)/shard_map/ppermute | solution.py:517
  77.2 0.0 copy-start.10
  77.2 0.0 copy-start.11
  77.2 6.8 %late.1 = (f32[512,256]{1,0:T(8,128)}, f32[1024,256]{1,0:T(8,128)}, f32[512,256]{1,0:T(8,128)S(1)}, f32[1,256]{1,0:T(1,128)}) custom-call(s32[1]{0:T(128)} %bitcast.pos_ref, bf16[2,4,256,256]{3,2,1,0:T(8,128)(2,1)S(1)} %copy-done.3, f32[4,1024,256]{2,1,0:T(8,128)S(1)} %early.1.acc_ref, f32[7,1024,256]{2,1,0:T(8,128)S(1)} %bitcast.4, ...), custom_call_target="tpu_custom_call" | custom-call | flops 1610612736 | bytes 13107200 | tf_op jit(solution)/shard_map/late/pallas_call | solution.py:482
  84.0 0.1 fusion.2
  84.0 1.1 %fusion = (f32[512,256]{1,0:T(8,128)}, f32[512,256]{1,0:T(8,128)}) fusion(f32[512,256]{1,0:T(8,128)S(1)} %copy-done.10, f32[512,128]{1,0:T(8,128)S(1)} %get-tuple-element.68, f32[512,128]{1,0:T(8,128)S(1)} %get-tuple-element.67, f32[512,256]{1,0:T(8,128)S(1)} %copy-done.11), kind=kLoop, calls=%fused_computation.1 | loop fusion | flops 393216 | bytes 2621440 | tf_op jit(solution)/shard_map/mul | solution.py:571
  (21 shorter events, 0.0 us)
Async XLA Ops:
  4.4 27.3 %collective-permute-start.3 = (f32[520,256]{1,0:T(8,128)}, f32[520,256]{1,0:T(8,128)S(1)}, u32[]{:S(2)}, u32[]{:S(2)}) collective-permute-start(f32[520,256]{1,0:T(8,128)} %get-tuple-element.35.refs_0_.rest_2_.rest_5_), channel_id=1, source_target_pairs={{4,0},{8,4},{12,8},{5,1},{9,5},{13,9},{6,2},{10,6},{14,10},{7,3},{... | collective-permute-start | bytes 1597448 | tf_op jit(solution)/shard_map/ppermute | solution.py:517
  5.7 26.1 %collective-permute-start.2 = (f32[520,256]{1,0:T(8,128)}, f32[520,256]{1,0:T(8,128)}, u32[]{:S(2)}, u32[]{:S(2)}) collective-permute-start(f32[520,256]{1,0:T(8,128)} %get-tuple-element.35.refs_0_.rest_2_.rest_5_), channel_id=1, source_target_pairs={{0,4},{4,8},{8,12},{1,5},{5,9},{9,13},{2,6},{6,10},{10,14},{3,7},{... | collective-permute-start | bytes 1597448 | tf_op jit(solution)/shard_map/ppermute | solution.py:517
  12.0 26.7 %collective-permute-start.1 = (f32[512,256]{1,0:T(8,128)}, f32[512,256]{1,0:T(8,128)}, u32[]{:S(2)}, u32[]{:S(2)}) collective-permute-start(f32[512,256]{1,0:T(8,128)} %get-tuple-element.34.refs_0_.rest_3_), channel_id=1, source_target_pairs={{4,0},{8,4},{12,8},{5,1},{9,5},{13,9},{6,2},{10,6},{14,10},{7,3},{... | collective-permute-start | bytes 1572872 | tf_op jit(solution)/shard_map/ppermute | solution.py:517
  13.3 25.4 %collective-permute-start = (f32[512,256]{1,0:T(8,128)}, f32[512,256]{1,0:T(8,128)}, u32[]{:S(2)}, u32[]{:S(2)}) collective-permute-start(f32[512,256]{1,0:T(8,128)} %get-tuple-element.34.refs_0_.rest_3_), channel_id=1, source_target_pairs={{0,4},{4,8},{8,12},{1,5},{5,9},{9,13},{2,6},{6,10},{10,14},{3,7},{... | collective-permute-start | bytes 1572872 | tf_op jit(solution)/shard_map/ppermute | solution.py:517
  18.7 1.2 %copy-start.1 = (bf16[2,4,256,256]{3,2,1,0:T(8,128)(2,1)S(1)}, bf16[2,4,256,256]{3,2,1,0:T(8,128)(2,1)}, u32[]{:S(2)}) copy-start(bf16[2,4,256,256]{3,2,1,0:T(8,128)(2,1)} %constant.11.clone.table_ref) | copy-start | bytes 3145732
  19.9 2.2 %copy-start.5 = (f32[4096,256]{1,0:T(8,128)S(1)}, f32[4096,256]{1,0:T(8,128)}, u32[]{:S(2)}) copy-start(f32[4096,256]{1,0:T(8,128)} %x_ref.1) | copy-start | bytes 12582916
  22.1 8.9 %copy-start.2 = (bf16[2,4,256,256]{3,2,1,0:T(8,128)(2,1)S(1)}, bf16[2,4,256,256]{3,2,1,0:T(8,128)(2,1)}, u32[]{:S(2)}) copy-start(bf16[2,4,256,256]{3,2,1,0:T(8,128)(2,1)} %constant.11.clone.table_ref) | copy-start | bytes 3145732
  22.1 8.9 %copy-start.4 = (f32[520,256]{1,0:T(8,128)S(1)}, f32[520,256]{1,0:T(8,128)}, u32[]{:S(2)}) copy-start(f32[520,256]{1,0:T(8,128)} %get-tuple-element.35.refs_0_.rest_2_.rest_5_) | copy-start | bytes 1597444
  28.1 2.9 %copy-start = (f32[7,1024,256]{2,1,0:T(8,128)}, f32[7,1024,256]{2,1,0:T(8,128)S(1)}, u32[]{:S(2)}) copy-start(f32[7,1024,256]{2,1,0:T(8,128)S(1)} %taps.1.win_own.win_left.win_right.win_two.win_near.win_far.win_ref) | copy-start | bytes 22020100
  31.7 11.1 %collective-permute-start.5 = (f32[520,256]{1,0:T(8,128)}, f32[520,256]{1,0:T(8,128)}, u32[]{:S(2)}, u32[]{:S(2)}) collective-permute-start(f32[520,256]{1,0:T(8,128)} %collective-permute-done.2.refs_0_.rest_6_), channel_id=1, source_target_pairs={{4,8},{8,12},{5,9},{9,13},{6,10},{10,14},{7,11},{11,15},{20,24},{2... | collective-permute-start | bytes 1597448 | tf_op jit(solution)/shard_map/ppermute | solution.py:517
  33.2 16.8 %collective-permute-start.6 = (f32[520,256]{1,0:T(8,128)S(1)}, f32[520,256]{1,0:T(8,128)}, u32[]{:S(2)}, u32[]{:S(2)}) collective-permute-start(f32[520,256]{1,0:T(8,128)S(1)} %collective-permute-done.3.refs_0_.rest_7_), channel_id=1, source_target_pairs={{8,4},{4,0},{9,5},{5,1},{10,6},{6,2},{11,7},{7,3},{24,20},{20,16},... | collective-permute-start | bytes 1597448 | tf_op jit(solution)/shard_map/ppermute | solution.py:517
  34.5 1.0 %copy-start.6 = (f32[512,256]{1,0:T(8,128)S(1)}, f32[512,256]{1,0:T(8,128)}, u32[]{:S(2)}) copy-start(f32[512,256]{1,0:T(8,128)} %get-tuple-element.34.refs_0_.rest_3_) | copy-start | bytes 1572868
  38.0 17.9 %slice-start = ((s8[7340032]{0:T(1024)(128)(4,1)}), s8[4194304]{0:T(1024)(128)(4,1)S(1)}, s32[]{:S(2)}) async-start(s8[7340032]{0:T(1024)(128)(4,1)} %bitcast.3), calls=%async_computation | async-start | bytes 8388608
  40.9 15.0 %slice-start.1 = ((s8[7340032]{0:T(1024)(128)(4,1)}), s8[3145728]{0:T(1024)(128)(4,1)S(1)}, s32[]{:S(2)}) async-start(s8[7340032]{0:T(1024)(128)(4,1)} %bitcast.3), calls=%async_computation.1 | async-start | bytes 6291456
  51.2 13.7 %collective-permute-start.7 = (f32[520,256]{1,0:T(8,128)S(1)}, f32[520,256]{1,0:T(8,128)S(1)}, u32[]{:S(2)}, u32[]{:S(2)}) collective-permute-start(f32[520,256]{1,0:T(8,128)S(1)} %add.6.refs_0_.rest_8_), channel_id=1, source_target_pairs={{4,0},{8,12},{5,1},{9,13},{6,2},{10,14},{7,3},{11,15},{20,16},{24,... | collective-permute-start | bytes 1597448 | tf_op jit(solution)/shard_map/ppermute | solution.py:517
  53.8 4.3 %collective-permute-start.4 = (f32[512,128]{1,0:T(8,128)S(1)}, f32[512,128]{1,0:T(8,128)S(1)}, u32[]{:S(2)}, u32[]{:S(2)}) collective-permute-start(f32[512,128]{1,0:T(8,128)S(1)} %get-tuple-element.64), channel_id=1, source_target_pairs={{4,8},{8,4},{5,9},{9,5},{6,10},{10,6},{7,11},{11,7},{20,24},{24,20... | collective-permute-start | bytes 786440 | tf_op jit(solution)/shard_map/ppermute | solution.py:517
  54.5 5.3 %collective-permute-start.8 = (f32[512,128]{1,0:T(8,128)S(1)}, f32[512,128]{1,0:T(8,128)S(1)}, u32[]{:S(2)}, u32[]{:S(2)}) collective-permute-start(f32[512,128]{1,0:T(8,128)S(1)} %get-tuple-element.63), channel_id=1, source_target_pairs={{4,8},{8,4},{5,9},{9,5},{6,10},{10,6},{7,11},{11,7},{20,24},{24,20... | collective-permute-start | bytes 786440 | tf_op jit(solution)/shard_map/ppermute | solution.py:517
  55.9 2.2 %copy-start.3 = (bf16[2,4,256,256]{3,2,1,0:T(8,128)(2,1)S(1)}, bf16[2,4,256,256]{3,2,1,0:T(8,128)(2,1)}, u32[]{:S(2)}) copy-start(bf16[2,4,256,256]{3,2,1,0:T(8,128)(2,1)} %constant.12.clone.inverse_ref) | copy-start | bytes 3145732
  59.8 17.3 %copy-start.7 = (f32[512,256]{1,0:T(8,128)S(1)}, f32[512,256]{1,0:T(8,128)}, u32[]{:S(2)}) copy-start(f32[512,256]{1,0:T(8,128)} %get-tuple-element.34.refs_0_.rest_3_) | copy-start | bytes 1572868
  59.8 17.3 %copy-start.8 = (f32[512,256]{1,0:T(8,128)S(1)}, f32[512,256]{1,0:T(8,128)}, u32[]{:S(2)}) copy-start(f32[512,256]{1,0:T(8,128)} %rest_11_.1) | copy-start | bytes 1572868
  59.8 17.3 %copy-start.9 = (f32[256]{0:T(256)S(1)}, f32[256]{0:T(256)}, u32[]{:S(2)}) copy-start(f32[256]{0:T(256)} %param.12) | copy-start | bytes 3076
  59.8 17.3 %collective-permute-start.9 = (f32[512,128]{1,0:T(8,128)S(1)}, f32[512,128]{1,0:T(8,128)S(1)}, u32[]{:S(2)}, u32[]{:S(2)}) collective-permute-start(f32[512,128]{1,0:T(8,128)S(1)} %get-tuple-element.55), channel_id=1, source_target_pairs={{4,0},{8,12},{5,1},{9,13},{6,2},{10,14},{7,3},{11,15},{20,16},{24,... | collective-permute-start | bytes 786440 | tf_op jit(solution)/shard_map/ppermute | solution.py:517
  63.0 21.0 %collective-permute-start.10 = (f32[512,128]{1,0:T(8,128)S(1)}, f32[512,128]{1,0:T(8,128)S(1)}, u32[]{:S(2)}, u32[]{:S(2)}) collective-permute-start(f32[512,128]{1,0:T(8,128)S(1)} %get-tuple-element.58), channel_id=1, source_target_pairs={{4,0},{8,12},{5,1},{9,13},{6,2},{10,14},{7,3},{11,15},{20,16},{24,... | collective-permute-start | bytes 786440 | tf_op jit(solution)/shard_map/ppermute | solution.py:517
  77.2 6.9 %copy-start.10 = (f32[512,256]{1,0:T(8,128)S(1)}, f32[512,256]{1,0:T(8,128)}, u32[]{:S(2)}) copy-start(f32[512,256]{1,0:T(8,128)} %key_ref.1) | copy-start | bytes 1572868
  77.2 6.9 %copy-start.11 = (f32[512,256]{1,0:T(8,128)S(1)}, f32[512,256]{1,0:T(8,128)}, u32[]{:S(2)}) copy-start(f32[512,256]{1,0:T(8,128)} %values_ref.1) | copy-start | bytes 1572868

commit v4 on v3

--- a/solution.py
+++ b/solution.py
@@ -132,12 +132,14 @@
     def store(group, value):
         out_ref[group * rows : (group + 1) * rows, :] = value
 
-    parts = [ref[...] for ref in x_refs]
-    transform(parts[0] if len(parts) == 1 else jnp.concatenate(parts, axis=1), table_ref, store)
+    x = x_refs[0][...]
+    for ref in x_refs[1:]:
+        x = x + ref[...]
+    transform(x, table_ref, store)
 
 
 def dft(table, seg, *xs):
-    width = sum(x.shape[1] for x in xs)
+    width = xs[0].shape[1]
     return pl.pallas_call(
         dft_kernel,
         grid=(1,),
@@ -220,17 +222,17 @@
         out_ref[i * sub : (i + 1) * sub, :] = quarter
 
 
-def back_partial(pos, table, inverse, windows, left, right, x, half, seg):
+def back_partial(pos, table, inverse, windows, left, right, x, seg):
     width = x.shape[1]
     n = (windows.shape[0] + 1) // 2
 
     def window(distance):
         return pl.BlockSpec(
             (1, 2 * seg, width),
-            lambda i, pos: (jnp.where(pos[0] == 1, n - 1 + distance, n - 1 - distance), 0, half),
+            lambda i, pos: (jnp.where(pos[0] == 1, n - 1 + distance, n - 1 - distance), 0, 0),
         )
 
-    near = pl.BlockSpec((2 * seg, width), lambda i, pos: (0, half))
+    near = whole_spec((2 * seg, width))
     return pl.pallas_call(
         partial_kernel,
         grid_spec=pltpu.PrefetchScalarGridSpec(
@@ -249,7 +251,7 @@
             scratch_shapes=[pltpu.VMEM((4, seg // 2, width), jnp.float32)],
         ),
         out_shape=[f32(2 * seg, width), f32(seg, width)],
-        compiler_params=params(20),
+        compiler_params=params(24),
         cost_estimate=cost(6 * seg * seg * width * 2, 24 * seg * width),
         name="partial",
     )(pos, table, inverse, windows, windows, left, right, x)
@@ -385,12 +387,12 @@
 def late_kernel(
     pos_ref, inverse_ref, acc_ref, win_ref, three_g, two_g, own_m, left_m, right_m, *rest
 ):
-    two_m, (gated_ref, mixed_ref, partial_ref), strips = rest[:2], rest[2:5], rest[5:10]
-    skip_ref, up_ref, query_out, filter_out, back_out, skip_out, x_high, x_low, z_ref = rest[10:]
+    two_m, gated_ref, mixed_ref = rest[:3]
+    strips, rest = rest[3:10], rest[10:]
+    skip_ref, up_ref, query_out, filter_out, back_out, skip_out, x_high, x_low, z_ref = rest
     group = pl.program_id(0)
     pos, sign = pos_ref[0], group_sign()
     rows, width = own_m.shape
-    half = width // 2
     sub = rows // 2
 
     def put(at, slot, value):
@@ -406,12 +408,8 @@
             def lags(tile, _):
                 re, im, read = tile_reader(tile, sub)
 
-                def read_two():
-                    parts = [read(ref) for ref in two_m]
-                    return tuple(jnp.concatenate([p[i] for p in parts], axis=1) for i in range(2))
-
                 gated = [None, None, None, functools.partial(read, two_g), functools.partial(read, three_g)]
-                mixed = [functools.partial(read, ref) for ref in (own_m, left_m, right_m)] + [read_two]
+                mixed = [functools.partial(read, ref) for ref in (own_m, left_m, right_m, two_m)]
                 total = [read(acc_ref, slot) for slot in range(4)]
                 if where in (0, 3):
                     total[0] = add(total[0], mul(read(win_ref, 0), gated[THREE]()))
@@ -447,26 +445,26 @@
                 if slot == 0:
                     query_out[at, :] = up_ref[at, :] * (quarter + skip_ref[...] * gated_ref[at, :])
                 elif slot == 1:
-                    back = quarter + skip_ref[...] * mixed_ref[at, :]
-                    back_out[at, :half] = back[:, :half] + partial_ref[at, :]
-                    back_out[at, half:] = back[:, half:]
+                    back_out[at, :] = quarter + skip_ref[...] * mixed_ref[at, :]
                 else:
                     base = (slot - 2) * seg + i * sub
                     filter_out[base : base + sub, :] = quarter
+        own, left, right, *far = (ref[...] for ref in strips)
+        blocks = (own, left, right, far[0] + far[1], far[2] + far[3])
         sources = (pos, pos - 1, pos + 1, jnp.where(pos < 2, pos + 2, pos - 2), 3 - pos)
         total = jnp.zeros((8, width), jnp.float32)
         for block in range(4):
             value = jnp.zeros((8, width), jnp.float32)
-            for where, (ref, source) in enumerate(zip(strips, sources)):
+            for where, (strip, source) in enumerate(zip(blocks, sources)):
                 hit = source == block
                 if where == THREE:
                     hit = jnp.logical_and(hit, jnp.logical_or(pos == 0, pos == 3))
-                value = value + jnp.where(hit, ref[...], 0.0)
+                value = value + jnp.where(hit, strip, 0.0)
             total = total + value
         skip_out[...] = jnp.sum(total, axis=0, keepdims=True)
 
 
-def late(pos, inverse, acc, windows, three_g, two_g, own_m, left_m, right_m, two_m, blocks, mixed, partial, skip, upstream):
+def late(pos, inverse, acc, windows, three_g, two_g, own_m, left_m, right_m, two_m, blocks, mixed, skip, upstream):
     seg, width = upstream.shape
     rows = seg // 2
     mid = windows.shape[0] // 2
@@ -477,7 +475,6 @@
         return jnp.where(p == 1, mid + 2, jnp.where(p == 2, mid - 2, ends)), i, 0
 
     group = pl.BlockSpec((rows, width), lambda i, pos: (i, 0))
-    group_half = pl.BlockSpec((rows, width // 2), lambda i, pos: (i, 0))
     strip = pl.BlockSpec((8, width), lambda i, pos: (seg // 8, 0))
     return pl.pallas_call(
         late_kernel,
@@ -488,12 +485,10 @@
                 pl.BlockSpec((2, 1, rows, rows), lambda i, pos: (0, i, 0, 0)),
                 pl.BlockSpec((4, rows, width), lambda i, pos: (0, i, 0)),
                 pl.BlockSpec((1, rows, width), win_at),
-                *[group] * 5,
-                *[group_half] * 2,
+                *[group] * 6,
                 whole_spec((seg, width)),
                 whole_spec((seg, width)),
-                whole_spec((seg, width // 2)),
-                *[strip] * 5,
+                *[strip] * 7,
                 whole_spec((1, width)),
                 whole_spec((seg, width)),
             ],
@@ -510,7 +505,7 @@
         compiler_params=params(20),
         cost_estimate=cost(12 * seg * seg * width * 2, 100 * seg * width),
         name="late",
-    )(pos, inverse, acc, windows, three_g, two_g, own_m, left_m, right_m, *two_m, blocks[0], mixed, partial, *blocks, skip, upstream)
+    )(pos, inverse, acc, windows, three_g, two_g, own_m, left_m, right_m, two_m, blocks[0], mixed, *blocks, skip, upstream)
 
 
 def send(x, *pairs):
@@ -529,7 +524,6 @@
     seg, width = values.shape
     forward_np, inverse_np = tables(seg)
     table, inverse = jnp.asarray(forward_np), jnp.asarray(inverse_np)
-    half = width // 2
     position = lax.axis_index("ctx")
     pos = position.astype(jnp.int32).reshape(1)
     after = lax.optimization_barrier
@@ -541,33 +535,29 @@
     own_g = dft(table, seg, gated)
     left, right, windows, own_g = after((left, right, windows, own_g))
 
-    two_l, two_r = send(left, (1, 2), (2, 3)), send(right, (2, 1), (1, 0))
+    two = send(left, (1, 2), (2, 3)), send(right, (2, 1), (1, 0))
     own_m, left_g, right_g = dft(table, seg, mixed), dft(table, seg, left), dft(table, seg, right)
     left_x, right_x, own_m, left_g, right_g = after((left_x, right_x, own_m, left_g, right_g))
 
-    far = [jnp.where(position == 1, left_x[:, at], right_x[:, at]) for at in (slice(half), slice(half, None))]
-    two_m0, two_m1 = [send(x, (1, 2), (2, 1)) for x in far]
+    two_x = send(jnp.where(position == 1, left_x, right_x), (1, 2), (2, 1))
     left_m, right_m = dft(table, seg, left_x), dft(table, seg, right_x)
-    two_l, two_r, left_m, right_m = after((two_l, two_r, left_m, right_m))
-
-    two = two_l + two_r
-    three = send(two, (1, 0), (2, 3))
-    two_g = dft(table, seg, two)
+    *two, left_m, right_m = after((*two, left_m, right_m))
+
+    three = send(two[0], (2, 3)), send(two[1], (1, 0))
+    two_m, partial = back_partial(pos, table, inverse, windows, left_m, right_m, two_x, seg)
+    *two, partial = after((*two, partial))
+    partial = send(partial, (1, 0), (2, 3))
+    two_g = dft(table, seg, *two)
     acc = early(pos, windows, (own_g, left_g, right_g, two_g), (own_m, left_m, right_m), seg)
-    two_m0, acc = after((two_m0, acc))
-
-    spec_0, partial_0 = back_partial(pos, table, inverse, windows, left_m, right_m, two_m0, 0, seg)
-    two_m1, partial_0 = after((two_m1, partial_0))
-    partial_0 = send(partial_0, (1, 0), (2, 3))
-    spec_1, partial_1 = back_partial(pos, table, inverse, windows, left_m, right_m, two_m1, 1, seg)
-    partial_1 = send(partial_1, (1, 0), (2, 3))
-    three_g = dft(table, seg, three)
+    *three, acc = after((*three, acc))
+
+    three_g = dft(table, seg, *three)
     query_grad, filter_grad, back, skip_grad = late(
-        pos, inverse, acc, windows, three_g, two_g, own_m, left_m, right_m, (spec_0, spec_1),
-        (gated, left, right, two, three), mixed, partial_0, skip_gain[None, :], upstream,
-    )
-    back, partial_1 = after((back, partial_1))
-    back = jnp.concatenate([back[:, :half], back[:, half:] + partial_1], axis=1)
+        pos, inverse, acc, windows, three_g, two_g, own_m, left_m, right_m, two_m,
+        (gated, left, right, *two, *three), mixed, skip_gain[None, :], upstream,
+    )
+    back, partial = after((back, partial))
+    back = back + partial
     return (query_grad, back * values, back * key_gate, filter_grad, skip_grad[0])
 
 

time: 85.7 us -> 73.7 us (0.86)
  Pallas kernels: 31.3 us -> 25.4 us
  waiting for transfers between devices: 19.3 us -> 23.3 us
  local copies, waits for them, and re-layouts: 7.41 us -> 3.71 us
  starting transfers between devices: 22.4 us -> 18.7 us
  other arithmetic: 3.62 us -> 1.17 us
    ppermute x11 -> x10, waiting for transfers between devices: 19.3 us -> 23.3 us  [send(): return lax.ppermute(x, 'ctx', list(pairs))]
    ppermute x11 -> x10, starting transfers between devices: 22.4 us -> 18.7 us  [send(): return lax.ppermute(x, 'ctx', list(pairs))]
    unnamed x28 -> x22, local copies, waits for them, and re-layouts: 7.41 us -> 3.71 us
    pallas_call x8, Pallas kernels: 9.33 us -> 5.75 us  [dft(): pl.pallas_call(dft_kernel, grid=(1,), in_specs=[whole_spec(table.shape)]...]
    pallas_call x2 -> x1, Pallas kernels: 3.34 us -> 1.61 us  [back_partial(): pl.pallas_call(partial_kernel, grid_spec=pltpu.PrefetchScalarGridSpec(num...]
    add x1 -> x0, other arithmetic: 1.27 us -> none  [local_line(): two = two_l + two_r]
    select_n x1, other arithmetic: 1.24 us -> 0.07 us  [local_line(): two_x = send(jnp.where(position == 1, left_x, right_x), (1, 2), (2, 1))]
  transfers between devices with their start and end apart: 11 -> 10, of which waited for: 3 -> 5; matrix products, arithmetic and copies ran while one was open for 1% -> 0% of each run, Pallas kernels for 32% -> 29%
where the time goes in v4:
time: 73.7 us; the launch traced here: 73.2 us
  Pallas kernels  25.4 us (34%)
  waiting for transfers between devices  23.3 us (32%)
  starting transfers between devices  18.7 us (25%)
  local copies, waits for them, and re-layouts  3.71 us (5%)
  other arithmetic  1.17 us (2%)
  between operations  0.97 us (1%)
    ppermute x10, waiting for transfers between devices, send(): return lax.ppermute(x, 'ctx', list(pairs))  23.3 us
    ppermute x10, starting transfers between devices, send(): return lax.ppermute(x, 'ctx', list(pairs))  18.7 us
    pallas_call x1, Pallas kernels, late(): pl.pallas_call(late_kernel, grid_spec=pltpu.PrefetchScalarGridSpec(num_sc...  6.05 us
    pallas_call x1, Pallas kernels, taps_spectra(): pl.pallas_call(taps_kernel, grid=(blocks,), in_specs=[whole_spec(table.sh...  5.95 us
    pallas_call x8, Pallas kernels, dft(): pl.pallas_call(dft_kernel, grid=(1,), in_specs=[whole_spec(table.shape)]...  5.75 us
    pallas_call x1, Pallas kernels, prepare(): pl.pallas_call(prepare_kernel, grid=(steps,), in_specs=[block] * 4, out_s...  3.83 us
    unnamed x22, local copies, waits for them, and re-layouts  3.71 us
    pallas_call x1, Pallas kernels, early(): pl.pallas_call(early_kernel, grid_spec=pltpu.PrefetchScalarGridSpec(num_s...  2.18 us
  transfers between devices with their start and end apart: 10, of which 5 were waited for; matrix products, arithmetic and copies ran while one was open for 0% of the time, Pallas kernels for 29%

profile of v4, /device:TPU:0, one launch (start us, length us, event | category | flops | bytes accessed | tf_op | source)
XLA Modules:
  0.0 73.2 jit_solution(14985268285288860489)
XLA Ops:
  0.6 0.0 copy-start.1
  0.6 3.8 %prepare.1 = (f32[520,256]{1,0:T(8,128)}, f32[512,256]{1,0:T(8,128)}) custom-call(f32[512,256]{1,0:T(8,128)} %query_ref.1, f32[512,256]{1,0:T(8,128)} %key_ref.1, f32[512,256]{1,0:T(8,128)} %values_ref.1, f32[512,256]{1,0:T(8,128)} %rest_11_.1), custom_call_target="tpu_custom_call" | custom-call | flops 524288 | bytes 3145728 | tf_op jit(solution)/shard_map/prepare/pallas_call | solution.py:115
  4.5 1.3 %collective-permute-start.1 = (f32[520,256]{1,0:T(8,128)}, f32[520,256]{1,0:T(8,128)S(1)}, u32[]{:S(2)}, u32[]{:S(2)}) collective-permute-start(f32[520,256]{1,0:T(8,128)} %get-tuple-element.34.refs_0_.rest_1_.rest_3_), channel_id=1, source_target_pairs={{4,0},{8,4},{12,8},{5,1},{9,5},{13,9},{6,2},{10,6},{14,10},{7,3},{... | collective-permute-start | bytes 1597448 | tf_op jit(solution)/shard_map/ppermute | solution.py:512
  5.8 5.6 %collective-permute-start = (f32[520,256]{1,0:T(8,128)}, f32[520,256]{1,0:T(8,128)S(1)}, u32[]{:S(2)}, u32[]{:S(2)}) collective-permute-start(f32[520,256]{1,0:T(8,128)} %get-tuple-element.34.refs_0_.rest_1_.rest_3_), channel_id=1, source_target_pairs={{0,4},{4,8},{8,12},{1,5},{5,9},{9,13},{2,6},{6,10},{10,14},{3,7},{... | collective-permute-start | bytes 1597448 | tf_op jit(solution)/shard_map/ppermute | solution.py:512
  11.4 1.3 %collective-permute-start.5 = (f32[512,256]{1,0:T(8,128)}, f32[512,256]{1,0:T(8,128)S(1)}, u32[]{:S(2)}, u32[]{:S(2)}) collective-permute-start(f32[512,256]{1,0:T(8,128)} %get-tuple-element.37.refs_0_.rest_2_), channel_id=1, source_target_pairs={{4,0},{8,4},{12,8},{5,1},{9,5},{13,9},{6,2},{10,6},{14,10},{7,3},{... | collective-permute-start | bytes 1572872 | tf_op jit(solution)/shard_map/ppermute | solution.py:512
  12.7 4.6 %collective-permute-start.4 = (f32[512,256]{1,0:T(8,128)}, f32[512,256]{1,0:T(8,128)S(1)}, u32[]{:S(2)}, u32[]{:S(2)}) collective-permute-start(f32[512,256]{1,0:T(8,128)} %get-tuple-element.37.refs_0_.rest_2_), channel_id=1, source_target_pairs={{0,4},{4,8},{8,12},{1,5},{5,9},{9,13},{2,6},{6,10},{10,14},{3,7},{... | collective-permute-start | bytes 1572872 | tf_op jit(solution)/shard_map/ppermute | solution.py:512
  17.3 0.0 copy-start
  17.3 1.2 %copy-done = bf16[2,4,256,256]{3,2,1,0:T(8,128)(2,1)S(1)} copy-done((bf16[2,4,256,256]{3,2,1,0:T(8,128)(2,1)S(1)}, bf16[2,4,256,256]{3,2,1,0:T(8,128)(2,1)}, u32[]{:S(2)}) %copy-start) | copy-done | bytes 1048600
  18.5 1.0 %copy-done.2 = f32[520,256]{1,0:T(8,128)S(1)} copy-done((f32[520,256]{1,0:T(8,128)S(1)}, f32[520,256]{1,0:T(8,128)}, u32[]{:S(2)}) %copy-start.2) | copy-done | bytes 532504
  19.5 0.7 dft.8.own_g
  20.2 0.0 copy-start.6
  20.3 1.4 %copy-done.6 = f32[512,256]{1,0:T(8,128)S(1)} copy-done((f32[512,256]{1,0:T(8,128)S(1)}, f32[512,256]{1,0:T(8,128)}, u32[]{:S(2)}) %copy-start.6) | copy-done | bytes 524312
  21.6 0.7 dft.9.own_m
  22.4 0.0 copy-done.1
  22.4 6.0 %taps.1.win_near.win_far.win_own.win_left.win_right.win_two.win_ref = f32[7,1024,256]{2,1,0:T(8,128)S(1)} custom-call(bf16[2,4,256,256]{3,2,1,0:T(8,128)(2,1)S(1)} %copy-done.1, f32[4096,256]{1,0:T(8,128)S(1)} %copy-done.4), custom_call_target="tpu_custom_call" | custom-call | flops 3221225472 | bytes 12582912 | tf_op jit(solution)/shard_map/taps/pallas_call | solution.py:178
  28.3 0.0 collective-permute-done.1.refs_0_.rest_5_
  28.4 0.0 collective-permute-done.refs_0_.rest_4_
  28.4 0.7 collective-permute-start.2
  29.1 1.3 %collective-permute-start.3 = (f32[520,256]{1,0:T(8,128)S(1)}, f32[520,256]{1,0:T(8,128)S(1)}, u32[]{:S(2)}, u32[]{:S(2)}) collective-permute-start(f32[520,256]{1,0:T(8,128)S(1)} %collective-permute-done.1.refs_0_.rest_5_), channel_id=1, source_target_pairs={{8,4},{4,0},{9,5},{5,1},{10,6},{6,2},{11,7},{7,3},{24,20},{20,16},... | collective-permute-start | bytes 1597448 | tf_op jit(solution)/shard_map/ppermute | solution.py:512
  30.4 0.7 dft.10.left_g
  31.1 0.0 copy-start.5
  31.1 0.7 dft.11.right_g
  31.8 1.1 %collective-permute-done.5.refs_0_ = f32[512,256]{1,0:T(8,128)S(1)} collective-permute-done((f32[512,256]{1,0:T(8,128)}, f32[512,256]{1,0:T(8,128)S(1)}, u32[]{:S(2)}, u32[]{:S(2)}) %collective-permute-start.5) | collective-permute-done | bytes 524320 | tf_op jit(solution)/shard_map/ppermute | solution.py:512
  32.9 1.3 %collective-permute-done.4.refs_0_ = f32[512,256]{1,0:T(8,128)S(1)} collective-permute-done((f32[512,256]{1,0:T(8,128)}, f32[512,256]{1,0:T(8,128)S(1)}, u32[]{:S(2)}, u32[]{:S(2)}) %collective-permute-start.4) | collective-permute-done | bytes 524320 | tf_op jit(solution)/shard_map/ppermute | solution.py:512
  34.2 0.1 broadcast_select_fusion
  34.3 0.7 collective-permute-start.8
  35.0 0.7 dft.13.right_ref.right_m
  35.7 0.7 dft.12.left_ref.left_m
  36.4 0.0 collective-permute-done.2.refs_0_.rest_6_
  36.4 10.1 %collective-permute-done.3.refs_1_.rest_7_ = f32[520,256]{1,0:T(8,128)S(1)} collective-permute-done((f32[520,256]{1,0:T(8,128)S(1)}, f32[520,256]{1,0:T(8,128)S(1)}, u32[]{:S(2)}, u32[]{:S(2)}) %collective-permute-start.3) | collective-permute-done | bytes 532512 | tf_op jit(solution)/shard_map/ppermute | solution.py:512
  46.5 0.7 collective-permute-start.6
  47.2 1.3 %collective-permute-start.7 = (f32[520,256]{1,0:T(8,128)S(1)}, f32[520,256]{1,0:T(8,128)S(1)}, u32[]{:S(2)}, u32[]{:S(2)}) collective-permute-start(f32[520,256]{1,0:T(8,128)S(1)} %collective-permute-done.3.refs_1_.rest_7_), channel_id=1, source_target_pairs={{4,0},{5,1},{6,2},{7,3},{20,16},{21,17},{22,18},{23,19}} | collective-permute-start | bytes 1597448 | tf_op jit(solution)/shard_map/ppermute | solution.py:512
  48.5 0.0 collective-permute-done.8.x_ref
  48.5 1.6 %partial.1 = (f32[1024,256]{1,0:T(8,128)S(1)}, f32[512,256]{1,0:T(8,128)S(1)}) custom-call(s32[1]{0:T(128)} %bitcast.pos_ref, bf16[2,4,256,256]{3,2,1,0:T(8,128)(2,1)S(1)} %copy-done.1, bf16[2,4,256,256]{3,2,1,0:T(8,128)(2,1)S(1)} %copy-done.5, f32[7,1024,256]{2,1,0:T(8,128)S(1)} %taps.1.win_near.win_far.win_own.win_left.win_right.win_two.win_ref, ...), custom_call_target="tpu_custom_call" | custom-call | flops 805306368 | bytes 3145728 | tf_op jit(solution)/shard_map/partial/pallas_call | solution.py:236
  50.1 1.3 %collective-permute-start.9 = (f32[512,256]{1,0:T(8,128)S(1)}, f32[512,256]{1,0:T(8,128)S(1)}, u32[]{:S(2)}, u32[]{:S(2)}) collective-permute-start(f32[512,256]{1,0:T(8,128)S(1)} %get-tuple-element.58), channel_id=1, source_target_pairs={{4,0},{8,12},{5,1},{9,13},{6,2},{10,14},{7,3},{11,15},{20,16},{24,... | collective-permute-start | bytes 1572872 | tf_op jit(solution)/shard_map/ppermute | solution.py:512
  51.4 0.7 %dft.14.two_g = f32[1024,256]{1,0:T(8,128)S(1)} custom-call(bf16[2,4,256,256]{3,2,1,0:T(8,128)(2,1)S(1)} %copy-done.1, f32[520,256]{1,0:T(8,128)S(1)} %collective-permute-done.2.refs_0_.rest_6_, f32[520,256]{1,0:T(8,128)S(1)} %collective-permute-done.3.refs_1_.rest_7_), custom_call_target="tpu_custom_call" | custom-call | flops 402653184 | bytes 1572864 | tf_op jit(solution)/shard_map/dft/pallas_call | solution.py:143
  52.2 0.0 copy-start.3
  52.2 0.0 copy-start.7
  52.2 0.0 copy-start.8
  52.2 2.2 %early.1.acc_ref = f32[4,1024,256]{2,1,0:T(8,128)S(1)} custom-call(s32[1]{0:T(128)} %bitcast.pos_ref, f32[7,1024,256]{2,1,0:T(8,128)S(1)} %taps.1.win_near.win_far.win_own.win_left.win_right.win_two.win_ref, f32[7,1024,256]{2,1,0:T(8,128)S(1)} %taps.1.win_near.win_far.win_own.win_left.win_right.win_two.win_ref, ...), custom_call_target="tpu_custom_call" | custom-call | flops 26214400 | bytes 15728640 | tf_op jit(solution)/shard_map/early/pallas_call | solution.py:366
  54.4 0.0 collective-permute-done.6.refs_0_.rest_8_
  54.4 6.5 %collective-permute-done.7.refs_1_.rest_9_ = f32[520,256]{1,0:T(8,128)S(1)} collective-permute-done((f32[520,256]{1,0:T(8,128)S(1)}, f32[520,256]{1,0:T(8,128)S(1)}, u32[]{:S(2)}, u32[]{:S(2)}) %collective-permute-start.7) | collective-permute-done | bytes 532512 | tf_op jit(solution)/shard_map/ppermute | solution.py:512
  60.9 0.7 %dft.15.three_g = f32[1024,256]{1,0:T(8,128)S(1)} custom-call(bf16[2,4,256,256]{3,2,1,0:T(8,128)(2,1)S(1)} %copy-done.1, f32[520,256]{1,0:T(8,128)S(1)} %collective-permute-done.6.refs_0_.rest_8_, f32[520,256]{1,0:T(8,128)S(1)} %collective-permute-done.7.refs_1_.rest_9_), custom_call_target="tpu_custom_call" | custom-call | flops 402653184 | bytes 1572864 | tf_op jit(solution)/shard_map/dft/pallas_call | solution.py:143
  61.6 0.0 copy-start.9
  61.7 0.0 copy-start.10
  61.7 6.0 %late.1 = (f32[512,256]{1,0:T(8,128)}, f32[1024,256]{1,0:T(8,128)}, f32[512,256]{1,0:T(8,128)S(1)}, f32[1,256]{1,0:T(1,128)}) custom-call(s32[1]{0:T(128)} %bitcast.pos_ref, bf16[2,4,256,256]{3,2,1,0:T(8,128)(2,1)S(1)} %copy-done.5, f32[4,1024,256]{2,1,0:T(8,128)S(1)} %early.1.acc_ref, ...), custom_call_target="tpu_custom_call" | custom-call | flops 1610612736 | bytes 13107200 | tf_op jit(solution)/shard_map/late/pallas_call | solution.py:479
  67.7 4.4 %collective-permute-done.9 = f32[512,256]{1,0:T(8,128)S(1)} collective-permute-done((f32[512,256]{1,0:T(8,128)S(1)}, f32[512,256]{1,0:T(8,128)S(1)}, u32[]{:S(2)}, u32[]{:S(2)}) %collective-permute-start.9) | collective-permute-done | bytes 524320 | tf_op jit(solution)/shard_map/ppermute | solution.py:512
  72.1 1.1 %add_multiply_fusion = (f32[512,256]{1,0:T(8,128)}, f32[512,256]{1,0:T(8,128)}) fusion(f32[512,256]{1,0:T(8,128)S(1)} %copy-done.9, f32[512,256]{1,0:T(8,128)S(1)} %get-tuple-element.59, f32[512,256]{1,0:T(8,128)S(1)} %collective-permute-done.9, f32[512,256]{1,0:T(8,128)S(1)} %copy-done.10), kind=kLoop, calls=%fused_computation.1 | loop fusion | flops 393216 | bytes 3145728 | tf_op jit(solution)/shard_map/mul | solution.py:561
  (9 shorter events, 0.0 us)
Async XLA Ops:
  0.6 21.7 %copy-start.1 = (bf16[2,4,256,256]{3,2,1,0:T(8,128)(2,1)S(1)}, bf16[2,4,256,256]{3,2,1,0:T(8,128)(2,1)}, u32[]{:S(2)}) copy-start(bf16[2,4,256,256]{3,2,1,0:T(8,128)(2,1)} %constant.11.clone.table_ref) | copy-start | bytes 3145732
  4.5 23.9 %collective-permute-start.1 = (f32[520,256]{1,0:T(8,128)}, f32[520,256]{1,0:T(8,128)S(1)}, u32[]{:S(2)}, u32[]{:S(2)}) collective-permute-start(f32[520,256]{1,0:T(8,128)} %get-tuple-element.34.refs_0_.rest_1_.rest_3_), channel_id=1, source_target_pairs={{4,0},{8,4},{12,8},{5,1},{9,5},{13,9},{6,2},{10,6},{14,10},{7,3},{... | collective-permute-start | bytes 1597448 | tf_op jit(solution)/shard_map/ppermute | solution.py:512
  5.8 22.6 %collective-permute-start = (f32[520,256]{1,0:T(8,128)}, f32[520,256]{1,0:T(8,128)S(1)}, u32[]{:S(2)}, u32[]{:S(2)}) collective-permute-start(f32[520,256]{1,0:T(8,128)} %get-tuple-element.34.refs_0_.rest_1_.rest_3_), channel_id=1, source_target_pairs={{0,4},{4,8},{8,12},{1,5},{5,9},{9,13},{2,6},{6,10},{10,14},{3,7},{... | collective-permute-start | bytes 1597448 | tf_op jit(solution)/shard_map/ppermute | solution.py:512
  11.4 21.6 %collective-permute-start.5 = (f32[512,256]{1,0:T(8,128)}, f32[512,256]{1,0:T(8,128)S(1)}, u32[]{:S(2)}, u32[]{:S(2)}) collective-permute-start(f32[512,256]{1,0:T(8,128)} %get-tuple-element.37.refs_0_.rest_2_), channel_id=1, source_target_pairs={{4,0},{8,4},{12,8},{5,1},{9,5},{13,9},{6,2},{10,6},{14,10},{7,3},{... | collective-permute-start | bytes 1572872 | tf_op jit(solution)/shard_map/ppermute | solution.py:512
  12.7 21.6 %collective-permute-start.4 = (f32[512,256]{1,0:T(8,128)}, f32[512,256]{1,0:T(8,128)S(1)}, u32[]{:S(2)}, u32[]{:S(2)}) collective-permute-start(f32[512,256]{1,0:T(8,128)} %get-tuple-element.37.refs_0_.rest_2_), channel_id=1, source_target_pairs={{0,4},{4,8},{8,12},{1,5},{5,9},{9,13},{2,6},{6,10},{10,14},{3,7},{... | collective-permute-start | bytes 1572872 | tf_op jit(solution)/shard_map/ppermute | solution.py:512
  17.3 1.2 %copy-start = (bf16[2,4,256,256]{3,2,1,0:T(8,128)(2,1)S(1)}, bf16[2,4,256,256]{3,2,1,0:T(8,128)(2,1)}, u32[]{:S(2)}) copy-start(bf16[2,4,256,256]{3,2,1,0:T(8,128)(2,1)} %constant.11.clone.table_ref) | copy-start | bytes 3145732
  18.5 1.0 %copy-start.2 = (f32[520,256]{1,0:T(8,128)S(1)}, f32[520,256]{1,0:T(8,128)}, u32[]{:S(2)}) copy-start(f32[520,256]{1,0:T(8,128)} %get-tuple-element.34.refs_0_.rest_1_.rest_3_) | copy-start | bytes 1597444
  19.5 2.9 %copy-start.4 = (f32[4096,256]{1,0:T(8,128)S(1)}, f32[4096,256]{1,0:T(8,128)}, u32[]{:S(2)}) copy-start(f32[4096,256]{1,0:T(8,128)} %x_ref.1) | copy-start | bytes 12582916
  20.2 1.4 %copy-start.6 = (f32[512,256]{1,0:T(8,128)S(1)}, f32[512,256]{1,0:T(8,128)}, u32[]{:S(2)}) copy-start(f32[512,256]{1,0:T(8,128)} %get-tuple-element.37.refs_0_.rest_2_) | copy-start | bytes 1572868
  28.4 8.1 %collective-permute-start.2 = (f32[520,256]{1,0:T(8,128)S(1)}, f32[520,256]{1,0:T(8,128)S(1)}, u32[]{:S(2)}, u32[]{:S(2)}) collective-permute-start(f32[520,256]{1,0:T(8,128)S(1)} %collective-permute-done.refs_0_.rest_4_), channel_id=1, source_target_pairs={{4,8},{8,12},{5,9},{9,13},{6,10},{10,14},{7,11},{11,15},{20,24},{2... | collective-permute-start | bytes 1597448 | tf_op jit(solution)/shard_map/ppermute | solution.py:512
  29.1 17.4 %collective-permute-start.3 = (f32[520,256]{1,0:T(8,128)S(1)}, f32[520,256]{1,0:T(8,128)S(1)}, u32[]{:S(2)}, u32[]{:S(2)}) collective-permute-start(f32[520,256]{1,0:T(8,128)S(1)} %collective-permute-done.1.refs_0_.rest_5_), channel_id=1, source_target_pairs={{8,4},{4,0},{9,5},{5,1},{10,6},{6,2},{11,7},{7,3},{24,20},{20,16},... | collective-permute-start | bytes 1597448 | tf_op jit(solution)/shard_map/ppermute | solution.py:512
  31.1 17.4 %copy-start.5 = (bf16[2,4,256,256]{3,2,1,0:T(8,128)(2,1)S(1)}, bf16[2,4,256,256]{3,2,1,0:T(8,128)(2,1)}, u32[]{:S(2)}) copy-start(bf16[2,4,256,256]{3,2,1,0:T(8,128)(2,1)} %constant.12.clone.inverse_ref) | copy-start | bytes 3145732
  34.3 14.2 %collective-permute-start.8 = (f32[512,256]{1,0:T(8,128)S(1)}, f32[512,256]{1,0:T(8,128)S(1)}, u32[]{:S(2)}, u32[]{:S(2)}) collective-permute-start(f32[512,256]{1,0:T(8,128)S(1)} %broadcast_select_fusion), channel_id=1, source_target_pairs={{4,8},{8,4},{5,9},{9,5},{6,10},{10,6},{7,11},{11,7},{20,24},{24,20... | collective-permute-start | bytes 1572872 | tf_op jit(solution)/shard_map/ppermute | solution.py:512
  46.5 7.9 %collective-permute-start.6 = (f32[520,256]{1,0:T(8,128)S(1)}, f32[520,256]{1,0:T(8,128)S(1)}, u32[]{:S(2)}, u32[]{:S(2)}) collective-permute-start(f32[520,256]{1,0:T(8,128)S(1)} %collective-permute-done.2.refs_0_.rest_6_), channel_id=1, source_target_pairs={{8,12},{9,13},{10,14},{11,15},{24,28},{25,29},{26,30},{27,31}} | collective-permute-start | bytes 1597448 | tf_op jit(solution)/shard_map/ppermute | solution.py:512
  47.2 13.7 %collective-permute-start.7 = (f32[520,256]{1,0:T(8,128)S(1)}, f32[520,256]{1,0:T(8,128)S(1)}, u32[]{:S(2)}, u32[]{:S(2)}) collective-permute-start(f32[520,256]{1,0:T(8,128)S(1)} %collective-permute-done.3.refs_1_.rest_7_), channel_id=1, source_target_pairs={{4,0},{5,1},{6,2},{7,3},{20,16},{21,17},{22,18},{23,19}} | collective-permute-start | bytes 1597448 | tf_op jit(solution)/shard_map/ppermute | solution.py:512
  50.1 22.0 %collective-permute-start.9 = (f32[512,256]{1,0:T(8,128)S(1)}, f32[512,256]{1,0:T(8,128)S(1)}, u32[]{:S(2)}, u32[]{:S(2)}) collective-permute-start(f32[512,256]{1,0:T(8,128)S(1)} %get-tuple-element.58), channel_id=1, source_target_pairs={{4,0},{8,12},{5,1},{9,13},{6,2},{10,14},{7,3},{11,15},{20,16},{24,... | collective-permute-start | bytes 1572872 | tf_op jit(solution)/shard_map/ppermute | solution.py:512
  52.2 9.5 %copy-start.3 = (f32[520,256]{1,0:T(8,128)S(1)}, f32[520,256]{1,0:T(8,128)}, u32[]{:S(2)}) copy-start(f32[520,256]{1,0:T(8,128)} %get-tuple-element.34.refs_0_.rest_1_.rest_3_) | copy-start | bytes 1597444
  52.2 9.4 %copy-start.7 = (f32[512,256]{1,0:T(8,128)S(1)}, f32[512,256]{1,0:T(8,128)}, u32[]{:S(2)}) copy-start(f32[512,256]{1,0:T(8,128)} %rest_11_.1) | copy-start | bytes 1572868
  52.2 9.4 %copy-start.8 = (f32[256]{0:T(256)S(1)}, f32[256]{0:T(256)}, u32[]{:S(2)}) copy-start(f32[256]{0:T(256)} %param.12) | copy-start | bytes 3076
  61.6 10.5 %copy-start.9 = (f32[512,256]{1,0:T(8,128)S(1)}, f32[512,256]{1,0:T(8,128)}, u32[]{:S(2)}) copy-start(f32[512,256]{1,0:T(8,128)} %key_ref.1) | copy-start | bytes 1572868
  61.7 10.5 %copy-start.10 = (f32[512,256]{1,0:T(8,128)S(1)}, f32[512,256]{1,0:T(8,128)}, u32[]{:S(2)}) copy-start(f32[512,256]{1,0:T(8,128)} %values_ref.1) | copy-start | bytes 1572868

commit v5 on v4

--- a/solution.py
+++ b/solution.py
@@ -84,45 +84,29 @@
     return jax.ShapeDtypeStruct(shape, jnp.float32)
 
 
-def prepare_kernel(query_ref, key_ref, values_ref, up_ref, gated_ref, mixed_ref, sum_ref):
-    step = pl.program_id(0)
-    rows, width = key_ref.shape
-    gated = key_ref[...] * values_ref[...]
+def mix_kernel(gated_ref, up_ref, query_ref, mixed_ref):
+    seg, width = gated_ref.shape
     mixed = up_ref[...] * query_ref[...]
-    gated_ref[pl.ds(pl.multiple_of(step * rows, rows), rows), :] = gated
-    mixed_ref[...] = mixed
-    part = jnp.sum((gated * mixed).reshape(rows // 8, 8, width), axis=0)
-
-    @pl.when(step == 0)
-    def _():
-        sum_ref[...] = part
-
-    @pl.when(step > 0)
-    def _():
-        sum_ref[...] += part
-
-    @pl.when(step == pl.num_programs(0) - 1)
-    def _():
-        seg = gated_ref.shape[0] - 8
-        gated_ref[seg:, :] = sum_ref[...]
-
-
-def prepare(query_gate, key_gate, values, upstream):
-    seg, width = values.shape
-    steps = 4
-    rows = seg // steps
-    block = pl.BlockSpec((rows, width), lambda i: (i, 0))
+    mixed_ref[:seg, :] = mixed
+    mixed_ref[seg:, :] = jnp.sum((gated_ref[...] * mixed).reshape(seg // 8, 8, width), axis=0)
+
+
+def mix(gated, upstream, query_gate):
+    seg, width = gated.shape
     return pl.pallas_call(
-        prepare_kernel,
-        grid=(steps,),
-        in_specs=[block] * 4,
-        out_specs=[whole_spec((seg + 8, width)), block],
-        out_shape=[f32(seg + 8, width), f32(seg, width)],
-        scratch_shapes=[pltpu.VMEM((8, width), jnp.float32)],
-        compiler_params=params(56),
-        cost_estimate=cost(4 * seg * width, 24 * seg * width),
-        name="prepare",
-    )(query_gate, key_gate, values, upstream)
+        mix_kernel,
+        grid=(1,),
+        in_specs=[whole_spec((seg, width))] * 3,
+        out_specs=whole_spec((seg + 8, width)),
+        out_shape=f32(seg + 8, width),
+        compiler_params=params(12),
+        cost_estimate=cost(4 * seg * width, 16 * seg * width),
+        name="mix",
+    )(gated, upstream, query_gate)
+
+
+def strip_spec(seg, width):
+    return pl.BlockSpec((8, width), lambda *_: (seg // 8, 0))
 
 
 def dft_kernel(table_ref, *refs):
@@ -201,7 +185,8 @@
 
 
 def partial_kernel(
-    pos_ref, table_ref, inverse_ref, win_near, win_far, left_ref, right_ref, x_ref, far_ref, out_ref, z_ref
+    pos_ref, table_ref, inverse_ref, win_near, win_far, left_ref, right_ref, x_ref,
+    left_strip, right_strip, far_strip, far_ref, out_ref, z_ref
 ):
     rows = far_ref.shape[0] // 4
     sub = rows // 2
@@ -220,9 +205,11 @@
     quarters = gather_quarters([z_ref[g, :sub] for g in range(4)], [z_ref[g, sub:] for g in range(4)])
     for i, quarter in enumerate(quarters):
         out_ref[i * sub : (i + 1) * sub, :] = quarter
-
-
-def back_partial(pos, table, inverse, windows, left, right, x, seg):
+    out_ref[4 * sub : 4 * sub + 8, :] = jnp.where(is_left, left_strip[...], right_strip[...])
+    out_ref[4 * sub + 8 :, :] = far_strip[...]
+
+
+def back_partial(pos, table, inverse, windows, left, right, left_x, right_x, x, seg):
     width = x.shape[1]
     n = (windows.shape[0] + 1) // 2
 
@@ -246,15 +233,16 @@
                 near,
                 near,
                 whole_spec((seg, width)),
+                *[strip_spec(seg, width)] * 3,
             ],
-            out_specs=[whole_spec((2 * seg, width)), whole_spec((seg, width))],
+            out_specs=[whole_spec((2 * seg, width)), whole_spec((seg + 16, width))],
             scratch_shapes=[pltpu.VMEM((4, seg // 2, width), jnp.float32)],
         ),
-        out_shape=[f32(2 * seg, width), f32(seg, width)],
+        out_shape=[f32(2 * seg, width), f32(seg + 16, width)],
         compiler_params=params(24),
         cost_estimate=cost(6 * seg * seg * width * 2, 24 * seg * width),
         name="partial",
-    )(pos, table, inverse, windows, windows, left, right, x)
+    )(pos, table, inverse, windows, windows, left, right, x, left_x, right_x, x)
 
 
 OWN, LEFT, RIGHT, TWO, THREE = range(5)
@@ -387,9 +375,7 @@
 def late_kernel(
     pos_ref, inverse_ref, acc_ref, win_ref, three_g, two_g, own_m, left_m, right_m, *rest
 ):
-    two_m, gated_ref, mixed_ref = rest[:3]
-    strips, rest = rest[3:10], rest[10:]
-    skip_ref, up_ref, query_out, filter_out, back_out, skip_out, x_high, x_low, z_ref = rest
+    two_m, gated_ref, mixed_ref, skip_ref, up_ref, query_out, filter_out, back_out, x_high, x_low, z_ref = rest
     group = pl.program_id(0)
     pos, sign = pos_ref[0], group_sign()
     rows, width = own_m.shape
@@ -449,22 +435,9 @@
                 else:
                     base = (slot - 2) * seg + i * sub
                     filter_out[base : base + sub, :] = quarter
-        own, left, right, *far = (ref[...] for ref in strips)
-        blocks = (own, left, right, far[0] + far[1], far[2] + far[3])
-        sources = (pos, pos - 1, pos + 1, jnp.where(pos < 2, pos + 2, pos - 2), 3 - pos)
-        total = jnp.zeros((8, width), jnp.float32)
-        for block in range(4):
-            value = jnp.zeros((8, width), jnp.float32)
-            for where, (strip, source) in enumerate(zip(blocks, sources)):
-                hit = source == block
-                if where == THREE:
-                    hit = jnp.logical_and(hit, jnp.logical_or(pos == 0, pos == 3))
-                value = value + jnp.where(hit, strip, 0.0)
-            total = total + value
-        skip_out[...] = jnp.sum(total, axis=0, keepdims=True)
-
-
-def late(pos, inverse, acc, windows, three_g, two_g, own_m, left_m, right_m, two_m, blocks, mixed, skip, upstream):
+
+
+def late(pos, inverse, acc, windows, three_g, two_g, own_m, left_m, right_m, two_m, gated, mixed, skip, upstream):
     seg, width = upstream.shape
     rows = seg // 2
     mid = windows.shape[0] // 2
@@ -475,7 +448,6 @@
         return jnp.where(p == 1, mid + 2, jnp.where(p == 2, mid - 2, ends)), i, 0
 
     group = pl.BlockSpec((rows, width), lambda i, pos: (i, 0))
-    strip = pl.BlockSpec((8, width), lambda i, pos: (seg // 8, 0))
     return pl.pallas_call(
         late_kernel,
         grid_spec=pltpu.PrefetchScalarGridSpec(
@@ -488,24 +460,68 @@
                 *[group] * 6,
                 whole_spec((seg, width)),
                 whole_spec((seg, width)),
-                *[strip] * 7,
                 whole_spec((1, width)),
                 whole_spec((seg, width)),
             ],
-            out_specs=[
-                whole_spec((seg, width)), whole_spec((2 * seg, width)), whole_spec((seg, width)), whole_spec((1, width)),
-            ],
+            out_specs=[whole_spec((seg, width)), whole_spec((2 * seg, width)), whole_spec((seg, width))],
             scratch_shapes=[
                 pltpu.VMEM((rows, 4 * width), jnp.bfloat16),
                 pltpu.VMEM((rows, 4 * width), jnp.bfloat16),
                 pltpu.VMEM((4, rows, 4 * width), jnp.float32),
             ],
         ),
-        out_shape=[f32(seg, width), f32(2 * seg, width), f32(seg, width), f32(1, width)],
+        out_shape=[f32(seg, width), f32(2 * seg, width), f32(seg, width)],
         compiler_params=params(20),
         cost_estimate=cost(12 * seg * seg * width * 2, 100 * seg * width),
         name="late",
-    )(pos, inverse, acc, windows, three_g, two_g, own_m, left_m, right_m, two_m, blocks[0], mixed, *blocks, skip, upstream)
+    )(pos, inverse, acc, windows, three_g, two_g, own_m, left_m, right_m, two_m, gated, mixed, skip, upstream)
+
+
+def finish_kernel(
+    pos_ref, back_ref, key_ref, values_ref, partial_ref, own_strip, left_strip, right_strip, two_strip,
+    key_out, value_out, skip_out,
+):
+    pos = pos_ref[0]
+    seg = back_ref.shape[0]
+    back = back_ref[...] + partial_ref[:seg, :]
+    key_out[...] = back * values_ref[...]
+    value_out[...] = back * key_ref[...]
+    far = jnp.where(pos < 2, pos + 2, pos - 2)
+    strips = (
+        (own_strip[...], pos),
+        (left_strip[...], pos - 1),
+        (right_strip[...], pos + 1),
+        (two_strip[...] + partial_ref[seg : seg + 8, :], far),
+        (partial_ref[seg + 8 :, :], 3 - pos),
+    )
+    total = None
+    for block in range(4):
+        value = jnp.zeros_like(own_strip[...])
+        for where, (strip, source) in enumerate(strips):
+            hit = source == block
+            if where == THREE:
+                hit = jnp.logical_and(hit, jnp.logical_or(pos == 0, pos == 3))
+            value = value + jnp.where(hit, strip, 0.0)
+        total = value if total is None else total + value
+    skip_out[...] = jnp.sum(total, axis=0, keepdims=True)
+
+
+def finish(pos, back, key_gate, values, partial, mixed, left_x, right_x, two_x):
+    seg, width = back.shape
+    block = whole_spec((seg, width))
+    return pl.pallas_call(
+        finish_kernel,
+        grid_spec=pltpu.PrefetchScalarGridSpec(
+            num_scalar_prefetch=1,
+            grid=(1,),
+            in_specs=[block] * 3 + [whole_spec(partial.shape)] + [strip_spec(seg, width)] * 4,
+            out_specs=[block, block, whole_spec((1, width))],
+        ),
+        out_shape=[f32(seg, width), f32(seg, width), f32(1, width)],
+        compiler_params=params(12),
+        cost_estimate=cost(3 * seg * width, 24 * seg * width),
+        name="finish",
+    )(pos, back, key_gate, values, partial, mixed, left_x, right_x, two_x)
 
 
 def send(x, *pairs):
@@ -528,23 +544,24 @@
     pos = position.astype(jnp.int32).reshape(1)
     after = lax.optimization_barrier
 
-    gated, mixed = prepare(query_gate, key_gate, values, upstream)
+    gated = key_gate * values
     left, right = to_right(gated), to_left(gated)
+    mixed = mix(gated, upstream, query_gate)
     left_x, right_x = to_right(mixed), to_left(mixed)
+    own_g, own_m = dft(table, seg, gated), dft(table, seg, mixed)
+    left, right, filter_taps, own_g, own_m = after((left, right, filter_taps, own_g, own_m))
+
+    two = send(left, (1, 2), (2, 3)), send(right, (2, 1), (1, 0))
+    left_g, right_g = dft(table, seg, left), dft(table, seg, right)
     windows = taps_spectra(table, filter_taps, seg)
-    own_g = dft(table, seg, gated)
-    left, right, windows, own_g = after((left, right, windows, own_g))
-
-    two = send(left, (1, 2), (2, 3)), send(right, (2, 1), (1, 0))
-    own_m, left_g, right_g = dft(table, seg, mixed), dft(table, seg, left), dft(table, seg, right)
-    left_x, right_x, own_m, left_g, right_g = after((left_x, right_x, own_m, left_g, right_g))
+    left_x, right_x, windows, left_g, right_g = after((left_x, right_x, windows, left_g, right_g))
 
     two_x = send(jnp.where(position == 1, left_x, right_x), (1, 2), (2, 1))
     left_m, right_m = dft(table, seg, left_x), dft(table, seg, right_x)
     *two, left_m, right_m = after((*two, left_m, right_m))
 
     three = send(two[0], (2, 3)), send(two[1], (1, 0))
-    two_m, partial = back_partial(pos, table, inverse, windows, left_m, right_m, two_x, seg)
+    two_m, partial = back_partial(pos, table, inverse, windows, left_m, right_m, left_x, right_x, two_x, seg)
     *two, partial = after((*two, partial))
     partial = send(partial, (1, 0), (2, 3))
     two_g = dft(table, seg, *two)
@@ -552,13 +569,14 @@
     *three, acc = after((*three, acc))
 
     three_g = dft(table, seg, *three)
-    query_grad, filter_grad, back, skip_grad = late(
+    query_grad, filter_grad, back = late(
         pos, inverse, acc, windows, three_g, two_g, own_m, left_m, right_m, two_m,
-        (gated, left, right, *two, *three), mixed, skip_gain[None, :], upstream,
-    )
-    back, partial = after((back, partial))
-    back = back + partial
-    return (query_grad, back * values, back * key_gate, filter_grad, skip_grad[0])
+        gated, mixed, skip_gain[None, :], upstream,
+    )
+    key_grad, value_grad, skip_grad = finish(
+        pos, back, key_gate, values, partial, mixed, left_x, right_x, two_x
+    )
+    return (query_grad, key_grad, value_grad, filter_grad, skip_grad[0])
 
 
 def matmul(left, right):

time: 73.7 us -> 71.5 us (0.970)
  local copies, waits for them, and re-layouts: 3.71 us -> 2.13 us
  waiting for transfers between devices: 23.3 us -> 22 us
  starting transfers between devices: 18.7 us -> 19.6 us
    pallas_call x1 -> x2, Pallas kernels: 3.83 us -> 1.26 us  [the longest x1 1.13 us: finish(): pl.pallas_call(finish_kernel, grid_spec=pltpu.PrefetchScalarGridSpec(num_...]
    pallas_call x8, Pallas kernels: 5.75 us -> 7.81 us  [dft(): pl.pallas_call(dft_kernel, grid=(1,), in_specs=[whole_spec(table.shape)]...]
    unnamed x22 -> x18, local copies, waits for them, and re-layouts: 3.71 us -> 2.13 us
    ppermute x10, waiting for transfers between devices: 23.3 us -> 22 us  [send(): return lax.ppermute(x, 'ctx', list(pairs))]
    ppermute x10, starting transfers between devices: 18.7 us -> 19.6 us  [send(): return lax.ppermute(x, 'ctx', list(pairs))]
  transfers between devices with their start and end apart: 10 -> 10, of which waited for: 5 -> 5; matrix products, arithmetic and copies ran while one was open for 0% -> 0% of each run, Pallas kernels for 29% -> 33%
where the time goes in v5:
time: 71.5 us; the launch traced here: 70.9 us
  Pallas kernels  24.8 us (35%)
  waiting for transfers between devices  22 us (31%)
  starting transfers between devices  19.6 us (27%)
  local copies, waits for them, and re-layouts  2.13 us (3%)
  other arithmetic  1.43 us (2%)
  between operations  0.95 us (1%)
    ppermute x10, waiting for transfers between devices, send(): return lax.ppermute(x, 'ctx', list(pairs))  22 us
    ppermute x10, starting transfers between devices, send(): return lax.ppermute(x, 'ctx', list(pairs))  19.6 us
    pallas_call x8, Pallas kernels, dft(): pl.pallas_call(dft_kernel, grid=(1,), in_specs=[whole_spec(table.shape)]...  7.81 us
    pallas_call x1, Pallas kernels, late(): pl.pallas_call(late_kernel, grid_spec=pltpu.PrefetchScalarGridSpec(num_sc...  6 us
    pallas_call x1, Pallas kernels, taps_spectra(): pl.pallas_call(taps_kernel, grid=(blocks,), in_specs=[whole_spec(table.sh...  5.96 us
    pallas_call x1, Pallas kernels, early(): pl.pallas_call(early_kernel, grid_spec=pltpu.PrefetchScalarGridSpec(num_s...  2.18 us
    unnamed x18, local copies, waits for them, and re-layouts  2.13 us
    pallas_call x1, Pallas kernels, back_partial(): pl.pallas_call(partial_kernel, grid_spec=pltpu.PrefetchScalarGridSpec(num...  1.61 us
  transfers between devices with their start and end apart: 10, of which 5 were waited for; matrix products, arithmetic and copies ran while one was open for 0% of the time, Pallas kernels for 33%

profile of v5, /device:TPU:0, one launch (start us, length us, event | category | flops | bytes accessed | tf_op | source)
XLA Modules:
  0.0 70.9 jit_solution(11532252112208006821)
XLA Ops:
  0.6 0.0 copy-start
  0.6 1.4 %mul.3.refs_0_.gated_ref.rest_1_ = f32[512,256]{1,0:T(8,128)S(1)} multiply(f32[512,256]{1,0:T(8,128)} %key_ref.1, f32[512,256]{1,0:T(8,128)} %values_ref.1) | non-fusion elementwise | flops 131072 | bytes 1572864 | tf_op jit(solution)/shard_map/mul | solution.py:547
  2.0 1.3 %collective-permute-start.1 = (f32[512,256]{1,0:T(8,128)S(1)}, f32[512,256]{1,0:T(8,128)}, u32[]{:S(2)}, u32[]{:S(2)}) collective-permute-start(f32[512,256]{1,0:T(8,128)S(1)} %mul.3.refs_0_.gated_ref.rest_1_), channel_id=1, source_target_pairs={{4,0},{8,4},{12,8},{5,1},{9,5},{13,9},{6,2},{10,6},{14,10},{7,3},{... | collective-permute-start | bytes 1572872 | tf_op jit(solution)/shard_map/ppermute | solution.py:528
  3.3 6.4 %collective-permute-start = (f32[512,256]{1,0:T(8,128)S(1)}, f32[512,256]{1,0:T(8,128)}, u32[]{:S(2)}, u32[]{:S(2)}) collective-permute-start(f32[512,256]{1,0:T(8,128)S(1)} %mul.3.refs_0_.gated_ref.rest_1_), channel_id=1, source_target_pairs={{0,4},{4,8},{8,12},{1,5},{5,9},{9,13},{2,6},{6,10},{10,14},{3,7},{... | collective-permute-start | bytes 1572872 | tf_op jit(solution)/shard_map/ppermute | solution.py:528
  9.7 1.0 %copy-done.5 = f32[512,256]{1,0:T(8,128)S(1)} copy-done((f32[512,256]{1,0:T(8,128)S(1)}, f32[512,256]{1,0:T(8,128)}, u32[]{:S(2)}) %copy-start.5) | copy-done | bytes 524312
  10.7 1.0 %copy-done.7 = f32[512,256]{1,0:T(8,128)S(1)} copy-done((f32[512,256]{1,0:T(8,128)S(1)}, f32[512,256]{1,0:T(8,128)}, u32[]{:S(2)}) %copy-start.7) | copy-done | bytes 524312
  11.7 0.1 mix.1.refs_0_.rest_2_.own_strip
  11.9 1.3 %collective-permute-start.5 = (f32[520,256]{1,0:T(8,128)S(1)}, f32[520,256]{1,0:T(8,128)S(1)}, u32[]{:S(2)}, u32[]{:S(2)}) collective-permute-start(f32[520,256]{1,0:T(8,128)S(1)} %mix.1.refs_0_.rest_2_.own_strip), channel_id=1, source_target_pairs={{4,0},{8,4},{12,8},{5,1},{9,5},{13,9},{6,2},{10,6},{14,10},{7,3},{... | collective-permute-start | bytes 1597448 | tf_op jit(solution)/shard_map/ppermute | solution.py:528
  13.2 4.6 %collective-permute-start.4 = (f32[520,256]{1,0:T(8,128)S(1)}, f32[520,256]{1,0:T(8,128)S(1)}, u32[]{:S(2)}, u32[]{:S(2)}) collective-permute-start(f32[520,256]{1,0:T(8,128)S(1)} %mix.1.refs_0_.rest_2_.own_strip), channel_id=1, source_target_pairs={{0,4},{4,8},{8,12},{1,5},{5,9},{9,13},{2,6},{6,10},{10,14},{3,7},{... | collective-permute-start | bytes 1597448 | tf_op jit(solution)/shard_map/ppermute | solution.py:528
  17.8 0.0 copy-done
  17.8 0.7 %dft.9.own_m = f32[1024,256]{1,0:T(8,128)S(1)} custom-call(bf16[2,4,256,256]{3,2,1,0:T(8,128)(2,1)S(1)} %copy-done, f32[520,256]{1,0:T(8,128)S(1)} %mix.1.refs_0_.rest_2_.own_strip), custom_call_target="tpu_custom_call" | custom-call | flops 402653184 | bytes 1572864 | tf_op jit(solution)/shard_map/dft/pallas_call | solution.py:127
  18.5 0.0 copy-start.1
  18.5 0.7 %dft.8.own_g = f32[1024,256]{1,0:T(8,128)S(1)} custom-call(bf16[2,4,256,256]{3,2,1,0:T(8,128)(2,1)S(1)} %copy-done, f32[512,256]{1,0:T(8,128)S(1)} %mul.3.refs_0_.gated_ref.rest_1_), custom_call_target="tpu_custom_call" | custom-call | flops 402653184 | bytes 1572864 | tf_op jit(solution)/shard_map/dft/pallas_call | solution.py:127
  19.2 0.6 collective-permute-done.1.refs_0_
  19.8 1.4 %collective-permute-done.refs_0_ = f32[512,256]{1,0:T(8,128)} collective-permute-done((f32[512,256]{1,0:T(8,128)S(1)}, f32[512,256]{1,0:T(8,128)}, u32[]{:S(2)}, u32[]{:S(2)}) %collective-permute-start) | collective-permute-done | bytes 524320 | tf_op jit(solution)/shard_map/ppermute | solution.py:528
  21.2 0.7 collective-permute-start.2
  21.9 1.3 %collective-permute-start.3 = (f32[512,256]{1,0:T(8,128)}, f32[512,256]{1,0:T(8,128)S(1)}, u32[]{:S(2)}, u32[]{:S(2)}) collective-permute-start(f32[512,256]{1,0:T(8,128)} %collective-permute-done.1.refs_0_), channel_id=1, source_target_pairs={{8,4},{4,0},{9,5},{5,1},{10,6},{6,2},{11,7},{7,3},{24,20},{20,16},... | collective-permute-start | bytes 1572872 | tf_op jit(solution)/shard_map/ppermute | solution.py:528
  23.2 1.7 %dft.10.left_g = f32[1024,256]{1,0:T(8,128)S(1)} custom-call(bf16[2,4,256,256]{3,2,1,0:T(8,128)(2,1)S(1)} %copy-done, f32[512,256]{1,0:T(8,128)} %collective-permute-done.refs_0_), custom_call_target="tpu_custom_call" | custom-call | flops 402653184 | bytes 1572864 | tf_op jit(solution)/shard_map/dft/pallas_call | solution.py:127
  24.9 1.8 %dft.11.right_g = f32[1024,256]{1,0:T(8,128)S(1)} custom-call(bf16[2,4,256,256]{3,2,1,0:T(8,128)(2,1)S(1)} %copy-done, f32[512,256]{1,0:T(8,128)} %collective-permute-done.1.refs_0_), custom_call_target="tpu_custom_call" | custom-call | flops 402653184 | bytes 1572864 | tf_op jit(solution)/shard_map/dft/pallas_call | solution.py:127
  26.7 0.0 copy-done.1
  26.7 6.0 %taps.1.win_near.win_far.win_own.win_left.win_right.win_two.win_ref = f32[7,1024,256]{2,1,0:T(8,128)S(1)} custom-call(bf16[2,4,256,256]{3,2,1,0:T(8,128)(2,1)S(1)} %copy-done, f32[4096,256]{1,0:T(8,128)S(1)} %copy-done.1), custom_call_target="tpu_custom_call" | custom-call | flops 3221225472 | bytes 12582912 | tf_op jit(solution)/shard_map/taps/pallas_call | solution.py:162
  32.7 0.0 copy-start.2
  32.7 0.0 collective-permute-done.5.refs_0_.right_strip
  32.7 0.0 collective-permute-done.4.refs_0_.left_strip
  32.7 0.1 broadcast_select_fusion
  32.8 0.8 %collective-permute-start.8 = (f32[520,256]{1,0:T(8,128)S(1)}, f32[520,256]{1,0:T(8,128)S(1)}, u32[]{:S(2)}, u32[]{:S(2)}) collective-permute-start(f32[520,256]{1,0:T(8,128)S(1)} %broadcast_select_fusion), channel_id=1, source_target_pairs={{4,8},{8,4},{5,9},{9,5},{6,10},{10,6},{7,11},{11,7},{20,24},{24,20... | collective-permute-start | bytes 1597448 | tf_op jit(solution)/shard_map/ppermute | solution.py:528
  33.6 0.7 %dft.12.left_ref.left_m = f32[1024,256]{1,0:T(8,128)S(1)} custom-call(bf16[2,4,256,256]{3,2,1,0:T(8,128)(2,1)S(1)} %copy-done, f32[520,256]{1,0:T(8,128)S(1)} %collective-permute-done.4.refs_0_.left_strip), custom_call_target="tpu_custom_call" | custom-call | flops 402653184 | bytes 1572864 | tf_op jit(solution)/shard_map/dft/pallas_call | solution.py:127
  34.3 0.7 %dft.13.right_ref.right_m = f32[1024,256]{1,0:T(8,128)S(1)} custom-call(bf16[2,4,256,256]{3,2,1,0:T(8,128)(2,1)S(1)} %copy-done, f32[520,256]{1,0:T(8,128)S(1)} %collective-permute-done.5.refs_0_.right_strip), custom_call_target="tpu_custom_call" | custom-call | flops 402653184 | bytes 1572864 | tf_op jit(solution)/shard_map/dft/pallas_call | solution.py:127
  35.1 0.0 collective-permute-done.2.refs_0_
  35.1 6.4 %collective-permute-done.3.refs_1_ = f32[512,256]{1,0:T(8,128)S(1)} collective-permute-done((f32[512,256]{1,0:T(8,128)}, f32[512,256]{1,0:T(8,128)S(1)}, u32[]{:S(2)}, u32[]{:S(2)}) %collective-permute-start.3) | collective-permute-done | bytes 524320 | tf_op jit(solution)/shard_map/ppermute | solution.py:528
  41.5 0.7 collective-permute-start.6
  42.2 1.3 %collective-permute-start.7 = (f32[512,256]{1,0:T(8,128)S(1)}, f32[512,256]{1,0:T(8,128)S(1)}, u32[]{:S(2)}, u32[]{:S(2)}) collective-permute-start(f32[512,256]{1,0:T(8,128)S(1)} %collective-permute-done.3.refs_1_), channel_id=1, source_target_pairs={{4,0},{5,1},{6,2},{7,3},{20,16},{21,17},{22,18},{23,19}} | collective-permute-start | bytes 1572872 | tf_op jit(solution)/shard_map/ppermute | solution.py:528
  43.5 0.0 collective-permute-done.8.x_ref.far_strip.two_strip
  43.5 0.0 copy-done.2
  43.5 1.6 %partial.1 = (f32[1024,256]{1,0:T(8,128)S(1)}, f32[528,256]{1,0:T(8,128)S(1)}) custom-call(s32[1]{0:T(128)} %bitcast.pos_ref, bf16[2,4,256,256]{3,2,1,0:T(8,128)(2,1)S(1)} %copy-done, bf16[2,4,256,256]{3,2,1,0:T(8,128)(2,1)S(1)} %copy-done.2, f32[7,1024,256]{2,1,0:T(8,128)S(1)} %taps.1.win_near.win_far.win_own.win_left.win_right.win_two.win_ref, ...), custom_call_target="tpu_custom_call" | custom-call | flops 805306368 | bytes 3145728 | tf_op jit(solution)/shard_map/partial/pallas_call | solution.py:223
  45.1 1.3 %collective-permute-start.9 = (f32[528,256]{1,0:T(8,128)S(1)}, f32[528,256]{1,0:T(8,128)S(1)}, u32[]{:S(2)}, u32[]{:S(2)}) collective-permute-start(f32[528,256]{1,0:T(8,128)S(1)} %get-tuple-element.56), channel_id=1, source_target_pairs={{4,0},{8,12},{5,1},{9,13},{6,2},{10,14},{7,3},{11,15},{20,16},{24,... | collective-permute-start | bytes 1622024 | tf_op jit(solution)/shard_map/ppermute | solution.py:528
  46.4 0.7 %dft.14.two_g = f32[1024,256]{1,0:T(8,128)S(1)} custom-call(bf16[2,4,256,256]{3,2,1,0:T(8,128)(2,1)S(1)} %copy-done, f32[512,256]{1,0:T(8,128)S(1)} %collective-permute-done.2.refs_0_, f32[512,256]{1,0:T(8,128)S(1)} %collective-permute-done.3.refs_1_), custom_call_target="tpu_custom_call" | custom-call | flops 402653184 | bytes 1572864 | tf_op jit(solution)/shard_map/dft/pallas_call | solution.py:127
  47.2 0.0 copy-start.6
  47.2 0.0 copy-start.8
  47.2 2.2 %early.1.acc_ref = f32[4,1024,256]{2,1,0:T(8,128)S(1)} custom-call(s32[1]{0:T(128)} %bitcast.pos_ref, f32[7,1024,256]{2,1,0:T(8,128)S(1)} %taps.1.win_near.win_far.win_own.win_left.win_right.win_two.win_ref, f32[7,1024,256]{2,1,0:T(8,128)S(1)} %taps.1.win_near.win_far.win_own.win_left.win_right.win_two.win_ref, ...), custom_call_target="tpu_custom_call" | custom-call | flops 26214400 | bytes 15728640 | tf_op jit(solution)/shard_map/early/pallas_call | solution.py:354
  49.4 0.0 collective-permute-done.6.refs_0_
  49.4 7.8 %collective-permute-done.7.refs_1_ = f32[512,256]{1,0:T(8,128)S(1)} collective-permute-done((f32[512,256]{1,0:T(8,128)S(1)}, f32[512,256]{1,0:T(8,128)S(1)}, u32[]{:S(2)}, u32[]{:S(2)}) %collective-permute-start.7) | collective-permute-done | bytes 524320 | tf_op jit(solution)/shard_map/ppermute | solution.py:528
  57.2 0.7 %dft.15.three_g = f32[1024,256]{1,0:T(8,128)S(1)} custom-call(bf16[2,4,256,256]{3,2,1,0:T(8,128)(2,1)S(1)} %copy-done, f32[512,256]{1,0:T(8,128)S(1)} %collective-permute-done.6.refs_0_, f32[512,256]{1,0:T(8,128)S(1)} %collective-permute-done.7.refs_1_), custom_call_target="tpu_custom_call" | custom-call | flops 402653184 | bytes 1572864 | tf_op jit(solution)/shard_map/dft/pallas_call | solution.py:127
  58.0 0.0 copy-start.3
  58.0 0.0 copy-start.4
  58.0 6.0 %late.1 = (f32[512,256]{1,0:T(8,128)}, f32[1024,256]{1,0:T(8,128)}, f32[512,256]{1,0:T(8,128)S(1)}) custom-call(s32[1]{0:T(128)} %bitcast.pos_ref, bf16[2,4,256,256]{3,2,1,0:T(8,128)(2,1)S(1)} %copy-done.2, f32[4,1024,256]{2,1,0:T(8,128)S(1)} %early.1.acc_ref, f32[7,1024,256]{2,1,0:T(8,128)S(1)} %taps.1.win_near.win_far.win_own.win_left.win_right.win_two.win_ref, ...), custom_call_target="tpu_custom_call" | custom-call | flops 1610612736 | bytes 13107200 | tf_op jit(solution)/shard_map/late/pallas_call | solution.py:451
  64.0 5.8 %collective-permute-done.9.partial_ref = f32[528,256]{1,0:T(8,128)S(1)} collective-permute-done((f32[528,256]{1,0:T(8,128)S(1)}, f32[528,256]{1,0:T(8,128)S(1)}, u32[]{:S(2)}, u32[]{:S(2)}) %collective-permute-start.9) | collective-permute-done | bytes 540704 | tf_op jit(solution)/shard_map/ppermute | solution.py:528
  69.8 1.1 %finish.1 = (f32[512,256]{1,0:T(8,128)}, f32[512,256]{1,0:T(8,128)}, f32[1,256]{1,0:T(1,128)}) custom-call(s32[1]{0:T(128)} %bitcast.pos_ref, f32[512,256]{1,0:T(8,128)S(1)} %get-tuple-element.55.back_ref, f32[512,256]{1,0:T(8,128)S(1)} %copy-done.3, f32[512,256]{1,0:T(8,128)S(1)} %copy-done.4, f32[528,256]{1,0:T(8,128)S(1)} %collective-permute-done.9.partial_ref, ...), custom_call_target="tpu_custom_call" | custom-call | flops 393216 | bytes 3145728 | tf_op jit(solution)/shard_map/finish/pallas_call | solution.py:512
  (6 shorter events, 0.0 us)
Async XLA Ops:
  0.6 17.1 %copy-start = (bf16[2,4,256,256]{3,2,1,0:T(8,128)(2,1)S(1)}, bf16[2,4,256,256]{3,2,1,0:T(8,128)(2,1)}, u32[]{:S(2)}) copy-start(bf16[2,4,256,256]{3,2,1,0:T(8,128)(2,1)} %constant.11.clone.table_ref) | copy-start | bytes 3145732
  2.0 17.8 %collective-permute-start.1 = (f32[512,256]{1,0:T(8,128)S(1)}, f32[512,256]{1,0:T(8,128)}, u32[]{:S(2)}, u32[]{:S(2)}) collective-permute-start(f32[512,256]{1,0:T(8,128)S(1)} %mul.3.refs_0_.gated_ref.rest_1_), channel_id=1, source_target_pairs={{4,0},{8,4},{12,8},{5,1},{9,5},{13,9},{6,2},{10,6},{14,10},{7,3},{... | collective-permute-start | bytes 1572872 | tf_op jit(solution)/shard_map/ppermute | solution.py:528
  3.3 17.9 %collective-permute-start = (f32[512,256]{1,0:T(8,128)S(1)}, f32[512,256]{1,0:T(8,128)}, u32[]{:S(2)}, u32[]{:S(2)}) collective-permute-start(f32[512,256]{1,0:T(8,128)S(1)} %mul.3.refs_0_.gated_ref.rest_1_), channel_id=1, source_target_pairs={{0,4},{4,8},{8,12},{1,5},{5,9},{9,13},{2,6},{6,10},{10,14},{3,7},{... | collective-permute-start | bytes 1572872 | tf_op jit(solution)/shard_map/ppermute | solution.py:528
  9.7 1.0 %copy-start.5 = (f32[512,256]{1,0:T(8,128)S(1)}, f32[512,256]{1,0:T(8,128)}, u32[]{:S(2)}) copy-start(f32[512,256]{1,0:T(8,128)} %rest_4_.1) | copy-start | bytes 1572868
  10.7 1.0 %copy-start.7 = (f32[512,256]{1,0:T(8,128)S(1)}, f32[512,256]{1,0:T(8,128)}, u32[]{:S(2)}) copy-start(f32[512,256]{1,0:T(8,128)} %query_ref.1) | copy-start | bytes 1572868
  11.9 20.8 %collective-permute-start.5 = (f32[520,256]{1,0:T(8,128)S(1)}, f32[520,256]{1,0:T(8,128)S(1)}, u32[]{:S(2)}, u32[]{:S(2)}) collective-permute-start(f32[520,256]{1,0:T(8,128)S(1)} %mix.1.refs_0_.rest_2_.own_strip), channel_id=1, source_target_pairs={{4,0},{8,4},{12,8},{5,1},{9,5},{13,9},{6,2},{10,6},{14,10},{7,3},{... | collective-permute-start | bytes 1597448 | tf_op jit(solution)/shard_map/ppermute | solution.py:528
  13.2 19.5 %collective-permute-start.4 = (f32[520,256]{1,0:T(8,128)S(1)}, f32[520,256]{1,0:T(8,128)S(1)}, u32[]{:S(2)}, u32[]{:S(2)}) collective-permute-start(f32[520,256]{1,0:T(8,128)S(1)} %mix.1.refs_0_.rest_2_.own_strip), channel_id=1, source_target_pairs={{0,4},{4,8},{8,12},{1,5},{5,9},{9,13},{2,6},{6,10},{10,14},{3,7},{... | collective-permute-start | bytes 1597448 | tf_op jit(solution)/shard_map/ppermute | solution.py:528
  18.5 8.2 %copy-start.1 = (f32[4096,256]{1,0:T(8,128)S(1)}, f32[4096,256]{1,0:T(8,128)}, u32[]{:S(2)}) copy-start(f32[4096,256]{1,0:T(8,128)} %x_ref) | copy-start | bytes 12582916
  21.2 13.9 %collective-permute-start.2 = (f32[512,256]{1,0:T(8,128)}, f32[512,256]{1,0:T(8,128)S(1)}, u32[]{:S(2)}, u32[]{:S(2)}) collective-permute-start(f32[512,256]{1,0:T(8,128)} %collective-permute-done.refs_0_), channel_id=1, source_target_pairs={{4,8},{8,12},{5,9},{9,13},{6,10},{10,14},{7,11},{11,15},{20,24},{2... | collective-permute-start | bytes 1572872 | tf_op jit(solution)/shard_map/ppermute | solution.py:528
  21.9 19.6 %collective-permute-start.3 = (f32[512,256]{1,0:T(8,128)}, f32[512,256]{1,0:T(8,128)S(1)}, u32[]{:S(2)}, u32[]{:S(2)}) collective-permute-start(f32[512,256]{1,0:T(8,128)} %collective-permute-done.1.refs_0_), channel_id=1, source_target_pairs={{8,4},{4,0},{9,5},{5,1},{10,6},{6,2},{11,7},{7,3},{24,20},{20,16},... | collective-permute-start | bytes 1572872 | tf_op jit(solution)/shard_map/ppermute | solution.py:528
  32.7 10.8 %copy-start.2 = (bf16[2,4,256,256]{3,2,1,0:T(8,128)(2,1)S(1)}, bf16[2,4,256,256]{3,2,1,0:T(8,128)(2,1)}, u32[]{:S(2)}) copy-start(bf16[2,4,256,256]{3,2,1,0:T(8,128)(2,1)} %constant.12.clone.inverse_ref) | copy-start | bytes 3145732
  32.8 10.7 %collective-permute-start.8 = (f32[520,256]{1,0:T(8,128)S(1)}, f32[520,256]{1,0:T(8,128)S(1)}, u32[]{:S(2)}, u32[]{:S(2)}) collective-permute-start(f32[520,256]{1,0:T(8,128)S(1)} %broadcast_select_fusion), channel_id=1, source_target_pairs={{4,8},{8,4},{5,9},{9,5},{6,10},{10,6},{7,11},{11,7},{20,24},{24,20... | collective-permute-start | bytes 1597448 | tf_op jit(solution)/shard_map/ppermute | solution.py:528
  41.5 7.9 %collective-permute-start.6 = (f32[512,256]{1,0:T(8,128)S(1)}, f32[512,256]{1,0:T(8,128)S(1)}, u32[]{:S(2)}, u32[]{:S(2)}) collective-permute-start(f32[512,256]{1,0:T(8,128)S(1)} %collective-permute-done.2.refs_0_), channel_id=1, source_target_pairs={{8,12},{9,13},{10,14},{11,15},{24,28},{25,29},{26,30},{27,31}} | collective-permute-start | bytes 1572872 | tf_op jit(solution)/shard_map/ppermute | solution.py:528
  42.2 15.0 %collective-permute-start.7 = (f32[512,256]{1,0:T(8,128)S(1)}, f32[512,256]{1,0:T(8,128)S(1)}, u32[]{:S(2)}, u32[]{:S(2)}) collective-permute-start(f32[512,256]{1,0:T(8,128)S(1)} %collective-permute-done.3.refs_1_), channel_id=1, source_target_pairs={{4,0},{5,1},{6,2},{7,3},{20,16},{21,17},{22,18},{23,19}} | collective-permute-start | bytes 1572872 | tf_op jit(solution)/shard_map/ppermute | solution.py:528
  45.1 24.7 %collective-permute-start.9 = (f32[528,256]{1,0:T(8,128)S(1)}, f32[528,256]{1,0:T(8,128)S(1)}, u32[]{:S(2)}, u32[]{:S(2)}) collective-permute-start(f32[528,256]{1,0:T(8,128)S(1)} %get-tuple-element.56), channel_id=1, source_target_pairs={{4,0},{8,12},{5,1},{9,13},{6,2},{10,14},{7,3},{11,15},{20,16},{24,... | collective-permute-start | bytes 1622024 | tf_op jit(solution)/shard_map/ppermute | solution.py:528
  47.2 10.8 %copy-start.6 = (f32[512,256]{1,0:T(8,128)S(1)}, f32[512,256]{1,0:T(8,128)}, u32[]{:S(2)}) copy-start(f32[512,256]{1,0:T(8,128)} %rest_4_.1) | copy-start | bytes 1572868
  47.2 10.8 %copy-start.8 = (f32[256]{0:T(256)S(1)}, f32[256]{0:T(256)}, u32[]{:S(2)}) copy-start(f32[256]{0:T(256)} %param.12) | copy-start | bytes 3076
  58.0 11.8 %copy-start.3 = (f32[512,256]{1,0:T(8,128)S(1)}, f32[512,256]{1,0:T(8,128)}, u32[]{:S(2)}) copy-start(f32[512,256]{1,0:T(8,128)} %key_ref.1) | copy-start | bytes 1572868
  58.0 11.8 %copy-start.4 = (f32[512,256]{1,0:T(8,128)S(1)}, f32[512,256]{1,0:T(8,128)}, u32[]{:S(2)}) copy-start(f32[512,256]{1,0:T(8,128)} %values_ref.1) | copy-start | bytes 1572868

commit v6 on v5

--- a/solution.py
+++ b/solution.py
@@ -185,18 +185,16 @@
 
 
 def partial_kernel(
-    pos_ref, table_ref, inverse_ref, win_near, win_far, left_ref, right_ref, x_ref,
-    left_strip, right_strip, far_strip, far_ref, out_ref, z_ref
+    pos_ref, table_ref, inverse_ref, win_near, win_far, next_ref, x_ref, next_strip, far_strip, far_ref, out_ref, z_ref
 ):
     rows = far_ref.shape[0] // 4
     sub = rows // 2
-    is_left = pos_ref[0] != 1
     for group, part in enumerate(spread(x_ref[...])):
         base = group * rows
         far = dot3(table_ref, group, *split(part))
         far_ref[base : base + rows, :] = far
         re, im = slice(base, base + sub), slice(base + sub, base + rows)
-        near = tuple(jnp.where(is_left, left_ref[at, :], right_ref[at, :]) for at in (re, im))
+        near = (next_ref[re, :], next_ref[im, :])
         total = add(
             conj_mul((win_near[0, re, :], win_near[0, im, :]), near),
             conj_mul((win_far[0, re, :], win_far[0, im, :]), (far[:sub], far[sub:])),
@@ -205,11 +203,11 @@
     quarters = gather_quarters([z_ref[g, :sub] for g in range(4)], [z_ref[g, sub:] for g in range(4)])
     for i, quarter in enumerate(quarters):
         out_ref[i * sub : (i + 1) * sub, :] = quarter
-    out_ref[4 * sub : 4 * sub + 8, :] = jnp.where(is_left, left_strip[...], right_strip[...])
+    out_ref[4 * sub : 4 * sub + 8, :] = next_strip[...]
     out_ref[4 * sub + 8 :, :] = far_strip[...]
 
 
-def back_partial(pos, table, inverse, windows, left, right, left_x, right_x, x, seg):
+def back_partial(pos, table, inverse, windows, next_m, next_x, x, seg):
     width = x.shape[1]
     n = (windows.shape[0] + 1) // 2
 
@@ -219,7 +217,6 @@
             lambda i, pos: (jnp.where(pos[0] == 1, n - 1 + distance, n - 1 - distance), 0, 0),
         )
 
-    near = whole_spec((2 * seg, width))
     return pl.pallas_call(
         partial_kernel,
         grid_spec=pltpu.PrefetchScalarGridSpec(
@@ -230,10 +227,9 @@
                 whole_spec(inverse.shape),
                 window(2),
                 window(3),
-                near,
-                near,
+                whole_spec((2 * seg, width)),
                 whole_spec((seg, width)),
-                *[strip_spec(seg, width)] * 3,
+                *[strip_spec(seg, width)] * 2,
             ],
             out_specs=[whole_spec((2 * seg, width)), whole_spec((seg + 16, width))],
             scratch_shapes=[pltpu.VMEM((4, seg // 2, width), jnp.float32)],
@@ -242,23 +238,23 @@
         compiler_params=params(24),
         cost_estimate=cost(6 * seg * seg * width * 2, 24 * seg * width),
         name="partial",
-    )(pos, table, inverse, windows, windows, left, right, x, left_x, right_x, x)
-
-
-OWN, LEFT, RIGHT, TWO, THREE = range(5)
+    )(pos, table, inverse, windows, windows, next_m, x, next_x, x)
+
+
+OWN, OUTER, NEXT, TWO, THREE = range(5)
 PAIRS = (
-    ((), ((OWN, THREE),), ((OWN, TWO), (RIGHT, THREE))),
+    ((), ((OWN, THREE),), ((OWN, TWO), (NEXT, THREE))),
     (
-        ((LEFT, RIGHT), (OWN, TWO)),
-        ((LEFT, OWN), (OWN, RIGHT), (RIGHT, TWO)),
-        ((LEFT, LEFT), (OWN, OWN), (RIGHT, RIGHT), (TWO, TWO)),
+        ((OUTER, NEXT), (OWN, TWO)),
+        ((OUTER, OWN), (OWN, NEXT), (NEXT, TWO)),
+        ((OUTER, OUTER), (OWN, OWN), (NEXT, NEXT), (TWO, TWO)),
     ),
     (
-        ((TWO, TWO), (LEFT, LEFT), (OWN, OWN), (RIGHT, RIGHT)),
-        ((LEFT, TWO), (OWN, LEFT), (RIGHT, OWN)),
-        ((OWN, TWO), (RIGHT, LEFT)),
+        ((TWO, TWO), (NEXT, NEXT), (OWN, OWN), (OUTER, OUTER)),
+        ((NEXT, TWO), (OWN, NEXT), (OUTER, OWN)),
+        ((OWN, TWO), (OUTER, NEXT)),
     ),
-    (((LEFT, THREE), (OWN, TWO)), ((OWN, THREE),), ()),
+    (((NEXT, THREE), (OWN, TWO)), ((OWN, THREE),), ()),
 )
 
 
@@ -302,7 +298,7 @@
 
 
 def early_kernel(
-    pos_ref, win_own, win_left, win_right, win_two, own_g, left_g, right_g, two_g, own_m, left_m, right_m, out_ref
+    pos_ref, win_own, win_outer, win_next, win_two, own_g, outer_g, next_g, two_g, own_m, outer_m, next_m, out_ref
 ):
     pos, sign = pos_ref[0], group_sign()
     rows = own_g.shape[0]
@@ -316,12 +312,12 @@
 
     def sums(tile, _):
         re, im, read = tile_reader(tile, sub)
-        own, left, right = read(win_own, 0), read(win_left, 0), read(win_right, 0)
-        conv = add(mul(own, read(own_g)), mul(left, read(left_g)))
-        conv = add(conv, add(mul(right, read(right_g)), mul(read(win_two, 0), read(two_g))))
+        own, outer, ahead = read(win_own, 0), read(win_outer, 0), read(win_next, 0)
+        conv = add(mul(own, read(own_g)), mul(outer, read(outer_g)))
+        conv = add(conv, add(mul(ahead, read(next_g)), mul(read(win_two, 0), read(two_g))))
         put((re, im), 0, conv)
-        back = add(conj_mul(own, read(own_m)), conj_mul(right, read(left_m)))
-        put((re, im), 1, add(back, conj_mul(left, read(right_m))))
+        back = add(conj_mul(own, read(own_m)), conj_mul(ahead, read(outer_m)))
+        put((re, im), 1, add(back, conj_mul(outer, read(next_m))))
         return _
 
     lax.fori_loop(0, count, sums, 0)
@@ -331,8 +327,8 @@
         def _():
             def lags(tile, _):
                 re, im, read = tile_reader(tile, sub)
-                gated = [functools.partial(read, ref) for ref in (own_g, left_g, right_g, two_g)]
-                mixed = [functools.partial(read, ref) for ref in (own_m, left_m, right_m)]
+                gated = [functools.partial(read, ref) for ref in (own_g, outer_g, next_g, two_g)]
+                mixed = [functools.partial(read, ref) for ref in (own_m, outer_m, next_m)]
                 for slot, value in enumerate(pair_sums(distances, gated, mixed, sign, False)):
                     if value is None:
                         value = (jnp.zeros_like(own_g[re, :]),) * 2
@@ -358,8 +354,8 @@
             grid=(4,),
             in_specs=[
                 window(lambda p: mid),
-                window(lambda p: mid + 1),
-                window(lambda p: mid - 1),
+                window(lambda p: jnp.where(p < 2, mid + 1, mid - 1)),
+                window(lambda p: jnp.where(p < 2, mid - 1, mid + 1)),
                 window(lambda p: jnp.where(p < 2, mid - 2, mid + 2)),
             ]
             + [group] * 7,
@@ -373,7 +369,7 @@
 
 
 def late_kernel(
-    pos_ref, inverse_ref, acc_ref, win_ref, three_g, two_g, own_m, left_m, right_m, *rest
+    pos_ref, inverse_ref, acc_ref, win_ref, three_g, two_g, own_m, outer_m, next_m, *rest
 ):
     two_m, gated_ref, mixed_ref, skip_ref, up_ref, query_out, filter_out, back_out, x_high, x_low, z_ref = rest
     group = pl.program_id(0)
@@ -395,7 +391,7 @@
                 re, im, read = tile_reader(tile, sub)
 
                 gated = [None, None, None, functools.partial(read, two_g), functools.partial(read, three_g)]
-                mixed = [functools.partial(read, ref) for ref in (own_m, left_m, right_m, two_m)]
+                mixed = [functools.partial(read, ref) for ref in (own_m, outer_m, next_m, two_m)]
                 total = [read(acc_ref, slot) for slot in range(4)]
                 if where in (0, 3):
                     total[0] = add(total[0], mul(read(win_ref, 0), gated[THREE]()))
@@ -437,7 +433,7 @@
                     filter_out[base : base + sub, :] = quarter
 
 
-def late(pos, inverse, acc, windows, three_g, two_g, own_m, left_m, right_m, two_m, gated, mixed, skip, upstream):
+def late(pos, inverse, acc, windows, three_g, two_g, own_m, outer_m, next_m, two_m, gated, mixed, skip, upstream):
     seg, width = upstream.shape
     rows = seg // 2
     mid = windows.shape[0] // 2
@@ -474,11 +470,11 @@
         compiler_params=params(20),
         cost_estimate=cost(12 * seg * seg * width * 2, 100 * seg * width),
         name="late",
-    )(pos, inverse, acc, windows, three_g, two_g, own_m, left_m, right_m, two_m, gated, mixed, skip, upstream)
+    )(pos, inverse, acc, windows, three_g, two_g, own_m, outer_m, next_m, two_m, gated, mixed, skip, upstream)
 
 
 def finish_kernel(
-    pos_ref, back_ref, key_ref, values_ref, partial_ref, own_strip, left_strip, right_strip, two_strip,
+    pos_ref, back_ref, key_ref, values_ref, partial_ref, own_strip, outer_strip, out_strip, across_strip, two_strip,
     key_out, value_out, skip_out,
 ):
     pos = pos_ref[0]
@@ -489,24 +485,21 @@
     far = jnp.where(pos < 2, pos + 2, pos - 2)
     strips = (
         (own_strip[...], pos),
-        (left_strip[...], pos - 1),
-        (right_strip[...], pos + 1),
+        (outer_strip[...], jnp.where(pos < 2, 0, 3)),
+        (out_strip[...] + across_strip[...], jnp.where(pos < 2, pos + 1, pos - 1)),
         (two_strip[...] + partial_ref[seg : seg + 8, :], far),
         (partial_ref[seg + 8 :, :], 3 - pos),
     )
     total = None
     for block in range(4):
         value = jnp.zeros_like(own_strip[...])
-        for where, (strip, source) in enumerate(strips):
-            hit = source == block
-            if where == THREE:
-                hit = jnp.logical_and(hit, jnp.logical_or(pos == 0, pos == 3))
-            value = value + jnp.where(hit, strip, 0.0)
+        for strip, source in strips:
+            value = value + jnp.where(source == block, strip, 0.0)
         total = value if total is None else total + value
     skip_out[...] = jnp.sum(total, axis=0, keepdims=True)
 
 
-def finish(pos, back, key_gate, values, partial, mixed, left_x, right_x, two_x):
+def finish(pos, back, key_gate, values, partial, *mixed):
     seg, width = back.shape
     block = whole_spec((seg, width))
     return pl.pallas_call(
@@ -514,67 +507,72 @@
         grid_spec=pltpu.PrefetchScalarGridSpec(
             num_scalar_prefetch=1,
             grid=(1,),
-            in_specs=[block] * 3 + [whole_spec(partial.shape)] + [strip_spec(seg, width)] * 4,
+            in_specs=[block] * 3 + [whole_spec(partial.shape)] + [strip_spec(seg, width)] * len(mixed),
             out_specs=[block, block, whole_spec((1, width))],
         ),
         out_shape=[f32(seg, width), f32(seg, width), f32(1, width)],
         compiler_params=params(12),
         cost_estimate=cost(3 * seg * width, 24 * seg * width),
         name="finish",
-    )(pos, back, key_gate, values, partial, mixed, left_x, right_x, two_x)
+    )(pos, back, key_gate, values, partial, *mixed)
 
 
 def send(x, *pairs):
     return lax.ppermute(x, "ctx", list(pairs))
 
 
-def to_right(x):
-    return send(x, (0, 1), (1, 2), (2, 3))
-
-
-def to_left(x):
-    return send(x, (1, 0), (2, 1), (3, 2))
+def across(x):
+    return send(x, (1, 2), (2, 1))
+
+
+def outward(x):
+    return send(x, (1, 0), (2, 3))
+
+
+def inward(x):
+    return send(x, (0, 1), (3, 2))
 
 
 def local_line(query_gate, key_gate, values, filter_taps, skip_gain, upstream):
     seg, width = values.shape
     forward_np, inverse_np = tables(seg)
     table, inverse = jnp.asarray(forward_np), jnp.asarray(inverse_np)
-    position = lax.axis_index("ctx")
-    pos = position.astype(jnp.int32).reshape(1)
+    pos = lax.axis_index("ctx").astype(jnp.int32).reshape(1)
     after = lax.optimization_barrier
 
     gated = key_gate * values
-    left, right = to_right(gated), to_left(gated)
+    outer = inward(gated)
+    next_g = (outward(gated), across(gated))
     mixed = mix(gated, upstream, query_gate)
-    left_x, right_x = to_right(mixed), to_left(mixed)
+    outer_x = inward(mixed)
+    next_x = (outward(mixed), across(mixed))
     own_g, own_m = dft(table, seg, gated), dft(table, seg, mixed)
-    left, right, filter_taps, own_g, own_m = after((left, right, filter_taps, own_g, own_m))
-
-    two = send(left, (1, 2), (2, 3)), send(right, (2, 1), (1, 0))
-    left_g, right_g = dft(table, seg, left), dft(table, seg, right)
+    outer, *next_g, filter_taps, own_g, own_m = after((outer, *next_g, filter_taps, own_g, own_m))
+
+    two = outward(next_g[1]), across(outer)
+    outer_g, next_g = dft(table, seg, outer), dft(table, seg, *next_g)
     windows = taps_spectra(table, filter_taps, seg)
-    left_x, right_x, windows, left_g, right_g = after((left_x, right_x, windows, left_g, right_g))
-
-    two_x = send(jnp.where(position == 1, left_x, right_x), (1, 2), (2, 1))
-    left_m, right_m = dft(table, seg, left_x), dft(table, seg, right_x)
-    *two, left_m, right_m = after((*two, left_m, right_m))
-
-    three = send(two[0], (2, 3)), send(two[1], (1, 0))
-    two_m, partial = back_partial(pos, table, inverse, windows, left_m, right_m, left_x, right_x, two_x, seg)
+    outer_x, *next_x, windows, outer_g, next_g = after((outer_x, *next_x, windows, outer_g, next_g))
+
+    two_x = across(outer_x)
+    outer_m, next_m = dft(table, seg, outer_x), dft(table, seg, *next_x)
+    *two, outer_m, next_m = after((*two, outer_m, next_m))
+
+    three = outward(two[1])
+    two_m, partial = back_partial(pos, table, inverse, windows, next_m, next_x[1], two_x, seg)
     *two, partial = after((*two, partial))
-    partial = send(partial, (1, 0), (2, 3))
+    partial = outward(partial)
     two_g = dft(table, seg, *two)
-    acc = early(pos, windows, (own_g, left_g, right_g, two_g), (own_m, left_m, right_m), seg)
-    *three, acc = after((*three, acc))
-
-    three_g = dft(table, seg, *three)
+    acc = early(pos, windows, (own_g, outer_g, next_g, two_g), (own_m, outer_m, next_m), seg)
+    three, acc = after((three, acc))
+
+    three_g = dft(table, seg, three)
     query_grad, filter_grad, back = late(
-        pos, inverse, acc, windows, three_g, two_g, own_m, left_m, right_m, two_m,
+        pos, inverse, acc, windows, three_g, two_g, own_m, outer_m, next_m, two_m,
         gated, mixed, skip_gain[None, :], upstream,
     )
     key_grad, value_grad, skip_grad = finish(
-        pos, back, key_gate, values, partial, mixed, left_x, right_x, two_x
+        pos, back, key_gate, values, partial, mixed, outer_x, *next_x, two_x
     )
     return (query_grad, key_grad, value_grad, filter_grad, skip_grad[0])
 

time: 71.5 us -> 79.5 us (1.11)
  the two profiles are of different devices: /device:TPU:0 before, /device:TPU:10 now
where the time goes in v6:
time: 79.5 us; the launch traced here: 78.9 us
  Pallas kernels  28.5 us (36%)
  starting transfers between devices  26.8 us (34%)
  local copies, waits for them, and re-layouts  12 us (15%)
  waiting for transfers between devices  9.01 us (11%)
  other arithmetic  1.42 us (2%)
  between operations  1.14 us (1%)
    ppermute x11, starting transfers between devices, send(): return lax.ppermute(x, 'ctx', list(pairs))  26.8 us
    unnamed x62, local copies, waits for them, and re-layouts  12 us
    ppermute x11, waiting for transfers between devices, send(): return lax.ppermute(x, 'ctx', list(pairs))  9.01 us
    pallas_call x8, Pallas kernels, dft(): pl.pallas_call(dft_kernel, grid=(1,), in_specs=[whole_spec(table.shape)]...  8.88 us
    pallas_call x1, Pallas kernels, taps_spectra(): pl.pallas_call(taps_kernel, grid=(blocks,), in_specs=[whole_spec(table.sh...  5.95 us
    pallas_call x1, Pallas kernels, late(): pl.pallas_call(late_kernel, grid_spec=pltpu.PrefetchScalarGridSpec(num_sc...  5.73 us
    pallas_call x1, Pallas kernels, early(): pl.pallas_call(early_kernel, grid_spec=pltpu.PrefetchScalarGridSpec(num_s...  3.23 us
    pallas_call x1, Pallas kernels, back_partial(): pl.pallas_call(partial_kernel, grid_spec=pltpu.PrefetchScalarGridSpec(num...  2.79 us
  transfers between devices with their start and end apart: 11, of which 3 were waited for; matrix products, arithmetic and copies ran while one was open for 0% of the time, Pallas kernels for 34%

profile of v6, /device:TPU:10, one launch (start us, length us, event | category | flops | bytes accessed | tf_op | source)
XLA Modules:
  0.0 78.9 jit_solution(7812218754792094581)
XLA Ops:
  0.6 0.0 copy-start.3
  0.7 1.4 %mul.3.refs_0_.gated_ref.rest_1_ = f32[512,256]{1,0:T(8,128)S(1)} multiply(f32[512,256]{1,0:T(8,128)} %key_ref.1, f32[512,256]{1,0:T(8,128)} %values_ref.1) | non-fusion elementwise | flops 131072 | bytes 1572864 | tf_op jit(solution)/shard_map/mul | solution.py:543
  2.1 0.0 copy-start.8
  2.1 3.6 %collective-permute-start.2 = (f32[512,256]{1,0:T(8,128)S(1)}, f32[512,256]{1,0:T(8,128)S(1)}, u32[]{:S(2)}, u32[]{:S(2)}) collective-permute-start(f32[512,256]{1,0:T(8,128)S(1)} %mul.3.refs_0_.gated_ref.rest_1_), channel_id=1, source_target_pairs={{4,8},{8,4},{5,9},{9,5},{6,10},{10,6},{7,11},{11,7},{20,24},{24,20... | collective-permute-start | bytes 1572872 | tf_op jit(solution)/shard_map/ppermute | solution.py:521
  5.7 1.3 %collective-permute-start.1 = (f32[512,256]{1,0:T(8,128)S(1)}, f32[512,256]{1,0:T(8,128)S(1)}, u32[]{:S(2)}, u32[]{:S(2)}) collective-permute-start(f32[512,256]{1,0:T(8,128)S(1)} %mul.3.refs_0_.gated_ref.rest_1_), channel_id=1, source_target_pairs={{4,0},{8,12},{5,1},{9,13},{6,2},{10,14},{7,3},{11,15},{20,16},{24,... | collective-permute-start | bytes 1572872 | tf_op jit(solution)/shard_map/ppermute | solution.py:521
  7.0 1.3 %collective-permute-start = (f32[512,256]{1,0:T(8,128)S(1)}, f32[512,256]{1,0:T(8,128)S(1)}, u32[]{:S(2)}, u32[]{:S(2)}) collective-permute-start(f32[512,256]{1,0:T(8,128)S(1)} %mul.3.refs_0_.gated_ref.rest_1_), channel_id=1, source_target_pairs={{0,4},{12,8},{1,5},{13,9},{2,6},{14,10},{3,7},{15,11},{16,20},{28,... | collective-permute-start | bytes 1572872 | tf_op jit(solution)/shard_map/ppermute | solution.py:521
  8.3 0.0 copy-start.25
  8.4 1.0 %copy-done.25 = f32[512,256]{1,0:T(8,128)S(1)} copy-done((f32[512,256]{1,0:T(8,128)S(1)}, f32[512,256]{1,0:T(8,128)}, u32[]{:S(2)}) %copy-start.25) | copy-done | bytes 524312
  9.4 1.0 %copy-done.27 = f32[512,256]{1,0:T(8,128)S(1)} copy-done((f32[512,256]{1,0:T(8,128)S(1)}, f32[512,256]{1,0:T(8,128)}, u32[]{:S(2)}) %copy-start.27) | copy-done | bytes 524312
  10.4 0.1 mix.1.refs_0_.rest_2_.own_strip
  10.5 2.9 %collective-permute-start.7 = (f32[520,256]{1,0:T(8,128)S(1)}, f32[520,256]{1,0:T(8,128)S(1)}, u32[]{:S(2)}, u32[]{:S(2)}) collective-permute-start(f32[520,256]{1,0:T(8,128)S(1)} %mix.1.refs_0_.rest_2_.own_strip), channel_id=1, source_target_pairs={{4,8},{8,4},{5,9},{9,5},{6,10},{10,6},{7,11},{11,7},{20,24},{24,20... | collective-permute-start | bytes 1597448 | tf_op jit(solution)/shard_map/ppermute | solution.py:521
  13.4 2.4 %collective-permute-start.6 = (f32[520,256]{1,0:T(8,128)S(1)}, f32[520,256]{1,0:T(8,128)S(1)}, u32[]{:S(2)}, u32[]{:S(2)}) collective-permute-start(f32[520,256]{1,0:T(8,128)S(1)} %mix.1.refs_0_.rest_2_.own_strip), channel_id=1, source_target_pairs={{4,0},{8,12},{5,1},{9,13},{6,2},{10,14},{7,3},{11,15},{20,16},{24,... | collective-permute-start | bytes 1597448 | tf_op jit(solution)/shard_map/ppermute | solution.py:521
  15.8 3.1 %collective-permute-done.2.refs_1_ = f32[512,256]{1,0:T(8,128)S(1)} collective-permute-done((f32[512,256]{1,0:T(8,128)S(1)}, f32[512,256]{1,0:T(8,128)S(1)}, u32[]{:S(2)}, u32[]{:S(2)}) %collective-permute-start.2) | collective-permute-done | bytes 524320 | tf_op jit(solution)/shard_map/ppermute | solution.py:521
  18.9 1.3 %collective-permute-start.5 = (f32[520,256]{1,0:T(8,128)S(1)}, f32[520,256]{1,0:T(8,128)}, u32[]{:S(2)}, u32[]{:S(2)}) collective-permute-start(f32[520,256]{1,0:T(8,128)S(1)} %mix.1.refs_0_.rest_2_.own_strip), channel_id=1, source_target_pairs={{0,4},{12,8},{1,5},{13,9},{2,6},{14,10},{3,7},{15,11},{16,20},{28,... | collective-permute-start | bytes 1597448 | tf_op jit(solution)/shard_map/ppermute | solution.py:521
  20.2 0.7 dft.9.own_m
  20.9 0.7 dft.8.own_g
  21.7 0.0 copy-start.17
  21.7 1.0 %copy-done.17 = f32[1024,256]{1,0:T(8,128)} copy-done((f32[1024,256]{1,0:T(8,128)}, f32[1024,256]{1,0:T(8,128)S(1)}, u32[]{:S(2)}) %copy-start.17) | copy-done | bytes 1048600
  22.6 0.7 collective-permute-done.refs_0_
  23.4 4.6 %collective-permute-start.3 = (f32[512,256]{1,0:T(8,128)S(1)}, f32[512,256]{1,0:T(8,128)S(1)}, u32[]{:S(2)}, u32[]{:S(2)}) collective-permute-start(f32[512,256]{1,0:T(8,128)S(1)} %collective-permute-done.2.refs_1_), channel_id=1, source_target_pairs={{4,0},{8,12},{5,1},{9,13},{6,2},{10,14},{7,3},{11,15},{20,16},{24,... | collective-permute-start | bytes 1572872 | tf_op jit(solution)/shard_map/ppermute | solution.py:521
  28.0 3.5 %collective-permute-start.4 = (f32[512,256]{1,0:T(8,128)S(1)}, f32[512,256]{1,0:T(8,128)}, u32[]{:S(2)}, u32[]{:S(2)}) collective-permute-start(f32[512,256]{1,0:T(8,128)S(1)} %collective-permute-done.refs_0_), channel_id=1, source_target_pairs={{4,8},{8,4},{5,9},{9,5},{6,10},{10,6},{7,11},{11,7},{20,24},{24,20... | collective-permute-start | bytes 1572872 | tf_op jit(solution)/shard_map/ppermute | solution.py:521
  31.5 5.9 %taps.1.win_near.win_far.win_own.win_outer.win_next.win_two.win_ref = f32[7,1024,256]{2,1,0:T(8,128)S(1)} custom-call(bf16[2,4,256,256]{3,2,1,0:T(8,128)(2,1)S(1)} %copy-done.3, f32[4096,256]{1,0:T(8,128)S(1)} %copy-done.12), custom_call_target="tpu_custom_call" | custom-call | flops 3221225472 | bytes 12582912 | tf_op jit(solution)/shard_map/taps/pallas_call | solution.py:162
  37.5 0.7 dft.10.outer_g
  38.2 1.5 %copy-done.19 = f32[1024,256]{1,0:T(8,128)} copy-done((f32[1024,256]{1,0:T(8,128)}, f32[1024,256]{1,0:T(8,128)S(1)}, u32[]{:S(2)}) %copy-start.19) | copy-done | bytes 1048600
  39.7 0.7 dft.11.next_g
  40.5 1.0 %copy-done.15 = f32[1024,256]{1,0:T(8,128)} copy-done((f32[1024,256]{1,0:T(8,128)}, f32[1024,256]{1,0:T(8,128)S(1)}, u32[]{:S(2)}) %copy-start.15) | copy-done | bytes 1048600
  41.5 2.4 %collective-permute-start.9 = (f32[520,256]{1,0:T(8,128)}, f32[520,256]{1,0:T(8,128)}, u32[]{:S(2)}, u32[]{:S(2)}) collective-permute-start(f32[520,256]{1,0:T(8,128)} %collective-permute-done.5.refs_0_.outer_strip), channel_id=1, source_target_pairs={{4,8},{8,4},{5,9},{9,5},{6,10},{10,6},{7,11},{11,7},{20,24},{24,20... | collective-permute-start | bytes 1597448 | tf_op jit(solution)/shard_map/ppermute | solution.py:521
  43.8 1.8 %dft.12.outer_m = f32[1024,256]{1,0:T(8,128)S(1)} custom-call(bf16[2,4,256,256]{3,2,1,0:T(8,128)(2,1)S(1)} %copy-done.3, f32[520,256]{1,0:T(8,128)} %collective-permute-done.5.refs_0_.outer_strip), custom_call_target="tpu_custom_call" | custom-call | flops 402653184 | bytes 1572864 | tf_op jit(solution)/shard_map/dft/pallas_call | solution.py:127
  45.6 0.7 dft.13.next_ref.next_m
  46.4 0.2 copy-done.4
  46.6 0.8 %copy-done.28 = f32[512,256]{1,0:T(8,128)} copy-done((f32[512,256]{1,0:T(8,128)}, f32[512,256]{1,0:T(8,128)S(1)}, u32[]{:S(2)}) %copy-start.28) | copy-done | bytes 524312
  47.4 2.1 %collective-permute-start.8 = (f32[512,256]{1,0:T(8,128)}, f32[512,256]{1,0:T(8,128)}, u32[]{:S(2)}, u32[]{:S(2)}) collective-permute-start(f32[512,256]{1,0:T(8,128)} %collective-permute-done.4.refs_1_), channel_id=1, source_target_pairs={{4,0},{8,12},{5,1},{9,13},{6,2},{10,14},{7,3},{11,15},{20,16},{24,... | collective-permute-start | bytes 1572872 | tf_op jit(solution)/shard_map/ppermute | solution.py:521
  49.5 5.2 %collective-permute-done.9.x_ref.far_strip.two_strip = f32[520,256]{1,0:T(8,128)} collective-permute-done((f32[520,256]{1,0:T(8,128)}, f32[520,256]{1,0:T(8,128)}, u32[]{:S(2)}, u32[]{:S(2)}) %collective-permute-start.9) | collective-permute-done | bytes 532512 | tf_op jit(solution)/shard_map/ppermute | solution.py:521
  54.7 3.1 %copy-done.1 = f32[7,1024,256]{2,1,0:T(8,128)S(1)} copy-done((f32[7,1024,256]{2,1,0:T(8,128)S(1)}, f32[7,1024,256]{2,1,0:T(8,128)}, u32[]{:S(2)}) %copy-start.1) | copy-done | bytes 7340056
  57.7 1.0 %copy-done.11 = f32[520,256]{1,0:T(8,128)S(1)} copy-done((f32[520,256]{1,0:T(8,128)S(1)}, f32[520,256]{1,0:T(8,128)}, u32[]{:S(2)}) %copy-start.11) | copy-done | bytes 532504
  58.8 1.2 %copy-done.13 = bf16[2,4,256,256]{3,2,1,0:T(8,128)(2,1)S(1)} copy-done((bf16[2,4,256,256]{3,2,1,0:T(8,128)(2,1)S(1)}, bf16[2,4,256,256]{3,2,1,0:T(8,128)(2,1)}, u32[]{:S(2)}) %copy-start.13) | copy-done | bytes 1048600
  60.0 0.0 copy-start.18
  60.0 2.8 %partial.1 = (f32[1024,256]{1,0:T(8,128)S(1)}, f32[528,256]{1,0:T(8,128)S(1)}) custom-call(s32[1]{0:T(128)} %bitcast.pos_ref, bf16[2,4,256,256]{3,2,1,0:T(8,128)(2,1)S(1)} %copy-done.3, bf16[2,4,256,256]{3,2,1,0:T(8,128)(2,1)S(1)} %copy-done.13, f32[7,1024,256]{2,1,0:T(8,128)S(1)} %copy-done.1, f32[7,1024,256]{2,1,0:T(8,128)S(1)} %copy-done.1, ...), custom_call_target="tpu_custom_call" | custom-call | flops 805306368 | bytes 3145728 | tf_op jit(solution)/shard_map/partial/pallas_call | solution.py:220
  62.8 1.5 %collective-permute-start.10 = (f32[528,256]{1,0:T(8,128)S(1)}, f32[528,256]{1,0:T(8,128)S(1)}, u32[]{:S(2)}, u32[]{:S(2)}) collective-permute-start(f32[528,256]{1,0:T(8,128)S(1)} %get-tuple-element.58), channel_id=1, source_target_pairs={{4,0},{8,12},{5,1},{9,13},{6,2},{10,14},{7,3},{11,15},{20,16},{24,... | collective-permute-start | bytes 1622024 | tf_op jit(solution)/shard_map/ppermute | solution.py:521
  64.3 1.8 %dft.14.two_g = f32[1024,256]{1,0:T(8,128)S(1)} custom-call(bf16[2,4,256,256]{3,2,1,0:T(8,128)(2,1)S(1)} %copy-done.3, f32[512,256]{1,0:T(8,128)S(1)} %copy-done.29, f32[512,256]{1,0:T(8,128)} %collective-permute-done.4.refs_1_), custom_call_target="tpu_custom_call" | custom-call | flops 402653184 | bytes 1572864 | tf_op jit(solution)/shard_map/dft/pallas_call | solution.py:127
  66.2 0.0 copy-start.9
  66.2 0.0 copy-start.14
  66.2 0.0 copy-start.30
  66.2 3.2 %early.1.acc_ref = f32[4,1024,256]{2,1,0:T(8,128)S(1)} custom-call(s32[1]{0:T(128)} %bitcast.pos_ref, f32[7,1024,256]{2,1,0:T(8,128)S(1)} %copy-done.2, f32[7,1024,256]{2,1,0:T(8,128)S(1)} %copy-done.2, f32[7,1024,256]{2,1,0:T(8,128)S(1)} %copy-done.2, f32[7,1024,256]{2,1,0:T(8,128)S(1)} %copy-done.2, f32[1024,256]{1,0:T(8,128)S(1)} %copy-done.18, ...), custom_call_target="tpu_custom_call" | custom-call | flops 26214400 | bytes 15728640 | tf_op jit(solution)/shard_map/early/pallas_call | solution.py:350
  69.4 1.8 %dft.15.three_g = f32[1024,256]{1,0:T(8,128)S(1)} custom-call(bf16[2,4,256,256]{3,2,1,0:T(8,128)(2,1)S(1)} %copy-done.3, f32[512,256]{1,0:T(8,128)} %collective-permute-done.8.refs_0_), custom_call_target="tpu_custom_call" | custom-call | flops 402653184 | bytes 1572864 | tf_op jit(solution)/shard_map/dft/pallas_call | solution.py:127
  71.3 0.0 copy-start.23
  71.3 5.7 %late.1 = (f32[512,256]{1,0:T(8,128)}, f32[1024,256]{1,0:T(8,128)}, f32[512,256]{1,0:T(8,128)S(1)}) custom-call(s32[1]{0:T(128)} %bitcast.pos_ref, bf16[2,4,256,256]{3,2,1,0:T(8,128)(2,1)S(1)} %copy-done.14, f32[4,1024,256]{2,1,0:T(8,128)S(1)} %early.1.acc_ref, f32[7,1024,256]{2,1,0:T(8,128)S(1)} %copy-done.2, f32[1024,256]{1,0:T(8,128)S(1)} %dft.15.three_g, ...), custom_call_target="tpu_custom_call" | custom-call | flops 1610612736 | bytes 13107200 | tf_op jit(solution)/shard_map/late/pallas_call | solution.py:447
  77.0 1.8 %finish.1 = (f32[512,256]{1,0:T(8,128)}, f32[512,256]{1,0:T(8,128)}, f32[1,256]{1,0:T(1,128)}) custom-call(s32[1]{0:T(128)} %bitcast.pos_ref, f32[512,256]{1,0:T(8,128)S(1)} %get-tuple-element.57.back_ref, f32[512,256]{1,0:T(8,128)S(1)} %copy-done.23, f32[512,256]{1,0:T(8,128)S(1)} %copy-done.24, f32[528,256]{1,0:T(8,128)S(1)} %collective-permute-done.10.partial_ref, ...), custom_call_target="tpu_custom_call" | custom-call | flops 393216 | bytes 3145728 | tf_op jit(solution)/shard_map/finish/pallas_call | solution.py:505
  (51 shorter events, 0.1 us)
Async XLA Ops:
  0.6 19.6 %copy-start.3 = (bf16[2,4,256,256]{3,2,1,0:T(8,128)(2,1)S(1)}, bf16[2,4,256,256]{3,2,1,0:T(8,128)(2,1)}, u32[]{:S(2)}) copy-start(bf16[2,4,256,256]{3,2,1,0:T(8,128)(2,1)} %constant.9.clone.table_ref) | copy-start | bytes 3145732
  0.6 30.9 %copy-start.12 = (f32[4096,256]{1,0:T(8,128)S(1)}, f32[4096,256]{1,0:T(8,128)}, u32[]{:S(2)}) copy-start(f32[4096,256]{1,0:T(8,128)} %x_ref) | copy-start | bytes 12582916
  2.1 35.4 %copy-start.8 = (f32[512,256]{1,0:T(8,128)}, f32[512,256]{1,0:T(8,128)S(1)}, u32[]{:S(2)}) copy-start(f32[512,256]{1,0:T(8,128)S(1)} %mul.3.refs_0_.gated_ref.rest_1_) | copy-start | bytes 1572868
  2.1 16.8 %collective-permute-start.2 = (f32[512,256]{1,0:T(8,128)S(1)}, f32[512,256]{1,0:T(8,128)S(1)}, u32[]{:S(2)}, u32[]{:S(2)}) collective-permute-start(f32[512,256]{1,0:T(8,128)S(1)} %mul.3.refs_0_.gated_ref.rest_1_), channel_id=1, source_target_pairs={{4,8},{8,4},{5,9},{9,5},{6,10},{10,6},{7,11},{11,7},{20,24},{24,20... | collective-permute-start | bytes 1572872 | tf_op jit(solution)/shard_map/ppermute | solution.py:521
  5.7 16.9 %collective-permute-start.1 = (f32[512,256]{1,0:T(8,128)S(1)}, f32[512,256]{1,0:T(8,128)S(1)}, u32[]{:S(2)}, u32[]{:S(2)}) collective-permute-start(f32[512,256]{1,0:T(8,128)S(1)} %mul.3.refs_0_.gated_ref.rest_1_), channel_id=1, source_target_pairs={{4,0},{8,12},{5,1},{9,13},{6,2},{10,14},{7,3},{11,15},{20,16},{24,... | collective-permute-start | bytes 1572872 | tf_op jit(solution)/shard_map/ppermute | solution.py:521
  7.0 16.3 %collective-permute-start = (f32[512,256]{1,0:T(8,128)S(1)}, f32[512,256]{1,0:T(8,128)S(1)}, u32[]{:S(2)}, u32[]{:S(2)}) collective-permute-start(f32[512,256]{1,0:T(8,128)S(1)} %mul.3.refs_0_.gated_ref.rest_1_), channel_id=1, source_target_pairs={{0,4},{12,8},{1,5},{13,9},{2,6},{14,10},{3,7},{15,11},{16,20},{28,... | collective-permute-start | bytes 1572872 | tf_op jit(solution)/shard_map/ppermute | solution.py:521
  8.3 1.0 %copy-start.25 = (f32[512,256]{1,0:T(8,128)S(1)}, f32[512,256]{1,0:T(8,128)}, u32[]{:S(2)}) copy-start(f32[512,256]{1,0:T(8,128)} %rest_4_.1) | copy-start | bytes 1572868
  9.4 1.0 %copy-start.27 = (f32[512,256]{1,0:T(8,128)S(1)}, f32[512,256]{1,0:T(8,128)}, u32[]{:S(2)}) copy-start(f32[512,256]{1,0:T(8,128)} %query_ref.1) | copy-start | bytes 1572868
  10.5 27.0 %copy-start.6 = (f32[520,256]{1,0:T(8,128)}, f32[520,256]{1,0:T(8,128)S(1)}, u32[]{:S(2)}) copy-start(f32[520,256]{1,0:T(8,128)S(1)} %mix.1.refs_0_.rest_2_.own_strip) | copy-start | bytes 1597444
  10.5 30.9 %collective-permute-start.7 = (f32[520,256]{1,0:T(8,128)S(1)}, f32[520,256]{1,0:T(8,128)S(1)}, u32[]{:S(2)}, u32[]{:S(2)}) collective-permute-start(f32[520,256]{1,0:T(8,128)S(1)} %mix.1.refs_0_.rest_2_.own_strip), channel_id=1, source_target_pairs={{4,8},{8,4},{5,9},{9,5},{6,10},{10,6},{7,11},{11,7},{20,24},{24,20... | collective-permute-start | bytes 1597448 | tf_op jit(solution)/shard_map/ppermute | solution.py:521
  13.4 28.0 %collective-permute-start.6 = (f32[520,256]{1,0:T(8,128)S(1)}, f32[520,256]{1,0:T(8,128)S(1)}, u32[]{:S(2)}, u32[]{:S(2)}) collective-permute-start(f32[520,256]{1,0:T(8,128)S(1)} %mix.1.refs_0_.rest_2_.own_strip), channel_id=1, source_target_pairs={{4,0},{8,12},{5,1},{9,13},{6,2},{10,14},{7,3},{11,15},{20,16},{24,... | collective-permute-start | bytes 1597448 | tf_op jit(solution)/shard_map/ppermute | solution.py:521
  18.9 22.5 %collective-permute-start.5 = (f32[520,256]{1,0:T(8,128)S(1)}, f32[520,256]{1,0:T(8,128)}, u32[]{:S(2)}, u32[]{:S(2)}) collective-permute-start(f32[520,256]{1,0:T(8,128)S(1)} %mix.1.refs_0_.rest_2_.own_strip), channel_id=1, source_target_pairs={{0,4},{12,8},{1,5},{13,9},{2,6},{14,10},{3,7},{15,11},{16,20},{28,... | collective-permute-start | bytes 1597448 | tf_op jit(solution)/shard_map/ppermute | solution.py:521
  21.7 1.0 %copy-start.17 = (f32[1024,256]{1,0:T(8,128)}, f32[1024,256]{1,0:T(8,128)S(1)}, u32[]{:S(2)}) copy-start(f32[1024,256]{1,0:T(8,128)S(1)} %dft.8.own_g) | copy-start | bytes 3145732
  23.4 23.2 %collective-permute-start.3 = (f32[512,256]{1,0:T(8,128)S(1)}, f32[512,256]{1,0:T(8,128)S(1)}, u32[]{:S(2)}, u32[]{:S(2)}) collective-permute-start(f32[512,256]{1,0:T(8,128)S(1)} %collective-permute-done.2.refs_1_), channel_id=1, source_target_pairs={{4,0},{8,12},{5,1},{9,13},{6,2},{10,14},{7,3},{11,15},{20,16},{24,... | collective-permute-start | bytes 1572872 | tf_op jit(solution)/shard_map/ppermute | solution.py:521
  28.0 19.4 %collective-permute-start.4 = (f32[512,256]{1,0:T(8,128)S(1)}, f32[512,256]{1,0:T(8,128)}, u32[]{:S(2)}, u32[]{:S(2)}) collective-permute-start(f32[512,256]{1,0:T(8,128)S(1)} %collective-permute-done.refs_0_), channel_id=1, source_target_pairs={{4,8},{8,4},{5,9},{9,5},{6,10},{10,6},{7,11},{11,7},{20,24},{24,20... | collective-permute-start | bytes 1572872 | tf_op jit(solution)/shard_map/ppermute | solution.py:521
  37.5 8.1 %copy-start = (f32[7,1024,256]{2,1,0:T(8,128)}, f32[7,1024,256]{2,1,0:T(8,128)S(1)}, u32[]{:S(2)}) copy-start(f32[7,1024,256]{2,1,0:T(8,128)S(1)} %taps.1.win_near.win_far.win_own.win_outer.win_next.win_two.win_ref) | copy-start | bytes 22020100
  38.2 1.5 %copy-start.19 = (f32[1024,256]{1,0:T(8,128)}, f32[1024,256]{1,0:T(8,128)S(1)}, u32[]{:S(2)}) copy-start(f32[1024,256]{1,0:T(8,128)S(1)} %dft.10.outer_g) | copy-start | bytes 3145732
  40.4 1.0 %copy-start.15 = (f32[1024,256]{1,0:T(8,128)}, f32[1024,256]{1,0:T(8,128)S(1)}, u32[]{:S(2)}) copy-start(f32[1024,256]{1,0:T(8,128)S(1)} %dft.11.next_g) | copy-start | bytes 3145732
  41.4 5.2 %copy-start.10 = (f32[520,256]{1,0:T(8,128)}, f32[520,256]{1,0:T(8,128)S(1)}, u32[]{:S(2)}) copy-start(f32[520,256]{1,0:T(8,128)S(1)} %collective-permute-done.7.refs_1_.next_strip.across_strip) | copy-start | bytes 1597444
  41.4 5.9 %copy-start.21 = (f32[520,256]{1,0:T(8,128)}, f32[520,256]{1,0:T(8,128)S(1)}, u32[]{:S(2)}) copy-start(f32[520,256]{1,0:T(8,128)S(1)} %collective-permute-done.6.refs_0_.out_strip) | copy-start | bytes 1597444
  41.5 13.2 %collective-permute-start.9 = (f32[520,256]{1,0:T(8,128)}, f32[520,256]{1,0:T(8,128)}, u32[]{:S(2)}, u32[]{:S(2)}) collective-permute-start(f32[520,256]{1,0:T(8,128)} %collective-permute-done.5.refs_0_.outer_strip), channel_id=1, source_target_pairs={{4,8},{8,4},{5,9},{9,5},{6,10},{10,6},{7,11},{11,7},{20,24},{24,20... | collective-permute-start | bytes 1597448 | tf_op jit(solution)/shard_map/ppermute | solution.py:521
  45.6 1.0 %copy-start.4 = (f32[1024,256]{1,0:T(8,128)}, f32[1024,256]{1,0:T(8,128)S(1)}, u32[]{:S(2)}) copy-start(f32[1024,256]{1,0:T(8,128)S(1)} %dft.12.outer_m) | copy-start | bytes 3145732
  46.6 0.8 %copy-start.28 = (f32[512,256]{1,0:T(8,128)}, f32[512,256]{1,0:T(8,128)S(1)}, u32[]{:S(2)}) copy-start(f32[512,256]{1,0:T(8,128)S(1)} %collective-permute-done.3.refs_0_) | copy-start | bytes 1572868
  47.4 22.1 %collective-permute-start.8 = (f32[512,256]{1,0:T(8,128)}, f32[512,256]{1,0:T(8,128)}, u32[]{:S(2)}, u32[]{:S(2)}) collective-permute-start(f32[512,256]{1,0:T(8,128)} %collective-permute-done.4.refs_1_), channel_id=1, source_target_pairs={{4,0},{8,12},{5,1},{9,13},{6,2},{10,14},{7,3},{11,15},{20,16},{24,... | collective-permute-start | bytes 1572872 | tf_op jit(solution)/shard_map/ppermute | solution.py:521
  54.7 3.1 %copy-start.1 = (f32[7,1024,256]{2,1,0:T(8,128)S(1)}, f32[7,1024,256]{2,1,0:T(8,128)}, u32[]{:S(2)}) copy-start(f32[7,1024,256]{2,1,0:T(8,128)} %copy-done) | copy-start | bytes 22020100
  57.7 1.0 %copy-start.11 = (f32[520,256]{1,0:T(8,128)S(1)}, f32[520,256]{1,0:T(8,128)}, u32[]{:S(2)}) copy-start(f32[520,256]{1,0:T(8,128)} %copy-done.10) | copy-start | bytes 1597444
  58.8 1.2 %copy-start.13 = (bf16[2,4,256,256]{3,2,1,0:T(8,128)(2,1)S(1)}, bf16[2,4,256,256]{3,2,1,0:T(8,128)(2,1)}, u32[]{:S(2)}) copy-start(bf16[2,4,256,256]{3,2,1,0:T(8,128)(2,1)} %constant.10.clone.inverse_ref) | copy-start | bytes 3145732
  60.0 4.3 %copy-start.29 = (f32[512,256]{1,0:T(8,128)S(1)}, f32[512,256]{1,0:T(8,128)}, u32[]{:S(2)}) copy-start(f32[512,256]{1,0:T(8,128)} %copy-done.28) | copy-start | bytes 1572868
  60.0 6.1 %copy-start.2 = (f32[7,1024,256]{2,1,0:T(8,128)S(1)}, f32[7,1024,256]{2,1,0:T(8,128)}, u32[]{:S(2)}) copy-start(f32[7,1024,256]{2,1,0:T(8,128)} %copy-done) | copy-start | bytes 22020100
  60.0 6.1 %copy-start.5 = (f32[1024,256]{1,0:T(8,128)S(1)}, f32[1024,256]{1,0:T(8,128)}, u32[]{:S(2)}) copy-start(f32[1024,256]{1,0:T(8,128)} %copy-done.4) | copy-start | bytes 3145732
  60.0 6.1 %copy-start.16 = (f32[1024,256]{1,0:T(8,128)S(1)}, f32[1024,256]{1,0:T(8,128)}, u32[]{:S(2)}) copy-start(f32[1024,256]{1,0:T(8,128)} %copy-done.15) | copy-start | bytes 3145732
  60.0 6.1 %copy-start.18 = (f32[1024,256]{1,0:T(8,128)S(1)}, f32[1024,256]{1,0:T(8,128)}, u32[]{:S(2)}) copy-start(f32[1024,256]{1,0:T(8,128)} %copy-done.17) | copy-start | bytes 3145732
  60.0 6.1 %copy-start.20 = (f32[1024,256]{1,0:T(8,128)S(1)}, f32[1024,256]{1,0:T(8,128)}, u32[]{:S(2)}) copy-start(f32[1024,256]{1,0:T(8,128)} %copy-done.19) | copy-start | bytes 3145732
  62.8 14.2 %collective-permute-start.10 = (f32[528,256]{1,0:T(8,128)S(1)}, f32[528,256]{1,0:T(8,128)S(1)}, u32[]{:S(2)}, u32[]{:S(2)}) collective-permute-start(f32[528,256]{1,0:T(8,128)S(1)} %get-tuple-element.58), channel_id=1, source_target_pairs={{4,0},{8,12},{5,1},{9,13},{6,2},{10,14},{7,3},{11,15},{20,16},{24,... | collective-permute-start | bytes 1622024 | tf_op jit(solution)/shard_map/ppermute | solution.py:521
  66.1 5.1 %copy-start.7 = (f32[520,256]{1,0:T(8,128)S(1)}, f32[520,256]{1,0:T(8,128)}, u32[]{:S(2)}) copy-start(f32[520,256]{1,0:T(8,128)} %copy-done.6) | copy-start | bytes 1597444
  66.2 5.1 %copy-start.9 = (f32[512,256]{1,0:T(8,128)S(1)}, f32[512,256]{1,0:T(8,128)}, u32[]{:S(2)}) copy-start(f32[512,256]{1,0:T(8,128)} %copy-done.8) | copy-start | bytes 1572868
  66.2 5.1 %copy-start.14 = (bf16[2,4,256,256]{3,2,1,0:T(8,128)(2,1)S(1)}, bf16[2,4,256,256]{3,2,1,0:T(8,128)(2,1)}, u32[]{:S(2)}) copy-start(bf16[2,4,256,256]{3,2,1,0:T(8,128)(2,1)} %constant.10.clone.inverse_ref) | copy-start | bytes 3145732
  66.2 5.1 %copy-start.26 = (f32[512,256]{1,0:T(8,128)S(1)}, f32[512,256]{1,0:T(8,128)}, u32[]{:S(2)}) copy-start(f32[512,256]{1,0:T(8,128)} %rest_4_.1) | copy-start | bytes 1572868
  66.2 5.1 %copy-start.30 = (f32[256]{0:T(256)S(1)}, f32[256]{0:T(256)}, u32[]{:S(2)}) copy-start(f32[256]{0:T(256)} %param.12) | copy-start | bytes 3076
  71.3 5.8 %copy-start.22 = (f32[520,256]{1,0:T(8,128)S(1)}, f32[520,256]{1,0:T(8,128)}, u32[]{:S(2)}) copy-start(f32[520,256]{1,0:T(8,128)} %copy-done.21) | copy-start | bytes 1597444
  71.3 5.8 %copy-start.23 = (f32[512,256]{1,0:T(8,128)S(1)}, f32[512,256]{1,0:T(8,128)}, u32[]{:S(2)}) copy-start(f32[512,256]{1,0:T(8,128)} %key_ref.1) | copy-start | bytes 1572868
  71.3 5.8 %copy-start.24 = (f32[512,256]{1,0:T(8,128)S(1)}, f32[512,256]{1,0:T(8,128)}, u32[]{:S(2)}) copy-start(f32[512,256]{1,0:T(8,128)} %values_ref.1) | copy-start | bytes 1572868

commit v7 on v6

--- a/solution.py
+++ b/solution.py
@@ -109,31 +109,37 @@
     return pl.BlockSpec((8, width), lambda *_: (seg // 8, 0))
 
 
-def dft_kernel(table_ref, *refs):
+def dft_kernel(choose, pos_ref, table_ref, *refs):
     *x_refs, out_ref = refs
     rows = out_ref.shape[0] // 4
+    inner = jnp.logical_or(pos_ref[0] == 1, pos_ref[0] == 2)
 
     def store(group, value):
         out_ref[group * rows : (group + 1) * rows, :] = value
 
     x = x_refs[0][...]
-    for ref in x_refs[1:]:
-        x = x + ref[...]
+    if choose:
+        x = jnp.where(inner, x, x_refs[1][...] if len(x_refs) == 2 else 0.0)
+    elif len(x_refs) == 2:
+        x = x + x_refs[1][...]
     transform(x, table_ref, store)
 
 
-def dft(table, seg, *xs):
+def dft(pos, table, seg, *xs, choose=False):
     width = xs[0].shape[1]
     return pl.pallas_call(
-        dft_kernel,
-        grid=(1,),
-        in_specs=[whole_spec(table.shape)] + [whole_spec((seg, x.shape[1])) for x in xs],
-        out_specs=whole_spec((2 * seg, width)),
+        functools.partial(dft_kernel, choose),
+        grid_spec=pltpu.PrefetchScalarGridSpec(
+            num_scalar_prefetch=1,
+            grid=(1,),
+            in_specs=[whole_spec(table.shape)] + [whole_spec((seg, width))] * len(xs),
+            out_specs=whole_spec((2 * seg, width)),
+        ),
         out_shape=f32(2 * seg, width),
         compiler_params=params(12),
         cost_estimate=cost(3 * seg * seg * width * 2, 12 * seg * width),
         name="dft",
-    )(table, *xs)
+    )(pos, table, *xs)
 
 
 def taps_kernel(table_ref, x_ref, out_ref, last_ref):
@@ -474,7 +480,7 @@
 
 
 def finish_kernel(
-    pos_ref, back_ref, key_ref, values_ref, partial_ref, own_strip, outer_strip, out_strip, across_strip, two_strip,
+    pos_ref, back_ref, key_ref, values_ref, partial_ref, own_strip, beside_strip, across_strip, two_strip,
     key_out, value_out, skip_out,
 ):
     pos = pos_ref[0]
@@ -485,8 +491,8 @@
     far = jnp.where(pos < 2, pos + 2, pos - 2)
     strips = (
         (own_strip[...], pos),
-        (outer_strip[...], jnp.where(pos < 2, 0, 3)),
-        (out_strip[...] + across_strip[...], jnp.where(pos < 2, pos + 1, pos - 1)),
+        (beside_strip[...], jnp.where(pos % 2 == 0, pos + 1, pos - 1)),
+        (across_strip[...], 3 - pos),
         (two_strip[...] + partial_ref[seg : seg + 8, :], far),
         (partial_ref[seg + 8 :, :], 3 - pos),
     )
@@ -529,8 +535,8 @@
     return send(x, (1, 0), (2, 3))
 
 
-def inward(x):
-    return send(x, (0, 1), (3, 2))
+def beside(x):
+    return send(x, (0, 1), (1, 0), (2, 3), (3, 2))
 
 
 def local_line(query_gate, key_gate, values, filter_taps, skip_gain, upstream):
@@ -541,38 +547,38 @@
     after = lax.optimization_barrier
 
     gated = key_gate * values
-    outer = inward(gated)
-    next_g = (outward(gated), across(gated))
+    side, over = beside(gated), across(gated)
     mixed = mix(gated, upstream, query_gate)
-    outer_x = inward(mixed)
-    next_x = (outward(mixed), across(mixed))
-    own_g, own_m = dft(table, seg, gated), dft(table, seg, mixed)
-    outer, *next_g, filter_taps, own_g, own_m = after((outer, *next_g, filter_taps, own_g, own_m))
-
-    two = outward(next_g[1]), across(outer)
-    outer_g, next_g = dft(table, seg, outer), dft(table, seg, *next_g)
+    side_x, over_x = beside(mixed), across(mixed)
+    own_g, own_m = dft(pos, table, seg, gated), dft(pos, table, seg, mixed)
+    side, over, filter_taps, own_g, own_m = after((side, over, filter_taps, own_g, own_m))
+
+    two = across(side), outward(over)
+    outer_g = dft(pos, table, seg, side, choose=True)
+    next_g = dft(pos, table, seg, over, side, choose=True)
     windows = taps_spectra(table, filter_taps, seg)
-    outer_x, *next_x, windows, outer_g, next_g = after((outer_x, *next_x, windows, outer_g, next_g))
-
-    two_x = across(outer_x)
-    outer_m, next_m = dft(table, seg, outer_x), dft(table, seg, *next_x)
+    side_x, over_x, windows, outer_g, next_g = after((side_x, over_x, windows, outer_g, next_g))
+
+    two_x = across(side_x)
+    outer_m = dft(pos, table, seg, side_x, choose=True)
+    next_m = dft(pos, table, seg, over_x, side_x, choose=True)
     *two, outer_m, next_m = after((*two, outer_m, next_m))
 
-    three = outward(two[1])
-    two_m, partial = back_partial(pos, table, inverse, windows, next_m, next_x[1], two_x, seg)
+    three = outward(two[0])
+    two_m, partial = back_partial(pos, table, inverse, windows, next_m, over_x, two_x, seg)
     *two, partial = after((*two, partial))
     partial = outward(partial)
-    two_g = dft(table, seg, *two)
+    two_g = dft(pos, table, seg, *two)
     acc = early(pos, windows, (own_g, outer_g, next_g, two_g), (own_m, outer_m, next_m), seg)
     three, acc = after((three, acc))
 
-    three_g = dft(table, seg, three)
+    three_g = dft(pos, table, seg, three)
     query_grad, filter_grad, back = late(
         pos, inverse, acc, windows, three_g, two_g, own_m, outer_m, next_m, two_m,
         gated, mixed, skip_gain[None, :], upstream,
     )
     key_grad, value_grad, skip_grad = finish(
-        pos, back, key_gate, values, partial, mixed, outer_x, *next_x, two_x
+        pos, back, key_gate, values, partial, mixed, side_x, over_x, two_x
     )
     return (query_grad, key_grad, value_grad, filter_grad, skip_grad[0])
 

time: 79.5 us -> 70.7 us (0.89)
  the two profiles are of different devices: /device:TPU:10 before, /device:TPU:0 now
where the time goes in v7:
time: 70.7 us; the launch traced here: 70.3 us
  waiting for transfers between devices  25.9 us (37%)
  Pallas kernels  25.1 us (36%)
  starting transfers between devices  14.9 us (21%)
  local copies, waits for them, and re-layouts  2.12 us (3%)
  other arithmetic  1.36 us (2%)
  between operations  0.89 us (1%)
    ppermute x9, waiting for transfers between devices, send(): return lax.ppermute(x, 'ctx', list(pairs))  25.9 us
    ppermute x9, starting transfers between devices, send(): return lax.ppermute(x, 'ctx', list(pairs))  14.9 us
    pallas_call x8, Pallas kernels, dft(): pl.pallas_call(functools.partial(dft_kernel, choose), grid_spec=pltpu.Pre...  8.07 us
    pallas_call x1, Pallas kernels, late(): pl.pallas_call(late_kernel, grid_spec=pltpu.PrefetchScalarGridSpec(num_sc...  6.02 us
    pallas_call x1, Pallas kernels, taps_spectra(): pl.pallas_call(taps_kernel, grid=(blocks,), in_specs=[whole_spec(table.sh...  5.95 us
    pallas_call x1, Pallas kernels, early(): pl.pallas_call(early_kernel, grid_spec=pltpu.PrefetchScalarGridSpec(num_s...  2.23 us
    unnamed x18, local copies, waits for them, and re-layouts  2.12 us
    pallas_call x1, Pallas kernels, back_partial(): pl.pallas_call(partial_kernel, grid_spec=pltpu.PrefetchScalarGridSpec(num...  1.59 us
  transfers between devices with their start and end apart: 9, of which 4 were waited for; matrix products, arithmetic and copies ran while one was open for 0% of the time, Pallas kernels for 34%

profile of v7, /device:TPU:0, one launch (start us, length us, event | category | flops | bytes accessed | tf_op | source)
XLA Modules:
  0.0 70.3 jit_solution(5398671454589087224)
XLA Ops:
  0.6 0.0 copy-start
  0.6 1.4 %mul.3.refs_0_.gated_ref.rest_1_ = f32[512,256]{1,0:T(8,128)S(1)} multiply(f32[512,256]{1,0:T(8,128)} %key_ref.1, f32[512,256]{1,0:T(8,128)} %values_ref.1) | non-fusion elementwise | flops 131072 | bytes 1572864 | tf_op jit(solution)/shard_map/mul | solution.py:549
  2.0 1.5 %collective-permute-start.1 = (f32[512,256]{1,0:T(8,128)S(1)}, f32[512,256]{1,0:T(8,128)}, u32[]{:S(2)}, u32[]{:S(2)}) collective-permute-start(f32[512,256]{1,0:T(8,128)S(1)} %mul.3.refs_0_.gated_ref.rest_1_), channel_id=1, source_target_pairs={{4,8},{8,4},{5,9},{9,5},{6,10},{10,6},{7,11},{11,7},{20,24},{24,20... | collective-permute-start | bytes 1572872 | tf_op jit(solution)/shard_map/ppermute | solution.py:527
  3.5 5.1 %collective-permute-start = (f32[512,256]{1,0:T(8,128)S(1)}, f32[512,256]{1,0:T(8,128)}, u32[]{:S(2)}, u32[]{:S(2)}) collective-permute-start(f32[512,256]{1,0:T(8,128)S(1)} %mul.3.refs_0_.gated_ref.rest_1_), channel_id=1, source_target_pairs={{0,4},{4,0},{8,12},{12,8},{1,5},{5,1},{9,13},{13,9},{2,6},{6,2},{1... | collective-permute-start | bytes 1572872 | tf_op jit(solution)/shard_map/ppermute | solution.py:527
  8.6 1.0 %copy-done.5 = f32[512,256]{1,0:T(8,128)S(1)} copy-done((f32[512,256]{1,0:T(8,128)S(1)}, f32[512,256]{1,0:T(8,128)}, u32[]{:S(2)}) %copy-start.5) | copy-done | bytes 524312
  9.6 1.0 %copy-done.7 = f32[512,256]{1,0:T(8,128)S(1)} copy-done((f32[512,256]{1,0:T(8,128)S(1)}, f32[512,256]{1,0:T(8,128)}, u32[]{:S(2)}) %copy-start.7) | copy-done | bytes 524312
  10.7 0.1 mix.1.refs_0_.rest_2_.own_strip
  10.8 0.7 collective-permute-start.5
  11.5 2.3 %collective-permute-start.4 = (f32[520,256]{1,0:T(8,128)S(1)}, f32[520,256]{1,0:T(8,128)S(1)}, u32[]{:S(2)}, u32[]{:S(2)}) collective-permute-start(f32[520,256]{1,0:T(8,128)S(1)} %mix.1.refs_0_.rest_2_.own_strip), channel_id=1, source_target_pairs={{0,4},{4,0},{8,12},{12,8},{1,5},{5,1},{9,13},{13,9},{2,6},{6,2},{1... | collective-permute-start | bytes 1597448 | tf_op jit(solution)/shard_map/ppermute | solution.py:527
  13.8 0.0 copy-done
  13.8 0.7 %dft.9.own_m = f32[1024,256]{1,0:T(8,128)S(1)} custom-call(s32[1]{0:T(128)} %bitcast.pos_ref, bf16[2,4,256,256]{3,2,1,0:T(8,128)(2,1)S(1)} %copy-done, f32[520,256]{1,0:T(8,128)S(1)} %mix.1.refs_0_.rest_2_.own_strip), custom_call_target="tpu_custom_call" | custom-call | flops 402653184 | bytes 1572864 | tf_op jit(solution)/shard_map/dft/pallas_call | solution.py:130
  14.6 0.7 %dft.8.own_g = f32[1024,256]{1,0:T(8,128)S(1)} custom-call(s32[1]{0:T(128)} %bitcast.pos_ref, bf16[2,4,256,256]{3,2,1,0:T(8,128)(2,1)S(1)} %copy-done, f32[512,256]{1,0:T(8,128)S(1)} %mul.3.refs_0_.gated_ref.rest_1_), custom_call_target="tpu_custom_call" | custom-call | flops 402653184 | bytes 1572864 | tf_op jit(solution)/shard_map/dft/pallas_call | solution.py:130
  15.3 0.0 collective-permute-done.1.refs_0_
  15.3 6.2 %collective-permute-done.refs_0_.refs_1_ = f32[512,256]{1,0:T(8,128)} collective-permute-done((f32[512,256]{1,0:T(8,128)S(1)}, f32[512,256]{1,0:T(8,128)}, u32[]{:S(2)}, u32[]{:S(2)}) %collective-permute-start) | collective-permute-done | bytes 524320 | tf_op jit(solution)/shard_map/ppermute | solution.py:527
  21.5 1.3 %collective-permute-start.3 = (f32[512,256]{1,0:T(8,128)}, f32[512,256]{1,0:T(8,128)S(1)}, u32[]{:S(2)}, u32[]{:S(2)}) collective-permute-start(f32[512,256]{1,0:T(8,128)} %collective-permute-done.1.refs_0_), channel_id=1, source_target_pairs={{4,0},{8,12},{5,1},{9,13},{6,2},{10,14},{7,3},{11,15},{20,16},{24,... | collective-permute-start | bytes 1572872 | tf_op jit(solution)/shard_map/ppermute | solution.py:527
  22.8 0.7 collective-permute-start.2
  23.5 0.0 copy-done.1
  23.5 6.0 %taps.1.win_near.win_far.win_own.win_outer.win_next.win_two.win_ref = f32[7,1024,256]{2,1,0:T(8,128)S(1)} custom-call(bf16[2,4,256,256]{3,2,1,0:T(8,128)(2,1)S(1)} %copy-done, f32[4096,256]{1,0:T(8,128)S(1)} %copy-done.1), custom_call_target="tpu_custom_call" | custom-call | flops 3221225472 | bytes 12582912 | tf_op jit(solution)/shard_map/taps/pallas_call | solution.py:168
  29.4 1.9 %dft.11.next_g = f32[1024,256]{1,0:T(8,128)S(1)} custom-call(s32[1]{0:T(128)} %bitcast.pos_ref, bf16[2,4,256,256]{3,2,1,0:T(8,128)(2,1)S(1)} %copy-done, f32[512,256]{1,0:T(8,128)} %collective-permute-done.1.refs_0_, f32[512,256]{1,0:T(8,128)} %collective-permute-done.refs_0_.refs_1_), custom_call_target="tpu_custom_call" | custom-call | flops 402653184 | bytes 1572864 | tf_op jit(solution)/shard_map/dft/pallas_call | solution.py:130
  31.4 0.0 copy-start.2
  31.4 1.8 %dft.10.outer_g = f32[1024,256]{1,0:T(8,128)S(1)} custom-call(s32[1]{0:T(128)} %bitcast.pos_ref, bf16[2,4,256,256]{3,2,1,0:T(8,128)(2,1)S(1)} %copy-done, f32[512,256]{1,0:T(8,128)} %collective-permute-done.refs_0_.refs_1_), custom_call_target="tpu_custom_call" | custom-call | flops 402653184 | bytes 1572864 | tf_op jit(solution)/shard_map/dft/pallas_call | solution.py:130
  33.2 0.0 collective-permute-done.5.refs_0_.next_strip.across_strip
  33.2 0.0 collective-permute-done.4.refs_0_.refs_1_.beside_strip
  33.2 0.7 collective-permute-start.7
  33.9 0.7 %dft.12.outer_m = f32[1024,256]{1,0:T(8,128)S(1)} custom-call(s32[1]{0:T(128)} %bitcast.pos_ref, bf16[2,4,256,256]{3,2,1,0:T(8,128)(2,1)S(1)} %copy-done, f32[520,256]{1,0:T(8,128)S(1)} %collective-permute-done.4.refs_0_.refs_1_.beside_strip), custom_call_target="tpu_custom_call" | custom-call | flops 402653184 | bytes 1572864 | tf_op jit(solution)/shard_map/dft/pallas_call | solution.py:130
  34.7 0.7 %dft.13.next_ref.next_m = f32[1024,256]{1,0:T(8,128)S(1)} custom-call(s32[1]{0:T(128)} %bitcast.pos_ref, bf16[2,4,256,256]{3,2,1,0:T(8,128)(2,1)S(1)} %copy-done, f32[520,256]{1,0:T(8,128)S(1)} %collective-permute-done.5.refs_0_.next_strip.across_strip, f32[520,256]{1,0:T(8,128)S(1)} %collective-permute-done.4.refs_0_.refs_1_.beside_strip), custom_call_target="tpu_custom_call" | custom-call | flops 402653184 | bytes 1572864 | tf_op jit(solution)/shard_map/dft/pallas_call | solution.py:130
  35.4 7.5 %collective-permute-done.3.refs_1_ = f32[512,256]{1,0:T(8,128)S(1)} collective-permute-done((f32[512,256]{1,0:T(8,128)}, f32[512,256]{1,0:T(8,128)S(1)}, u32[]{:S(2)}, u32[]{:S(2)}) %collective-permute-start.3) | collective-permute-done | bytes 524320 | tf_op jit(solution)/shard_map/ppermute | solution.py:527
  42.9 0.0 collective-permute-done.2.refs_0_
  42.9 1.3 %collective-permute-start.6 = (f32[512,256]{1,0:T(8,128)S(1)}, f32[512,256]{1,0:T(8,128)S(1)}, u32[]{:S(2)}, u32[]{:S(2)}) collective-permute-start(f32[512,256]{1,0:T(8,128)S(1)} %collective-permute-done.2.refs_0_), channel_id=1, source_target_pairs={{4,0},{8,12},{5,1},{9,13},{6,2},{10,14},{7,3},{11,15},{20,16},{24,... | collective-permute-start | bytes 1572872 | tf_op jit(solution)/shard_map/ppermute | solution.py:527
  44.2 0.0 collective-permute-done.7.x_ref.far_strip.two_strip
  44.2 0.0 copy-done.2
  44.2 1.6 %partial.1 = (f32[1024,256]{1,0:T(8,128)S(1)}, f32[528,256]{1,0:T(8,128)S(1)}) custom-call(s32[1]{0:T(128)} %bitcast.pos_ref, bf16[2,4,256,256]{3,2,1,0:T(8,128)(2,1)S(1)} %copy-done, bf16[2,4,256,256]{3,2,1,0:T(8,128)(2,1)S(1)} %copy-done.2, f32[7,1024,256]{2,1,0:T(8,128)S(1)} %taps.1.win_near.win_far.win_own.win_outer.win_next.win_two.win_ref, ...), custom_call_target="tpu_custom_call" | custom-call | flops 805306368 | bytes 3145728 | tf_op jit(solution)/shard_map/partial/pallas_call | solution.py:226
  45.8 1.3 %collective-permute-start.8 = (f32[528,256]{1,0:T(8,128)S(1)}, f32[528,256]{1,0:T(8,128)S(1)}, u32[]{:S(2)}, u32[]{:S(2)}) collective-permute-start(f32[528,256]{1,0:T(8,128)S(1)} %get-tuple-element.54), channel_id=1, source_target_pairs={{4,0},{8,12},{5,1},{9,13},{6,2},{10,14},{7,3},{11,15},{20,16},{24,... | collective-permute-start | bytes 1622024 | tf_op jit(solution)/shard_map/ppermute | solution.py:527
  47.1 0.7 %dft.14.two_g = f32[1024,256]{1,0:T(8,128)S(1)} custom-call(s32[1]{0:T(128)} %bitcast.pos_ref, bf16[2,4,256,256]{3,2,1,0:T(8,128)(2,1)S(1)} %copy-done, f32[512,256]{1,0:T(8,128)S(1)} %collective-permute-done.2.refs_0_, f32[512,256]{1,0:T(8,128)S(1)} %collective-permute-done.3.refs_1_), custom_call_target="tpu_custom_call" | custom-call | flops 402653184 | bytes 1572864 | tf_op jit(solution)/shard_map/dft/pallas_call | solution.py:130
  47.8 0.0 copy-start.6
  47.8 0.0 copy-start.8
  47.8 2.2 %early.1.acc_ref = f32[4,1024,256]{2,1,0:T(8,128)S(1)} custom-call(s32[1]{0:T(128)} %bitcast.pos_ref, f32[7,1024,256]{2,1,0:T(8,128)S(1)} %taps.1.win_near.win_far.win_own.win_outer.win_next.win_two.win_ref, f32[7,1024,256]{2,1,0:T(8,128)S(1)} %taps.1.win_near.win_far.win_own.win_outer.win_next.win_two.win_ref, ...), custom_call_target="tpu_custom_call" | custom-call | flops 26214400 | bytes 15728640 | tf_op jit(solution)/shard_map/early/pallas_call | solution.py:356
  50.1 7.6 %collective-permute-done.6.refs_0_ = f32[512,256]{1,0:T(8,128)S(1)} collective-permute-done((f32[512,256]{1,0:T(8,128)S(1)}, f32[512,256]{1,0:T(8,128)S(1)}, u32[]{:S(2)}, u32[]{:S(2)}) %collective-permute-start.6) | collective-permute-done | bytes 524320 | tf_op jit(solution)/shard_map/ppermute | solution.py:527
  57.7 0.7 %dft.15.three_g = f32[1024,256]{1,0:T(8,128)S(1)} custom-call(s32[1]{0:T(128)} %bitcast.pos_ref, bf16[2,4,256,256]{3,2,1,0:T(8,128)(2,1)S(1)} %copy-done, f32[512,256]{1,0:T(8,128)S(1)} %collective-permute-done.6.refs_0_), custom_call_target="tpu_custom_call" | custom-call | flops 402653184 | bytes 1572864 | tf_op jit(solution)/shard_map/dft/pallas_call | solution.py:130
  58.4 0.0 copy-done.6
  58.4 0.0 copy-done.8
  58.5 0.0 copy-start.3
  58.5 0.0 copy-start.4
  58.5 6.0 %late.1 = (f32[512,256]{1,0:T(8,128)}, f32[1024,256]{1,0:T(8,128)}, f32[512,256]{1,0:T(8,128)S(1)}) custom-call(s32[1]{0:T(128)} %bitcast.pos_ref, bf16[2,4,256,256]{3,2,1,0:T(8,128)(2,1)S(1)} %copy-done.2, f32[4,1024,256]{2,1,0:T(8,128)S(1)} %early.1.acc_ref, f32[7,1024,256]{2,1,0:T(8,128)S(1)} %taps.1.win_near.win_far.win_own.win_outer.win_next.win_two.win_ref, ...), custom_call_target="tpu_custom_call" | custom-call | flops 1610612736 | bytes 13107200 | tf_op jit(solution)/shard_map/late/pallas_call | solution.py:453
  64.5 4.6 %collective-permute-done.8.partial_ref = f32[528,256]{1,0:T(8,128)S(1)} collective-permute-done((f32[528,256]{1,0:T(8,128)S(1)}, f32[528,256]{1,0:T(8,128)S(1)}, u32[]{:S(2)}, u32[]{:S(2)}) %collective-permute-start.8) | collective-permute-done | bytes 540704 | tf_op jit(solution)/shard_map/ppermute | solution.py:527
  69.1 0.0 copy-done.3
  69.1 0.0 copy-done.4
  69.1 1.1 %finish.1 = (f32[512,256]{1,0:T(8,128)}, f32[512,256]{1,0:T(8,128)}, f32[1,256]{1,0:T(1,128)}) custom-call(s32[1]{0:T(128)} %bitcast.pos_ref, f32[512,256]{1,0:T(8,128)S(1)} %get-tuple-element.53.back_ref, f32[512,256]{1,0:T(8,128)S(1)} %copy-done.3, f32[512,256]{1,0:T(8,128)S(1)} %copy-done.4, f32[528,256]{1,0:T(8,128)S(1)} %collective-permute-done.8.partial_ref, ...), custom_call_target="tpu_custom_call" | custom-call | flops 393216 | bytes 3145728 | tf_op jit(solution)/shard_map/finish/pallas_call | solution.py:511
  (3 shorter events, 0.0 us)
Async XLA Ops:
  0.6 13.2 %copy-start = (bf16[2,4,256,256]{3,2,1,0:T(8,128)(2,1)S(1)}, bf16[2,4,256,256]{3,2,1,0:T(8,128)(2,1)}, u32[]{:S(2)}) copy-start(bf16[2,4,256,256]{3,2,1,0:T(8,128)(2,1)} %constant.9.clone.table_ref) | copy-start | bytes 3145732
  2.0 13.3 %collective-permute-start.1 = (f32[512,256]{1,0:T(8,128)S(1)}, f32[512,256]{1,0:T(8,128)}, u32[]{:S(2)}, u32[]{:S(2)}) collective-permute-start(f32[512,256]{1,0:T(8,128)S(1)} %mul.3.refs_0_.gated_ref.rest_1_), channel_id=1, source_target_pairs={{4,8},{8,4},{5,9},{9,5},{6,10},{10,6},{7,11},{11,7},{20,24},{24,20... | collective-permute-start | bytes 1572872 | tf_op jit(solution)/shard_map/ppermute | solution.py:527
  3.5 18.0 %collective-permute-start = (f32[512,256]{1,0:T(8,128)S(1)}, f32[512,256]{1,0:T(8,128)}, u32[]{:S(2)}, u32[]{:S(2)}) collective-permute-start(f32[512,256]{1,0:T(8,128)S(1)} %mul.3.refs_0_.gated_ref.rest_1_), channel_id=1, source_target_pairs={{0,4},{4,0},{8,12},{12,8},{1,5},{5,1},{9,13},{13,9},{2,6},{6,2},{1... | collective-permute-start | bytes 1572872 | tf_op jit(solution)/shard_map/ppermute | solution.py:527
  8.6 1.0 %copy-start.5 = (f32[512,256]{1,0:T(8,128)S(1)}, f32[512,256]{1,0:T(8,128)}, u32[]{:S(2)}) copy-start(f32[512,256]{1,0:T(8,128)} %rest_4_.1) | copy-start | bytes 1572868
  9.6 1.0 %copy-start.7 = (f32[512,256]{1,0:T(8,128)S(1)}, f32[512,256]{1,0:T(8,128)}, u32[]{:S(2)}) copy-start(f32[512,256]{1,0:T(8,128)} %query_ref.1) | copy-start | bytes 1572868
  10.8 22.4 %collective-permute-start.5 = (f32[520,256]{1,0:T(8,128)S(1)}, f32[520,256]{1,0:T(8,128)S(1)}, u32[]{:S(2)}, u32[]{:S(2)}) collective-permute-start(f32[520,256]{1,0:T(8,128)S(1)} %mix.1.refs_0_.rest_2_.own_strip), channel_id=1, source_target_pairs={{4,8},{8,4},{5,9},{9,5},{6,10},{10,6},{7,11},{11,7},{20,24},{24,20... | collective-permute-start | bytes 1597448 | tf_op jit(solution)/shard_map/ppermute | solution.py:527
  11.5 21.7 %collective-permute-start.4 = (f32[520,256]{1,0:T(8,128)S(1)}, f32[520,256]{1,0:T(8,128)S(1)}, u32[]{:S(2)}, u32[]{:S(2)}) collective-permute-start(f32[520,256]{1,0:T(8,128)S(1)} %mix.1.refs_0_.rest_2_.own_strip), channel_id=1, source_target_pairs={{0,4},{4,0},{8,12},{12,8},{1,5},{5,1},{9,13},{13,9},{2,6},{6,2},{1... | collective-permute-start | bytes 1597448 | tf_op jit(solution)/shard_map/ppermute | solution.py:527
  13.8 9.6 %copy-start.1 = (f32[4096,256]{1,0:T(8,128)S(1)}, f32[4096,256]{1,0:T(8,128)}, u32[]{:S(2)}) copy-start(f32[4096,256]{1,0:T(8,128)} %x_ref) | copy-start | bytes 12582916
  21.5 21.4 %collective-permute-start.3 = (f32[512,256]{1,0:T(8,128)}, f32[512,256]{1,0:T(8,128)S(1)}, u32[]{:S(2)}, u32[]{:S(2)}) collective-permute-start(f32[512,256]{1,0:T(8,128)} %collective-permute-done.1.refs_0_), channel_id=1, source_target_pairs={{4,0},{8,12},{5,1},{9,13},{6,2},{10,14},{7,3},{11,15},{20,16},{24,... | collective-permute-start | bytes 1572872 | tf_op jit(solution)/shard_map/ppermute | solution.py:527
  22.8 20.1 %collective-permute-start.2 = (f32[512,256]{1,0:T(8,128)}, f32[512,256]{1,0:T(8,128)S(1)}, u32[]{:S(2)}, u32[]{:S(2)}) collective-permute-start(f32[512,256]{1,0:T(8,128)} %collective-permute-done.refs_0_.refs_1_), channel_id=1, source_target_pairs={{4,8},{8,4},{5,9},{9,5},{6,10},{10,6},{7,11},{11,7},{20,24},{24,20... | collective-permute-start | bytes 1572872 | tf_op jit(solution)/shard_map/ppermute | solution.py:527
  31.4 12.8 %copy-start.2 = (bf16[2,4,256,256]{3,2,1,0:T(8,128)(2,1)S(1)}, bf16[2,4,256,256]{3,2,1,0:T(8,128)(2,1)}, u32[]{:S(2)}) copy-start(bf16[2,4,256,256]{3,2,1,0:T(8,128)(2,1)} %constant.10.clone.inverse_ref) | copy-start | bytes 3145732
  33.2 10.9 %collective-permute-start.7 = (f32[520,256]{1,0:T(8,128)S(1)}, f32[520,256]{1,0:T(8,128)S(1)}, u32[]{:S(2)}, u32[]{:S(2)}) collective-permute-start(f32[520,256]{1,0:T(8,128)S(1)} %collective-permute-done.4.refs_0_.refs_1_.beside_strip), channel_id=1, source_target_pairs={{4,8},{8,4},{5,9},{9,5},{6,10},{10,6},{7,11},{11,7},{20,24},{24,20... | collective-permute-start | bytes 1597448 | tf_op jit(solution)/shard_map/ppermute | solution.py:527
  42.9 14.8 %collective-permute-start.6 = (f32[512,256]{1,0:T(8,128)S(1)}, f32[512,256]{1,0:T(8,128)S(1)}, u32[]{:S(2)}, u32[]{:S(2)}) collective-permute-start(f32[512,256]{1,0:T(8,128)S(1)} %collective-permute-done.2.refs_0_), channel_id=1, source_target_pairs={{4,0},{8,12},{5,1},{9,13},{6,2},{10,14},{7,3},{11,15},{20,16},{24,... | collective-permute-start | bytes 1572872 | tf_op jit(solution)/shard_map/ppermute | solution.py:527
  45.8 23.4 %collective-permute-start.8 = (f32[528,256]{1,0:T(8,128)S(1)}, f32[528,256]{1,0:T(8,128)S(1)}, u32[]{:S(2)}, u32[]{:S(2)}) collective-permute-start(f32[528,256]{1,0:T(8,128)S(1)} %get-tuple-element.54), channel_id=1, source_target_pairs={{4,0},{8,12},{5,1},{9,13},{6,2},{10,14},{7,3},{11,15},{20,16},{24,... | collective-permute-start | bytes 1622024 | tf_op jit(solution)/shard_map/ppermute | solution.py:527
  47.8 10.6 %copy-start.6 = (f32[512,256]{1,0:T(8,128)S(1)}, f32[512,256]{1,0:T(8,128)}, u32[]{:S(2)}) copy-start(f32[512,256]{1,0:T(8,128)} %rest_4_.1) | copy-start | bytes 1572868
  47.8 10.6 %copy-start.8 = (f32[256]{0:T(256)S(1)}, f32[256]{0:T(256)}, u32[]{:S(2)}) copy-start(f32[256]{0:T(256)} %param.12) | copy-start | bytes 3076
  58.5 10.7 %copy-start.3 = (f32[512,256]{1,0:T(8,128)S(1)}, f32[512,256]{1,0:T(8,128)}, u32[]{:S(2)}) copy-start(f32[512,256]{1,0:T(8,128)} %key_ref.1) | copy-start | bytes 1572868
  58.5 10.7 %copy-start.4 = (f32[512,256]{1,0:T(8,128)S(1)}, f32[512,256]{1,0:T(8,128)}, u32[]{:S(2)}) copy-start(f32[512,256]{1,0:T(8,128)} %values_ref.1) | copy-start | bytes 1572868

commit v8 on v7

--- a/solution.py
+++ b/solution.py
@@ -191,36 +191,33 @@
 
 
 def partial_kernel(
-    pos_ref, table_ref, inverse_ref, win_near, win_far, next_ref, x_ref, next_strip, far_strip, far_ref, out_ref, z_ref
+    pos_ref, inverse_ref, win_own, win_outer, own_ref, outer_ref, own_strip, outer_strip, out_ref, z_ref
 ):
-    rows = far_ref.shape[0] // 4
+    rows = own_ref.shape[0] // 4
     sub = rows // 2
-    for group, part in enumerate(spread(x_ref[...])):
+    for group in range(4):
         base = group * rows
-        far = dot3(table_ref, group, *split(part))
-        far_ref[base : base + rows, :] = far
         re, im = slice(base, base + sub), slice(base + sub, base + rows)
-        near = (next_ref[re, :], next_ref[im, :])
         total = add(
-            conj_mul((win_near[0, re, :], win_near[0, im, :]), near),
-            conj_mul((win_far[0, re, :], win_far[0, im, :]), (far[:sub], far[sub:])),
+            conj_mul((win_own[0, re, :], win_own[0, im, :]), (own_ref[re, :], own_ref[im, :])),
+            conj_mul((win_outer[0, re, :], win_outer[0, im, :]), (outer_ref[re, :], outer_ref[im, :])),
         )
         z_ref[group] = dot3(inverse_ref, group, *split(jnp.concatenate(total, axis=0)))
     quarters = gather_quarters([z_ref[g, :sub] for g in range(4)], [z_ref[g, sub:] for g in range(4)])
     for i, quarter in enumerate(quarters):
         out_ref[i * sub : (i + 1) * sub, :] = quarter
-    out_ref[4 * sub : 4 * sub + 8, :] = next_strip[...]
-    out_ref[4 * sub + 8 :, :] = far_strip[...]
-
-
-def back_partial(pos, table, inverse, windows, next_m, next_x, x, seg):
-    width = x.shape[1]
+    out_ref[4 * sub : 4 * sub + 8, :] = own_strip[...]
+    out_ref[4 * sub + 8 :, :] = outer_strip[...]
+
+
+def back_partial(pos, inverse, windows, own_m, outer_m, own_x, outer_x, seg):
+    width = own_m.shape[1]
     n = (windows.shape[0] + 1) // 2
 
     def window(distance):
         return pl.BlockSpec(
             (1, 2 * seg, width),
-            lambda i, pos: (jnp.where(pos[0] == 1, n - 1 + distance, n - 1 - distance), 0, 0),
+            lambda i, pos: (jnp.where(pos[0] == 2, n - 1 + distance, n - 1 - distance), 0, 0),
         )
 
     return pl.pallas_call(
@@ -229,22 +226,20 @@
             num_scalar_prefetch=1,
             grid=(1,),
             in_specs=[
-                whole_spec(table.shape),
                 whole_spec(inverse.shape),
                 window(2),
                 window(3),
-                whole_spec((2 * seg, width)),
-                whole_spec((seg, width)),
+                *[whole_spec((2 * seg, width))] * 2,
                 *[strip_spec(seg, width)] * 2,
             ],
-            out_specs=[whole_spec((2 * seg, width)), whole_spec((seg + 16, width))],
+            out_specs=whole_spec((seg + 16, width)),
             scratch_shapes=[pltpu.VMEM((4, seg // 2, width), jnp.float32)],
         ),
-        out_shape=[f32(2 * seg, width), f32(seg + 16, width)],
+        out_shape=f32(seg + 16, width),
         compiler_params=params(24),
-        cost_estimate=cost(6 * seg * seg * width * 2, 24 * seg * width),
+        cost_estimate=cost(3 * seg * seg * width * 2, 24 * seg * width),
         name="partial",
-    )(pos, table, inverse, windows, windows, next_m, x, next_x, x)
+    )(pos, inverse, windows, windows, own_m, outer_m, own_x, outer_x)
 
 
 OWN, OUTER, NEXT, TWO, THREE = range(5)
@@ -553,7 +548,7 @@
     own_g, own_m = dft(pos, table, seg, gated), dft(pos, table, seg, mixed)
     side, over, filter_taps, own_g, own_m = after((side, over, filter_taps, own_g, own_m))
 
-    two = across(side), outward(over)
+    over_two, out_two = across(side), outward(over)
     outer_g = dft(pos, table, seg, side, choose=True)
     next_g = dft(pos, table, seg, over, side, choose=True)
     windows = taps_spectra(table, filter_taps, seg)
@@ -562,15 +557,16 @@
     two_x = across(side_x)
     outer_m = dft(pos, table, seg, side_x, choose=True)
     next_m = dft(pos, table, seg, over_x, side_x, choose=True)
-    *two, outer_m, next_m = after((*two, outer_m, next_m))
-
-    three = outward(two[0])
-    two_m, partial = back_partial(pos, table, inverse, windows, next_m, over_x, two_x, seg)
-    *two, partial = after((*two, partial))
-    partial = outward(partial)
-    two_g = dft(pos, table, seg, *two)
+    partial = back_partial(pos, inverse, windows, own_m, outer_m, mixed, side_x, seg)
+    over_two, next_m, partial = after((over_two, next_m, partial))
+
+    three = outward(over_two)
+    two_g = dft(pos, table, seg, over_two, out_two)
     acc = early(pos, windows, (own_g, outer_g, next_g, two_g), (own_m, outer_m, next_m), seg)
-    three, acc = after((three, acc))
+    partial, acc = after((partial, acc))
+    partial = send(partial, (2, 0), (1, 3))
+    two_m = dft(pos, table, seg, two_x)
+    three, two_m = after((three, two_m))
 
     three_g = dft(pos, table, seg, three)
     query_grad, filter_grad, back = late(

time: 70.7 us -> 76.7 us (1.085)
  waiting for transfers between devices: 25.9 us -> 32.2 us
    ppermute x9, waiting for transfers between devices: 25.9 us -> 32.2 us  [send(): return lax.ppermute(x, 'ctx', list(pairs))]
    pallas_call x8 -> x9, Pallas kernels: 8.07 us -> 8.7 us  [dft(): pl.pallas_call(functools.partial(dft_kernel, choose), grid_spec=pltpu.Pre...]
  transfers between devices with their start and end apart: 9 -> 9, of which waited for: 4 -> 3; matrix products, arithmetic and copies ran while one was open for 0% -> 0% of each run, Pallas kernels for 34% -> 32%
where the time goes in v8:
time: 76.7 us; the launch traced here: 76.3 us
  waiting for transfers between devices  32.2 us (42%)
  Pallas kernels  25.3 us (33%)
  starting transfers between devices  14.4 us (19%)
  local copies, waits for them, and re-layouts  2.13 us (3%)
  other arithmetic  1.36 us (2%)
  between operations  0.92 us (1%)
    ppermute x9, waiting for transfers between devices, send(): return lax.ppermute(x, 'ctx', list(pairs))  32.2 us
    ppermute x9, starting transfers between devices, send(): return lax.ppermute(x, 'ctx', list(pairs))  14.4 us
    pallas_call x9, Pallas kernels, dft(): pl.pallas_call(functools.partial(dft_kernel, choose), grid_spec=pltpu.Pre...  8.7 us
    pallas_call x1, Pallas kernels, late(): pl.pallas_call(late_kernel, grid_spec=pltpu.PrefetchScalarGridSpec(num_sc...  6.03 us
    pallas_call x1, Pallas kernels, taps_spectra(): pl.pallas_call(taps_kernel, grid=(blocks,), in_specs=[whole_spec(table.sh...  5.95 us
    pallas_call x1, Pallas kernels, early(): pl.pallas_call(early_kernel, grid_spec=pltpu.PrefetchScalarGridSpec(num_s...  2.28 us
    unnamed x18, local copies, waits for them, and re-layouts  2.13 us
  transfers between devices with their start and end apart: 9, of which 3 were waited for; matrix products, arithmetic and copies ran while one was open for 0% of the time, Pallas kernels for 32%

profile of v8, /device:TPU:0, one launch (start us, length us, event | category | flops | bytes accessed | tf_op | source)
XLA Modules:
  0.0 76.3 jit_solution(16901996988797476662)
XLA Ops:
  0.6 0.0 copy-start
  0.6 1.4 %mul.3.refs_0_.gated_ref.rest_1_ = f32[512,256]{1,0:T(8,128)S(1)} multiply(f32[512,256]{1,0:T(8,128)} %key_ref.1, f32[512,256]{1,0:T(8,128)} %values_ref.1) | non-fusion elementwise | flops 131072 | bytes 1572864 | tf_op jit(solution)/shard_map/mul | solution.py:544
  2.0 3.1 %collective-permute-start = (f32[512,256]{1,0:T(8,128)S(1)}, f32[512,256]{1,0:T(8,128)}, u32[]{:S(2)}, u32[]{:S(2)}) collective-permute-start(f32[512,256]{1,0:T(8,128)S(1)} %mul.3.refs_0_.gated_ref.rest_1_), channel_id=1, source_target_pairs={{0,4},{4,0},{8,12},{12,8},{1,5},{5,1},{9,13},{13,9},{2,6},{6,2},{1... | collective-permute-start | bytes 1572872 | tf_op jit(solution)/shard_map/ppermute | solution.py:522
  5.1 1.5 %collective-permute-start.1 = (f32[512,256]{1,0:T(8,128)S(1)}, f32[512,256]{1,0:T(8,128)}, u32[]{:S(2)}, u32[]{:S(2)}) collective-permute-start(f32[512,256]{1,0:T(8,128)S(1)} %mul.3.refs_0_.gated_ref.rest_1_), channel_id=1, source_target_pairs={{4,8},{8,4},{5,9},{9,5},{6,10},{10,6},{7,11},{11,7},{20,24},{24,20... | collective-permute-start | bytes 1572872 | tf_op jit(solution)/shard_map/ppermute | solution.py:522
  6.5 1.0 %copy-done.5 = f32[512,256]{1,0:T(8,128)S(1)} copy-done((f32[512,256]{1,0:T(8,128)S(1)}, f32[512,256]{1,0:T(8,128)}, u32[]{:S(2)}) %copy-start.5) | copy-done | bytes 524312
  7.6 1.0 %copy-done.7 = f32[512,256]{1,0:T(8,128)S(1)} copy-done((f32[512,256]{1,0:T(8,128)S(1)}, f32[512,256]{1,0:T(8,128)}, u32[]{:S(2)}) %copy-start.7) | copy-done | bytes 524312
  8.6 0.1 mix.1.refs_0_.own_strip.rest_2_
  8.8 3.7 %collective-permute-start.3 = (f32[520,256]{1,0:T(8,128)S(1)}, f32[520,256]{1,0:T(8,128)S(1)}, u32[]{:S(2)}, u32[]{:S(2)}) collective-permute-start(f32[520,256]{1,0:T(8,128)S(1)} %mix.1.refs_0_.own_strip.rest_2_), channel_id=1, source_target_pairs={{0,4},{4,0},{8,12},{12,8},{1,5},{5,1},{9,13},{13,9},{2,6},{6,2},{1... | collective-permute-start | bytes 1597448 | tf_op jit(solution)/shard_map/ppermute | solution.py:522
  12.4 0.7 collective-permute-start.4
  13.1 0.0 copy-done
  13.1 0.7 dft.9.own_g
  13.9 0.0 copy-start.1
  13.9 0.7 dft.10.own_ref.own_m
  14.6 3.4 %collective-permute-done.refs_0_.refs_1_ = f32[512,256]{1,0:T(8,128)} collective-permute-done((f32[512,256]{1,0:T(8,128)S(1)}, f32[512,256]{1,0:T(8,128)}, u32[]{:S(2)}, u32[]{:S(2)}) %collective-permute-start) | collective-permute-done | bytes 524320 | tf_op jit(solution)/shard_map/ppermute | solution.py:522
  17.9 0.0 collective-permute-done.1.refs_0_
  18.0 0.7 collective-permute-start.2
  18.6 1.3 %collective-permute-start.5 = (f32[512,256]{1,0:T(8,128)}, f32[512,256]{1,0:T(8,128)S(1)}, u32[]{:S(2)}, u32[]{:S(2)}) collective-permute-start(f32[512,256]{1,0:T(8,128)} %collective-permute-done.1.refs_0_), channel_id=1, source_target_pairs={{4,0},{8,12},{5,1},{9,13},{6,2},{10,14},{7,3},{11,15},{20,16},{24,... | collective-permute-start | bytes 1572872 | tf_op jit(solution)/shard_map/ppermute | solution.py:522
  19.9 1.7 %dft.11.outer_g = f32[1024,256]{1,0:T(8,128)S(1)} custom-call(s32[1]{0:T(128)} %bitcast.pos_ref, bf16[2,4,256,256]{3,2,1,0:T(8,128)(2,1)S(1)} %copy-done, f32[512,256]{1,0:T(8,128)} %collective-permute-done.refs_0_.refs_1_), custom_call_target="tpu_custom_call" | custom-call | flops 402653184 | bytes 1572864 | tf_op jit(solution)/shard_map/dft/pallas_call | solution.py:130
  21.7 1.9 %dft.12.next_g = f32[1024,256]{1,0:T(8,128)S(1)} custom-call(s32[1]{0:T(128)} %bitcast.pos_ref, bf16[2,4,256,256]{3,2,1,0:T(8,128)(2,1)S(1)} %copy-done, f32[512,256]{1,0:T(8,128)} %collective-permute-done.1.refs_0_, f32[512,256]{1,0:T(8,128)} %collective-permute-done.refs_0_.refs_1_), custom_call_target="tpu_custom_call" | custom-call | flops 402653184 | bytes 1572864 | tf_op jit(solution)/shard_map/dft/pallas_call | solution.py:130
  23.6 0.0 copy-done.1
  23.6 6.0 %taps.1.win_own.win_outer.win_next.win_two.win_ref = f32[7,1024,256]{2,1,0:T(8,128)S(1)} custom-call(bf16[2,4,256,256]{3,2,1,0:T(8,128)(2,1)S(1)} %copy-done, f32[4096,256]{1,0:T(8,128)S(1)} %copy-done.1), custom_call_target="tpu_custom_call" | custom-call | flops 3221225472 | bytes 12582912 | tf_op jit(solution)/shard_map/taps/pallas_call | solution.py:168
  29.6 0.0 copy-start.2
  29.6 0.0 collective-permute-done.3.refs_1_.refs_0_.outer_strip.beside_strip
  29.6 0.0 collective-permute-done.4.refs_0_.across_strip
  29.6 0.8 %collective-permute-start.7 = (f32[520,256]{1,0:T(8,128)S(1)}, f32[520,256]{1,0:T(8,128)S(1)}, u32[]{:S(2)}, u32[]{:S(2)}) collective-permute-start(f32[520,256]{1,0:T(8,128)S(1)} %collective-permute-done.3.refs_1_.refs_0_.outer_strip.beside_strip), channel_id=1, source_target_pairs={{4,8},{8,4},{5,9},{9,5},{6,10},{10,6},{7,11},{11,7},{20,24},{24,20... | collective-permute-start | bytes 1597448 | tf_op jit(solution)/shard_map/ppermute | solution.py:522
  30.5 0.7 dft.14.outer_ref.outer_m
  31.2 0.7 dft.13.next_m
  31.9 0.0 copy-done.2
  31.9 1.0 %partial.1 = f32[528,256]{1,0:T(8,128)S(1)} custom-call(s32[1]{0:T(128)} %bitcast.pos_ref, bf16[2,4,256,256]{3,2,1,0:T(8,128)(2,1)S(1)} %copy-done.2, f32[7,1024,256]{2,1,0:T(8,128)S(1)} %taps.1.win_own.win_outer.win_next.win_two.win_ref, f32[7,1024,256]{2,1,0:T(8,128)S(1)} %taps.1.win_own.win_outer.win_next.win_two.win_ref, ...), custom_call_target="tpu_custom_call" | custom-call | flops 402653184 | bytes 3145728 | tf_op jit(solution)/shard_map/partial/pallas_call | solution.py:223
  33.0 0.0 collective-permute-done.2.refs_0_
  33.0 1.3 %collective-permute-start.6 = (f32[512,256]{1,0:T(8,128)S(1)}, f32[512,256]{1,0:T(8,128)S(1)}, u32[]{:S(2)}, u32[]{:S(2)}) collective-permute-start(f32[512,256]{1,0:T(8,128)S(1)} %collective-permute-done.2.refs_0_), channel_id=1, source_target_pairs={{4,0},{8,12},{5,1},{9,13},{6,2},{10,14},{7,3},{11,15},{20,16},{24,... | collective-permute-start | bytes 1572872 | tf_op jit(solution)/shard_map/ppermute | solution.py:522
  34.3 5.3 %collective-permute-done.5.refs_1_ = f32[512,256]{1,0:T(8,128)S(1)} collective-permute-done((f32[512,256]{1,0:T(8,128)}, f32[512,256]{1,0:T(8,128)S(1)}, u32[]{:S(2)}, u32[]{:S(2)}) %collective-permute-start.5) | collective-permute-done | bytes 524320 | tf_op jit(solution)/shard_map/ppermute | solution.py:522
  39.7 0.7 dft.15.two_g
  40.4 2.3 %early.1.acc_ref = f32[4,1024,256]{2,1,0:T(8,128)S(1)} custom-call(s32[1]{0:T(128)} %bitcast.pos_ref, f32[7,1024,256]{2,1,0:T(8,128)S(1)} %taps.1.win_own.win_outer.win_next.win_two.win_ref, f32[7,1024,256]{2,1,0:T(8,128)S(1)} %taps.1.win_own.win_outer.win_next.win_two.win_ref, f32[7,1024,256]{2,1,0:T(8,128)S(1)} %taps.1.win_own.win_outer.win_next.win_two.win_ref, ...), custom_call_target="tpu_custom_call" | custom-call | flops 26214400 | bytes 15728640 | tf_op jit(solution)/shard_map/early/pallas_call | solution.py:351
  42.7 0.0 copy-start.6
  42.7 0.0 copy-start.8
  42.7 1.4 %collective-permute-start.8 = (f32[528,256]{1,0:T(8,128)S(1)}, f32[528,256]{1,0:T(8,128)S(1)}, u32[]{:S(2)}, u32[]{:S(2)}) collective-permute-start(f32[528,256]{1,0:T(8,128)S(1)} %partial.1), channel_id=1, source_target_pairs={{8,0},{4,12},{9,1},{5,13},{10,2},{6,14},{11,3},{7,15},{24,16},{20,... | collective-permute-start | bytes 1622024 | tf_op jit(solution)/shard_map/ppermute | solution.py:522
  44.1 0.0 collective-permute-done.7.refs_0_.two_strip
  44.1 0.7 dft.16.rest_0_
  44.9 23.5 %collective-permute-done.6.refs_0_ = f32[512,256]{1,0:T(8,128)S(1)} collective-permute-done((f32[512,256]{1,0:T(8,128)S(1)}, f32[512,256]{1,0:T(8,128)S(1)}, u32[]{:S(2)}, u32[]{:S(2)}) %collective-permute-start.6) | collective-permute-done | bytes 524320 | tf_op jit(solution)/shard_map/ppermute | solution.py:522
  68.3 0.7 dft.17.three_g
  69.0 0.0 copy-done.6
  69.1 0.0 copy-start.3
  69.1 0.0 copy-start.4
  69.1 6.0 %late.1 = (f32[512,256]{1,0:T(8,128)}, f32[1024,256]{1,0:T(8,128)}, f32[512,256]{1,0:T(8,128)S(1)}) custom-call(s32[1]{0:T(128)} %bitcast.pos_ref, bf16[2,4,256,256]{3,2,1,0:T(8,128)(2,1)S(1)} %copy-done.2, f32[4,1024,256]{2,1,0:T(8,128)S(1)} %early.1.acc_ref, f32[7,1024,256]{2,1,0:T(8,128)S(1)} %taps.1.win_own.win_outer.win_next.win_two.win_ref, ...), custom_call_target="tpu_custom_call" | custom-call | flops 1610612736 | bytes 13107200 | tf_op jit(solution)/shard_map/late/pallas_call | solution.py:448
  75.1 0.0 collective-permute-done.8.partial_ref
  75.1 0.0 copy-done.4
  75.1 1.1 %finish.1 = (f32[512,256]{1,0:T(8,128)}, f32[512,256]{1,0:T(8,128)}, f32[1,256]{1,0:T(1,128)}) custom-call(s32[1]{0:T(128)} %bitcast.pos_ref, f32[512,256]{1,0:T(8,128)S(1)} %get-tuple-element.45.back_ref, f32[512,256]{1,0:T(8,128)S(1)} %copy-done.3, f32[512,256]{1,0:T(8,128)S(1)} %copy-done.4, f32[528,256]{1,0:T(8,128)S(1)} %collective-permute-done.8.partial_ref, ...), custom_call_target="tpu_custom_call" | custom-call | flops 393216 | bytes 3145728 | tf_op jit(solution)/shard_map/finish/pallas_call | solution.py:506
  (4 shorter events, 0.0 us)
Async XLA Ops:
  0.6 12.5 %copy-start = (bf16[2,4,256,256]{3,2,1,0:T(8,128)(2,1)S(1)}, bf16[2,4,256,256]{3,2,1,0:T(8,128)(2,1)}, u32[]{:S(2)}) copy-start(bf16[2,4,256,256]{3,2,1,0:T(8,128)(2,1)} %constant.9.clone.table_ref) | copy-start | bytes 3145732
  2.0 15.9 %collective-permute-start = (f32[512,256]{1,0:T(8,128)S(1)}, f32[512,256]{1,0:T(8,128)}, u32[]{:S(2)}, u32[]{:S(2)}) collective-permute-start(f32[512,256]{1,0:T(8,128)S(1)} %mul.3.refs_0_.gated_ref.rest_1_), channel_id=1, source_target_pairs={{0,4},{4,0},{8,12},{12,8},{1,5},{5,1},{9,13},{13,9},{2,6},{6,2},{1... | collective-permute-start | bytes 1572872 | tf_op jit(solution)/shard_map/ppermute | solution.py:522
  5.1 12.9 %collective-permute-start.1 = (f32[512,256]{1,0:T(8,128)S(1)}, f32[512,256]{1,0:T(8,128)}, u32[]{:S(2)}, u32[]{:S(2)}) collective-permute-start(f32[512,256]{1,0:T(8,128)S(1)} %mul.3.refs_0_.gated_ref.rest_1_), channel_id=1, source_target_pairs={{4,8},{8,4},{5,9},{9,5},{6,10},{10,6},{7,11},{11,7},{20,24},{24,20... | collective-permute-start | bytes 1572872 | tf_op jit(solution)/shard_map/ppermute | solution.py:522
  6.5 1.0 %copy-start.5 = (f32[512,256]{1,0:T(8,128)S(1)}, f32[512,256]{1,0:T(8,128)}, u32[]{:S(2)}) copy-start(f32[512,256]{1,0:T(8,128)} %rest_4_.1) | copy-start | bytes 1572868
  7.6 1.0 %copy-start.7 = (f32[512,256]{1,0:T(8,128)S(1)}, f32[512,256]{1,0:T(8,128)}, u32[]{:S(2)}) copy-start(f32[512,256]{1,0:T(8,128)} %query_ref.1) | copy-start | bytes 1572868
  8.8 20.8 %collective-permute-start.3 = (f32[520,256]{1,0:T(8,128)S(1)}, f32[520,256]{1,0:T(8,128)S(1)}, u32[]{:S(2)}, u32[]{:S(2)}) collective-permute-start(f32[520,256]{1,0:T(8,128)S(1)} %mix.1.refs_0_.own_strip.rest_2_), channel_id=1, source_target_pairs={{0,4},{4,0},{8,12},{12,8},{1,5},{5,1},{9,13},{13,9},{2,6},{6,2},{1... | collective-permute-start | bytes 1597448 | tf_op jit(solution)/shard_map/ppermute | solution.py:522
  12.4 17.2 %collective-permute-start.4 = (f32[520,256]{1,0:T(8,128)S(1)}, f32[520,256]{1,0:T(8,128)S(1)}, u32[]{:S(2)}, u32[]{:S(2)}) collective-permute-start(f32[520,256]{1,0:T(8,128)S(1)} %mix.1.refs_0_.own_strip.rest_2_), channel_id=1, source_target_pairs={{4,8},{8,4},{5,9},{9,5},{6,10},{10,6},{7,11},{11,7},{20,24},{24,20... | collective-permute-start | bytes 1597448 | tf_op jit(solution)/shard_map/ppermute | solution.py:522
  13.9 9.8 %copy-start.1 = (f32[4096,256]{1,0:T(8,128)S(1)}, f32[4096,256]{1,0:T(8,128)}, u32[]{:S(2)}) copy-start(f32[4096,256]{1,0:T(8,128)} %x_ref) | copy-start | bytes 12582916
  18.0 15.1 %collective-permute-start.2 = (f32[512,256]{1,0:T(8,128)}, f32[512,256]{1,0:T(8,128)S(1)}, u32[]{:S(2)}, u32[]{:S(2)}) collective-permute-start(f32[512,256]{1,0:T(8,128)} %collective-permute-done.refs_0_.refs_1_), channel_id=1, source_target_pairs={{4,8},{8,4},{5,9},{9,5},{6,10},{10,6},{7,11},{11,7},{20,24},{24,20... | collective-permute-start | bytes 1572872 | tf_op jit(solution)/shard_map/ppermute | solution.py:522
  18.6 21.0 %collective-permute-start.5 = (f32[512,256]{1,0:T(8,128)}, f32[512,256]{1,0:T(8,128)S(1)}, u32[]{:S(2)}, u32[]{:S(2)}) collective-permute-start(f32[512,256]{1,0:T(8,128)} %collective-permute-done.1.refs_0_), channel_id=1, source_target_pairs={{4,0},{8,12},{5,1},{9,13},{6,2},{10,14},{7,3},{11,15},{20,16},{24,... | collective-permute-start | bytes 1572872 | tf_op jit(solution)/shard_map/ppermute | solution.py:522
  29.6 2.3 %copy-start.2 = (bf16[2,4,256,256]{3,2,1,0:T(8,128)(2,1)S(1)}, bf16[2,4,256,256]{3,2,1,0:T(8,128)(2,1)}, u32[]{:S(2)}) copy-start(bf16[2,4,256,256]{3,2,1,0:T(8,128)(2,1)} %constant.10.clone.inverse_ref) | copy-start | bytes 3145732
  29.6 14.5 %collective-permute-start.7 = (f32[520,256]{1,0:T(8,128)S(1)}, f32[520,256]{1,0:T(8,128)S(1)}, u32[]{:S(2)}, u32[]{:S(2)}) collective-permute-start(f32[520,256]{1,0:T(8,128)S(1)} %collective-permute-done.3.refs_1_.refs_0_.outer_strip.beside_strip), channel_id=1, source_target_pairs={{4,8},{8,4},{5,9},{9,5},{6,10},{10,6},{7,11},{11,7},{20,24},{24,20... | collective-permute-start | bytes 1597448 | tf_op jit(solution)/shard_map/ppermute | solution.py:522
  33.0 35.3 %collective-permute-start.6 = (f32[512,256]{1,0:T(8,128)S(1)}, f32[512,256]{1,0:T(8,128)S(1)}, u32[]{:S(2)}, u32[]{:S(2)}) collective-permute-start(f32[512,256]{1,0:T(8,128)S(1)} %collective-permute-done.2.refs_0_), channel_id=1, source_target_pairs={{4,0},{8,12},{5,1},{9,13},{6,2},{10,14},{7,3},{11,15},{20,16},{24,... | collective-permute-start | bytes 1572872 | tf_op jit(solution)/shard_map/ppermute | solution.py:522
  42.7 26.4 %copy-start.6 = (f32[512,256]{1,0:T(8,128)S(1)}, f32[512,256]{1,0:T(8,128)}, u32[]{:S(2)}) copy-start(f32[512,256]{1,0:T(8,128)} %rest_4_.1) | copy-start | bytes 1572868
  42.7 26.4 %copy-start.8 = (f32[256]{0:T(256)S(1)}, f32[256]{0:T(256)}, u32[]{:S(2)}) copy-start(f32[256]{0:T(256)} %param.12) | copy-start | bytes 3076
  42.7 32.4 %collective-permute-start.8 = (f32[528,256]{1,0:T(8,128)S(1)}, f32[528,256]{1,0:T(8,128)S(1)}, u32[]{:S(2)}, u32[]{:S(2)}) collective-permute-start(f32[528,256]{1,0:T(8,128)S(1)} %partial.1), channel_id=1, source_target_pairs={{8,0},{4,12},{9,1},{5,13},{10,2},{6,14},{11,3},{7,15},{24,16},{20,... | collective-permute-start | bytes 1622024 | tf_op jit(solution)/shard_map/ppermute | solution.py:522
  69.1 6.1 %copy-start.3 = (f32[512,256]{1,0:T(8,128)S(1)}, f32[512,256]{1,0:T(8,128)}, u32[]{:S(2)}) copy-start(f32[512,256]{1,0:T(8,128)} %key_ref.1) | copy-start | bytes 1572868
  69.1 6.0 %copy-start.4 = (f32[512,256]{1,0:T(8,128)S(1)}, f32[512,256]{1,0:T(8,128)}, u32[]{:S(2)}) copy-start(f32[512,256]{1,0:T(8,128)} %values_ref.1) | copy-start | bytes 1572868

commit v9 on v7

--- a/solution.py
+++ b/solution.py
@@ -84,29 +84,26 @@
     return jax.ShapeDtypeStruct(shape, jnp.float32)
 
 
-def mix_kernel(gated_ref, up_ref, query_ref, mixed_ref):
+def mix_kernel(gated_ref, up_ref, query_ref, mixed_ref, sum_ref):
     seg, width = gated_ref.shape
     mixed = up_ref[...] * query_ref[...]
-    mixed_ref[:seg, :] = mixed
-    mixed_ref[seg:, :] = jnp.sum((gated_ref[...] * mixed).reshape(seg // 8, 8, width), axis=0)
+    mixed_ref[...] = mixed
+    sum_ref[...] = jnp.sum((gated_ref[...] * mixed).reshape(seg // 8, 8, width), axis=0)
 
 
 def mix(gated, upstream, query_gate):
     seg, width = gated.shape
+    block = whole_spec((seg, width))
     return pl.pallas_call(
         mix_kernel,
         grid=(1,),
-        in_specs=[whole_spec((seg, width))] * 3,
-        out_specs=whole_spec((seg + 8, width)),
-        out_shape=f32(seg + 8, width),
+        in_specs=[block] * 3,
+        out_specs=[block, whole_spec((8, width))],
+        out_shape=[f32(seg, width), f32(8, width)],
         compiler_params=params(12),
         cost_estimate=cost(4 * seg * width, 16 * seg * width),
         name="mix",
     )(gated, upstream, query_gate)
-
-
-def strip_spec(seg, width):
-    return pl.BlockSpec((8, width), lambda *_: (seg // 8, 0))
 
 
 def dft_kernel(choose, pos_ref, table_ref, *refs):
@@ -191,7 +188,7 @@
 
 
 def partial_kernel(
-    pos_ref, table_ref, inverse_ref, win_near, win_far, next_ref, x_ref, next_strip, far_strip, far_ref, out_ref, z_ref
+    pos_ref, table_ref, inverse_ref, win_near, win_far, next_ref, x_ref, far_ref, out_ref, z_ref
 ):
     rows = far_ref.shape[0] // 4
     sub = rows // 2
@@ -209,11 +206,9 @@
     quarters = gather_quarters([z_ref[g, :sub] for g in range(4)], [z_ref[g, sub:] for g in range(4)])
     for i, quarter in enumerate(quarters):
         out_ref[i * sub : (i + 1) * sub, :] = quarter
-    out_ref[4 * sub : 4 * sub + 8, :] = next_strip[...]
-    out_ref[4 * sub + 8 :, :] = far_strip[...]
-
-
-def back_partial(pos, table, inverse, windows, next_m, next_x, x, seg):
+
+
+def back_partial(pos, table, inverse, windows, next_m, x, seg):
     width = x.shape[1]
     n = (windows.shape[0] + 1) // 2
 
@@ -235,16 +230,15 @@
                 window(3),
                 whole_spec((2 * seg, width)),
                 whole_spec((seg, width)),
-                *[strip_spec(seg, width)] * 2,
             ],
-            out_specs=[whole_spec((2 * seg, width)), whole_spec((seg + 16, width))],
+            out_specs=[whole_spec((2 * seg, width)), whole_spec((seg, width))],
             scratch_shapes=[pltpu.VMEM((4, seg // 2, width), jnp.float32)],
         ),
-        out_shape=[f32(2 * seg, width), f32(seg + 16, width)],
+        out_shape=[f32(2 * seg, width), f32(seg, width)],
         compiler_params=params(24),
         cost_estimate=cost(6 * seg * seg * width * 2, 24 * seg * width),
         name="partial",
-    )(pos, table, inverse, windows, windows, next_m, x, next_x, x)
+    )(pos, table, inverse, windows, windows, next_m, x)
 
 
 OWN, OUTER, NEXT, TWO, THREE = range(5)
@@ -479,48 +473,28 @@
     )(pos, inverse, acc, windows, three_g, two_g, own_m, outer_m, next_m, two_m, gated, mixed, skip, upstream)
 
 
-def finish_kernel(
-    pos_ref, back_ref, key_ref, values_ref, partial_ref, own_strip, beside_strip, across_strip, two_strip,
-    key_out, value_out, skip_out,
-):
-    pos = pos_ref[0]
-    seg = back_ref.shape[0]
-    back = back_ref[...] + partial_ref[:seg, :]
+def finish_kernel(back_ref, key_ref, values_ref, partial_ref, pair_ref, other_ref, key_out, value_out, skip_out):
+    back = back_ref[...] + partial_ref[...]
     key_out[...] = back * values_ref[...]
     value_out[...] = back * key_ref[...]
-    far = jnp.where(pos < 2, pos + 2, pos - 2)
-    strips = (
-        (own_strip[...], pos),
-        (beside_strip[...], jnp.where(pos % 2 == 0, pos + 1, pos - 1)),
-        (across_strip[...], 3 - pos),
-        (two_strip[...] + partial_ref[seg : seg + 8, :], far),
-        (partial_ref[seg + 8 :, :], 3 - pos),
-    )
-    total = None
-    for block in range(4):
-        value = jnp.zeros_like(own_strip[...])
-        for strip, source in strips:
-            value = value + jnp.where(source == block, strip, 0.0)
-        total = value if total is None else total + value
-    skip_out[...] = jnp.sum(total, axis=0, keepdims=True)
-
-
-def finish(pos, back, key_gate, values, partial, *mixed):
+    skip_out[...] = jnp.sum(pair_ref[...] + other_ref[...], axis=0, keepdims=True)
+
+
+def finish(back, key_gate, values, partial, pair, other):
     seg, width = back.shape
-    block = whole_spec((seg, width))
+    steps = 2
+    block = pl.BlockSpec((seg // steps, width), lambda i: (i, 0))
+    strip = whole_spec((8, width))
     return pl.pallas_call(
         finish_kernel,
-        grid_spec=pltpu.PrefetchScalarGridSpec(
-            num_scalar_prefetch=1,
-            grid=(1,),
-            in_specs=[block] * 3 + [whole_spec(partial.shape)] + [strip_spec(seg, width)] * len(mixed),
-            out_specs=[block, block, whole_spec((1, width))],
-        ),
+        grid=(steps,),
+        in_specs=[block] * 4 + [strip] * 2,
+        out_specs=[block, block, whole_spec((1, width))],
         out_shape=[f32(seg, width), f32(seg, width), f32(1, width)],
         compiler_params=params(12),
         cost_estimate=cost(3 * seg * width, 24 * seg * width),
         name="finish",
-    )(pos, back, key_gate, values, partial, *mixed)
+    )(back, key_gate, values, partial, pair, other)
 
 
 def send(x, *pairs):
@@ -548,38 +522,39 @@
 
     gated = key_gate * values
     side, over = beside(gated), across(gated)
-    mixed = mix(gated, upstream, query_gate)
+    mixed, strip = mix(gated, upstream, query_gate)
     side_x, over_x = beside(mixed), across(mixed)
     own_g, own_m = dft(pos, table, seg, gated), dft(pos, table, seg, mixed)
     side, over, filter_taps, own_g, own_m = after((side, over, filter_taps, own_g, own_m))
 
-    two = across(side), outward(over)
+    over_two, out_two = across(side), outward(over)
     outer_g = dft(pos, table, seg, side, choose=True)
     next_g = dft(pos, table, seg, over, side, choose=True)
     windows = taps_spectra(table, filter_taps, seg)
-    side_x, over_x, windows, outer_g, next_g = after((side_x, over_x, windows, outer_g, next_g))
+    side_x, over_x, windows, outer_g, next_g, strip = after((side_x, over_x, windows, outer_g, next_g, strip))
 
     two_x = across(side_x)
+    beside_strip = beside(strip)
     outer_m = dft(pos, table, seg, side_x, choose=True)
     next_m = dft(pos, table, seg, over_x, side_x, choose=True)
-    *two, outer_m, next_m = after((*two, outer_m, next_m))
-
-    three = outward(two[0])
-    two_m, partial = back_partial(pos, table, inverse, windows, next_m, over_x, two_x, seg)
-    *two, partial = after((*two, partial))
+    over_two, outer_m, next_m, beside_strip = after((over_two, outer_m, next_m, beside_strip))
+
+    three = outward(over_two)
+    pair = strip + beside_strip
+    two_g = dft(pos, table, seg, over_two, out_two)
+    acc = early(pos, windows, (own_g, outer_g, next_g, two_g), (own_m, outer_m, next_m), seg)
+    two_x, acc = after((two_x, acc))
+
+    two_m, partial = back_partial(pos, table, inverse, windows, next_m, two_x, seg)
+    partial, pair = after((partial, pair))
     partial = outward(partial)
-    two_g = dft(pos, table, seg, *two)
-    acc = early(pos, windows, (own_g, outer_g, next_g, two_g), (own_m, outer_m, next_m), seg)
-    three, acc = after((three, acc))
-
+    other = send(pair, (0, 2), (2, 0), (1, 3), (3, 1))
     three_g = dft(pos, table, seg, three)
     query_grad, filter_grad, back = late(
         pos, inverse, acc, windows, three_g, two_g, own_m, outer_m, next_m, two_m,
         gated, mixed, skip_gain[None, :], upstream,
     )
-    key_grad, value_grad, skip_grad = finish(
-        pos, back, key_gate, values, partial, mixed, side_x, over_x, two_x
-    )
+    key_grad, value_grad, skip_grad = finish(back, key_gate, values, partial, pair, other)
     return (query_grad, key_grad, value_grad, filter_grad, skip_grad[0])
 
 

time: 70.7 us -> 70.5 us (level)
  waiting for transfers between devices: 25.9 us -> 10.2 us
  starting transfers between devices: 14.9 us -> 29.5 us
  local copies, waits for them, and re-layouts: 2.12 us -> 3.35 us
    ppermute x9 -> x11, waiting for transfers between devices: 25.9 us -> 10.2 us  [send(): return lax.ppermute(x, 'ctx', list(pairs))]
    ppermute x9 -> x11, starting transfers between devices: 14.9 us -> 29.5 us  [send(): return lax.ppermute(x, 'ctx', list(pairs))]
    unnamed x18 -> x20, local copies, waits for them, and re-layouts: 2.12 us -> 3.35 us
  transfers between devices with their start and end apart: 9 -> 11, of which waited for: 4 -> 4; matrix products, arithmetic and copies ran while one was open for 0% -> 0% of each run, Pallas kernels for 34% -> 34%
where the time goes in v9:
time: 70.5 us; the launch traced here: 70 us
  starting transfers between devices  29.5 us (42%)
  Pallas kernels  24.7 us (35%)
  waiting for transfers between devices  10.2 us (14%)
  local copies, waits for them, and re-layouts  3.35 us (5%)
  other arithmetic  1.36 us (2%)
  between operations  0.9 us (1%)
    ppermute x11, starting transfers between devices, send(): return lax.ppermute(x, 'ctx', list(pairs))  29.5 us
    ppermute x11, waiting for transfers between devices, send(): return lax.ppermute(x, 'ctx', list(pairs))  10.2 us
    pallas_call x8, Pallas kernels, dft(): pl.pallas_call(functools.partial(dft_kernel, choose), grid_spec=pltpu.Pre...  7.82 us
    pallas_call x1, Pallas kernels, late(): pl.pallas_call(late_kernel, grid_spec=pltpu.PrefetchScalarGridSpec(num_sc...  6.01 us
    pallas_call x1, Pallas kernels, taps_spectra(): pl.pallas_call(taps_kernel, grid=(blocks,), in_specs=[whole_spec(table.sh...  5.95 us
    unnamed x20, local copies, waits for them, and re-layouts  3.35 us
    pallas_call x1, Pallas kernels, early(): pl.pallas_call(early_kernel, grid_spec=pltpu.PrefetchScalarGridSpec(num_s...  2.2 us
    pallas_call x1, Pallas kernels, back_partial(): pl.pallas_call(partial_kernel, grid_spec=pltpu.PrefetchScalarGridSpec(num...  1.62 us
  transfers between devices with their start and end apart: 11, of which 4 were waited for; matrix products, arithmetic and copies ran while one was open for 0% of the time, Pallas kernels for 34%

profile of v9, /device:TPU:0, one launch (start us, length us, event | category | flops | bytes accessed | tf_op | source)
XLA Modules:
  0.0 70.0 jit_solution(13395171664680006684)
XLA Ops:
  0.6 0.0 copy-start.1
  0.6 1.4 %mul.3.gated_ref.refs_0_.rest_1_ = f32[512,256]{1,0:T(8,128)S(1)} multiply(f32[512,256]{1,0:T(8,128)} %key_ref.1, f32[512,256]{1,0:T(8,128)} %values_ref.1) | non-fusion elementwise | flops 131072 | bytes 1572864 | tf_op jit(solution)/shard_map/mul | solution.py:523
  2.0 1.5 %collective-permute-start.3 = (f32[512,256]{1,0:T(8,128)S(1)}, f32[512,256]{1,0:T(8,128)}, u32[]{:S(2)}, u32[]{:S(2)}) collective-permute-start(f32[512,256]{1,0:T(8,128)S(1)} %mul.3.gated_ref.refs_0_.rest_1_), channel_id=1, source_target_pairs={{4,8},{8,4},{5,9},{9,5},{6,10},{10,6},{7,11},{11,7},{20,24},{24,20... | collective-permute-start | bytes 1572872 | tf_op jit(solution)/shard_map/ppermute | solution.py:501
  3.5 5.1 %collective-permute-start.2 = (f32[512,256]{1,0:T(8,128)S(1)}, f32[512,256]{1,0:T(8,128)S(1)}, u32[]{:S(2)}, u32[]{:S(2)}) collective-permute-start(f32[512,256]{1,0:T(8,128)S(1)} %mul.3.gated_ref.refs_0_.rest_1_), channel_id=1, source_target_pairs={{0,4},{4,0},{8,12},{12,8},{1,5},{5,1},{9,13},{13,9},{2,6},{6,2},{1... | collective-permute-start | bytes 1572872 | tf_op jit(solution)/shard_map/ppermute | solution.py:501
  8.6 1.0 %copy-done.4 = f32[512,256]{1,0:T(8,128)S(1)} copy-done((f32[512,256]{1,0:T(8,128)S(1)}, f32[512,256]{1,0:T(8,128)}, u32[]{:S(2)}) %copy-start.4) | copy-done | bytes 524312
  9.6 1.0 %copy-done.8 = f32[512,256]{1,0:T(8,128)S(1)} copy-done((f32[512,256]{1,0:T(8,128)S(1)}, f32[512,256]{1,0:T(8,128)}, u32[]{:S(2)}) %copy-start.8) | copy-done | bytes 524312
  10.7 0.1 mix.1
  10.7 1.5 %collective-permute-start.1 = (f32[512,256]{1,0:T(8,128)S(1)}, f32[512,256]{1,0:T(8,128)}, u32[]{:S(2)}, u32[]{:S(2)}) collective-permute-start(f32[512,256]{1,0:T(8,128)S(1)} %get-tuple-element.34.refs_0_.rest_2_), channel_id=1, source_target_pairs={{4,8},{8,4},{5,9},{9,5},{6,10},{10,6},{7,11},{11,7},{20,24},{24,20... | collective-permute-start | bytes 1572872 | tf_op jit(solution)/shard_map/ppermute | solution.py:501
  12.2 1.6 %collective-permute-start = (f32[512,256]{1,0:T(8,128)S(1)}, f32[512,256]{1,0:T(8,128)S(1)}, u32[]{:S(2)}, u32[]{:S(2)}) collective-permute-start(f32[512,256]{1,0:T(8,128)S(1)} %get-tuple-element.34.refs_0_.rest_2_), channel_id=1, source_target_pairs={{0,4},{4,0},{8,12},{12,8},{1,5},{5,1},{9,13},{13,9},{2,6},{6,2},{1... | collective-permute-start | bytes 1572872 | tf_op jit(solution)/shard_map/ppermute | solution.py:501
  13.8 1.2 %copy-done = bf16[2,4,256,256]{3,2,1,0:T(8,128)(2,1)S(1)} copy-done((bf16[2,4,256,256]{3,2,1,0:T(8,128)(2,1)S(1)}, bf16[2,4,256,256]{3,2,1,0:T(8,128)(2,1)}, u32[]{:S(2)}) %copy-start) | copy-done | bytes 1048600
  15.0 0.7 %dft.9.own_m = f32[1024,256]{1,0:T(8,128)S(1)} custom-call(s32[1]{0:T(128)} %bitcast.pos_ref, bf16[2,4,256,256]{3,2,1,0:T(8,128)(2,1)S(1)} %copy-done, f32[512,256]{1,0:T(8,128)S(1)} %get-tuple-element.34.refs_0_.rest_2_), custom_call_target="tpu_custom_call" | custom-call | flops 402653184 | bytes 1572864 | tf_op jit(solution)/shard_map/dft/pallas_call | solution.py:127
  15.7 0.7 %dft.8.own_g = f32[1024,256]{1,0:T(8,128)S(1)} custom-call(s32[1]{0:T(128)} %bitcast.pos_ref, bf16[2,4,256,256]{3,2,1,0:T(8,128)(2,1)S(1)} %copy-done, f32[512,256]{1,0:T(8,128)S(1)} %mul.3.gated_ref.refs_0_.rest_1_), custom_call_target="tpu_custom_call" | custom-call | flops 402653184 | bytes 1572864 | tf_op jit(solution)/shard_map/dft/pallas_call | solution.py:127
  16.5 0.0 collective-permute-done.3.refs_0_
  16.5 4.9 %collective-permute-done.2.refs_0_.refs_1_ = f32[512,256]{1,0:T(8,128)S(1)} collective-permute-done((f32[512,256]{1,0:T(8,128)S(1)}, f32[512,256]{1,0:T(8,128)S(1)}, u32[]{:S(2)}, u32[]{:S(2)}) %collective-permute-start.2) | collective-permute-done | bytes 524320 | tf_op jit(solution)/shard_map/ppermute | solution.py:501
  21.4 1.3 %collective-permute-start.7 = (f32[512,256]{1,0:T(8,128)}, f32[512,256]{1,0:T(8,128)S(1)}, u32[]{:S(2)}, u32[]{:S(2)}) collective-permute-start(f32[512,256]{1,0:T(8,128)} %collective-permute-done.3.refs_0_), channel_id=1, source_target_pairs={{4,0},{8,12},{5,1},{9,13},{6,2},{10,14},{7,3},{11,15},{20,16},{24,... | collective-permute-start | bytes 1572872 | tf_op jit(solution)/shard_map/ppermute | solution.py:501
  22.7 0.7 collective-permute-start.5
  23.4 0.0 copy-done.1
  23.4 0.0 copy-done.2
  23.4 5.9 %taps.1.win_own.win_outer.win_next.win_two.win_near.win_far.win_ref = f32[7,1024,256]{2,1,0:T(8,128)S(1)} custom-call(bf16[2,4,256,256]{3,2,1,0:T(8,128)(2,1)S(1)} %copy-done.1, f32[4096,256]{1,0:T(8,128)S(1)} %copy-done.2), custom_call_target="tpu_custom_call" | custom-call | flops 3221225472 | bytes 12582912 | tf_op jit(solution)/shard_map/taps/pallas_call | solution.py:165
  29.3 1.8 %dft.11.next_g = f32[1024,256]{1,0:T(8,128)S(1)} custom-call(s32[1]{0:T(128)} %bitcast.pos_ref, bf16[2,4,256,256]{3,2,1,0:T(8,128)(2,1)S(1)} %copy-done.1, f32[512,256]{1,0:T(8,128)} %collective-permute-done.3.refs_0_, f32[512,256]{1,0:T(8,128)S(1)} %collective-permute-done.2.refs_0_.refs_1_), custom_call_target="tpu_custom_call" | custom-call | flops 402653184 | bytes 1572864 | tf_op jit(solution)/shard_map/dft/pallas_call | solution.py:127
  31.1 0.7 %dft.10.outer_g = f32[1024,256]{1,0:T(8,128)S(1)} custom-call(s32[1]{0:T(128)} %bitcast.pos_ref, bf16[2,4,256,256]{3,2,1,0:T(8,128)(2,1)S(1)} %copy-done.1, f32[512,256]{1,0:T(8,128)S(1)} %collective-permute-done.2.refs_0_.refs_1_), custom_call_target="tpu_custom_call" | custom-call | flops 402653184 | bytes 1572864 | tf_op jit(solution)/shard_map/dft/pallas_call | solution.py:127
  31.8 0.0 collective-permute-done.1.refs_0_
  31.8 0.8 %collective-permute-done.refs_0_.refs_1_ = f32[512,256]{1,0:T(8,128)S(1)} collective-permute-done((f32[512,256]{1,0:T(8,128)S(1)}, f32[512,256]{1,0:T(8,128)S(1)}, u32[]{:S(2)}, u32[]{:S(2)}) %collective-permute-start) | collective-permute-done | bytes 524320 | tf_op jit(solution)/shard_map/ppermute | solution.py:501
  32.6 0.7 collective-permute-start.4
  33.3 6.5 %collective-permute-start.6 = (f32[8,256]{1,0:T(8,128)S(1)}, f32[8,256]{1,0:T(8,128)S(1)}, u32[]{:S(2)}, u32[]{:S(2)}) collective-permute-start(f32[8,256]{1,0:T(8,128)S(1)} %get-tuple-element.45), channel_id=1, source_target_pairs={{0,4},{4,0},{8,12},{12,8},{1,5},{5,1},{9,13},{13,9},{2,6},{6,2},{1... | collective-permute-start | bytes 24584 | tf_op jit(solution)/shard_map/ppermute | solution.py:501
  39.8 0.7 %dft.12.outer_m = f32[1024,256]{1,0:T(8,128)S(1)} custom-call(s32[1]{0:T(128)} %bitcast.pos_ref, bf16[2,4,256,256]{3,2,1,0:T(8,128)(2,1)S(1)} %copy-done.1, f32[512,256]{1,0:T(8,128)S(1)} %collective-permute-done.refs_0_.refs_1_), custom_call_target="tpu_custom_call" | custom-call | flops 402653184 | bytes 1572864 | tf_op jit(solution)/shard_map/dft/pallas_call | solution.py:127
  40.5 1.8 %dft.13.next_m.next_ref = f32[1024,256]{1,0:T(8,128)S(1)} custom-call(s32[1]{0:T(128)} %bitcast.pos_ref, bf16[2,4,256,256]{3,2,1,0:T(8,128)(2,1)S(1)} %copy-done.1, f32[512,256]{1,0:T(8,128)} %collective-permute-done.1.refs_0_, f32[512,256]{1,0:T(8,128)S(1)} %collective-permute-done.refs_0_.refs_1_), custom_call_target="tpu_custom_call" | custom-call | flops 402653184 | bytes 1572864 | tf_op jit(solution)/shard_map/dft/pallas_call | solution.py:127
  42.2 0.6 collective-permute-done.6
  42.9 0.0 collective-permute-done.5.refs_0_
  42.9 1.3 %collective-permute-start.8 = (f32[512,256]{1,0:T(8,128)S(1)}, f32[512,256]{1,0:T(8,128)S(1)}, u32[]{:S(2)}, u32[]{:S(2)}) collective-permute-start(f32[512,256]{1,0:T(8,128)S(1)} %collective-permute-done.5.refs_0_), channel_id=1, source_target_pairs={{4,0},{8,12},{5,1},{9,13},{6,2},{10,14},{7,3},{11,15},{20,16},{24,... | collective-permute-start | bytes 1572872 | tf_op jit(solution)/shard_map/ppermute | solution.py:501
  44.2 0.0 collective-permute-done.7.refs_1_
  44.2 0.7 %dft.14.two_g = f32[1024,256]{1,0:T(8,128)S(1)} custom-call(s32[1]{0:T(128)} %bitcast.pos_ref, bf16[2,4,256,256]{3,2,1,0:T(8,128)(2,1)S(1)} %copy-done.1, f32[512,256]{1,0:T(8,128)S(1)} %collective-permute-done.5.refs_0_, f32[512,256]{1,0:T(8,128)S(1)} %collective-permute-done.7.refs_1_), custom_call_target="tpu_custom_call" | custom-call | flops 402653184 | bytes 1572864 | tf_op jit(solution)/shard_map/dft/pallas_call | solution.py:127
  44.9 0.0 copy-start.3
  44.9 2.2 %early.1.acc_ref = f32[4,1024,256]{2,1,0:T(8,128)S(1)} custom-call(s32[1]{0:T(128)} %bitcast.pos_ref, f32[7,1024,256]{2,1,0:T(8,128)S(1)} %taps.1.win_own.win_outer.win_next.win_two.win_near.win_far.win_ref, f32[7,1024,256]{2,1,0:T(8,128)S(1)} %taps.1.win_own.win_outer.win_next.win_two.win_near.win_far.win_ref, ...), custom_call_target="tpu_custom_call" | custom-call | flops 26214400 | bytes 15728640 | tf_op jit(solution)/shard_map/early/pallas_call | solution.py:350
  47.1 0.0 copy-start.5
  47.2 0.0 copy-start.9
  47.2 0.0 collective-permute-done.4.x_ref
  47.2 1.6 %partial.1 = (f32[1024,256]{1,0:T(8,128)S(1)}, f32[512,256]{1,0:T(8,128)S(1)}) custom-call(s32[1]{0:T(128)} %bitcast.pos_ref, bf16[2,4,256,256]{3,2,1,0:T(8,128)(2,1)S(1)} %copy-done.1, bf16[2,4,256,256]{3,2,1,0:T(8,128)(2,1)S(1)} %copy-done.3, f32[7,1024,256]{2,1,0:T(8,128)S(1)} %taps.1.win_own.win_outer.win_next.win_two.win_near.win_far.win_ref, ...), custom_call_target="tpu_custom_call" | custom-call | flops 805306368 | bytes 3145728 | tf_op jit(solution)/shard_map/partial/pallas_call | solution.py:221
  48.8 1.3 %collective-permute-start.9 = (f32[512,256]{1,0:T(8,128)S(1)}, f32[512,256]{1,0:T(8,128)S(1)}, u32[]{:S(2)}, u32[]{:S(2)}) collective-permute-start(f32[512,256]{1,0:T(8,128)S(1)} %get-tuple-element.57), channel_id=1, source_target_pairs={{4,0},{8,12},{5,1},{9,13},{6,2},{10,14},{7,3},{11,15},{20,16},{24,... | collective-permute-start | bytes 1572872 | tf_op jit(solution)/shard_map/ppermute | solution.py:501
  50.1 8.2 %collective-permute-start.10 = (f32[8,256]{1,0:T(8,128)S(1)}, f32[8,256]{1,0:T(8,128)S(1)}, u32[]{:S(2)}, u32[]{:S(2)}) collective-permute-start(f32[8,256]{1,0:T(8,128)S(1)} %add.3.pair_ref), channel_id=1, source_target_pairs={{0,8},{8,0},{4,12},{12,4},{1,9},{9,1},{5,13},{13,5},{2,10},{10,2},... | collective-permute-start | bytes 24584 | tf_op jit(solution)/shard_map/ppermute | solution.py:501
  58.3 0.0 collective-permute-done.8.refs_0_
  58.3 0.7 %dft.15.three_g = f32[1024,256]{1,0:T(8,128)S(1)} custom-call(s32[1]{0:T(128)} %bitcast.pos_ref, bf16[2,4,256,256]{3,2,1,0:T(8,128)(2,1)S(1)} %copy-done.1, f32[512,256]{1,0:T(8,128)S(1)} %collective-permute-done.8.refs_0_), custom_call_target="tpu_custom_call" | custom-call | flops 402653184 | bytes 1572864 | tf_op jit(solution)/shard_map/dft/pallas_call | solution.py:127
  59.1 0.0 copy-start.6
  59.1 0.0 copy-start.7
  59.1 6.0 %late.1 = (f32[512,256]{1,0:T(8,128)}, f32[1024,256]{1,0:T(8,128)}, f32[512,256]{1,0:T(8,128)S(1)}) custom-call(s32[1]{0:T(128)} %bitcast.pos_ref, bf16[2,4,256,256]{3,2,1,0:T(8,128)(2,1)S(1)} %copy-done.3, f32[4,1024,256]{2,1,0:T(8,128)S(1)} %early.1.acc_ref, f32[7,1024,256]{2,1,0:T(8,128)S(1)} %taps.1.win_own.win_outer.win_next.win_two.win_near.win_far.win_ref, ...), custom_call_target="tpu_custom_call" | custom-call | flops 1610612736 | bytes 13107200 | tf_op jit(solution)/shard_map/late/pallas_call | solution.py:447
  65.1 0.0 collective-permute-done.10.other_ref
  65.1 3.9 %collective-permute-done.9.partial_ref = f32[512,256]{1,0:T(8,128)S(1)} collective-permute-done((f32[512,256]{1,0:T(8,128)S(1)}, f32[512,256]{1,0:T(8,128)S(1)}, u32[]{:S(2)}, u32[]{:S(2)}) %collective-permute-start.9) | collective-permute-done | bytes 524320 | tf_op jit(solution)/shard_map/ppermute | solution.py:501
  69.0 1.1 %finish.1 = (f32[512,256]{1,0:T(8,128)}, f32[512,256]{1,0:T(8,128)}, f32[1,256]{1,0:T(1,128)}) custom-call(f32[512,256]{1,0:T(8,128)S(1)} %get-tuple-element.54.back_ref, f32[512,256]{1,0:T(8,128)S(1)} %copy-done.6, f32[512,256]{1,0:T(8,128)S(1)} %copy-done.7, f32[512,256]{1,0:T(8,128)S(1)} %collective-permute-done.9.partial_ref, f32[8,256]{1,0:T(8,128)S(1)} %add.3.pair_ref, ...), custom_call_target="tpu_custom_call" | custom-call | flops 393216 | bytes 3145728 | tf_op jit(solution)/shard_map/finish/pallas_call | solution.py:488
  (10 shorter events, 0.0 us)
Async XLA Ops:
  0.6 22.7 %copy-start.1 = (bf16[2,4,256,256]{3,2,1,0:T(8,128)(2,1)S(1)}, bf16[2,4,256,256]{3,2,1,0:T(8,128)(2,1)}, u32[]{:S(2)}) copy-start(bf16[2,4,256,256]{3,2,1,0:T(8,128)(2,1)} %constant.9.clone.table_ref) | copy-start | bytes 3145732
  2.0 14.5 %collective-permute-start.3 = (f32[512,256]{1,0:T(8,128)S(1)}, f32[512,256]{1,0:T(8,128)}, u32[]{:S(2)}, u32[]{:S(2)}) collective-permute-start(f32[512,256]{1,0:T(8,128)S(1)} %mul.3.gated_ref.refs_0_.rest_1_), channel_id=1, source_target_pairs={{4,8},{8,4},{5,9},{9,5},{6,10},{10,6},{7,11},{11,7},{20,24},{24,20... | collective-permute-start | bytes 1572872 | tf_op jit(solution)/shard_map/ppermute | solution.py:501
  3.5 17.9 %collective-permute-start.2 = (f32[512,256]{1,0:T(8,128)S(1)}, f32[512,256]{1,0:T(8,128)S(1)}, u32[]{:S(2)}, u32[]{:S(2)}) collective-permute-start(f32[512,256]{1,0:T(8,128)S(1)} %mul.3.gated_ref.refs_0_.rest_1_), channel_id=1, source_target_pairs={{0,4},{4,0},{8,12},{12,8},{1,5},{5,1},{9,13},{13,9},{2,6},{6,2},{1... | collective-permute-start | bytes 1572872 | tf_op jit(solution)/shard_map/ppermute | solution.py:501
  8.6 1.0 %copy-start.4 = (f32[512,256]{1,0:T(8,128)S(1)}, f32[512,256]{1,0:T(8,128)}, u32[]{:S(2)}) copy-start(f32[512,256]{1,0:T(8,128)} %rest_4_.1) | copy-start | bytes 1572868
  9.6 1.0 %copy-start.8 = (f32[512,256]{1,0:T(8,128)S(1)}, f32[512,256]{1,0:T(8,128)}, u32[]{:S(2)}) copy-start(f32[512,256]{1,0:T(8,128)} %query_ref.1) | copy-start | bytes 1572868
  10.7 21.1 %collective-permute-start.1 = (f32[512,256]{1,0:T(8,128)S(1)}, f32[512,256]{1,0:T(8,128)}, u32[]{:S(2)}, u32[]{:S(2)}) collective-permute-start(f32[512,256]{1,0:T(8,128)S(1)} %get-tuple-element.34.refs_0_.rest_2_), channel_id=1, source_target_pairs={{4,8},{8,4},{5,9},{9,5},{6,10},{10,6},{7,11},{11,7},{20,24},{24,20... | collective-permute-start | bytes 1572872 | tf_op jit(solution)/shard_map/ppermute | solution.py:501
  12.2 20.4 %collective-permute-start = (f32[512,256]{1,0:T(8,128)S(1)}, f32[512,256]{1,0:T(8,128)S(1)}, u32[]{:S(2)}, u32[]{:S(2)}) collective-permute-start(f32[512,256]{1,0:T(8,128)S(1)} %get-tuple-element.34.refs_0_.rest_2_), channel_id=1, source_target_pairs={{0,4},{4,0},{8,12},{12,8},{1,5},{5,1},{9,13},{13,9},{2,6},{6,2},{1... | collective-permute-start | bytes 1572872 | tf_op jit(solution)/shard_map/ppermute | solution.py:501
  13.8 1.2 %copy-start = (bf16[2,4,256,256]{3,2,1,0:T(8,128)(2,1)S(1)}, bf16[2,4,256,256]{3,2,1,0:T(8,128)(2,1)}, u32[]{:S(2)}) copy-start(bf16[2,4,256,256]{3,2,1,0:T(8,128)(2,1)} %constant.9.clone.table_ref) | copy-start | bytes 3145732
  15.0 8.4 %copy-start.2 = (f32[4096,256]{1,0:T(8,128)S(1)}, f32[4096,256]{1,0:T(8,128)}, u32[]{:S(2)}) copy-start(f32[4096,256]{1,0:T(8,128)} %x_ref) | copy-start | bytes 12582916
  21.4 22.8 %collective-permute-start.7 = (f32[512,256]{1,0:T(8,128)}, f32[512,256]{1,0:T(8,128)S(1)}, u32[]{:S(2)}, u32[]{:S(2)}) collective-permute-start(f32[512,256]{1,0:T(8,128)} %collective-permute-done.3.refs_0_), channel_id=1, source_target_pairs={{4,0},{8,12},{5,1},{9,13},{6,2},{10,14},{7,3},{11,15},{20,16},{24,... | collective-permute-start | bytes 1572872 | tf_op jit(solution)/shard_map/ppermute | solution.py:501
  22.7 20.2 %collective-permute-start.5 = (f32[512,256]{1,0:T(8,128)S(1)}, f32[512,256]{1,0:T(8,128)S(1)}, u32[]{:S(2)}, u32[]{:S(2)}) collective-permute-start(f32[512,256]{1,0:T(8,128)S(1)} %collective-permute-done.2.refs_0_.refs_1_), channel_id=1, source_target_pairs={{4,8},{8,4},{5,9},{9,5},{6,10},{10,6},{7,11},{11,7},{20,24},{24,20... | collective-permute-start | bytes 1572872 | tf_op jit(solution)/shard_map/ppermute | solution.py:501
  32.6 14.6 %collective-permute-start.4 = (f32[512,256]{1,0:T(8,128)S(1)}, f32[512,256]{1,0:T(8,128)S(1)}, u32[]{:S(2)}, u32[]{:S(2)}) collective-permute-start(f32[512,256]{1,0:T(8,128)S(1)} %collective-permute-done.refs_0_.refs_1_), channel_id=1, source_target_pairs={{4,8},{8,4},{5,9},{9,5},{6,10},{10,6},{7,11},{11,7},{20,24},{24,20... | collective-permute-start | bytes 1572872 | tf_op jit(solution)/shard_map/ppermute | solution.py:501
  33.3 9.6 %collective-permute-start.6 = (f32[8,256]{1,0:T(8,128)S(1)}, f32[8,256]{1,0:T(8,128)S(1)}, u32[]{:S(2)}, u32[]{:S(2)}) collective-permute-start(f32[8,256]{1,0:T(8,128)S(1)} %get-tuple-element.45), channel_id=1, source_target_pairs={{0,4},{4,0},{8,12},{12,8},{1,5},{5,1},{9,13},{13,9},{2,6},{6,2},{1... | collective-permute-start | bytes 24584 | tf_op jit(solution)/shard_map/ppermute | solution.py:501
  42.9 15.4 %collective-permute-start.8 = (f32[512,256]{1,0:T(8,128)S(1)}, f32[512,256]{1,0:T(8,128)S(1)}, u32[]{:S(2)}, u32[]{:S(2)}) collective-permute-start(f32[512,256]{1,0:T(8,128)S(1)} %collective-permute-done.5.refs_0_), channel_id=1, source_target_pairs={{4,0},{8,12},{5,1},{9,13},{6,2},{10,14},{7,3},{11,15},{20,16},{24,... | collective-permute-start | bytes 1572872 | tf_op jit(solution)/shard_map/ppermute | solution.py:501
  44.9 2.3 %copy-start.3 = (bf16[2,4,256,256]{3,2,1,0:T(8,128)(2,1)S(1)}, bf16[2,4,256,256]{3,2,1,0:T(8,128)(2,1)}, u32[]{:S(2)}) copy-start(bf16[2,4,256,256]{3,2,1,0:T(8,128)(2,1)} %constant.10.clone.inverse_ref) | copy-start | bytes 3145732
  47.1 11.9 %copy-start.5 = (f32[512,256]{1,0:T(8,128)S(1)}, f32[512,256]{1,0:T(8,128)}, u32[]{:S(2)}) copy-start(f32[512,256]{1,0:T(8,128)} %rest_4_.1) | copy-start | bytes 1572868
  47.2 11.9 %copy-start.9 = (f32[256]{0:T(256)S(1)}, f32[256]{0:T(256)}, u32[]{:S(2)}) copy-start(f32[256]{0:T(256)} %param.12) | copy-start | bytes 3076
  48.8 20.2 %collective-permute-start.9 = (f32[512,256]{1,0:T(8,128)S(1)}, f32[512,256]{1,0:T(8,128)S(1)}, u32[]{:S(2)}, u32[]{:S(2)}) collective-permute-start(f32[512,256]{1,0:T(8,128)S(1)} %get-tuple-element.57), channel_id=1, source_target_pairs={{4,0},{8,12},{5,1},{9,13},{6,2},{10,14},{7,3},{11,15},{20,16},{24,... | collective-permute-start | bytes 1572872 | tf_op jit(solution)/shard_map/ppermute | solution.py:501
  50.1 15.0 %collective-permute-start.10 = (f32[8,256]{1,0:T(8,128)S(1)}, f32[8,256]{1,0:T(8,128)S(1)}, u32[]{:S(2)}, u32[]{:S(2)}) collective-permute-start(f32[8,256]{1,0:T(8,128)S(1)} %add.3.pair_ref), channel_id=1, source_target_pairs={{0,8},{8,0},{4,12},{12,4},{1,9},{9,1},{5,13},{13,5},{2,10},{10,2},... | collective-permute-start | bytes 24584 | tf_op jit(solution)/shard_map/ppermute | solution.py:501
  59.1 9.9 %copy-start.6 = (f32[512,256]{1,0:T(8,128)S(1)}, f32[512,256]{1,0:T(8,128)}, u32[]{:S(2)}) copy-start(f32[512,256]{1,0:T(8,128)} %key_ref.1) | copy-start | bytes 1572868
  59.1 9.9 %copy-start.7 = (f32[512,256]{1,0:T(8,128)S(1)}, f32[512,256]{1,0:T(8,128)}, u32[]{:S(2)}) copy-start(f32[512,256]{1,0:T(8,128)} %values_ref.1) | copy-start | bytes 1572868

commit v10 on v9

--- a/solution.py
+++ b/solution.py
@@ -533,10 +533,11 @@
     windows = taps_spectra(table, filter_taps, seg)
     side_x, over_x, windows, outer_g, next_g, strip = after((side_x, over_x, windows, outer_g, next_g, strip))
 
-    two_x = across(side_x)
     beside_strip = beside(strip)
     outer_m = dft(pos, table, seg, side_x, choose=True)
     next_m = dft(pos, table, seg, over_x, side_x, choose=True)
+    side_x, outer_m, next_m = after((side_x, outer_m, next_m))
+    two_x = across(side_x)
     over_two, outer_m, next_m, beside_strip = after((over_two, outer_m, next_m, beside_strip))
 
     three = outward(over_two)

time: 70.5 us -> 70.3 us (level)
  waiting for transfers between devices: 10.2 us -> 13.5 us
  Pallas kernels: 24.7 us -> 22.9 us
  starting transfers between devices: 29.5 us -> 28 us
    ppermute x11, waiting for transfers between devices: 10.2 us -> 13.5 us  [send(): return lax.ppermute(x, 'ctx', list(pairs))]
    pallas_call x8, Pallas kernels: 7.82 us -> 5.83 us  [dft(): pl.pallas_call(functools.partial(dft_kernel, choose), grid_spec=pltpu.Pre...]
    ppermute x11, starting transfers between devices: 29.5 us -> 28 us  [send(): return lax.ppermute(x, 'ctx', list(pairs))]
  transfers between devices with their start and end apart: 11 -> 11, of which waited for: 4 -> 4; matrix products, arithmetic and copies ran while one was open for 0% -> 0% of each run, Pallas kernels for 34% -> 31%
where the time goes in v10:
time: 70.3 us; the launch traced here: 69.9 us
  starting transfers between devices  28 us (40%)
  Pallas kernels  22.9 us (33%)
  waiting for transfers between devices  13.5 us (19%)
  local copies, waits for them, and re-layouts  3.35 us (5%)
  other arithmetic  1.27 us (2%)
  between operations  0.91 us (1%)
    ppermute x11, starting transfers between devices, send(): return lax.ppermute(x, 'ctx', list(pairs))  28 us
    ppermute x11, waiting for transfers between devices, send(): return lax.ppermute(x, 'ctx', list(pairs))  13.5 us
    pallas_call x1, Pallas kernels, taps_spectra(): pl.pallas_call(taps_kernel, grid=(blocks,), in_specs=[whole_spec(table.sh...  6.08 us
    pallas_call x1, Pallas kernels, late(): pl.pallas_call(late_kernel, grid_spec=pltpu.PrefetchScalarGridSpec(num_sc...  6.01 us
    pallas_call x8, Pallas kernels, dft(): pl.pallas_call(functools.partial(dft_kernel, choose), grid_spec=pltpu.Pre...  5.83 us
    unnamed x20, local copies, waits for them, and re-layouts  3.35 us
    pallas_call x1, Pallas kernels, early(): pl.pallas_call(early_kernel, grid_spec=pltpu.PrefetchScalarGridSpec(num_s...  2.2 us
    pallas_call x1, Pallas kernels, back_partial(): pl.pallas_call(partial_kernel, grid_spec=pltpu.PrefetchScalarGridSpec(num...  1.64 us
  transfers between devices with their start and end apart: 11, of which 4 were waited for; matrix products, arithmetic and copies ran while one was open for 0% of the time, Pallas kernels for 31%

profile of v10, /device:TPU:0, one launch (start us, length us, event | category | flops | bytes accessed | tf_op | source)
XLA Modules:
  0.0 69.9 jit_solution(14062839190518834245)
XLA Ops:
  0.6 1.3 %mul.3.gated_ref.refs_0_.rest_1_ = f32[512,256]{1,0:T(8,128)S(1)} multiply(f32[512,256]{1,0:T(8,128)} %key_ref.1, f32[512,256]{1,0:T(8,128)} %values_ref.1) | non-fusion elementwise | flops 131072 | bytes 1572864 | tf_op jit(solution)/shard_map/mul | solution.py:523
  1.9 0.7 collective-permute-start.3
  2.6 5.9 %collective-permute-start.2 = (f32[512,256]{1,0:T(8,128)S(1)}, f32[512,256]{1,0:T(8,128)S(1)}, u32[]{:S(2)}, u32[]{:S(2)}) collective-permute-start(f32[512,256]{1,0:T(8,128)S(1)} %mul.3.gated_ref.refs_0_.rest_1_), channel_id=1, source_target_pairs={{0,4},{4,0},{8,12},{12,8},{1,5},{5,1},{9,13},{13,9},{2,6},{6,2},{1... | collective-permute-start | bytes 1572872 | tf_op jit(solution)/shard_map/ppermute | solution.py:501
  8.5 1.0 %copy-done.4 = f32[512,256]{1,0:T(8,128)S(1)} copy-done((f32[512,256]{1,0:T(8,128)S(1)}, f32[512,256]{1,0:T(8,128)}, u32[]{:S(2)}) %copy-start.4) | copy-done | bytes 524312
  9.5 1.0 %copy-done.8 = f32[512,256]{1,0:T(8,128)S(1)} copy-done((f32[512,256]{1,0:T(8,128)S(1)}, f32[512,256]{1,0:T(8,128)}, u32[]{:S(2)}) %copy-start.8) | copy-done | bytes 524312
  10.6 0.1 mix.1
  10.6 0.7 collective-permute-start.1
  11.3 1.7 %collective-permute-start = (f32[512,256]{1,0:T(8,128)S(1)}, f32[512,256]{1,0:T(8,128)S(1)}, u32[]{:S(2)}, u32[]{:S(2)}) collective-permute-start(f32[512,256]{1,0:T(8,128)S(1)} %get-tuple-element.37.refs_0_.rest_2_), channel_id=1, source_target_pairs={{0,4},{4,0},{8,12},{12,8},{1,5},{5,1},{9,13},{13,9},{2,6},{6,2},{1... | collective-permute-start | bytes 1572872 | tf_op jit(solution)/shard_map/ppermute | solution.py:501
  13.1 1.2 %copy-done = bf16[2,4,256,256]{3,2,1,0:T(8,128)(2,1)S(1)} copy-done((bf16[2,4,256,256]{3,2,1,0:T(8,128)(2,1)S(1)}, bf16[2,4,256,256]{3,2,1,0:T(8,128)(2,1)}, u32[]{:S(2)}) %copy-start) | copy-done | bytes 1048600
  14.3 0.7 %dft.9.own_m = f32[1024,256]{1,0:T(8,128)S(1)} custom-call(s32[1]{0:T(128)} %bitcast.pos_ref, bf16[2,4,256,256]{3,2,1,0:T(8,128)(2,1)S(1)} %copy-done, f32[512,256]{1,0:T(8,128)S(1)} %get-tuple-element.37.refs_0_.rest_2_), custom_call_target="tpu_custom_call" | custom-call | flops 402653184 | bytes 1572864 | tf_op jit(solution)/shard_map/dft/pallas_call | solution.py:127
  15.0 0.7 %dft.8.own_g = f32[1024,256]{1,0:T(8,128)S(1)} custom-call(s32[1]{0:T(128)} %bitcast.pos_ref, bf16[2,4,256,256]{3,2,1,0:T(8,128)(2,1)S(1)} %copy-done, f32[512,256]{1,0:T(8,128)S(1)} %mul.3.gated_ref.refs_0_.rest_1_), custom_call_target="tpu_custom_call" | custom-call | flops 402653184 | bytes 1572864 | tf_op jit(solution)/shard_map/dft/pallas_call | solution.py:127
  15.8 0.0 collective-permute-done.3.refs_0_
  15.8 5.5 %collective-permute-done.2.refs_0_.refs_1_ = f32[512,256]{1,0:T(8,128)S(1)} collective-permute-done((f32[512,256]{1,0:T(8,128)S(1)}, f32[512,256]{1,0:T(8,128)S(1)}, u32[]{:S(2)}, u32[]{:S(2)}) %collective-permute-start.2) | collective-permute-done | bytes 524320 | tf_op jit(solution)/shard_map/ppermute | solution.py:501
  21.3 1.3 %collective-permute-start.7 = (f32[512,256]{1,0:T(8,128)S(1)}, f32[512,256]{1,0:T(8,128)S(1)}, u32[]{:S(2)}, u32[]{:S(2)}) collective-permute-start(f32[512,256]{1,0:T(8,128)S(1)} %collective-permute-done.3.refs_0_), channel_id=1, source_target_pairs={{4,0},{8,12},{5,1},{9,13},{6,2},{10,14},{7,3},{11,15},{20,16},{24,... | collective-permute-start | bytes 1572872 | tf_op jit(solution)/shard_map/ppermute | solution.py:501
  22.6 0.7 collective-permute-start.5
  23.3 0.7 %dft.11.next_g = f32[1024,256]{1,0:T(8,128)S(1)} custom-call(s32[1]{0:T(128)} %bitcast.pos_ref, bf16[2,4,256,256]{3,2,1,0:T(8,128)(2,1)S(1)} %copy-done, f32[512,256]{1,0:T(8,128)S(1)} %collective-permute-done.3.refs_0_, f32[512,256]{1,0:T(8,128)S(1)} %collective-permute-done.2.refs_0_.refs_1_), custom_call_target="tpu_custom_call" | custom-call | flops 402653184 | bytes 1572864 | tf_op jit(solution)/shard_map/dft/pallas_call | solution.py:127
  24.0 0.0 copy-done.1
  24.0 0.0 copy-done.2
  24.0 6.1 %taps.1.win_own.win_outer.win_next.win_two.win_near.win_far.win_ref = f32[7,1024,256]{2,1,0:T(8,128)S(1)} custom-call(bf16[2,4,256,256]{3,2,1,0:T(8,128)(2,1)S(1)} %copy-done.1, f32[4096,256]{1,0:T(8,128)S(1)} %copy-done.2), custom_call_target="tpu_custom_call" | custom-call | flops 3221225472 | bytes 12582912 | tf_op jit(solution)/shard_map/taps/pallas_call | solution.py:165
  30.1 0.7 %dft.10.outer_g = f32[1024,256]{1,0:T(8,128)S(1)} custom-call(s32[1]{0:T(128)} %bitcast.pos_ref, bf16[2,4,256,256]{3,2,1,0:T(8,128)(2,1)S(1)} %copy-done.1, f32[512,256]{1,0:T(8,128)S(1)} %collective-permute-done.2.refs_0_.refs_1_), custom_call_target="tpu_custom_call" | custom-call | flops 402653184 | bytes 1572864 | tf_op jit(solution)/shard_map/dft/pallas_call | solution.py:127
  30.9 0.0 collective-permute-done.1.refs_0_
  30.9 1.6 %collective-permute-done.refs_0_.refs_1_ = f32[512,256]{1,0:T(8,128)S(1)} collective-permute-done((f32[512,256]{1,0:T(8,128)S(1)}, f32[512,256]{1,0:T(8,128)S(1)}, u32[]{:S(2)}, u32[]{:S(2)}) %collective-permute-start) | collective-permute-done | bytes 524320 | tf_op jit(solution)/shard_map/ppermute | solution.py:501
  32.5 0.7 %dft.12.outer_m = f32[1024,256]{1,0:T(8,128)S(1)} custom-call(s32[1]{0:T(128)} %bitcast.pos_ref, bf16[2,4,256,256]{3,2,1,0:T(8,128)(2,1)S(1)} %copy-done.1, f32[512,256]{1,0:T(8,128)S(1)} %collective-permute-done.refs_0_.refs_1_), custom_call_target="tpu_custom_call" | custom-call | flops 402653184 | bytes 1572864 | tf_op jit(solution)/shard_map/dft/pallas_call | solution.py:127
  33.2 0.8 %dft.13.next_m.next_ref = f32[1024,256]{1,0:T(8,128)S(1)} custom-call(s32[1]{0:T(128)} %bitcast.pos_ref, bf16[2,4,256,256]{3,2,1,0:T(8,128)(2,1)S(1)} %copy-done.1, f32[512,256]{1,0:T(8,128)S(1)} %collective-permute-done.1.refs_0_, f32[512,256]{1,0:T(8,128)S(1)} %collective-permute-done.refs_0_.refs_1_), custom_call_target="tpu_custom_call" | custom-call | flops 402653184 | bytes 1572864 | tf_op jit(solution)/shard_map/dft/pallas_call | solution.py:127
  34.0 0.7 collective-permute-start.4
  34.7 5.6 %collective-permute-start.6 = (f32[8,256]{1,0:T(8,128)S(1)}, f32[8,256]{1,0:T(8,128)S(1)}, u32[]{:S(2)}, u32[]{:S(2)}) collective-permute-start(f32[8,256]{1,0:T(8,128)S(1)} %get-tuple-element.51), channel_id=1, source_target_pairs={{0,4},{4,0},{8,12},{12,8},{1,5},{5,1},{9,13},{13,9},{2,6},{6,2},{1... | collective-permute-start | bytes 24584 | tf_op jit(solution)/shard_map/ppermute | solution.py:501
  40.3 2.5 %collective-permute-done.6 = f32[8,256]{1,0:T(8,128)S(1)} collective-permute-done((f32[8,256]{1,0:T(8,128)S(1)}, f32[8,256]{1,0:T(8,128)S(1)}, u32[]{:S(2)}, u32[]{:S(2)}) %collective-permute-start.6) | collective-permute-done | bytes 8224 | tf_op jit(solution)/shard_map/ppermute | solution.py:501
  42.8 0.0 collective-permute-done.5.refs_0_
  42.8 1.3 %collective-permute-start.8 = (f32[512,256]{1,0:T(8,128)S(1)}, f32[512,256]{1,0:T(8,128)S(1)}, u32[]{:S(2)}, u32[]{:S(2)}) collective-permute-start(f32[512,256]{1,0:T(8,128)S(1)} %collective-permute-done.5.refs_0_), channel_id=1, source_target_pairs={{4,0},{8,12},{5,1},{9,13},{6,2},{10,14},{7,3},{11,15},{20,16},{24,... | collective-permute-start | bytes 1572872 | tf_op jit(solution)/shard_map/ppermute | solution.py:501
  44.1 0.0 collective-permute-done.7.refs_1_
  44.1 0.7 %dft.14.two_g = f32[1024,256]{1,0:T(8,128)S(1)} custom-call(s32[1]{0:T(128)} %bitcast.pos_ref, bf16[2,4,256,256]{3,2,1,0:T(8,128)(2,1)S(1)} %copy-done.1, f32[512,256]{1,0:T(8,128)S(1)} %collective-permute-done.5.refs_0_, f32[512,256]{1,0:T(8,128)S(1)} %collective-permute-done.7.refs_1_), custom_call_target="tpu_custom_call" | custom-call | flops 402653184 | bytes 1572864 | tf_op jit(solution)/shard_map/dft/pallas_call | solution.py:127
  44.8 0.0 copy-start.3
  44.8 2.2 %early.1.acc_ref = f32[4,1024,256]{2,1,0:T(8,128)S(1)} custom-call(s32[1]{0:T(128)} %bitcast.pos_ref, f32[7,1024,256]{2,1,0:T(8,128)S(1)} %taps.1.win_own.win_outer.win_next.win_two.win_near.win_far.win_ref, f32[7,1024,256]{2,1,0:T(8,128)S(1)} %taps.1.win_own.win_outer.win_next.win_two.win_near.win_far.win_ref, ...), custom_call_target="tpu_custom_call" | custom-call | flops 26214400 | bytes 15728640 | tf_op jit(solution)/shard_map/early/pallas_call | solution.py:350
  47.1 0.0 copy-start.5
  47.1 0.0 copy-start.9
  47.1 0.0 collective-permute-done.4.x_ref
  47.1 1.6 %partial.1 = (f32[1024,256]{1,0:T(8,128)S(1)}, f32[512,256]{1,0:T(8,128)S(1)}) custom-call(s32[1]{0:T(128)} %bitcast.pos_ref, bf16[2,4,256,256]{3,2,1,0:T(8,128)(2,1)S(1)} %copy-done.1, bf16[2,4,256,256]{3,2,1,0:T(8,128)(2,1)S(1)} %copy-done.3, f32[7,1024,256]{2,1,0:T(8,128)S(1)} %taps.1.win_own.win_outer.win_next.win_two.win_near.win_far.win_ref, ...), custom_call_target="tpu_custom_call" | custom-call | flops 805306368 | bytes 3145728 | tf_op jit(solution)/shard_map/partial/pallas_call | solution.py:221
  48.7 1.3 %collective-permute-start.9 = (f32[512,256]{1,0:T(8,128)S(1)}, f32[512,256]{1,0:T(8,128)S(1)}, u32[]{:S(2)}, u32[]{:S(2)}) collective-permute-start(f32[512,256]{1,0:T(8,128)S(1)} %get-tuple-element.63), channel_id=1, source_target_pairs={{4,0},{8,12},{5,1},{9,13},{6,2},{10,14},{7,3},{11,15},{20,16},{24,... | collective-permute-start | bytes 1572872 | tf_op jit(solution)/shard_map/ppermute | solution.py:501
  50.0 8.2 %collective-permute-start.10 = (f32[8,256]{1,0:T(8,128)S(1)}, f32[8,256]{1,0:T(8,128)S(1)}, u32[]{:S(2)}, u32[]{:S(2)}) collective-permute-start(f32[8,256]{1,0:T(8,128)S(1)} %add.3.pair_ref), channel_id=1, source_target_pairs={{0,8},{8,0},{4,12},{12,4},{1,9},{9,1},{5,13},{13,5},{2,10},{10,2},... | collective-permute-start | bytes 24584 | tf_op jit(solution)/shard_map/ppermute | solution.py:501
  58.2 0.0 collective-permute-done.8.refs_0_
  58.2 0.7 %dft.15.three_g = f32[1024,256]{1,0:T(8,128)S(1)} custom-call(s32[1]{0:T(128)} %bitcast.pos_ref, bf16[2,4,256,256]{3,2,1,0:T(8,128)(2,1)S(1)} %copy-done.1, f32[512,256]{1,0:T(8,128)S(1)} %collective-permute-done.8.refs_0_), custom_call_target="tpu_custom_call" | custom-call | flops 402653184 | bytes 1572864 | tf_op jit(solution)/shard_map/dft/pallas_call | solution.py:127
  59.0 0.0 copy-start.6
  59.0 0.0 copy-start.7
  59.0 6.0 %late.1 = (f32[512,256]{1,0:T(8,128)}, f32[1024,256]{1,0:T(8,128)}, f32[512,256]{1,0:T(8,128)S(1)}) custom-call(s32[1]{0:T(128)} %bitcast.pos_ref, bf16[2,4,256,256]{3,2,1,0:T(8,128)(2,1)S(1)} %copy-done.3, f32[4,1024,256]{2,1,0:T(8,128)S(1)} %early.1.acc_ref, f32[7,1024,256]{2,1,0:T(8,128)S(1)} %taps.1.win_own.win_outer.win_next.win_two.win_near.win_far.win_ref, ...), custom_call_target="tpu_custom_call" | custom-call | flops 1610612736 | bytes 13107200 | tf_op jit(solution)/shard_map/late/pallas_call | solution.py:447
  65.0 0.0 collective-permute-done.10.other_ref
  65.0 3.8 %collective-permute-done.9.partial_ref = f32[512,256]{1,0:T(8,128)S(1)} collective-permute-done((f32[512,256]{1,0:T(8,128)S(1)}, f32[512,256]{1,0:T(8,128)S(1)}, u32[]{:S(2)}, u32[]{:S(2)}) %collective-permute-start.9) | collective-permute-done | bytes 524320 | tf_op jit(solution)/shard_map/ppermute | solution.py:501
  68.9 0.0 copy-done.7
  68.9 1.1 %finish.1 = (f32[512,256]{1,0:T(8,128)}, f32[512,256]{1,0:T(8,128)}, f32[1,256]{1,0:T(1,128)}) custom-call(f32[512,256]{1,0:T(8,128)S(1)} %get-tuple-element.60.back_ref, f32[512,256]{1,0:T(8,128)S(1)} %copy-done.6, f32[512,256]{1,0:T(8,128)S(1)} %copy-done.7, f32[512,256]{1,0:T(8,128)S(1)} %collective-permute-done.9.partial_ref, f32[8,256]{1,0:T(8,128)S(1)} %add.3.pair_ref, ...), custom_call_target="tpu_custom_call" | custom-call | flops 393216 | bytes 3145728 | tf_op jit(solution)/shard_map/finish/pallas_call | solution.py:488
  (10 shorter events, 0.0 us)
Async XLA Ops:
  1.9 13.9 %collective-permute-start.3 = (f32[512,256]{1,0:T(8,128)S(1)}, f32[512,256]{1,0:T(8,128)S(1)}, u32[]{:S(2)}, u32[]{:S(2)}) collective-permute-start(f32[512,256]{1,0:T(8,128)S(1)} %mul.3.gated_ref.refs_0_.rest_1_), channel_id=1, source_target_pairs={{4,8},{8,4},{5,9},{9,5},{6,10},{10,6},{7,11},{11,7},{20,24},{24,20... | collective-permute-start | bytes 1572872 | tf_op jit(solution)/shard_map/ppermute | solution.py:501
  2.6 18.7 %collective-permute-start.2 = (f32[512,256]{1,0:T(8,128)S(1)}, f32[512,256]{1,0:T(8,128)S(1)}, u32[]{:S(2)}, u32[]{:S(2)}) collective-permute-start(f32[512,256]{1,0:T(8,128)S(1)} %mul.3.gated_ref.refs_0_.rest_1_), channel_id=1, source_target_pairs={{0,4},{4,0},{8,12},{12,8},{1,5},{5,1},{9,13},{13,9},{2,6},{6,2},{1... | collective-permute-start | bytes 1572872 | tf_op jit(solution)/shard_map/ppermute | solution.py:501
  8.5 1.0 %copy-start.4 = (f32[512,256]{1,0:T(8,128)S(1)}, f32[512,256]{1,0:T(8,128)}, u32[]{:S(2)}) copy-start(f32[512,256]{1,0:T(8,128)} %rest_4_.1) | copy-start | bytes 1572868
  9.5 1.0 %copy-start.8 = (f32[512,256]{1,0:T(8,128)S(1)}, f32[512,256]{1,0:T(8,128)}, u32[]{:S(2)}) copy-start(f32[512,256]{1,0:T(8,128)} %query_ref.1) | copy-start | bytes 1572868
  10.6 20.2 %collective-permute-start.1 = (f32[512,256]{1,0:T(8,128)S(1)}, f32[512,256]{1,0:T(8,128)S(1)}, u32[]{:S(2)}, u32[]{:S(2)}) collective-permute-start(f32[512,256]{1,0:T(8,128)S(1)} %get-tuple-element.37.refs_0_.rest_2_), channel_id=1, source_target_pairs={{4,8},{8,4},{5,9},{9,5},{6,10},{10,6},{7,11},{11,7},{20,24},{24,20... | collective-permute-start | bytes 1572872 | tf_op jit(solution)/shard_map/ppermute | solution.py:501
  11.3 21.2 %collective-permute-start = (f32[512,256]{1,0:T(8,128)S(1)}, f32[512,256]{1,0:T(8,128)S(1)}, u32[]{:S(2)}, u32[]{:S(2)}) collective-permute-start(f32[512,256]{1,0:T(8,128)S(1)} %get-tuple-element.37.refs_0_.rest_2_), channel_id=1, source_target_pairs={{0,4},{4,0},{8,12},{12,8},{1,5},{5,1},{9,13},{13,9},{2,6},{6,2},{1... | collective-permute-start | bytes 1572872 | tf_op jit(solution)/shard_map/ppermute | solution.py:501
  13.1 1.2 %copy-start = (bf16[2,4,256,256]{3,2,1,0:T(8,128)(2,1)S(1)}, bf16[2,4,256,256]{3,2,1,0:T(8,128)(2,1)}, u32[]{:S(2)}) copy-start(bf16[2,4,256,256]{3,2,1,0:T(8,128)(2,1)} %constant.9.clone.table_ref) | copy-start | bytes 3145732
  14.3 9.7 %copy-start.1 = (bf16[2,4,256,256]{3,2,1,0:T(8,128)(2,1)S(1)}, bf16[2,4,256,256]{3,2,1,0:T(8,128)(2,1)}, u32[]{:S(2)}) copy-start(bf16[2,4,256,256]{3,2,1,0:T(8,128)(2,1)} %constant.9.clone.table_ref) | copy-start | bytes 3145732
  14.3 9.7 %copy-start.2 = (f32[4096,256]{1,0:T(8,128)S(1)}, f32[4096,256]{1,0:T(8,128)}, u32[]{:S(2)}) copy-start(f32[4096,256]{1,0:T(8,128)} %x_ref) | copy-start | bytes 12582916
  21.3 22.8 %collective-permute-start.7 = (f32[512,256]{1,0:T(8,128)S(1)}, f32[512,256]{1,0:T(8,128)S(1)}, u32[]{:S(2)}, u32[]{:S(2)}) collective-permute-start(f32[512,256]{1,0:T(8,128)S(1)} %collective-permute-done.3.refs_0_), channel_id=1, source_target_pairs={{4,0},{8,12},{5,1},{9,13},{6,2},{10,14},{7,3},{11,15},{20,16},{24,... | collective-permute-start | bytes 1572872 | tf_op jit(solution)/shard_map/ppermute | solution.py:501
  22.6 20.2 %collective-permute-start.5 = (f32[512,256]{1,0:T(8,128)S(1)}, f32[512,256]{1,0:T(8,128)S(1)}, u32[]{:S(2)}, u32[]{:S(2)}) collective-permute-start(f32[512,256]{1,0:T(8,128)S(1)} %collective-permute-done.2.refs_0_.refs_1_), channel_id=1, source_target_pairs={{4,8},{8,4},{5,9},{9,5},{6,10},{10,6},{7,11},{11,7},{20,24},{24,20... | collective-permute-start | bytes 1572872 | tf_op jit(solution)/shard_map/ppermute | solution.py:501
  34.0 13.1 %collective-permute-start.4 = (f32[512,256]{1,0:T(8,128)S(1)}, f32[512,256]{1,0:T(8,128)S(1)}, u32[]{:S(2)}, u32[]{:S(2)}) collective-permute-start(f32[512,256]{1,0:T(8,128)S(1)} %collective-permute-done.refs_0_.refs_1_), channel_id=1, source_target_pairs={{4,8},{8,4},{5,9},{9,5},{6,10},{10,6},{7,11},{11,7},{20,24},{24,20... | collective-permute-start | bytes 1572872 | tf_op jit(solution)/shard_map/ppermute | solution.py:501
  34.7 8.1 %collective-permute-start.6 = (f32[8,256]{1,0:T(8,128)S(1)}, f32[8,256]{1,0:T(8,128)S(1)}, u32[]{:S(2)}, u32[]{:S(2)}) collective-permute-start(f32[8,256]{1,0:T(8,128)S(1)} %get-tuple-element.51), channel_id=1, source_target_pairs={{0,4},{4,0},{8,12},{12,8},{1,5},{5,1},{9,13},{13,9},{2,6},{6,2},{1... | collective-permute-start | bytes 24584 | tf_op jit(solution)/shard_map/ppermute | solution.py:501
  42.8 15.5 %collective-permute-start.8 = (f32[512,256]{1,0:T(8,128)S(1)}, f32[512,256]{1,0:T(8,128)S(1)}, u32[]{:S(2)}, u32[]{:S(2)}) collective-permute-start(f32[512,256]{1,0:T(8,128)S(1)} %collective-permute-done.5.refs_0_), channel_id=1, source_target_pairs={{4,0},{8,12},{5,1},{9,13},{6,2},{10,14},{7,3},{11,15},{20,16},{24,... | collective-permute-start | bytes 1572872 | tf_op jit(solution)/shard_map/ppermute | solution.py:501
  44.8 2.3 %copy-start.3 = (bf16[2,4,256,256]{3,2,1,0:T(8,128)(2,1)S(1)}, bf16[2,4,256,256]{3,2,1,0:T(8,128)(2,1)}, u32[]{:S(2)}) copy-start(bf16[2,4,256,256]{3,2,1,0:T(8,128)(2,1)} %constant.10.clone.inverse_ref) | copy-start | bytes 3145732
  47.1 11.9 %copy-start.5 = (f32[512,256]{1,0:T(8,128)S(1)}, f32[512,256]{1,0:T(8,128)}, u32[]{:S(2)}) copy-start(f32[512,256]{1,0:T(8,128)} %rest_4_.1) | copy-start | bytes 1572868
  47.1 11.9 %copy-start.9 = (f32[256]{0:T(256)S(1)}, f32[256]{0:T(256)}, u32[]{:S(2)}) copy-start(f32[256]{0:T(256)} %param.12) | copy-start | bytes 3076
  48.7 20.1 %collective-permute-start.9 = (f32[512,256]{1,0:T(8,128)S(1)}, f32[512,256]{1,0:T(8,128)S(1)}, u32[]{:S(2)}, u32[]{:S(2)}) collective-permute-start(f32[512,256]{1,0:T(8,128)S(1)} %get-tuple-element.63), channel_id=1, source_target_pairs={{4,0},{8,12},{5,1},{9,13},{6,2},{10,14},{7,3},{11,15},{20,16},{24,... | collective-permute-start | bytes 1572872 | tf_op jit(solution)/shard_map/ppermute | solution.py:501
  50.0 15.0 %collective-permute-start.10 = (f32[8,256]{1,0:T(8,128)S(1)}, f32[8,256]{1,0:T(8,128)S(1)}, u32[]{:S(2)}, u32[]{:S(2)}) collective-permute-start(f32[8,256]{1,0:T(8,128)S(1)} %add.3.pair_ref), channel_id=1, source_target_pairs={{0,8},{8,0},{4,12},{12,4},{1,9},{9,1},{5,13},{13,5},{2,10},{10,2},... | collective-permute-start | bytes 24584 | tf_op jit(solution)/shard_map/ppermute | solution.py:501
  59.0 9.9 %copy-start.6 = (f32[512,256]{1,0:T(8,128)S(1)}, f32[512,256]{1,0:T(8,128)}, u32[]{:S(2)}) copy-start(f32[512,256]{1,0:T(8,128)} %key_ref.1) | copy-start | bytes 1572868
  59.0 9.9 %copy-start.7 = (f32[512,256]{1,0:T(8,128)S(1)}, f32[512,256]{1,0:T(8,128)}, u32[]{:S(2)}) copy-start(f32[512,256]{1,0:T(8,128)} %values_ref.1) | copy-start | bytes 1572868

commit v11 on v10

--- a/solution.py
+++ b/solution.py
@@ -84,11 +84,33 @@
     return jax.ShapeDtypeStruct(shape, jnp.float32)
 
 
+def block_sums(gated, mixed):
+    seg, width = gated.shape
+    return jnp.sum((gated * mixed).reshape(seg // 8, 8, width), axis=0)
+
+
+def sums_kernel(gated_ref, mixed_ref, out_ref):
+    out_ref[...] = block_sums(gated_ref[...], mixed_ref[...])
+
+
+def sums(gated, mixed):
+    seg, width = gated.shape
+    return pl.pallas_call(
+        sums_kernel,
+        grid=(1,),
+        in_specs=[whole_spec((seg, width))] * 2,
+        out_specs=whole_spec((8, width)),
+        out_shape=f32(8, width),
+        compiler_params=params(8),
+        cost_estimate=cost(2 * seg * width, 8 * seg * width),
+        name="sums",
+    )(gated, mixed)
+
+
 def mix_kernel(gated_ref, up_ref, query_ref, mixed_ref, sum_ref):
-    seg, width = gated_ref.shape
     mixed = up_ref[...] * query_ref[...]
     mixed_ref[...] = mixed
-    sum_ref[...] = jnp.sum((gated_ref[...] * mixed).reshape(seg // 8, 8, width), axis=0)
+    sum_ref[...] = block_sums(gated_ref[...], mixed)
 
 
 def mix(gated, upstream, query_gate):
@@ -188,35 +210,37 @@
 
 
 def partial_kernel(
-    pos_ref, table_ref, inverse_ref, win_near, win_far, next_ref, x_ref, far_ref, out_ref, z_ref
+    pos_ref, table_ref, inverse_ref, win_near, win_far, next_ref, x_ref, gated_ref, near_sums, out_ref, z_ref
 ):
-    rows = far_ref.shape[0] // 4
+    rows = next_ref.shape[0] // 4
     sub = rows // 2
     for group, part in enumerate(spread(x_ref[...])):
         base = group * rows
         far = dot3(table_ref, group, *split(part))
-        far_ref[base : base + rows, :] = far
         re, im = slice(base, base + sub), slice(base + sub, base + rows)
-        near = (next_ref[re, :], next_ref[im, :])
         total = add(
-            conj_mul((win_near[0, re, :], win_near[0, im, :]), near),
+            conj_mul((win_near[0, re, :], win_near[0, im, :]), (next_ref[re, :], next_ref[im, :])),
             conj_mul((win_far[0, re, :], win_far[0, im, :]), (far[:sub], far[sub:])),
         )
         z_ref[group] = dot3(inverse_ref, group, *split(jnp.concatenate(total, axis=0)))
     quarters = gather_quarters([z_ref[g, :sub] for g in range(4)], [z_ref[g, sub:] for g in range(4)])
     for i, quarter in enumerate(quarters):
         out_ref[i * sub : (i + 1) * sub, :] = quarter
-
-
-def back_partial(pos, table, inverse, windows, next_m, x, seg):
-    width = x.shape[1]
+    out_ref[4 * sub :, :] = near_sums[...] + block_sums(gated_ref[...], x_ref[...])
+
+
+def back_partial(pos, table, inverse, windows, next_m, x, gated, near_sums, half, seg):
+    width = x.shape[1] // 2
     n = (windows.shape[0] + 1) // 2
 
     def window(distance):
         return pl.BlockSpec(
             (1, 2 * seg, width),
-            lambda i, pos: (jnp.where(pos[0] == 1, n - 1 + distance, n - 1 - distance), 0, 0),
+            lambda i, pos: (jnp.where(pos[0] == 1, n - 1 + distance, n - 1 - distance), 0, half),
         )
+
+    def lanes(rows):
+        return pl.BlockSpec((rows, width), lambda i, pos: (0, half))
 
     return pl.pallas_call(
         partial_kernel,
@@ -228,17 +252,19 @@
                 whole_spec(inverse.shape),
                 window(2),
                 window(3),
-                whole_spec((2 * seg, width)),
-                whole_spec((seg, width)),
+                lanes(2 * seg),
+                lanes(seg),
+                lanes(seg),
+                lanes(8),
             ],
-            out_specs=[whole_spec((2 * seg, width)), whole_spec((seg, width))],
+            out_specs=whole_spec((seg + 8, width)),
             scratch_shapes=[pltpu.VMEM((4, seg // 2, width), jnp.float32)],
         ),
-        out_shape=[f32(2 * seg, width), f32(seg, width)],
+        out_shape=f32(seg + 8, width),
         compiler_params=params(24),
         cost_estimate=cost(6 * seg * seg * width * 2, 24 * seg * width),
         name="partial",
-    )(pos, table, inverse, windows, windows, next_m, x)
+    )(pos, table, inverse, windows, windows, next_m, x, gated, near_sums)
 
 
 OWN, OUTER, NEXT, TWO, THREE = range(5)
@@ -473,28 +499,35 @@
     )(pos, inverse, acc, windows, three_g, two_g, own_m, outer_m, next_m, two_m, gated, mixed, skip, upstream)
 
 
-def finish_kernel(back_ref, key_ref, values_ref, partial_ref, pair_ref, other_ref, key_out, value_out, skip_out):
-    back = back_ref[...] + partial_ref[...]
+def finish_kernel(back_ref, key_ref, values_ref, made_ref, sent_ref, own_ref, side_ref, *rest):
+    key_out, value_out, skip_out = rest[-3:]
+    seg = back_ref.shape[0]
+    back = back_ref[...] + sent_ref[:seg, :]
     key_out[...] = back * values_ref[...]
     value_out[...] = back * key_ref[...]
-    skip_out[...] = jnp.sum(pair_ref[...] + other_ref[...], axis=0, keepdims=True)
-
-
-def finish(back, key_gate, values, partial, pair, other):
-    seg, width = back.shape
-    steps = 2
-    block = pl.BlockSpec((seg // steps, width), lambda i: (i, 0))
-    strip = whole_spec((8, width))
+    total = (own_ref[...] + side_ref[...]) + (made_ref[seg:, :] + sent_ref[seg:, :])
+    skip_out[...] = jnp.sum(total, axis=0, keepdims=True)
+
+
+def finish(back, key_gate, values, made, sent, own_sums, side_sums, half, before=()):
+    seg, full = back.shape
+    width = full // 2
+
+    def lanes(rows):
+        return pl.BlockSpec((rows, width), lambda i: (0, half))
+
+    held = pl.BlockSpec(memory_space=pl.ANY)
     return pl.pallas_call(
         finish_kernel,
-        grid=(steps,),
-        in_specs=[block] * 4 + [strip] * 2,
-        out_specs=[block, block, whole_spec((1, width))],
-        out_shape=[f32(seg, width), f32(seg, width), f32(1, width)],
+        grid=(1,),
+        in_specs=[lanes(seg)] * 3 + [whole_spec((seg + 8, width))] * 2 + [lanes(8)] * 2 + [held] * len(before),
+        out_specs=[lanes(seg), lanes(seg), lanes(1)],
+        out_shape=[f32(seg, full), f32(seg, full), f32(1, full)],
+        input_output_aliases={7 + i: i for i in range(len(before))},
         compiler_params=params(12),
         cost_estimate=cost(3 * seg * width, 24 * seg * width),
         name="finish",
-    )(back, key_gate, values, partial, pair, other)
+    )(back, key_gate, values, made, sent, own_sums, side_sums, *before)
 
 
 def send(x, *pairs):
@@ -522,7 +555,7 @@
 
     gated = key_gate * values
     side, over = beside(gated), across(gated)
-    mixed, strip = mix(gated, upstream, query_gate)
+    mixed, own_sums = mix(gated, upstream, query_gate)
     side_x, over_x = beside(mixed), across(mixed)
     own_g, own_m = dft(pos, table, seg, gated), dft(pos, table, seg, mixed)
     side, over, filter_taps, own_g, own_m = after((side, over, filter_taps, own_g, own_m))
@@ -531,31 +564,34 @@
     outer_g = dft(pos, table, seg, side, choose=True)
     next_g = dft(pos, table, seg, over, side, choose=True)
     windows = taps_spectra(table, filter_taps, seg)
-    side_x, over_x, windows, outer_g, next_g, strip = after((side_x, over_x, windows, outer_g, next_g, strip))
-
-    beside_strip = beside(strip)
+    side_x, over_x, windows, outer_g, next_g = after((side_x, over_x, windows, outer_g, next_g))
+
     outer_m = dft(pos, table, seg, side_x, choose=True)
     next_m = dft(pos, table, seg, over_x, side_x, choose=True)
     side_x, outer_m, next_m = after((side_x, outer_m, next_m))
     two_x = across(side_x)
-    over_two, outer_m, next_m, beside_strip = after((over_two, outer_m, next_m, beside_strip))
+    side_sums, near_sums = sums(side, side_x), sums(over, over_x)
+    over_two, outer_m, next_m, side_sums, near_sums = after((over_two, outer_m, next_m, side_sums, near_sums))
 
     three = outward(over_two)
-    pair = strip + beside_strip
     two_g = dft(pos, table, seg, over_two, out_two)
     acc = early(pos, windows, (own_g, outer_g, next_g, two_g), (own_m, outer_m, next_m), seg)
     two_x, acc = after((two_x, acc))
 
-    two_m, partial = back_partial(pos, table, inverse, windows, next_m, two_x, seg)
-    partial, pair = after((partial, pair))
-    partial = outward(partial)
-    other = send(pair, (0, 2), (2, 0), (1, 3), (3, 1))
-    three_g = dft(pos, table, seg, three)
+    made_0 = back_partial(pos, table, inverse, windows, next_m, two_x, over_two, near_sums, 0, seg)
+    two_x, made_0 = after((two_x, made_0))
+    sent_0 = outward(made_0)
+    made_1 = back_partial(pos, table, inverse, windows, next_m, two_x, over_two, near_sums, 1, seg)
+    two_x, made_1 = after((two_x, made_1))
+    sent_1 = outward(made_1)
+    two_m, three_g = dft(pos, table, seg, two_x), dft(pos, table, seg, three)
     query_grad, filter_grad, back = late(
         pos, inverse, acc, windows, three_g, two_g, own_m, outer_m, next_m, two_m,
         gated, mixed, skip_gain[None, :], upstream,
     )
-    key_grad, value_grad, skip_grad = finish(back, key_gate, values, partial, pair, other)
+    done = finish(back, key_gate, values, made_0, sent_0, own_sums, side_sums, 0)
+    sent_1, *done = after((sent_1, *done))
+    key_grad, value_grad, skip_grad = finish(back, key_gate, values, made_1, sent_1, own_sums, side_sums, 1, done)
     return (query_grad, key_grad, value_grad, filter_grad, skip_grad[0])
 
 

time: 70.3 us -> 70.9 us (level)
  starting transfers between devices: 28 us -> 15.7 us
  waiting for transfers between devices: 13.5 us -> 23.1 us
  Pallas kernels: 22.9 us -> 26.1 us
    ppermute x11 -> x10, starting transfers between devices: 28 us -> 15.7 us  [send(): return lax.ppermute(x, 'ctx', list(pairs))]
    ppermute x11 -> x10, waiting for transfers between devices: 13.5 us -> 23.1 us  [send(): return lax.ppermute(x, 'ctx', list(pairs))]
    pallas_call x1 -> x2, Pallas kernels: 1.64 us -> 3.37 us  [back_partial(): pl.pallas_call(partial_kernel, grid_spec=pltpu.PrefetchScalarGridSpec(num...]
    pallas_call x1 -> x4, Pallas kernels: 1.05 us -> 1.97 us  [the longest x2 1.73 us: finish(): pl.pallas_call(finish_kernel, grid=(1,), in_specs=[lanes(seg)] * 3 + [who...]
    pallas_call x8 -> x9, Pallas kernels: 5.83 us -> 6.46 us  [dft(): pl.pallas_call(functools.partial(dft_kernel, choose), grid_spec=pltpu.Pre...]
  transfers between devices with their start and end apart: 11 -> 10, of which waited for: 4 -> 6; matrix products, arithmetic and copies ran while one was open for 0% -> 0% of each run, Pallas kernels for 31% -> 36%
where the time goes in v11:
time: 70.9 us; the launch traced here: 70.5 us
  Pallas kernels  26.1 us (37%)
  waiting for transfers between devices  23.1 us (33%)
  starting transfers between devices  15.7 us (22%)
  local copies, waits for them, and re-layouts  3.34 us (5%)
  other arithmetic  1.27 us (2%)
  between operations  0.94 us (1%)
    ppermute x10, waiting for transfers between devices, send(): return lax.ppermute(x, 'ctx', list(pairs))  23.1 us
    ppermute x10, starting transfers between devices, send(): return lax.ppermute(x, 'ctx', list(pairs))  15.7 us
    pallas_call x9, Pallas kernels, dft(): pl.pallas_call(functools.partial(dft_kernel, choose), grid_spec=pltpu.Pre...  6.46 us
    pallas_call x1, Pallas kernels, late(): pl.pallas_call(late_kernel, grid_spec=pltpu.PrefetchScalarGridSpec(num_sc...  6.03 us
    pallas_call x1, Pallas kernels, taps_spectra(): pl.pallas_call(taps_kernel, grid=(blocks,), in_specs=[whole_spec(table.sh...  5.95 us
    pallas_call x2, Pallas kernels, back_partial(): pl.pallas_call(partial_kernel, grid_spec=pltpu.PrefetchScalarGridSpec(num...  3.37 us
    unnamed x20, local copies, waits for them, and re-layouts  3.34 us
    pallas_call x1, Pallas kernels, early(): pl.pallas_call(early_kernel, grid_spec=pltpu.PrefetchScalarGridSpec(num_s...  2.2 us
  transfers between devices with their start and end apart: 10, of which 6 were waited for; matrix products, arithmetic and copies ran while one was open for 0% of the time, Pallas kernels for 36%

profile of v11, /device:TPU:0, one launch (start us, length us, event | category | flops | bytes accessed | tf_op | source)
XLA Modules:
  0.0 70.5 jit_solution(13621191017081313985)
XLA Ops:
  0.6 1.3 %mul.3.gated_ref.refs_0_.rest_1_ = f32[512,256]{1,0:T(8,128)S(1)} multiply(f32[512,256]{1,0:T(8,128)} %key_ref.3, f32[512,256]{1,0:T(8,128)} %values_ref.3) | non-fusion elementwise | flops 131072 | bytes 1572864 | tf_op jit(solution)/shard_map/mul | solution.py:556
  1.9 3.1 %collective-permute-start.2 = (f32[512,256]{1,0:T(8,128)S(1)}, f32[512,256]{1,0:T(8,128)S(1)}, u32[]{:S(2)}, u32[]{:S(2)}) collective-permute-start(f32[512,256]{1,0:T(8,128)S(1)} %mul.3.gated_ref.refs_0_.rest_1_), channel_id=1, source_target_pairs={{0,4},{4,0},{8,12},{12,8},{1,5},{5,1},{9,13},{13,9},{2,6},{6,2},{1... | collective-permute-start | bytes 1572872 | tf_op jit(solution)/shard_map/ppermute | solution.py:534
  5.0 0.7 collective-permute-start.3
  5.7 0.0 copy-start.6
  5.7 1.0 %copy-done.6 = f32[512,256]{1,0:T(8,128)S(1)} copy-done((f32[512,256]{1,0:T(8,128)S(1)}, f32[512,256]{1,0:T(8,128)}, u32[]{:S(2)}) %copy-start.6) | copy-done | bytes 524312
  6.7 1.0 %copy-done.8 = f32[512,256]{1,0:T(8,128)S(1)} copy-done((f32[512,256]{1,0:T(8,128)S(1)}, f32[512,256]{1,0:T(8,128)}, u32[]{:S(2)}) %copy-start.8) | copy-done | bytes 524312
  7.8 0.1 mix.1
  7.8 4.4 %collective-permute-start = (f32[512,256]{1,0:T(8,128)S(1)}, f32[512,256]{1,0:T(8,128)S(1)}, u32[]{:S(2)}, u32[]{:S(2)}) collective-permute-start(f32[512,256]{1,0:T(8,128)S(1)} %get-tuple-element.44.refs_0_.rest_2_), channel_id=1, source_target_pairs={{0,4},{4,0},{8,12},{12,8},{1,5},{5,1},{9,13},{13,9},{2,6},{6,2},{1... | collective-permute-start | bytes 1572872 | tf_op jit(solution)/shard_map/ppermute | solution.py:534
  12.3 0.7 collective-permute-start.1
  13.0 0.0 copy-start
  13.0 1.2 %copy-done = bf16[2,4,256,256]{3,2,1,0:T(8,128)(2,1)S(1)} copy-done((bf16[2,4,256,256]{3,2,1,0:T(8,128)(2,1)S(1)}, bf16[2,4,256,256]{3,2,1,0:T(8,128)(2,1)}, u32[]{:S(2)}) %copy-start) | copy-done | bytes 1048600
  14.2 0.7 %dft.10.own_m = f32[1024,256]{1,0:T(8,128)S(1)} custom-call(s32[1]{0:T(128)} %bitcast.pos_ref, bf16[2,4,256,256]{3,2,1,0:T(8,128)(2,1)S(1)} %copy-done, f32[512,256]{1,0:T(8,128)S(1)} %get-tuple-element.44.refs_0_.rest_2_), custom_call_target="tpu_custom_call" | custom-call | flops 402653184 | bytes 1572864 | tf_op jit(solution)/shard_map/dft/pallas_call | solution.py:149
  14.9 0.0 copy-start.1
  14.9 0.0 copy-start.5
  14.9 0.7 %dft.9.own_g = f32[1024,256]{1,0:T(8,128)S(1)} custom-call(s32[1]{0:T(128)} %bitcast.pos_ref, bf16[2,4,256,256]{3,2,1,0:T(8,128)(2,1)S(1)} %copy-done, f32[512,256]{1,0:T(8,128)S(1)} %mul.3.gated_ref.refs_0_.rest_1_), custom_call_target="tpu_custom_call" | custom-call | flops 402653184 | bytes 1572864 | tf_op jit(solution)/shard_map/dft/pallas_call | solution.py:149
  15.7 2.1 %collective-permute-done.2.refs_0_.refs_1_.gated_ref = f32[512,256]{1,0:T(8,128)S(1)} collective-permute-done((f32[512,256]{1,0:T(8,128)S(1)}, f32[512,256]{1,0:T(8,128)S(1)}, u32[]{:S(2)}, u32[]{:S(2)}) %collective-permute-start.2) | collective-permute-done | bytes 524320 | tf_op jit(solution)/shard_map/ppermute | solution.py:534
  17.7 0.7 collective-permute-start.5
  18.4 1.3 %collective-permute-start.6 = (f32[512,256]{1,0:T(8,128)S(1)}, f32[512,256]{1,0:T(8,128)S(1)}, u32[]{:S(2)}, u32[]{:S(2)}) collective-permute-start(f32[512,256]{1,0:T(8,128)S(1)} %collective-permute-done.3.refs_0_.gated_ref), channel_id=1, source_target_pairs={{4,0},{8,12},{5,1},{9,13},{6,2},{10,14},{7,3},{11,15},{20,16},{24,... | collective-permute-start | bytes 1572872 | tf_op jit(solution)/shard_map/ppermute | solution.py:534
  19.7 0.7 %dft.12.next_g = f32[1024,256]{1,0:T(8,128)S(1)} custom-call(s32[1]{0:T(128)} %bitcast.pos_ref, bf16[2,4,256,256]{3,2,1,0:T(8,128)(2,1)S(1)} %copy-done, f32[512,256]{1,0:T(8,128)S(1)} %collective-permute-done.3.refs_0_.gated_ref, f32[512,256]{1,0:T(8,128)S(1)} %collective-permute-done.2.refs_0_.refs_1_.gated_ref), custom_call_target="tpu_custom_call" | custom-call | flops 402653184 | bytes 1572864 | tf_op jit(solution)/shard_map/dft/pallas_call | solution.py:149
  20.5 0.7 %dft.11.outer_g = f32[1024,256]{1,0:T(8,128)S(1)} custom-call(s32[1]{0:T(128)} %bitcast.pos_ref, bf16[2,4,256,256]{3,2,1,0:T(8,128)(2,1)S(1)} %copy-done, f32[512,256]{1,0:T(8,128)S(1)} %collective-permute-done.2.refs_0_.refs_1_.gated_ref), custom_call_target="tpu_custom_call" | custom-call | flops 402653184 | bytes 1572864 | tf_op jit(solution)/shard_map/dft/pallas_call | solution.py:149
  21.2 6.0 %taps.1.win_own.win_outer.win_next.win_two.win_near.win_far.win_ref = f32[7,1024,256]{2,1,0:T(8,128)S(1)} custom-call(bf16[2,4,256,256]{3,2,1,0:T(8,128)(2,1)S(1)} %copy-done.1, f32[4096,256]{1,0:T(8,128)S(1)} %copy-done.5), custom_call_target="tpu_custom_call" | custom-call | flops 3221225472 | bytes 12582912 | tf_op jit(solution)/shard_map/taps/pallas_call | solution.py:187
  27.2 1.8 %collective-permute-done.refs_0_.refs_1_.mixed_ref = f32[512,256]{1,0:T(8,128)S(1)} collective-permute-done((f32[512,256]{1,0:T(8,128)S(1)}, f32[512,256]{1,0:T(8,128)S(1)}, u32[]{:S(2)}, u32[]{:S(2)}) %collective-permute-start) | collective-permute-done | bytes 524320 | tf_op jit(solution)/shard_map/ppermute | solution.py:534
  29.0 0.7 %dft.13.outer_m = f32[1024,256]{1,0:T(8,128)S(1)} custom-call(s32[1]{0:T(128)} %bitcast.pos_ref, bf16[2,4,256,256]{3,2,1,0:T(8,128)(2,1)S(1)} %copy-done.1, f32[512,256]{1,0:T(8,128)S(1)} %collective-permute-done.refs_0_.refs_1_.mixed_ref), custom_call_target="tpu_custom_call" | custom-call | flops 402653184 | bytes 1572864 | tf_op jit(solution)/shard_map/dft/pallas_call | solution.py:149
  29.7 0.7 %dft.14.next_m.next_ref = f32[1024,256]{1,0:T(8,128)S(1)} custom-call(s32[1]{0:T(128)} %bitcast.pos_ref, bf16[2,4,256,256]{3,2,1,0:T(8,128)(2,1)S(1)} %copy-done.1, f32[512,256]{1,0:T(8,128)S(1)} %collective-permute-done.1.refs_0_.mixed_ref, f32[512,256]{1,0:T(8,128)S(1)} %collective-permute-done.refs_0_.refs_1_.mixed_ref), custom_call_target="tpu_custom_call" | custom-call | flops 402653184 | bytes 1572864 | tf_op jit(solution)/shard_map/dft/pallas_call | solution.py:149
  30.4 0.7 collective-permute-start.4
  31.1 0.1 sums.3.near_sums
  31.3 0.1 sums.2.side_ref
  31.4 1.3 %collective-permute-start.7 = (f32[512,256]{1,0:T(8,128)S(1)}, f32[512,256]{1,0:T(8,128)S(1)}, u32[]{:S(2)}, u32[]{:S(2)}) collective-permute-start(f32[512,256]{1,0:T(8,128)S(1)} %collective-permute-done.5.refs_0_.gated_ref), channel_id=1, source_target_pairs={{4,0},{8,12},{5,1},{9,13},{6,2},{10,14},{7,3},{11,15},{20,16},{24,... | collective-permute-start | bytes 1572872 | tf_op jit(solution)/shard_map/ppermute | solution.py:534
  32.7 6.7 %collective-permute-done.6.refs_1_ = f32[512,256]{1,0:T(8,128)S(1)} collective-permute-done((f32[512,256]{1,0:T(8,128)S(1)}, f32[512,256]{1,0:T(8,128)S(1)}, u32[]{:S(2)}, u32[]{:S(2)}) %collective-permute-start.6) | collective-permute-done | bytes 524320 | tf_op jit(solution)/shard_map/ppermute | solution.py:534
  39.4 0.7 %dft.15.two_g = f32[1024,256]{1,0:T(8,128)S(1)} custom-call(s32[1]{0:T(128)} %bitcast.pos_ref, bf16[2,4,256,256]{3,2,1,0:T(8,128)(2,1)S(1)} %copy-done.1, f32[512,256]{1,0:T(8,128)S(1)} %collective-permute-done.5.refs_0_.gated_ref, f32[512,256]{1,0:T(8,128)S(1)} %collective-permute-done.6.refs_1_), custom_call_target="tpu_custom_call" | custom-call | flops 402653184 | bytes 1572864 | tf_op jit(solution)/shard_map/dft/pallas_call | solution.py:149
  40.1 0.0 copy-start.2
  40.1 2.2 %early.1.acc_ref = f32[4,1024,256]{2,1,0:T(8,128)S(1)} custom-call(s32[1]{0:T(128)} %bitcast.pos_ref, f32[7,1024,256]{2,1,0:T(8,128)S(1)} %taps.1.win_own.win_outer.win_next.win_two.win_near.win_far.win_ref, f32[7,1024,256]{2,1,0:T(8,128)S(1)} %taps.1.win_own.win_outer.win_next.win_two.win_near.win_far.win_ref, ...), custom_call_target="tpu_custom_call" | custom-call | flops 26214400 | bytes 15728640 | tf_op jit(solution)/shard_map/early/pallas_call | solution.py:376
  42.4 1.7 %partial.2.made_ref = f32[520,128]{1,0:T(8,128)S(1)} custom-call(s32[1]{0:T(128)} %bitcast.pos_ref, bf16[2,4,256,256]{3,2,1,0:T(8,128)(2,1)S(1)} %copy-done.1, bf16[2,4,256,256]{3,2,1,0:T(8,128)(2,1)S(1)} %copy-done.2, f32[7,1024,256]{2,1,0:T(8,128)S(1)} %taps.1.win_own.win_outer.win_next.win_two.win_near.win_far.win_ref, ...), custom_call_target="tpu_custom_call" | custom-call | flops 402653184 | bytes 1572864 | tf_op jit(solution)/shard_map/partial/pallas_call | solution.py:245
  44.1 1.3 %collective-permute-start.9 = (f32[520,128]{1,0:T(8,128)S(1)}, f32[520,128]{1,0:T(8,128)S(1)}, u32[]{:S(2)}, u32[]{:S(2)}) collective-permute-start(f32[520,128]{1,0:T(8,128)S(1)} %partial.2.made_ref), channel_id=1, source_target_pairs={{4,0},{8,12},{5,1},{9,13},{6,2},{10,14},{7,3},{11,15},{20,16},{24,... | collective-permute-start | bytes 798728 | tf_op jit(solution)/shard_map/ppermute | solution.py:534
  45.4 1.7 %partial.3.made_ref = f32[520,128]{1,0:T(8,128)S(1)} custom-call(s32[1]{0:T(128)} %bitcast.pos_ref, bf16[2,4,256,256]{3,2,1,0:T(8,128)(2,1)S(1)} %copy-done.1, bf16[2,4,256,256]{3,2,1,0:T(8,128)(2,1)S(1)} %copy-done.2, f32[7,1024,256]{2,1,0:T(8,128)S(1)} %taps.1.win_own.win_outer.win_next.win_two.win_near.win_far.win_ref, ...), custom_call_target="tpu_custom_call" | custom-call | flops 402653184 | bytes 1572864 | tf_op jit(solution)/shard_map/partial/pallas_call | solution.py:245
  47.0 0.0 copy-start.7
  47.1 0.0 copy-start.9
  47.1 1.6 %collective-permute-start.8 = (f32[520,128]{1,0:T(8,128)S(1)}, f32[520,128]{1,0:T(8,128)S(1)}, u32[]{:S(2)}, u32[]{:S(2)}) collective-permute-start(f32[520,128]{1,0:T(8,128)S(1)} %partial.3.made_ref), channel_id=1, source_target_pairs={{4,0},{8,12},{5,1},{9,13},{6,2},{10,14},{7,3},{11,15},{20,16},{24,... | collective-permute-start | bytes 798728 | tf_op jit(solution)/shard_map/ppermute | solution.py:534
  48.7 0.7 %dft.17.rest_0_ = f32[1024,256]{1,0:T(8,128)S(1)} custom-call(s32[1]{0:T(128)} %bitcast.pos_ref, bf16[2,4,256,256]{3,2,1,0:T(8,128)(2,1)S(1)} %copy-done.1, f32[512,256]{1,0:T(8,128)S(1)} %collective-permute-done.4.x_ref.refs_0_), custom_call_target="tpu_custom_call" | custom-call | flops 402653184 | bytes 1572864 | tf_op jit(solution)/shard_map/dft/pallas_call | solution.py:149
  49.4 7.1 %collective-permute-done.7.refs_0_ = f32[512,256]{1,0:T(8,128)S(1)} collective-permute-done((f32[512,256]{1,0:T(8,128)S(1)}, f32[512,256]{1,0:T(8,128)S(1)}, u32[]{:S(2)}, u32[]{:S(2)}) %collective-permute-start.7) | collective-permute-done | bytes 524320 | tf_op jit(solution)/shard_map/ppermute | solution.py:534
  56.5 0.7 %dft.16.three_g = f32[1024,256]{1,0:T(8,128)S(1)} custom-call(s32[1]{0:T(128)} %bitcast.pos_ref, bf16[2,4,256,256]{3,2,1,0:T(8,128)(2,1)S(1)} %copy-done.1, f32[512,256]{1,0:T(8,128)S(1)} %collective-permute-done.7.refs_0_), custom_call_target="tpu_custom_call" | custom-call | flops 402653184 | bytes 1572864 | tf_op jit(solution)/shard_map/dft/pallas_call | solution.py:149
  57.2 0.0 copy-start.3
  57.2 0.0 copy-start.4
  57.2 6.0 %late.1 = (f32[512,256]{1,0:T(8,128)}, f32[1024,256]{1,0:T(8,128)}, f32[512,256]{1,0:T(8,128)S(1)}) custom-call(s32[1]{0:T(128)} %bitcast.pos_ref, bf16[2,4,256,256]{3,2,1,0:T(8,128)(2,1)S(1)} %copy-done.2, f32[4,1024,256]{2,1,0:T(8,128)S(1)} %early.1.acc_ref, f32[7,1024,256]{2,1,0:T(8,128)S(1)} %taps.1.win_own.win_outer.win_next.win_two.win_near.win_far.win_ref, ...), custom_call_target="tpu_custom_call" | custom-call | flops 1610612736 | bytes 13107200 | tf_op jit(solution)/shard_map/late/pallas_call | solution.py:473
  63.3 2.4 %collective-permute-done.9.sent_ref = f32[520,128]{1,0:T(8,128)S(1)} collective-permute-done((f32[520,128]{1,0:T(8,128)S(1)}, f32[520,128]{1,0:T(8,128)S(1)}, u32[]{:S(2)}, u32[]{:S(2)}) %collective-permute-start.9) | collective-permute-done | bytes 266272 | tf_op jit(solution)/shard_map/ppermute | solution.py:534
  65.7 0.9 %finish.2 = (f32[512,256]{1,0:T(8,128)}, f32[512,256]{1,0:T(8,128)}, f32[1,256]{1,0:T(1,128)}) custom-call(f32[512,256]{1,0:T(8,128)S(1)} %get-tuple-element.67.back_ref, f32[512,256]{1,0:T(8,128)S(1)} %copy-done.3, f32[512,256]{1,0:T(8,128)S(1)} %copy-done.4, f32[520,128]{1,0:T(8,128)S(1)} %partial.2.made_ref, ...), custom_call_target="tpu_custom_call" | custom-call | flops 196608 | bytes 1572864 | tf_op jit(solution)/shard_map/finish/pallas_call | solution.py:520
  66.5 3.1 %collective-permute-done.8.sent_ref = f32[520,128]{1,0:T(8,128)S(1)} collective-permute-done((f32[520,128]{1,0:T(8,128)S(1)}, f32[520,128]{1,0:T(8,128)S(1)}, u32[]{:S(2)}, u32[]{:S(2)}) %collective-permute-start.8) | collective-permute-done | bytes 266272 | tf_op jit(solution)/shard_map/ppermute | solution.py:534
  69.6 0.9 %finish.3 = (f32[512,256]{1,0:T(8,128)}, f32[512,256]{1,0:T(8,128)}, f32[1,256]{1,0:T(1,128)}) custom-call(f32[512,256]{1,0:T(8,128)S(1)} %get-tuple-element.67.back_ref, f32[512,256]{1,0:T(8,128)S(1)} %copy-done.3, f32[512,256]{1,0:T(8,128)S(1)} %copy-done.4, ...), custom_call_target="tpu_custom_call", output_to_operand_aliasing={{0}: (7, {}), {1}: (8, {}), {2}: (9, {})} | custom-call | flops 196608 | bytes 1572864 | tf_op jit(solution)/shard_map/finish/pallas_call | solution.py:520
  (12 shorter events, 0.0 us)
Async XLA Ops:
  1.9 15.8 %collective-permute-start.2 = (f32[512,256]{1,0:T(8,128)S(1)}, f32[512,256]{1,0:T(8,128)S(1)}, u32[]{:S(2)}, u32[]{:S(2)}) collective-permute-start(f32[512,256]{1,0:T(8,128)S(1)} %mul.3.gated_ref.refs_0_.rest_1_), channel_id=1, source_target_pairs={{0,4},{4,0},{8,12},{12,8},{1,5},{5,1},{9,13},{13,9},{2,6},{6,2},{1... | collective-permute-start | bytes 1572872 | tf_op jit(solution)/shard_map/ppermute | solution.py:534
  5.0 12.8 %collective-permute-start.3 = (f32[512,256]{1,0:T(8,128)S(1)}, f32[512,256]{1,0:T(8,128)S(1)}, u32[]{:S(2)}, u32[]{:S(2)}) collective-permute-start(f32[512,256]{1,0:T(8,128)S(1)} %mul.3.gated_ref.refs_0_.rest_1_), channel_id=1, source_target_pairs={{4,8},{8,4},{5,9},{9,5},{6,10},{10,6},{7,11},{11,7},{20,24},{24,20... | collective-permute-start | bytes 1572872 | tf_op jit(solution)/shard_map/ppermute | solution.py:534
  5.7 1.0 %copy-start.6 = (f32[512,256]{1,0:T(8,128)S(1)}, f32[512,256]{1,0:T(8,128)}, u32[]{:S(2)}) copy-start(f32[512,256]{1,0:T(8,128)} %rest_4_.1) | copy-start | bytes 1572868
  6.7 1.0 %copy-start.8 = (f32[512,256]{1,0:T(8,128)S(1)}, f32[512,256]{1,0:T(8,128)}, u32[]{:S(2)}) copy-start(f32[512,256]{1,0:T(8,128)} %query_ref.1) | copy-start | bytes 1572868
  7.8 21.1 %collective-permute-start = (f32[512,256]{1,0:T(8,128)S(1)}, f32[512,256]{1,0:T(8,128)S(1)}, u32[]{:S(2)}, u32[]{:S(2)}) collective-permute-start(f32[512,256]{1,0:T(8,128)S(1)} %get-tuple-element.44.refs_0_.rest_2_), channel_id=1, source_target_pairs={{0,4},{4,0},{8,12},{12,8},{1,5},{5,1},{9,13},{13,9},{2,6},{6,2},{1... | collective-permute-start | bytes 1572872 | tf_op jit(solution)/shard_map/ppermute | solution.py:534
  12.3 16.7 %collective-permute-start.1 = (f32[512,256]{1,0:T(8,128)S(1)}, f32[512,256]{1,0:T(8,128)S(1)}, u32[]{:S(2)}, u32[]{:S(2)}) collective-permute-start(f32[512,256]{1,0:T(8,128)S(1)} %get-tuple-element.44.refs_0_.rest_2_), channel_id=1, source_target_pairs={{4,8},{8,4},{5,9},{9,5},{6,10},{10,6},{7,11},{11,7},{20,24},{24,20... | collective-permute-start | bytes 1572872 | tf_op jit(solution)/shard_map/ppermute | solution.py:534
  13.0 1.2 %copy-start = (bf16[2,4,256,256]{3,2,1,0:T(8,128)(2,1)S(1)}, bf16[2,4,256,256]{3,2,1,0:T(8,128)(2,1)}, u32[]{:S(2)}) copy-start(bf16[2,4,256,256]{3,2,1,0:T(8,128)(2,1)} %constant.9.clone.table_ref) | copy-start | bytes 3145732
  14.9 6.3 %copy-start.1 = (bf16[2,4,256,256]{3,2,1,0:T(8,128)(2,1)S(1)}, bf16[2,4,256,256]{3,2,1,0:T(8,128)(2,1)}, u32[]{:S(2)}) copy-start(bf16[2,4,256,256]{3,2,1,0:T(8,128)(2,1)} %constant.9.clone.table_ref) | copy-start | bytes 3145732
  14.9 6.3 %copy-start.5 = (f32[4096,256]{1,0:T(8,128)S(1)}, f32[4096,256]{1,0:T(8,128)}, u32[]{:S(2)}) copy-start(f32[4096,256]{1,0:T(8,128)} %x_ref) | copy-start | bytes 12582916
  17.7 13.6 %collective-permute-start.5 = (f32[512,256]{1,0:T(8,128)S(1)}, f32[512,256]{1,0:T(8,128)S(1)}, u32[]{:S(2)}, u32[]{:S(2)}) collective-permute-start(f32[512,256]{1,0:T(8,128)S(1)} %collective-permute-done.2.refs_0_.refs_1_.gated_ref), channel_id=1, source_target_pairs={{4,8},{8,4},{5,9},{9,5},{6,10},{10,6},{7,11},{11,7},{20,24},{24,20... | collective-permute-start | bytes 1572872 | tf_op jit(solution)/shard_map/ppermute | solution.py:534
  18.4 20.9 %collective-permute-start.6 = (f32[512,256]{1,0:T(8,128)S(1)}, f32[512,256]{1,0:T(8,128)S(1)}, u32[]{:S(2)}, u32[]{:S(2)}) collective-permute-start(f32[512,256]{1,0:T(8,128)S(1)} %collective-permute-done.3.refs_0_.gated_ref), channel_id=1, source_target_pairs={{4,0},{8,12},{5,1},{9,13},{6,2},{10,14},{7,3},{11,15},{20,16},{24,... | collective-permute-start | bytes 1572872 | tf_op jit(solution)/shard_map/ppermute | solution.py:534
  30.4 11.9 %collective-permute-start.4 = (f32[512,256]{1,0:T(8,128)S(1)}, f32[512,256]{1,0:T(8,128)S(1)}, u32[]{:S(2)}, u32[]{:S(2)}) collective-permute-start(f32[512,256]{1,0:T(8,128)S(1)} %collective-permute-done.refs_0_.refs_1_.mixed_ref), channel_id=1, source_target_pairs={{4,8},{8,4},{5,9},{9,5},{6,10},{10,6},{7,11},{11,7},{20,24},{24,20... | collective-permute-start | bytes 1572872 | tf_op jit(solution)/shard_map/ppermute | solution.py:534
  31.4 25.1 %collective-permute-start.7 = (f32[512,256]{1,0:T(8,128)S(1)}, f32[512,256]{1,0:T(8,128)S(1)}, u32[]{:S(2)}, u32[]{:S(2)}) collective-permute-start(f32[512,256]{1,0:T(8,128)S(1)} %collective-permute-done.5.refs_0_.gated_ref), channel_id=1, source_target_pairs={{4,0},{8,12},{5,1},{9,13},{6,2},{10,14},{7,3},{11,15},{20,16},{24,... | collective-permute-start | bytes 1572872 | tf_op jit(solution)/shard_map/ppermute | solution.py:534
  40.1 2.2 %copy-start.2 = (bf16[2,4,256,256]{3,2,1,0:T(8,128)(2,1)S(1)}, bf16[2,4,256,256]{3,2,1,0:T(8,128)(2,1)}, u32[]{:S(2)}) copy-start(bf16[2,4,256,256]{3,2,1,0:T(8,128)(2,1)} %constant.10.clone.inverse_ref) | copy-start | bytes 3145732
  44.1 21.6 %collective-permute-start.9 = (f32[520,128]{1,0:T(8,128)S(1)}, f32[520,128]{1,0:T(8,128)S(1)}, u32[]{:S(2)}, u32[]{:S(2)}) collective-permute-start(f32[520,128]{1,0:T(8,128)S(1)} %partial.2.made_ref), channel_id=1, source_target_pairs={{4,0},{8,12},{5,1},{9,13},{6,2},{10,14},{7,3},{11,15},{20,16},{24,... | collective-permute-start | bytes 798728 | tf_op jit(solution)/shard_map/ppermute | solution.py:534
  47.0 10.1 %copy-start.7 = (f32[512,256]{1,0:T(8,128)S(1)}, f32[512,256]{1,0:T(8,128)}, u32[]{:S(2)}) copy-start(f32[512,256]{1,0:T(8,128)} %rest_4_.1) | copy-start | bytes 1572868
  47.1 10.1 %copy-start.9 = (f32[256]{0:T(256)S(1)}, f32[256]{0:T(256)}, u32[]{:S(2)}) copy-start(f32[256]{0:T(256)} %param.12) | copy-start | bytes 3076
  47.1 22.5 %collective-permute-start.8 = (f32[520,128]{1,0:T(8,128)S(1)}, f32[520,128]{1,0:T(8,128)S(1)}, u32[]{:S(2)}, u32[]{:S(2)}) collective-permute-start(f32[520,128]{1,0:T(8,128)S(1)} %partial.3.made_ref), channel_id=1, source_target_pairs={{4,0},{8,12},{5,1},{9,13},{6,2},{10,14},{7,3},{11,15},{20,16},{24,... | collective-permute-start | bytes 798728 | tf_op jit(solution)/shard_map/ppermute | solution.py:534
  57.2 8.5 %copy-start.3 = (f32[512,256]{1,0:T(8,128)S(1)}, f32[512,256]{1,0:T(8,128)}, u32[]{:S(2)}) copy-start(f32[512,256]{1,0:T(8,128)} %key_ref.3) | copy-start | bytes 1572868
  57.2 8.4 %copy-start.4 = (f32[512,256]{1,0:T(8,128)S(1)}, f32[512,256]{1,0:T(8,128)}, u32[]{:S(2)}) copy-start(f32[512,256]{1,0:T(8,128)} %values_ref.3) | copy-start | bytes 1572868

commit v12 on v11

--- a/solution.py
+++ b/solution.py
@@ -558,13 +558,13 @@
     mixed, own_sums = mix(gated, upstream, query_gate)
     side_x, over_x = beside(mixed), across(mixed)
     own_g, own_m = dft(pos, table, seg, gated), dft(pos, table, seg, mixed)
-    side, over, filter_taps, own_g, own_m = after((side, over, filter_taps, own_g, own_m))
+    over, side, filter_taps, own_g, own_m = after((over, side, filter_taps, own_g, own_m))
 
     over_two, out_two = across(side), outward(over)
     outer_g = dft(pos, table, seg, side, choose=True)
     next_g = dft(pos, table, seg, over, side, choose=True)
     windows = taps_spectra(table, filter_taps, seg)
-    side_x, over_x, windows, outer_g, next_g = after((side_x, over_x, windows, outer_g, next_g))
+    over_x, side_x, windows, outer_g, next_g = after((over_x, side_x, windows, outer_g, next_g))
 
     outer_m = dft(pos, table, seg, side_x, choose=True)
     next_m = dft(pos, table, seg, over_x, side_x, choose=True)

time: 70.9 us -> 69.7 us (0.983)
  waiting for transfers between devices: 23.1 us -> 21.8 us
    ppermute x10, waiting for transfers between devices: 23.1 us -> 21.8 us  [send(): return lax.ppermute(x, 'ctx', list(pairs))]
where the time goes in v12:
time: 69.7 us; the launch traced here: 69.3 us
  Pallas kernels  26.1 us (37%)
  waiting for transfers between devices  21.8 us (31%)
  starting transfers between devices  15.9 us (23%)
  local copies, waits for them, and re-layouts  3.35 us (5%)
  other arithmetic  1.27 us (2%)
  between operations  0.93 us (1%)
    ppermute x10, waiting for transfers between devices, send(): return lax.ppermute(x, 'ctx', list(pairs))  21.8 us
    ppermute x10, starting transfers between devices, send(): return lax.ppermute(x, 'ctx', list(pairs))  15.9 us
    pallas_call x9, Pallas kernels, dft(): pl.pallas_call(functools.partial(dft_kernel, choose), grid_spec=pltpu.Pre...  6.47 us
    pallas_call x1, Pallas kernels, late(): pl.pallas_call(late_kernel, grid_spec=pltpu.PrefetchScalarGridSpec(num_sc...  6.03 us
    pallas_call x1, Pallas kernels, taps_spectra(): pl.pallas_call(taps_kernel, grid=(blocks,), in_specs=[whole_spec(table.sh...  5.95 us
    pallas_call x2, Pallas kernels, back_partial(): pl.pallas_call(partial_kernel, grid_spec=pltpu.PrefetchScalarGridSpec(num...  3.38 us
    unnamed x20, local copies, waits for them, and re-layouts  3.35 us
    pallas_call x1, Pallas kernels, early(): pl.pallas_call(early_kernel, grid_spec=pltpu.PrefetchScalarGridSpec(num_s...  2.2 us
  transfers between devices with their start and end apart: 10, of which 6 were waited for; matrix products, arithmetic and copies ran while one was open for 0% of the time, Pallas kernels for 36%

profile of v12, /device:TPU:0, one launch (start us, length us, event | category | flops | bytes accessed | tf_op | source)
XLA Modules:
  0.0 69.3 jit_solution(15008271269954797411)
XLA Ops:
  0.6 1.3 %mul.3.gated_ref.refs_0_.rest_1_ = f32[512,256]{1,0:T(8,128)S(1)} multiply(f32[512,256]{1,0:T(8,128)} %key_ref.3, f32[512,256]{1,0:T(8,128)} %values_ref.3) | non-fusion elementwise | flops 131072 | bytes 1572864 | tf_op jit(solution)/shard_map/mul | solution.py:556
  1.9 0.7 %collective-permute-start.2 = (f32[512,256]{1,0:T(8,128)S(1)}, f32[512,256]{1,0:T(8,128)S(1)}, u32[]{:S(2)}, u32[]{:S(2)}) collective-permute-start(f32[512,256]{1,0:T(8,128)S(1)} %mul.3.gated_ref.refs_0_.rest_1_), channel_id=1, source_target_pairs={{4,8},{8,4},{5,9},{9,5},{6,10},{10,6},{7,11},{11,7},{20,24},{24,20... | collective-permute-start | bytes 1572872 | tf_op jit(solution)/shard_map/ppermute | solution.py:534
  2.6 5.9 %collective-permute-start.3 = (f32[512,256]{1,0:T(8,128)S(1)}, f32[512,256]{1,0:T(8,128)S(1)}, u32[]{:S(2)}, u32[]{:S(2)}) collective-permute-start(f32[512,256]{1,0:T(8,128)S(1)} %mul.3.gated_ref.refs_0_.rest_1_), channel_id=1, source_target_pairs={{0,4},{4,0},{8,12},{12,8},{1,5},{5,1},{9,13},{13,9},{2,6},{6,2},{1... | collective-permute-start | bytes 1572872 | tf_op jit(solution)/shard_map/ppermute | solution.py:534
  8.5 1.0 %copy-done.6 = f32[512,256]{1,0:T(8,128)S(1)} copy-done((f32[512,256]{1,0:T(8,128)S(1)}, f32[512,256]{1,0:T(8,128)}, u32[]{:S(2)}) %copy-start.6) | copy-done | bytes 524312
  9.5 1.0 %copy-done.8 = f32[512,256]{1,0:T(8,128)S(1)} copy-done((f32[512,256]{1,0:T(8,128)S(1)}, f32[512,256]{1,0:T(8,128)}, u32[]{:S(2)}) %copy-start.8) | copy-done | bytes 524312
  10.6 0.1 mix.1
  10.6 0.7 %collective-permute-start = (f32[512,256]{1,0:T(8,128)S(1)}, f32[512,256]{1,0:T(8,128)S(1)}, u32[]{:S(2)}, u32[]{:S(2)}) collective-permute-start(f32[512,256]{1,0:T(8,128)S(1)} %get-tuple-element.44.refs_0_.rest_2_), channel_id=1, source_target_pairs={{4,8},{8,4},{5,9},{9,5},{6,10},{10,6},{7,11},{11,7},{20,24},{24,20... | collective-permute-start | bytes 1572872 | tf_op jit(solution)/shard_map/ppermute | solution.py:534
  11.3 1.7 %collective-permute-start.1 = (f32[512,256]{1,0:T(8,128)S(1)}, f32[512,256]{1,0:T(8,128)S(1)}, u32[]{:S(2)}, u32[]{:S(2)}) collective-permute-start(f32[512,256]{1,0:T(8,128)S(1)} %get-tuple-element.44.refs_0_.rest_2_), channel_id=1, source_target_pairs={{0,4},{4,0},{8,12},{12,8},{1,5},{5,1},{9,13},{13,9},{2,6},{6,2},{1... | collective-permute-start | bytes 1572872 | tf_op jit(solution)/shard_map/ppermute | solution.py:534
  13.1 1.2 %copy-done = bf16[2,4,256,256]{3,2,1,0:T(8,128)(2,1)S(1)} copy-done((bf16[2,4,256,256]{3,2,1,0:T(8,128)(2,1)S(1)}, bf16[2,4,256,256]{3,2,1,0:T(8,128)(2,1)}, u32[]{:S(2)}) %copy-start) | copy-done | bytes 1048600
  14.3 0.7 %dft.10.own_m = f32[1024,256]{1,0:T(8,128)S(1)} custom-call(s32[1]{0:T(128)} %bitcast.pos_ref, bf16[2,4,256,256]{3,2,1,0:T(8,128)(2,1)S(1)} %copy-done, f32[512,256]{1,0:T(8,128)S(1)} %get-tuple-element.44.refs_0_.rest_2_), custom_call_target="tpu_custom_call" | custom-call | flops 402653184 | bytes 1572864 | tf_op jit(solution)/shard_map/dft/pallas_call | solution.py:149
  15.0 0.0 copy-start.1
  15.1 0.0 copy-start.5
  15.1 0.7 %dft.9.own_g = f32[1024,256]{1,0:T(8,128)S(1)} custom-call(s32[1]{0:T(128)} %bitcast.pos_ref, bf16[2,4,256,256]{3,2,1,0:T(8,128)(2,1)S(1)} %copy-done, f32[512,256]{1,0:T(8,128)S(1)} %mul.3.gated_ref.refs_0_.rest_1_), custom_call_target="tpu_custom_call" | custom-call | flops 402653184 | bytes 1572864 | tf_op jit(solution)/shard_map/dft/pallas_call | solution.py:149
  15.8 0.0 collective-permute-done.2.refs_0_.gated_ref
  15.8 5.5 %collective-permute-done.3.refs_0_.refs_1_.gated_ref = f32[512,256]{1,0:T(8,128)S(1)} collective-permute-done((f32[512,256]{1,0:T(8,128)S(1)}, f32[512,256]{1,0:T(8,128)S(1)}, u32[]{:S(2)}, u32[]{:S(2)}) %collective-permute-start.3) | collective-permute-done | bytes 524320 | tf_op jit(solution)/shard_map/ppermute | solution.py:534
  21.3 0.7 collective-permute-start.5
  22.0 1.3 %collective-permute-start.6 = (f32[512,256]{1,0:T(8,128)S(1)}, f32[512,256]{1,0:T(8,128)S(1)}, u32[]{:S(2)}, u32[]{:S(2)}) collective-permute-start(f32[512,256]{1,0:T(8,128)S(1)} %collective-permute-done.2.refs_0_.gated_ref), channel_id=1, source_target_pairs={{4,0},{8,12},{5,1},{9,13},{6,2},{10,14},{7,3},{11,15},{20,16},{24,... | collective-permute-start | bytes 1572872 | tf_op jit(solution)/shard_map/ppermute | solution.py:534
  23.3 0.7 %dft.12.next_g = f32[1024,256]{1,0:T(8,128)S(1)} custom-call(s32[1]{0:T(128)} %bitcast.pos_ref, bf16[2,4,256,256]{3,2,1,0:T(8,128)(2,1)S(1)} %copy-done, f32[512,256]{1,0:T(8,128)S(1)} %collective-permute-done.2.refs_0_.gated_ref, f32[512,256]{1,0:T(8,128)S(1)} %collective-permute-done.3.refs_0_.refs_1_.gated_ref), custom_call_target="tpu_custom_call" | custom-call | flops 402653184 | bytes 1572864 | tf_op jit(solution)/shard_map/dft/pallas_call | solution.py:149
  24.0 0.7 %dft.11.outer_g = f32[1024,256]{1,0:T(8,128)S(1)} custom-call(s32[1]{0:T(128)} %bitcast.pos_ref, bf16[2,4,256,256]{3,2,1,0:T(8,128)(2,1)S(1)} %copy-done, f32[512,256]{1,0:T(8,128)S(1)} %collective-permute-done.3.refs_0_.refs_1_.gated_ref), custom_call_target="tpu_custom_call" | custom-call | flops 402653184 | bytes 1572864 | tf_op jit(solution)/shard_map/dft/pallas_call | solution.py:149
  24.7 6.0 %taps.1.win_own.win_outer.win_next.win_two.win_near.win_far.win_ref = f32[7,1024,256]{2,1,0:T(8,128)S(1)} custom-call(bf16[2,4,256,256]{3,2,1,0:T(8,128)(2,1)S(1)} %copy-done.1, f32[4096,256]{1,0:T(8,128)S(1)} %copy-done.5), custom_call_target="tpu_custom_call" | custom-call | flops 3221225472 | bytes 12582912 | tf_op jit(solution)/shard_map/taps/pallas_call | solution.py:187
  30.7 1.8 %collective-permute-done.1.refs_0_.refs_1_.mixed_ref = f32[512,256]{1,0:T(8,128)S(1)} collective-permute-done((f32[512,256]{1,0:T(8,128)S(1)}, f32[512,256]{1,0:T(8,128)S(1)}, u32[]{:S(2)}, u32[]{:S(2)}) %collective-permute-start.1) | collective-permute-done | bytes 524320 | tf_op jit(solution)/shard_map/ppermute | solution.py:534
  32.5 0.7 %dft.13.outer_m = f32[1024,256]{1,0:T(8,128)S(1)} custom-call(s32[1]{0:T(128)} %bitcast.pos_ref, bf16[2,4,256,256]{3,2,1,0:T(8,128)(2,1)S(1)} %copy-done.1, f32[512,256]{1,0:T(8,128)S(1)} %collective-permute-done.1.refs_0_.refs_1_.mixed_ref), custom_call_target="tpu_custom_call" | custom-call | flops 402653184 | bytes 1572864 | tf_op jit(solution)/shard_map/dft/pallas_call | solution.py:149
  33.2 0.7 %dft.14.next_m.next_ref = f32[1024,256]{1,0:T(8,128)S(1)} custom-call(s32[1]{0:T(128)} %bitcast.pos_ref, bf16[2,4,256,256]{3,2,1,0:T(8,128)(2,1)S(1)} %copy-done.1, f32[512,256]{1,0:T(8,128)S(1)} %collective-permute-done.refs_0_.mixed_ref, f32[512,256]{1,0:T(8,128)S(1)} %collective-permute-done.1.refs_0_.refs_1_.mixed_ref), custom_call_target="tpu_custom_call" | custom-call | flops 402653184 | bytes 1572864 | tf_op jit(solution)/shard_map/dft/pallas_call | solution.py:149
  34.0 0.7 %collective-permute-start.4 = (f32[512,256]{1,0:T(8,128)S(1)}, f32[512,256]{1,0:T(8,128)S(1)}, u32[]{:S(2)}, u32[]{:S(2)}) collective-permute-start(f32[512,256]{1,0:T(8,128)S(1)} %collective-permute-done.1.refs_0_.refs_1_.mixed_ref), channel_id=1, source_target_pairs={{4,8},{8,4},{5,9},{9,5},{6,10},{10,6},{7,11},{11,7},{20,24},{24,20... | collective-permute-start | bytes 1572872 | tf_op jit(solution)/shard_map/ppermute | solution.py:534
  34.7 0.1 sums.3.near_sums
  34.8 0.1 sums.2.side_ref
  34.9 0.0 collective-permute-done.5.refs_0_.gated_ref
  34.9 1.3 %collective-permute-start.7 = (f32[512,256]{1,0:T(8,128)S(1)}, f32[512,256]{1,0:T(8,128)S(1)}, u32[]{:S(2)}, u32[]{:S(2)}) collective-permute-start(f32[512,256]{1,0:T(8,128)S(1)} %collective-permute-done.5.refs_0_.gated_ref), channel_id=1, source_target_pairs={{4,0},{8,12},{5,1},{9,13},{6,2},{10,14},{7,3},{11,15},{20,16},{24,... | collective-permute-start | bytes 1572872 | tf_op jit(solution)/shard_map/ppermute | solution.py:534
  36.2 6.4 %collective-permute-done.6.refs_1_ = f32[512,256]{1,0:T(8,128)S(1)} collective-permute-done((f32[512,256]{1,0:T(8,128)S(1)}, f32[512,256]{1,0:T(8,128)S(1)}, u32[]{:S(2)}, u32[]{:S(2)}) %collective-permute-start.6) | collective-permute-done | bytes 524320 | tf_op jit(solution)/shard_map/ppermute | solution.py:534
  42.6 0.7 %dft.15.two_g = f32[1024,256]{1,0:T(8,128)S(1)} custom-call(s32[1]{0:T(128)} %bitcast.pos_ref, bf16[2,4,256,256]{3,2,1,0:T(8,128)(2,1)S(1)} %copy-done.1, f32[512,256]{1,0:T(8,128)S(1)} %collective-permute-done.5.refs_0_.gated_ref, f32[512,256]{1,0:T(8,128)S(1)} %collective-permute-done.6.refs_1_), custom_call_target="tpu_custom_call" | custom-call | flops 402653184 | bytes 1572864 | tf_op jit(solution)/shard_map/dft/pallas_call | solution.py:149
  43.3 0.0 copy-start.2
  43.3 2.2 %early.1.acc_ref = f32[4,1024,256]{2,1,0:T(8,128)S(1)} custom-call(s32[1]{0:T(128)} %bitcast.pos_ref, f32[7,1024,256]{2,1,0:T(8,128)S(1)} %taps.1.win_own.win_outer.win_next.win_two.win_near.win_far.win_ref, f32[7,1024,256]{2,1,0:T(8,128)S(1)} %taps.1.win_own.win_outer.win_next.win_two.win_near.win_far.win_ref, ...), custom_call_target="tpu_custom_call" | custom-call | flops 26214400 | bytes 15728640 | tf_op jit(solution)/shard_map/early/pallas_call | solution.py:376
  45.6 1.7 %partial.2.made_ref = f32[520,128]{1,0:T(8,128)S(1)} custom-call(s32[1]{0:T(128)} %bitcast.pos_ref, bf16[2,4,256,256]{3,2,1,0:T(8,128)(2,1)S(1)} %copy-done.1, bf16[2,4,256,256]{3,2,1,0:T(8,128)(2,1)S(1)} %copy-done.2, f32[7,1024,256]{2,1,0:T(8,128)S(1)} %taps.1.win_own.win_outer.win_next.win_two.win_near.win_far.win_ref, ...), custom_call_target="tpu_custom_call" | custom-call | flops 402653184 | bytes 1572864 | tf_op jit(solution)/shard_map/partial/pallas_call | solution.py:245
  47.3 1.3 %collective-permute-start.9 = (f32[520,128]{1,0:T(8,128)S(1)}, f32[520,128]{1,0:T(8,128)S(1)}, u32[]{:S(2)}, u32[]{:S(2)}) collective-permute-start(f32[520,128]{1,0:T(8,128)S(1)} %partial.2.made_ref), channel_id=1, source_target_pairs={{4,0},{8,12},{5,1},{9,13},{6,2},{10,14},{7,3},{11,15},{20,16},{24,... | collective-permute-start | bytes 798728 | tf_op jit(solution)/shard_map/ppermute | solution.py:534
  48.6 1.7 %partial.3.made_ref = f32[520,128]{1,0:T(8,128)S(1)} custom-call(s32[1]{0:T(128)} %bitcast.pos_ref, bf16[2,4,256,256]{3,2,1,0:T(8,128)(2,1)S(1)} %copy-done.1, bf16[2,4,256,256]{3,2,1,0:T(8,128)(2,1)S(1)} %copy-done.2, f32[7,1024,256]{2,1,0:T(8,128)S(1)} %taps.1.win_own.win_outer.win_next.win_two.win_near.win_far.win_ref, ...), custom_call_target="tpu_custom_call" | custom-call | flops 402653184 | bytes 1572864 | tf_op jit(solution)/shard_map/partial/pallas_call | solution.py:245
  50.3 0.0 copy-start.7
  50.3 0.0 copy-start.9
  50.3 1.6 %collective-permute-start.8 = (f32[520,128]{1,0:T(8,128)S(1)}, f32[520,128]{1,0:T(8,128)S(1)}, u32[]{:S(2)}, u32[]{:S(2)}) collective-permute-start(f32[520,128]{1,0:T(8,128)S(1)} %partial.3.made_ref), channel_id=1, source_target_pairs={{4,0},{8,12},{5,1},{9,13},{6,2},{10,14},{7,3},{11,15},{20,16},{24,... | collective-permute-start | bytes 798728 | tf_op jit(solution)/shard_map/ppermute | solution.py:534
  51.9 0.7 %dft.17.rest_0_ = f32[1024,256]{1,0:T(8,128)S(1)} custom-call(s32[1]{0:T(128)} %bitcast.pos_ref, bf16[2,4,256,256]{3,2,1,0:T(8,128)(2,1)S(1)} %copy-done.1, f32[512,256]{1,0:T(8,128)S(1)} %collective-permute-done.4.x_ref.refs_0_), custom_call_target="tpu_custom_call" | custom-call | flops 402653184 | bytes 1572864 | tf_op jit(solution)/shard_map/dft/pallas_call | solution.py:149
  52.6 2.6 %collective-permute-done.7.refs_0_ = f32[512,256]{1,0:T(8,128)S(1)} collective-permute-done((f32[512,256]{1,0:T(8,128)S(1)}, f32[512,256]{1,0:T(8,128)S(1)}, u32[]{:S(2)}, u32[]{:S(2)}) %collective-permute-start.7) | collective-permute-done | bytes 524320 | tf_op jit(solution)/shard_map/ppermute | solution.py:534
  55.3 0.7 %dft.16.three_g = f32[1024,256]{1,0:T(8,128)S(1)} custom-call(s32[1]{0:T(128)} %bitcast.pos_ref, bf16[2,4,256,256]{3,2,1,0:T(8,128)(2,1)S(1)} %copy-done.1, f32[512,256]{1,0:T(8,128)S(1)} %collective-permute-done.7.refs_0_), custom_call_target="tpu_custom_call" | custom-call | flops 402653184 | bytes 1572864 | tf_op jit(solution)/shard_map/dft/pallas_call | solution.py:149
  56.0 0.0 copy-start.3
  56.0 0.0 copy-start.4
  56.0 6.0 %late.1 = (f32[512,256]{1,0:T(8,128)}, f32[1024,256]{1,0:T(8,128)}, f32[512,256]{1,0:T(8,128)S(1)}) custom-call(s32[1]{0:T(128)} %bitcast.pos_ref, bf16[2,4,256,256]{3,2,1,0:T(8,128)(2,1)S(1)} %copy-done.2, f32[4,1024,256]{2,1,0:T(8,128)S(1)} %early.1.acc_ref, f32[7,1024,256]{2,1,0:T(8,128)S(1)} %taps.1.win_own.win_outer.win_next.win_two.win_near.win_far.win_ref, ...), custom_call_target="tpu_custom_call" | custom-call | flops 1610612736 | bytes 13107200 | tf_op jit(solution)/shard_map/late/pallas_call | solution.py:473
  62.1 2.4 %collective-permute-done.9.sent_ref = f32[520,128]{1,0:T(8,128)S(1)} collective-permute-done((f32[520,128]{1,0:T(8,128)S(1)}, f32[520,128]{1,0:T(8,128)S(1)}, u32[]{:S(2)}, u32[]{:S(2)}) %collective-permute-start.9) | collective-permute-done | bytes 266272 | tf_op jit(solution)/shard_map/ppermute | solution.py:534
  64.5 0.9 %finish.2 = (f32[512,256]{1,0:T(8,128)}, f32[512,256]{1,0:T(8,128)}, f32[1,256]{1,0:T(1,128)}) custom-call(f32[512,256]{1,0:T(8,128)S(1)} %get-tuple-element.67.back_ref, f32[512,256]{1,0:T(8,128)S(1)} %copy-done.3, f32[512,256]{1,0:T(8,128)S(1)} %copy-done.4, f32[520,128]{1,0:T(8,128)S(1)} %partial.2.made_ref, ...), custom_call_target="tpu_custom_call" | custom-call | flops 196608 | bytes 1572864 | tf_op jit(solution)/shard_map/finish/pallas_call | solution.py:520
  65.3 3.0 %collective-permute-done.8.sent_ref = f32[520,128]{1,0:T(8,128)S(1)} collective-permute-done((f32[520,128]{1,0:T(8,128)S(1)}, f32[520,128]{1,0:T(8,128)S(1)}, u32[]{:S(2)}, u32[]{:S(2)}) %collective-permute-start.8) | collective-permute-done | bytes 266272 | tf_op jit(solution)/shard_map/ppermute | solution.py:534
  68.4 0.9 %finish.3 = (f32[512,256]{1,0:T(8,128)}, f32[512,256]{1,0:T(8,128)}, f32[1,256]{1,0:T(1,128)}) custom-call(f32[512,256]{1,0:T(8,128)S(1)} %get-tuple-element.67.back_ref, f32[512,256]{1,0:T(8,128)S(1)} %copy-done.3, f32[512,256]{1,0:T(8,128)S(1)} %copy-done.4, ...), custom_call_target="tpu_custom_call", output_to_operand_aliasing={{0}: (7, {}), {1}: (8, {}), {2}: (9, {})} | custom-call | flops 196608 | bytes 1572864 | tf_op jit(solution)/shard_map/finish/pallas_call | solution.py:520
  (12 shorter events, 0.0 us)
Async XLA Ops:
  1.9 13.9 %collective-permute-start.2 = (f32[512,256]{1,0:T(8,128)S(1)}, f32[512,256]{1,0:T(8,128)S(1)}, u32[]{:S(2)}, u32[]{:S(2)}) collective-permute-start(f32[512,256]{1,0:T(8,128)S(1)} %mul.3.gated_ref.refs_0_.rest_1_), channel_id=1, source_target_pairs={{4,8},{8,4},{5,9},{9,5},{6,10},{10,6},{7,11},{11,7},{20,24},{24,20... | collective-permute-start | bytes 1572872 | tf_op jit(solution)/shard_map/ppermute | solution.py:534
  2.6 18.7 %collective-permute-start.3 = (f32[512,256]{1,0:T(8,128)S(1)}, f32[512,256]{1,0:T(8,128)S(1)}, u32[]{:S(2)}, u32[]{:S(2)}) collective-permute-start(f32[512,256]{1,0:T(8,128)S(1)} %mul.3.gated_ref.refs_0_.rest_1_), channel_id=1, source_target_pairs={{0,4},{4,0},{8,12},{12,8},{1,5},{5,1},{9,13},{13,9},{2,6},{6,2},{1... | collective-permute-start | bytes 1572872 | tf_op jit(solution)/shard_map/ppermute | solution.py:534
  8.5 1.0 %copy-start.6 = (f32[512,256]{1,0:T(8,128)S(1)}, f32[512,256]{1,0:T(8,128)}, u32[]{:S(2)}) copy-start(f32[512,256]{1,0:T(8,128)} %rest_4_.1) | copy-start | bytes 1572868
  9.5 1.0 %copy-start.8 = (f32[512,256]{1,0:T(8,128)S(1)}, f32[512,256]{1,0:T(8,128)}, u32[]{:S(2)}) copy-start(f32[512,256]{1,0:T(8,128)} %query_ref.1) | copy-start | bytes 1572868
  10.6 20.1 %collective-permute-start = (f32[512,256]{1,0:T(8,128)S(1)}, f32[512,256]{1,0:T(8,128)S(1)}, u32[]{:S(2)}, u32[]{:S(2)}) collective-permute-start(f32[512,256]{1,0:T(8,128)S(1)} %get-tuple-element.44.refs_0_.rest_2_), channel_id=1, source_target_pairs={{4,8},{8,4},{5,9},{9,5},{6,10},{10,6},{7,11},{11,7},{20,24},{24,20... | collective-permute-start | bytes 1572872 | tf_op jit(solution)/shard_map/ppermute | solution.py:534
  11.3 21.2 %collective-permute-start.1 = (f32[512,256]{1,0:T(8,128)S(1)}, f32[512,256]{1,0:T(8,128)S(1)}, u32[]{:S(2)}, u32[]{:S(2)}) collective-permute-start(f32[512,256]{1,0:T(8,128)S(1)} %get-tuple-element.44.refs_0_.rest_2_), channel_id=1, source_target_pairs={{0,4},{4,0},{8,12},{12,8},{1,5},{5,1},{9,13},{13,9},{2,6},{6,2},{1... | collective-permute-start | bytes 1572872 | tf_op jit(solution)/shard_map/ppermute | solution.py:534
  13.1 1.2 %copy-start = (bf16[2,4,256,256]{3,2,1,0:T(8,128)(2,1)S(1)}, bf16[2,4,256,256]{3,2,1,0:T(8,128)(2,1)}, u32[]{:S(2)}) copy-start(bf16[2,4,256,256]{3,2,1,0:T(8,128)(2,1)} %constant.9.clone.table_ref) | copy-start | bytes 3145732
  15.0 9.7 %copy-start.1 = (bf16[2,4,256,256]{3,2,1,0:T(8,128)(2,1)S(1)}, bf16[2,4,256,256]{3,2,1,0:T(8,128)(2,1)}, u32[]{:S(2)}) copy-start(bf16[2,4,256,256]{3,2,1,0:T(8,128)(2,1)} %constant.9.clone.table_ref) | copy-start | bytes 3145732
  15.1 9.7 %copy-start.5 = (f32[4096,256]{1,0:T(8,128)S(1)}, f32[4096,256]{1,0:T(8,128)}, u32[]{:S(2)}) copy-start(f32[4096,256]{1,0:T(8,128)} %x_ref) | copy-start | bytes 12582916
  21.3 13.6 %collective-permute-start.5 = (f32[512,256]{1,0:T(8,128)S(1)}, f32[512,256]{1,0:T(8,128)S(1)}, u32[]{:S(2)}, u32[]{:S(2)}) collective-permute-start(f32[512,256]{1,0:T(8,128)S(1)} %collective-permute-done.3.refs_0_.refs_1_.gated_ref), channel_id=1, source_target_pairs={{4,8},{8,4},{5,9},{9,5},{6,10},{10,6},{7,11},{11,7},{20,24},{24,20... | collective-permute-start | bytes 1572872 | tf_op jit(solution)/shard_map/ppermute | solution.py:534
  22.0 20.6 %collective-permute-start.6 = (f32[512,256]{1,0:T(8,128)S(1)}, f32[512,256]{1,0:T(8,128)S(1)}, u32[]{:S(2)}, u32[]{:S(2)}) collective-permute-start(f32[512,256]{1,0:T(8,128)S(1)} %collective-permute-done.2.refs_0_.gated_ref), channel_id=1, source_target_pairs={{4,0},{8,12},{5,1},{9,13},{6,2},{10,14},{7,3},{11,15},{20,16},{24,... | collective-permute-start | bytes 1572872 | tf_op jit(solution)/shard_map/ppermute | solution.py:534
  34.0 11.6 %collective-permute-start.4 = (f32[512,256]{1,0:T(8,128)S(1)}, f32[512,256]{1,0:T(8,128)S(1)}, u32[]{:S(2)}, u32[]{:S(2)}) collective-permute-start(f32[512,256]{1,0:T(8,128)S(1)} %collective-permute-done.1.refs_0_.refs_1_.mixed_ref), channel_id=1, source_target_pairs={{4,8},{8,4},{5,9},{9,5},{6,10},{10,6},{7,11},{11,7},{20,24},{24,20... | collective-permute-start | bytes 1572872 | tf_op jit(solution)/shard_map/ppermute | solution.py:534
  34.9 20.4 %collective-permute-start.7 = (f32[512,256]{1,0:T(8,128)S(1)}, f32[512,256]{1,0:T(8,128)S(1)}, u32[]{:S(2)}, u32[]{:S(2)}) collective-permute-start(f32[512,256]{1,0:T(8,128)S(1)} %collective-permute-done.5.refs_0_.gated_ref), channel_id=1, source_target_pairs={{4,0},{8,12},{5,1},{9,13},{6,2},{10,14},{7,3},{11,15},{20,16},{24,... | collective-permute-start | bytes 1572872 | tf_op jit(solution)/shard_map/ppermute | solution.py:534
  43.3 2.2 %copy-start.2 = (bf16[2,4,256,256]{3,2,1,0:T(8,128)(2,1)S(1)}, bf16[2,4,256,256]{3,2,1,0:T(8,128)(2,1)}, u32[]{:S(2)}) copy-start(bf16[2,4,256,256]{3,2,1,0:T(8,128)(2,1)} %constant.10.clone.inverse_ref) | copy-start | bytes 3145732
  47.3 17.2 %collective-permute-start.9 = (f32[520,128]{1,0:T(8,128)S(1)}, f32[520,128]{1,0:T(8,128)S(1)}, u32[]{:S(2)}, u32[]{:S(2)}) collective-permute-start(f32[520,128]{1,0:T(8,128)S(1)} %partial.2.made_ref), channel_id=1, source_target_pairs={{4,0},{8,12},{5,1},{9,13},{6,2},{10,14},{7,3},{11,15},{20,16},{24,... | collective-permute-start | bytes 798728 | tf_op jit(solution)/shard_map/ppermute | solution.py:534
  50.3 5.7 %copy-start.7 = (f32[512,256]{1,0:T(8,128)S(1)}, f32[512,256]{1,0:T(8,128)}, u32[]{:S(2)}) copy-start(f32[512,256]{1,0:T(8,128)} %rest_4_.1) | copy-start | bytes 1572868
  50.3 5.7 %copy-start.9 = (f32[256]{0:T(256)S(1)}, f32[256]{0:T(256)}, u32[]{:S(2)}) copy-start(f32[256]{0:T(256)} %param.12) | copy-start | bytes 3076
  50.3 18.1 %collective-permute-start.8 = (f32[520,128]{1,0:T(8,128)S(1)}, f32[520,128]{1,0:T(8,128)S(1)}, u32[]{:S(2)}, u32[]{:S(2)}) collective-permute-start(f32[520,128]{1,0:T(8,128)S(1)} %partial.3.made_ref), channel_id=1, source_target_pairs={{4,0},{8,12},{5,1},{9,13},{6,2},{10,14},{7,3},{11,15},{20,16},{24,... | collective-permute-start | bytes 798728 | tf_op jit(solution)/shard_map/ppermute | solution.py:534
  56.0 8.5 %copy-start.3 = (f32[512,256]{1,0:T(8,128)S(1)}, f32[512,256]{1,0:T(8,128)}, u32[]{:S(2)}) copy-start(f32[512,256]{1,0:T(8,128)} %key_ref.3) | copy-start | bytes 1572868
  56.0 8.5 %copy-start.4 = (f32[512,256]{1,0:T(8,128)S(1)}, f32[512,256]{1,0:T(8,128)}, u32[]{:S(2)}) copy-start(f32[512,256]{1,0:T(8,128)} %values_ref.3) | copy-start | bytes 1572868

commit v13 on v12

--- a/solution.py
+++ b/solution.py
@@ -40,6 +40,10 @@
 def dot3(table_ref, group, high, low):
     t_high, t_low = table_ref[0, group], table_ref[1, group]
     dot = functools.partial(jnp.dot, preferred_element_type=jnp.float32)
+    width = high.shape[1]
+    if width <= 128:
+        both = dot(t_high, jnp.concatenate([high, low], axis=1))
+        return both[:, :width] + both[:, width:] + dot(t_low, high)
     return dot(t_high, high) + dot(t_high, low) + dot(t_low, high)
 
 

time: 69.7 us -> 69.4 us (level)
  Pallas kernels: 26.1 us -> 25.4 us
where the time goes in v13:
time: 69.4 us; the launch traced here: 68.9 us
  Pallas kernels  25.4 us (37%)
  waiting for transfers between devices  22.3 us (32%)
  starting transfers between devices  15.7 us (23%)
  local copies, waits for them, and re-layouts  3.35 us (5%)
  other arithmetic  1.27 us (2%)
  between operations  0.93 us (1%)
    ppermute x10, waiting for transfers between devices, send(): return lax.ppermute(x, 'ctx', list(pairs))  22.3 us
    ppermute x10, starting transfers between devices, send(): return lax.ppermute(x, 'ctx', list(pairs))  15.7 us
    pallas_call x9, Pallas kernels, dft(): pl.pallas_call(functools.partial(dft_kernel, choose), grid_spec=pltpu.Pre...  6.47 us
    pallas_call x1, Pallas kernels, late(): pl.pallas_call(late_kernel, grid_spec=pltpu.PrefetchScalarGridSpec(num_sc...  6.03 us
    pallas_call x1, Pallas kernels, taps_spectra(): pl.pallas_call(taps_kernel, grid=(blocks,), in_specs=[whole_spec(table.sh...  5.95 us
    unnamed x20, local copies, waits for them, and re-layouts  3.35 us
    pallas_call x2, Pallas kernels, back_partial(): pl.pallas_call(partial_kernel, grid_spec=pltpu.PrefetchScalarGridSpec(num...  2.73 us
    pallas_call x1, Pallas kernels, early(): pl.pallas_call(early_kernel, grid_spec=pltpu.PrefetchScalarGridSpec(num_s...  2.2 us
  transfers between devices with their start and end apart: 10, of which 6 were waited for; matrix products, arithmetic and copies ran while one was open for 0% of the time, Pallas kernels for 36%

profile of v13, /device:TPU:0, one launch (start us, length us, event | category | flops | bytes accessed | tf_op | source)
XLA Modules:
  0.0 68.9 jit_solution(4333036224664101934)
XLA Ops:
  0.6 1.3 %mul.3.gated_ref.refs_0_.rest_1_ = f32[512,256]{1,0:T(8,128)S(1)} multiply(f32[512,256]{1,0:T(8,128)} %key_ref.3, f32[512,256]{1,0:T(8,128)} %values_ref.3) | non-fusion elementwise | flops 131072 | bytes 1572864 | tf_op jit(solution)/shard_map/mul | solution.py:560
  1.9 0.7 %collective-permute-start.2 = (f32[512,256]{1,0:T(8,128)S(1)}, f32[512,256]{1,0:T(8,128)S(1)}, u32[]{:S(2)}, u32[]{:S(2)}) collective-permute-start(f32[512,256]{1,0:T(8,128)S(1)} %mul.3.gated_ref.refs_0_.rest_1_), channel_id=1, source_target_pairs={{4,8},{8,4},{5,9},{9,5},{6,10},{10,6},{7,11},{11,7},{20,24},{24,20... | collective-permute-start | bytes 1572872 | tf_op jit(solution)/shard_map/ppermute | solution.py:538
  2.6 5.9 %collective-permute-start.3 = (f32[512,256]{1,0:T(8,128)S(1)}, f32[512,256]{1,0:T(8,128)S(1)}, u32[]{:S(2)}, u32[]{:S(2)}) collective-permute-start(f32[512,256]{1,0:T(8,128)S(1)} %mul.3.gated_ref.refs_0_.rest_1_), channel_id=1, source_target_pairs={{0,4},{4,0},{8,12},{12,8},{1,5},{5,1},{9,13},{13,9},{2,6},{6,2},{1... | collective-permute-start | bytes 1572872 | tf_op jit(solution)/shard_map/ppermute | solution.py:538
  8.5 1.0 %copy-done.6 = f32[512,256]{1,0:T(8,128)S(1)} copy-done((f32[512,256]{1,0:T(8,128)S(1)}, f32[512,256]{1,0:T(8,128)}, u32[]{:S(2)}) %copy-start.6) | copy-done | bytes 524312
  9.5 1.0 %copy-done.8 = f32[512,256]{1,0:T(8,128)S(1)} copy-done((f32[512,256]{1,0:T(8,128)S(1)}, f32[512,256]{1,0:T(8,128)}, u32[]{:S(2)}) %copy-start.8) | copy-done | bytes 524312
  10.6 0.1 mix.1
  10.6 0.7 %collective-permute-start = (f32[512,256]{1,0:T(8,128)S(1)}, f32[512,256]{1,0:T(8,128)S(1)}, u32[]{:S(2)}, u32[]{:S(2)}) collective-permute-start(f32[512,256]{1,0:T(8,128)S(1)} %get-tuple-element.44.refs_0_.rest_2_), channel_id=1, source_target_pairs={{4,8},{8,4},{5,9},{9,5},{6,10},{10,6},{7,11},{11,7},{20,24},{24,20... | collective-permute-start | bytes 1572872 | tf_op jit(solution)/shard_map/ppermute | solution.py:538
  11.3 1.7 %collective-permute-start.1 = (f32[512,256]{1,0:T(8,128)S(1)}, f32[512,256]{1,0:T(8,128)S(1)}, u32[]{:S(2)}, u32[]{:S(2)}) collective-permute-start(f32[512,256]{1,0:T(8,128)S(1)} %get-tuple-element.44.refs_0_.rest_2_), channel_id=1, source_target_pairs={{0,4},{4,0},{8,12},{12,8},{1,5},{5,1},{9,13},{13,9},{2,6},{6,2},{1... | collective-permute-start | bytes 1572872 | tf_op jit(solution)/shard_map/ppermute | solution.py:538
  13.1 1.2 %copy-done = bf16[2,4,256,256]{3,2,1,0:T(8,128)(2,1)S(1)} copy-done((bf16[2,4,256,256]{3,2,1,0:T(8,128)(2,1)S(1)}, bf16[2,4,256,256]{3,2,1,0:T(8,128)(2,1)}, u32[]{:S(2)}) %copy-start) | copy-done | bytes 1048600
  14.3 0.7 %dft.10.own_m = f32[1024,256]{1,0:T(8,128)S(1)} custom-call(s32[1]{0:T(128)} %bitcast.pos_ref, bf16[2,4,256,256]{3,2,1,0:T(8,128)(2,1)S(1)} %copy-done, f32[512,256]{1,0:T(8,128)S(1)} %get-tuple-element.44.refs_0_.rest_2_), custom_call_target="tpu_custom_call" | custom-call | flops 402653184 | bytes 1572864 | tf_op jit(solution)/shard_map/dft/pallas_call | solution.py:153
  15.0 0.0 copy-start.1
  15.0 0.0 copy-start.5
  15.1 0.7 %dft.9.own_g = f32[1024,256]{1,0:T(8,128)S(1)} custom-call(s32[1]{0:T(128)} %bitcast.pos_ref, bf16[2,4,256,256]{3,2,1,0:T(8,128)(2,1)S(1)} %copy-done, f32[512,256]{1,0:T(8,128)S(1)} %mul.3.gated_ref.refs_0_.rest_1_), custom_call_target="tpu_custom_call" | custom-call | flops 402653184 | bytes 1572864 | tf_op jit(solution)/shard_map/dft/pallas_call | solution.py:153
  15.8 0.0 collective-permute-done.2.refs_0_.gated_ref
  15.8 5.5 %collective-permute-done.3.refs_0_.refs_1_.gated_ref = f32[512,256]{1,0:T(8,128)S(1)} collective-permute-done((f32[512,256]{1,0:T(8,128)S(1)}, f32[512,256]{1,0:T(8,128)S(1)}, u32[]{:S(2)}, u32[]{:S(2)}) %collective-permute-start.3) | collective-permute-done | bytes 524320 | tf_op jit(solution)/shard_map/ppermute | solution.py:538
  21.3 0.7 collective-permute-start.5
  22.0 1.3 %collective-permute-start.6 = (f32[512,256]{1,0:T(8,128)S(1)}, f32[512,256]{1,0:T(8,128)S(1)}, u32[]{:S(2)}, u32[]{:S(2)}) collective-permute-start(f32[512,256]{1,0:T(8,128)S(1)} %collective-permute-done.2.refs_0_.gated_ref), channel_id=1, source_target_pairs={{4,0},{8,12},{5,1},{9,13},{6,2},{10,14},{7,3},{11,15},{20,16},{24,... | collective-permute-start | bytes 1572872 | tf_op jit(solution)/shard_map/ppermute | solution.py:538
  23.3 0.7 %dft.12.next_g = f32[1024,256]{1,0:T(8,128)S(1)} custom-call(s32[1]{0:T(128)} %bitcast.pos_ref, bf16[2,4,256,256]{3,2,1,0:T(8,128)(2,1)S(1)} %copy-done, f32[512,256]{1,0:T(8,128)S(1)} %collective-permute-done.2.refs_0_.gated_ref, f32[512,256]{1,0:T(8,128)S(1)} %collective-permute-done.3.refs_0_.refs_1_.gated_ref), custom_call_target="tpu_custom_call" | custom-call | flops 402653184 | bytes 1572864 | tf_op jit(solution)/shard_map/dft/pallas_call | solution.py:153
  24.0 0.7 %dft.11.outer_g = f32[1024,256]{1,0:T(8,128)S(1)} custom-call(s32[1]{0:T(128)} %bitcast.pos_ref, bf16[2,4,256,256]{3,2,1,0:T(8,128)(2,1)S(1)} %copy-done, f32[512,256]{1,0:T(8,128)S(1)} %collective-permute-done.3.refs_0_.refs_1_.gated_ref), custom_call_target="tpu_custom_call" | custom-call | flops 402653184 | bytes 1572864 | tf_op jit(solution)/shard_map/dft/pallas_call | solution.py:153
  24.7 5.9 %taps.1.win_own.win_outer.win_next.win_two.win_near.win_far.win_ref = f32[7,1024,256]{2,1,0:T(8,128)S(1)} custom-call(bf16[2,4,256,256]{3,2,1,0:T(8,128)(2,1)S(1)} %copy-done.1, f32[4096,256]{1,0:T(8,128)S(1)} %copy-done.5), custom_call_target="tpu_custom_call" | custom-call | flops 3221225472 | bytes 12582912 | tf_op jit(solution)/shard_map/taps/pallas_call | solution.py:191
  30.7 1.8 %collective-permute-done.1.refs_0_.refs_1_.mixed_ref = f32[512,256]{1,0:T(8,128)S(1)} collective-permute-done((f32[512,256]{1,0:T(8,128)S(1)}, f32[512,256]{1,0:T(8,128)S(1)}, u32[]{:S(2)}, u32[]{:S(2)}) %collective-permute-start.1) | collective-permute-done | bytes 524320 | tf_op jit(solution)/shard_map/ppermute | solution.py:538
  32.5 0.7 %dft.13.outer_m = f32[1024,256]{1,0:T(8,128)S(1)} custom-call(s32[1]{0:T(128)} %bitcast.pos_ref, bf16[2,4,256,256]{3,2,1,0:T(8,128)(2,1)S(1)} %copy-done.1, f32[512,256]{1,0:T(8,128)S(1)} %collective-permute-done.1.refs_0_.refs_1_.mixed_ref), custom_call_target="tpu_custom_call" | custom-call | flops 402653184 | bytes 1572864 | tf_op jit(solution)/shard_map/dft/pallas_call | solution.py:153
  33.2 0.7 %dft.14.next_m.next_ref = f32[1024,256]{1,0:T(8,128)S(1)} custom-call(s32[1]{0:T(128)} %bitcast.pos_ref, bf16[2,4,256,256]{3,2,1,0:T(8,128)(2,1)S(1)} %copy-done.1, f32[512,256]{1,0:T(8,128)S(1)} %collective-permute-done.refs_0_.mixed_ref, f32[512,256]{1,0:T(8,128)S(1)} %collective-permute-done.1.refs_0_.refs_1_.mixed_ref), custom_call_target="tpu_custom_call" | custom-call | flops 402653184 | bytes 1572864 | tf_op jit(solution)/shard_map/dft/pallas_call | solution.py:153
  34.0 0.7 %collective-permute-start.4 = (f32[512,256]{1,0:T(8,128)S(1)}, f32[512,256]{1,0:T(8,128)S(1)}, u32[]{:S(2)}, u32[]{:S(2)}) collective-permute-start(f32[512,256]{1,0:T(8,128)S(1)} %collective-permute-done.1.refs_0_.refs_1_.mixed_ref), channel_id=1, source_target_pairs={{4,8},{8,4},{5,9},{9,5},{6,10},{10,6},{7,11},{11,7},{20,24},{24,20... | collective-permute-start | bytes 1572872 | tf_op jit(solution)/shard_map/ppermute | solution.py:538
  34.7 0.1 sums.3.near_sums
  34.8 0.1 sums.2.side_ref
  34.9 0.0 collective-permute-done.5.refs_0_.gated_ref
  34.9 1.3 %collective-permute-start.7 = (f32[512,256]{1,0:T(8,128)S(1)}, f32[512,256]{1,0:T(8,128)S(1)}, u32[]{:S(2)}, u32[]{:S(2)}) collective-permute-start(f32[512,256]{1,0:T(8,128)S(1)} %collective-permute-done.5.refs_0_.gated_ref), channel_id=1, source_target_pairs={{4,0},{8,12},{5,1},{9,13},{6,2},{10,14},{7,3},{11,15},{20,16},{24,... | collective-permute-start | bytes 1572872 | tf_op jit(solution)/shard_map/ppermute | solution.py:538
  36.2 6.4 %collective-permute-done.6.refs_1_ = f32[512,256]{1,0:T(8,128)S(1)} collective-permute-done((f32[512,256]{1,0:T(8,128)S(1)}, f32[512,256]{1,0:T(8,128)S(1)}, u32[]{:S(2)}, u32[]{:S(2)}) %collective-permute-start.6) | collective-permute-done | bytes 524320 | tf_op jit(solution)/shard_map/ppermute | solution.py:538
  42.6 0.7 %dft.15.two_g = f32[1024,256]{1,0:T(8,128)S(1)} custom-call(s32[1]{0:T(128)} %bitcast.pos_ref, bf16[2,4,256,256]{3,2,1,0:T(8,128)(2,1)S(1)} %copy-done.1, f32[512,256]{1,0:T(8,128)S(1)} %collective-permute-done.5.refs_0_.gated_ref, f32[512,256]{1,0:T(8,128)S(1)} %collective-permute-done.6.refs_1_), custom_call_target="tpu_custom_call" | custom-call | flops 402653184 | bytes 1572864 | tf_op jit(solution)/shard_map/dft/pallas_call | solution.py:153
  43.3 0.0 copy-start.2
  43.3 2.2 %early.1.acc_ref = f32[4,1024,256]{2,1,0:T(8,128)S(1)} custom-call(s32[1]{0:T(128)} %bitcast.pos_ref, f32[7,1024,256]{2,1,0:T(8,128)S(1)} %taps.1.win_own.win_outer.win_next.win_two.win_near.win_far.win_ref, f32[7,1024,256]{2,1,0:T(8,128)S(1)} %taps.1.win_own.win_outer.win_next.win_two.win_near.win_far.win_ref, ...), custom_call_target="tpu_custom_call" | custom-call | flops 26214400 | bytes 15728640 | tf_op jit(solution)/shard_map/early/pallas_call | solution.py:380
  45.6 1.4 %partial.2.made_ref = f32[520,128]{1,0:T(8,128)S(1)} custom-call(s32[1]{0:T(128)} %bitcast.pos_ref, bf16[2,4,256,256]{3,2,1,0:T(8,128)(2,1)S(1)} %copy-done.1, bf16[2,4,256,256]{3,2,1,0:T(8,128)(2,1)S(1)} %copy-done.2, f32[7,1024,256]{2,1,0:T(8,128)S(1)} %taps.1.win_own.win_outer.win_next.win_two.win_near.win_far.win_ref, ...), custom_call_target="tpu_custom_call" | custom-call | flops 402653184 | bytes 1572864 | tf_op jit(solution)/shard_map/partial/pallas_call | solution.py:249
  46.9 1.3 %collective-permute-start.9 = (f32[520,128]{1,0:T(8,128)S(1)}, f32[520,128]{1,0:T(8,128)S(1)}, u32[]{:S(2)}, u32[]{:S(2)}) collective-permute-start(f32[520,128]{1,0:T(8,128)S(1)} %partial.2.made_ref), channel_id=1, source_target_pairs={{4,0},{8,12},{5,1},{9,13},{6,2},{10,14},{7,3},{11,15},{20,16},{24,... | collective-permute-start | bytes 798728 | tf_op jit(solution)/shard_map/ppermute | solution.py:538
  48.2 1.4 %partial.3.made_ref = f32[520,128]{1,0:T(8,128)S(1)} custom-call(s32[1]{0:T(128)} %bitcast.pos_ref, bf16[2,4,256,256]{3,2,1,0:T(8,128)(2,1)S(1)} %copy-done.1, bf16[2,4,256,256]{3,2,1,0:T(8,128)(2,1)S(1)} %copy-done.2, f32[7,1024,256]{2,1,0:T(8,128)S(1)} %taps.1.win_own.win_outer.win_next.win_two.win_near.win_far.win_ref, ...), custom_call_target="tpu_custom_call" | custom-call | flops 402653184 | bytes 1572864 | tf_op jit(solution)/shard_map/partial/pallas_call | solution.py:249
  49.6 0.0 copy-start.7
  49.6 0.0 copy-start.9
  49.6 1.4 %collective-permute-start.8 = (f32[520,128]{1,0:T(8,128)S(1)}, f32[520,128]{1,0:T(8,128)S(1)}, u32[]{:S(2)}, u32[]{:S(2)}) collective-permute-start(f32[520,128]{1,0:T(8,128)S(1)} %partial.3.made_ref), channel_id=1, source_target_pairs={{4,0},{8,12},{5,1},{9,13},{6,2},{10,14},{7,3},{11,15},{20,16},{24,... | collective-permute-start | bytes 798728 | tf_op jit(solution)/shard_map/ppermute | solution.py:538
  51.1 0.7 %dft.17.rest_0_ = f32[1024,256]{1,0:T(8,128)S(1)} custom-call(s32[1]{0:T(128)} %bitcast.pos_ref, bf16[2,4,256,256]{3,2,1,0:T(8,128)(2,1)S(1)} %copy-done.1, f32[512,256]{1,0:T(8,128)S(1)} %collective-permute-done.4.x_ref.refs_0_), custom_call_target="tpu_custom_call" | custom-call | flops 402653184 | bytes 1572864 | tf_op jit(solution)/shard_map/dft/pallas_call | solution.py:153
  51.8 3.5 %collective-permute-done.7.refs_0_ = f32[512,256]{1,0:T(8,128)S(1)} collective-permute-done((f32[512,256]{1,0:T(8,128)S(1)}, f32[512,256]{1,0:T(8,128)S(1)}, u32[]{:S(2)}, u32[]{:S(2)}) %collective-permute-start.7) | collective-permute-done | bytes 524320 | tf_op jit(solution)/shard_map/ppermute | solution.py:538
  55.3 0.7 %dft.16.three_g = f32[1024,256]{1,0:T(8,128)S(1)} custom-call(s32[1]{0:T(128)} %bitcast.pos_ref, bf16[2,4,256,256]{3,2,1,0:T(8,128)(2,1)S(1)} %copy-done.1, f32[512,256]{1,0:T(8,128)S(1)} %collective-permute-done.7.refs_0_), custom_call_target="tpu_custom_call" | custom-call | flops 402653184 | bytes 1572864 | tf_op jit(solution)/shard_map/dft/pallas_call | solution.py:153
  56.0 0.0 copy-start.3
  56.0 0.0 copy-start.4
  56.0 6.0 %late.1 = (f32[512,256]{1,0:T(8,128)}, f32[1024,256]{1,0:T(8,128)}, f32[512,256]{1,0:T(8,128)S(1)}) custom-call(s32[1]{0:T(128)} %bitcast.pos_ref, bf16[2,4,256,256]{3,2,1,0:T(8,128)(2,1)S(1)} %copy-done.2, f32[4,1024,256]{2,1,0:T(8,128)S(1)} %early.1.acc_ref, f32[7,1024,256]{2,1,0:T(8,128)S(1)} %taps.1.win_own.win_outer.win_next.win_two.win_near.win_far.win_ref, ...), custom_call_target="tpu_custom_call" | custom-call | flops 1610612736 | bytes 13107200 | tf_op jit(solution)/shard_map/late/pallas_call | solution.py:477
  62.1 2.1 %collective-permute-done.9.sent_ref = f32[520,128]{1,0:T(8,128)S(1)} collective-permute-done((f32[520,128]{1,0:T(8,128)S(1)}, f32[520,128]{1,0:T(8,128)S(1)}, u32[]{:S(2)}, u32[]{:S(2)}) %collective-permute-start.9) | collective-permute-done | bytes 266272 | tf_op jit(solution)/shard_map/ppermute | solution.py:538
  64.2 0.9 %finish.2 = (f32[512,256]{1,0:T(8,128)}, f32[512,256]{1,0:T(8,128)}, f32[1,256]{1,0:T(1,128)}) custom-call(f32[512,256]{1,0:T(8,128)S(1)} %get-tuple-element.67.back_ref, f32[512,256]{1,0:T(8,128)S(1)} %copy-done.3, f32[512,256]{1,0:T(8,128)S(1)} %copy-done.4, f32[520,128]{1,0:T(8,128)S(1)} %partial.2.made_ref, ...), custom_call_target="tpu_custom_call" | custom-call | flops 196608 | bytes 1572864 | tf_op jit(solution)/shard_map/finish/pallas_call | solution.py:524
  65.0 3.0 %collective-permute-done.8.sent_ref = f32[520,128]{1,0:T(8,128)S(1)} collective-permute-done((f32[520,128]{1,0:T(8,128)S(1)}, f32[520,128]{1,0:T(8,128)S(1)}, u32[]{:S(2)}, u32[]{:S(2)}) %collective-permute-start.8) | collective-permute-done | bytes 266272 | tf_op jit(solution)/shard_map/ppermute | solution.py:538
  68.1 0.9 %finish.3 = (f32[512,256]{1,0:T(8,128)}, f32[512,256]{1,0:T(8,128)}, f32[1,256]{1,0:T(1,128)}) custom-call(f32[512,256]{1,0:T(8,128)S(1)} %get-tuple-element.67.back_ref, f32[512,256]{1,0:T(8,128)S(1)} %copy-done.3, f32[512,256]{1,0:T(8,128)S(1)} %copy-done.4, ...), custom_call_target="tpu_custom_call", output_to_operand_aliasing={{0}: (7, {}), {1}: (8, {}), {2}: (9, {})} | custom-call | flops 196608 | bytes 1572864 | tf_op jit(solution)/shard_map/finish/pallas_call | solution.py:524
  (12 shorter events, 0.0 us)
Async XLA Ops:
  1.9 13.9 %collective-permute-start.2 = (f32[512,256]{1,0:T(8,128)S(1)}, f32[512,256]{1,0:T(8,128)S(1)}, u32[]{:S(2)}, u32[]{:S(2)}) collective-permute-start(f32[512,256]{1,0:T(8,128)S(1)} %mul.3.gated_ref.refs_0_.rest_1_), channel_id=1, source_target_pairs={{4,8},{8,4},{5,9},{9,5},{6,10},{10,6},{7,11},{11,7},{20,24},{24,20... | collective-permute-start | bytes 1572872 | tf_op jit(solution)/shard_map/ppermute | solution.py:538
  2.6 18.7 %collective-permute-start.3 = (f32[512,256]{1,0:T(8,128)S(1)}, f32[512,256]{1,0:T(8,128)S(1)}, u32[]{:S(2)}, u32[]{:S(2)}) collective-permute-start(f32[512,256]{1,0:T(8,128)S(1)} %mul.3.gated_ref.refs_0_.rest_1_), channel_id=1, source_target_pairs={{0,4},{4,0},{8,12},{12,8},{1,5},{5,1},{9,13},{13,9},{2,6},{6,2},{1... | collective-permute-start | bytes 1572872 | tf_op jit(solution)/shard_map/ppermute | solution.py:538
  8.5 1.0 %copy-start.6 = (f32[512,256]{1,0:T(8,128)S(1)}, f32[512,256]{1,0:T(8,128)}, u32[]{:S(2)}) copy-start(f32[512,256]{1,0:T(8,128)} %rest_4_.1) | copy-start | bytes 1572868
  9.5 1.0 %copy-start.8 = (f32[512,256]{1,0:T(8,128)S(1)}, f32[512,256]{1,0:T(8,128)}, u32[]{:S(2)}) copy-start(f32[512,256]{1,0:T(8,128)} %query_ref.1) | copy-start | bytes 1572868
  10.6 20.1 %collective-permute-start = (f32[512,256]{1,0:T(8,128)S(1)}, f32[512,256]{1,0:T(8,128)S(1)}, u32[]{:S(2)}, u32[]{:S(2)}) collective-permute-start(f32[512,256]{1,0:T(8,128)S(1)} %get-tuple-element.44.refs_0_.rest_2_), channel_id=1, source_target_pairs={{4,8},{8,4},{5,9},{9,5},{6,10},{10,6},{7,11},{11,7},{20,24},{24,20... | collective-permute-start | bytes 1572872 | tf_op jit(solution)/shard_map/ppermute | solution.py:538
  11.3 21.2 %collective-permute-start.1 = (f32[512,256]{1,0:T(8,128)S(1)}, f32[512,256]{1,0:T(8,128)S(1)}, u32[]{:S(2)}, u32[]{:S(2)}) collective-permute-start(f32[512,256]{1,0:T(8,128)S(1)} %get-tuple-element.44.refs_0_.rest_2_), channel_id=1, source_target_pairs={{0,4},{4,0},{8,12},{12,8},{1,5},{5,1},{9,13},{13,9},{2,6},{6,2},{1... | collective-permute-start | bytes 1572872 | tf_op jit(solution)/shard_map/ppermute | solution.py:538
  13.1 1.2 %copy-start = (bf16[2,4,256,256]{3,2,1,0:T(8,128)(2,1)S(1)}, bf16[2,4,256,256]{3,2,1,0:T(8,128)(2,1)}, u32[]{:S(2)}) copy-start(bf16[2,4,256,256]{3,2,1,0:T(8,128)(2,1)} %constant.9.clone.table_ref) | copy-start | bytes 3145732
  15.0 9.7 %copy-start.1 = (bf16[2,4,256,256]{3,2,1,0:T(8,128)(2,1)S(1)}, bf16[2,4,256,256]{3,2,1,0:T(8,128)(2,1)}, u32[]{:S(2)}) copy-start(bf16[2,4,256,256]{3,2,1,0:T(8,128)(2,1)} %constant.9.clone.table_ref) | copy-start | bytes 3145732
  15.0 9.7 %copy-start.5 = (f32[4096,256]{1,0:T(8,128)S(1)}, f32[4096,256]{1,0:T(8,128)}, u32[]{:S(2)}) copy-start(f32[4096,256]{1,0:T(8,128)} %x_ref) | copy-start | bytes 12582916
  21.3 13.6 %collective-permute-start.5 = (f32[512,256]{1,0:T(8,128)S(1)}, f32[512,256]{1,0:T(8,128)S(1)}, u32[]{:S(2)}, u32[]{:S(2)}) collective-permute-start(f32[512,256]{1,0:T(8,128)S(1)} %collective-permute-done.3.refs_0_.refs_1_.gated_ref), channel_id=1, source_target_pairs={{4,8},{8,4},{5,9},{9,5},{6,10},{10,6},{7,11},{11,7},{20,24},{24,20... | collective-permute-start | bytes 1572872 | tf_op jit(solution)/shard_map/ppermute | solution.py:538
  22.0 20.6 %collective-permute-start.6 = (f32[512,256]{1,0:T(8,128)S(1)}, f32[512,256]{1,0:T(8,128)S(1)}, u32[]{:S(2)}, u32[]{:S(2)}) collective-permute-start(f32[512,256]{1,0:T(8,128)S(1)} %collective-permute-done.2.refs_0_.gated_ref), channel_id=1, source_target_pairs={{4,0},{8,12},{5,1},{9,13},{6,2},{10,14},{7,3},{11,15},{20,16},{24,... | collective-permute-start | bytes 1572872 | tf_op jit(solution)/shard_map/ppermute | solution.py:538
  34.0 11.6 %collective-permute-start.4 = (f32[512,256]{1,0:T(8,128)S(1)}, f32[512,256]{1,0:T(8,128)S(1)}, u32[]{:S(2)}, u32[]{:S(2)}) collective-permute-start(f32[512,256]{1,0:T(8,128)S(1)} %collective-permute-done.1.refs_0_.refs_1_.mixed_ref), channel_id=1, source_target_pairs={{4,8},{8,4},{5,9},{9,5},{6,10},{10,6},{7,11},{11,7},{20,24},{24,20... | collective-permute-start | bytes 1572872 | tf_op jit(solution)/shard_map/ppermute | solution.py:538
  34.9 20.4 %collective-permute-start.7 = (f32[512,256]{1,0:T(8,128)S(1)}, f32[512,256]{1,0:T(8,128)S(1)}, u32[]{:S(2)}, u32[]{:S(2)}) collective-permute-start(f32[512,256]{1,0:T(8,128)S(1)} %collective-permute-done.5.refs_0_.gated_ref), channel_id=1, source_target_pairs={{4,0},{8,12},{5,1},{9,13},{6,2},{10,14},{7,3},{11,15},{20,16},{24,... | collective-permute-start | bytes 1572872 | tf_op jit(solution)/shard_map/ppermute | solution.py:538
  43.3 2.2 %copy-start.2 = (bf16[2,4,256,256]{3,2,1,0:T(8,128)(2,1)S(1)}, bf16[2,4,256,256]{3,2,1,0:T(8,128)(2,1)}, u32[]{:S(2)}) copy-start(bf16[2,4,256,256]{3,2,1,0:T(8,128)(2,1)} %constant.10.clone.inverse_ref) | copy-start | bytes 3145732
  46.9 17.2 %collective-permute-start.9 = (f32[520,128]{1,0:T(8,128)S(1)}, f32[520,128]{1,0:T(8,128)S(1)}, u32[]{:S(2)}, u32[]{:S(2)}) collective-permute-start(f32[520,128]{1,0:T(8,128)S(1)} %partial.2.made_ref), channel_id=1, source_target_pairs={{4,0},{8,12},{5,1},{9,13},{6,2},{10,14},{7,3},{11,15},{20,16},{24,... | collective-permute-start | bytes 798728 | tf_op jit(solution)/shard_map/ppermute | solution.py:538
  49.6 6.4 %copy-start.7 = (f32[512,256]{1,0:T(8,128)S(1)}, f32[512,256]{1,0:T(8,128)}, u32[]{:S(2)}) copy-start(f32[512,256]{1,0:T(8,128)} %rest_4_.1) | copy-start | bytes 1572868
  49.6 6.4 %copy-start.9 = (f32[256]{0:T(256)S(1)}, f32[256]{0:T(256)}, u32[]{:S(2)}) copy-start(f32[256]{0:T(256)} %param.12) | copy-start | bytes 3076
  49.6 18.4 %collective-permute-start.8 = (f32[520,128]{1,0:T(8,128)S(1)}, f32[520,128]{1,0:T(8,128)S(1)}, u32[]{:S(2)}, u32[]{:S(2)}) collective-permute-start(f32[520,128]{1,0:T(8,128)S(1)} %partial.3.made_ref), channel_id=1, source_target_pairs={{4,0},{8,12},{5,1},{9,13},{6,2},{10,14},{7,3},{11,15},{20,16},{24,... | collective-permute-start | bytes 798728 | tf_op jit(solution)/shard_map/ppermute | solution.py:538
  56.0 8.1 %copy-start.3 = (f32[512,256]{1,0:T(8,128)S(1)}, f32[512,256]{1,0:T(8,128)}, u32[]{:S(2)}) copy-start(f32[512,256]{1,0:T(8,128)} %key_ref.3) | copy-start | bytes 1572868
  56.0 8.1 %copy-start.4 = (f32[512,256]{1,0:T(8,128)S(1)}, f32[512,256]{1,0:T(8,128)}, u32[]{:S(2)}) copy-start(f32[512,256]{1,0:T(8,128)} %values_ref.3) | copy-start | bytes 1572868

commit v14 on v13

--- a/solution.py
+++ b/solution.py
@@ -213,62 +213,78 @@
     return a[0] + b[0], a[1] + b[1]
 
 
-def partial_kernel(
-    pos_ref, table_ref, inverse_ref, win_near, win_far, next_ref, x_ref, gated_ref, near_sums, out_ref, z_ref
-):
-    rows = next_ref.shape[0] // 4
+def ahead_kernel(pos_ref, win_near, win_far, next_ref, near_ref, far_ref):
+    rows = next_ref.shape[0]
     sub = rows // 2
-    for group, part in enumerate(spread(x_ref[...])):
+    re, im = slice(0, sub), slice(sub, rows)
+    near = conj_mul((win_near[0, re, :], win_near[0, im, :]), (next_ref[re, :], next_ref[im, :]))
+    near_ref[re, :], near_ref[im, :] = near
+    far_ref[...] = win_far[0]
+
+
+def ahead(pos, windows, next_m, seg):
+    width = next_m.shape[1]
+    rows = seg // 2
+    n = (windows.shape[0] + 1) // 2
+
+    def window(distance):
+        return pl.BlockSpec(
+            (1, rows, width),
+            lambda i, pos: (jnp.where(pos[0] == 1, n - 1 + distance, n - 1 - distance), i, 0),
+        )
+
+    group = pl.BlockSpec((rows, width), lambda i, pos: (i, 0))
+    return pl.pallas_call(
+        ahead_kernel,
+        grid_spec=pltpu.PrefetchScalarGridSpec(
+            num_scalar_prefetch=1,
+            grid=(4,),
+            in_specs=[window(2), window(3), group],
+            out_specs=[group] * 2,
+        ),
+        out_shape=[f32(2 * seg, width)] * 2,
+        compiler_params=params(8),
+        cost_estimate=cost(12 * seg * width, 40 * seg * width),
+        name="ahead",
+    )(pos, windows, windows, next_m)
+
+
+def partial_kernel(half, table_ref, inverse_ref, near_ref, win_ref, x_ref, gated_ref, near_sums, out_ref, z_ref):
+    rows = near_ref.shape[0] // 4
+    sub = rows // 2
+    width = out_ref.shape[1]
+    lanes = slice(half * width, (half + 1) * width)
+    x = x_ref[:, lanes]
+    for group, part in enumerate(spread(x)):
         base = group * rows
         far = dot3(table_ref, group, *split(part))
         re, im = slice(base, base + sub), slice(base + sub, base + rows)
         total = add(
-            conj_mul((win_near[0, re, :], win_near[0, im, :]), (next_ref[re, :], next_ref[im, :])),
-            conj_mul((win_far[0, re, :], win_far[0, im, :]), (far[:sub], far[sub:])),
+            (near_ref[re, lanes], near_ref[im, lanes]),
+            conj_mul((win_ref[re, lanes], win_ref[im, lanes]), (far[:sub], far[sub:])),
         )
         z_ref[group] = dot3(inverse_ref, group, *split(jnp.concatenate(total, axis=0)))
     quarters = gather_quarters([z_ref[g, :sub] for g in range(4)], [z_ref[g, sub:] for g in range(4)])
     for i, quarter in enumerate(quarters):
         out_ref[i * sub : (i + 1) * sub, :] = quarter
-    out_ref[4 * sub :, :] = near_sums[...] + block_sums(gated_ref[...], x_ref[...])
-
-
-def back_partial(pos, table, inverse, windows, next_m, x, gated, near_sums, half, seg):
-    width = x.shape[1] // 2
-    n = (windows.shape[0] + 1) // 2
-
-    def window(distance):
-        return pl.BlockSpec(
-            (1, 2 * seg, width),
-            lambda i, pos: (jnp.where(pos[0] == 1, n - 1 + distance, n - 1 - distance), 0, half),
-        )
-
-    def lanes(rows):
-        return pl.BlockSpec((rows, width), lambda i, pos: (0, half))
-
-    return pl.pallas_call(
-        partial_kernel,
-        grid_spec=pltpu.PrefetchScalarGridSpec(
-            num_scalar_prefetch=1,
-            grid=(1,),
-            in_specs=[
-                whole_spec(table.shape),
-                whole_spec(inverse.shape),
-                window(2),
-                window(3),
-                lanes(2 * seg),
-                lanes(seg),
-                lanes(seg),
-                lanes(8),
-            ],
-            out_specs=whole_spec((seg + 8, width)),
-            scratch_shapes=[pltpu.VMEM((4, seg // 2, width), jnp.float32)],
-        ),
+    out_ref[4 * sub :, :] = near_sums[:, lanes] + block_sums(gated_ref[:, lanes], x)
+
+
+def back_partial(table, inverse, near, window, x, gated, near_sums, half):
+    seg, full = x.shape
+    width = full // 2
+    whole = (table, inverse, near, window, x, gated, near_sums)
+    return pl.pallas_call(
+        functools.partial(partial_kernel, half),
+        grid=(1,),
+        in_specs=[whole_spec(a.shape) for a in whole],
+        out_specs=whole_spec((seg + 8, width)),
         out_shape=f32(seg + 8, width),
+        scratch_shapes=[pltpu.VMEM((4, seg // 2, width), jnp.float32)],
         compiler_params=params(24),
         cost_estimate=cost(6 * seg * seg * width * 2, 24 * seg * width),
         name="partial",
-    )(pos, table, inverse, windows, windows, next_m, x, gated, near_sums)
+    )(*whole)
 
 
 OWN, OUTER, NEXT, TWO, THREE = range(5)
@@ -575,17 +591,18 @@
     side_x, outer_m, next_m = after((side_x, outer_m, next_m))
     two_x = across(side_x)
     side_sums, near_sums = sums(side, side_x), sums(over, over_x)
-    over_two, outer_m, next_m, side_sums, near_sums = after((over_two, outer_m, next_m, side_sums, near_sums))
+    near, far_window = ahead(pos, windows, next_m, seg)
+    over_two, near, far_window, side_sums, near_sums = after((over_two, near, far_window, side_sums, near_sums))
 
     three = outward(over_two)
     two_g = dft(pos, table, seg, over_two, out_two)
     acc = early(pos, windows, (own_g, outer_g, next_g, two_g), (own_m, outer_m, next_m), seg)
     two_x, acc = after((two_x, acc))
 
-    made_0 = back_partial(pos, table, inverse, windows, next_m, two_x, over_two, near_sums, 0, seg)
+    made_0 = back_partial(table, inverse, near, far_window, two_x, over_two, near_sums, 0)
     two_x, made_0 = after((two_x, made_0))
     sent_0 = outward(made_0)
-    made_1 = back_partial(pos, table, inverse, windows, next_m, two_x, over_two, near_sums, 1, seg)
+    made_1 = back_partial(table, inverse, near, far_window, two_x, over_two, near_sums, 1)
     two_x, made_1 = after((two_x, made_1))
     sent_1 = outward(made_1)
     two_m, three_g = dft(pos, table, seg, two_x), dft(pos, table, seg, three)

time: 69.4 us -> 69.5 us (level)
    pallas_call x2 -> x3, Pallas kernels: 2.73 us -> 3.01 us  [the longest x2 2.72 us: back_partial(): pl.pallas_call(functools.partial(partial_kernel, half), grid=(1,), in_spe...]
where the time goes in v14:
time: 69.5 us; the launch traced here: 69.1 us
  Pallas kernels  25.9 us (37%)
  waiting for transfers between devices  21.9 us (32%)
  starting transfers between devices  15.7 us (23%)
  local copies, waits for them, and re-layouts  3.35 us (5%)
  other arithmetic  1.27 us (2%)
  between operations  0.95 us (1%)
    ppermute x10, waiting for transfers between devices, send(): return lax.ppermute(x, 'ctx', list(pairs))  21.9 us
    ppermute x10, starting transfers between devices, send(): return lax.ppermute(x, 'ctx', list(pairs))  15.7 us
    pallas_call x9, Pallas kernels, dft(): pl.pallas_call(functools.partial(dft_kernel, choose), grid_spec=pltpu.Pre...  6.53 us
    pallas_call x1, Pallas kernels, taps_spectra(): pl.pallas_call(taps_kernel, grid=(blocks,), in_specs=[whole_spec(table.sh...  6.09 us
    pallas_call x1, Pallas kernels, late(): pl.pallas_call(late_kernel, grid_spec=pltpu.PrefetchScalarGridSpec(num_sc...  6.01 us
    unnamed x20, local copies, waits for them, and re-layouts  3.35 us
    pallas_call x2, Pallas kernels, back_partial(): pl.pallas_call(functools.partial(partial_kernel, half), grid=(1,), in_spe...  2.72 us
    pallas_call x1, Pallas kernels, early(): pl.pallas_call(early_kernel, grid_spec=pltpu.PrefetchScalarGridSpec(num_s...  2.2 us
  transfers between devices with their start and end apart: 10, of which 6 were waited for; matrix products, arithmetic and copies ran while one was open for 0% of the time, Pallas kernels for 36%

profile of v14, /device:TPU:0, one launch (start us, length us, event | category | flops | bytes accessed | tf_op | source)
XLA Modules:
  0.0 69.1 jit_solution(8945522843666826142)
XLA Ops:
  0.6 1.3 %mul.3.gated_ref.refs_0_.rest_1_ = f32[512,256]{1,0:T(8,128)S(1)} multiply(f32[512,256]{1,0:T(8,128)} %key_ref.3, f32[512,256]{1,0:T(8,128)} %values_ref.3) | non-fusion elementwise | flops 131072 | bytes 1572864 | tf_op jit(solution)/shard_map/mul | solution.py:576
  1.9 0.7 %collective-permute-start.2 = (f32[512,256]{1,0:T(8,128)S(1)}, f32[512,256]{1,0:T(8,128)S(1)}, u32[]{:S(2)}, u32[]{:S(2)}) collective-permute-start(f32[512,256]{1,0:T(8,128)S(1)} %mul.3.gated_ref.refs_0_.rest_1_), channel_id=1, source_target_pairs={{4,8},{8,4},{5,9},{9,5},{6,10},{10,6},{7,11},{11,7},{20,24},{24,20... | collective-permute-start | bytes 1572872 | tf_op jit(solution)/shard_map/ppermute | solution.py:554
  2.6 5.9 %collective-permute-start.3 = (f32[512,256]{1,0:T(8,128)S(1)}, f32[512,256]{1,0:T(8,128)S(1)}, u32[]{:S(2)}, u32[]{:S(2)}) collective-permute-start(f32[512,256]{1,0:T(8,128)S(1)} %mul.3.gated_ref.refs_0_.rest_1_), channel_id=1, source_target_pairs={{0,4},{4,0},{8,12},{12,8},{1,5},{5,1},{9,13},{13,9},{2,6},{6,2},{1... | collective-permute-start | bytes 1572872 | tf_op jit(solution)/shard_map/ppermute | solution.py:554
  8.5 1.0 %copy-done.6 = f32[512,256]{1,0:T(8,128)S(1)} copy-done((f32[512,256]{1,0:T(8,128)S(1)}, f32[512,256]{1,0:T(8,128)}, u32[]{:S(2)}) %copy-start.6) | copy-done | bytes 524312
  9.5 1.0 %copy-done.8 = f32[512,256]{1,0:T(8,128)S(1)} copy-done((f32[512,256]{1,0:T(8,128)S(1)}, f32[512,256]{1,0:T(8,128)}, u32[]{:S(2)}) %copy-start.8) | copy-done | bytes 524312
  10.6 0.1 mix.1
  10.6 0.7 %collective-permute-start = (f32[512,256]{1,0:T(8,128)S(1)}, f32[512,256]{1,0:T(8,128)S(1)}, u32[]{:S(2)}, u32[]{:S(2)}) collective-permute-start(f32[512,256]{1,0:T(8,128)S(1)} %get-tuple-element.46.refs_0_.rest_2_), channel_id=1, source_target_pairs={{4,8},{8,4},{5,9},{9,5},{6,10},{10,6},{7,11},{11,7},{20,24},{24,20... | collective-permute-start | bytes 1572872 | tf_op jit(solution)/shard_map/ppermute | solution.py:554
  11.3 1.7 %collective-permute-start.1 = (f32[512,256]{1,0:T(8,128)S(1)}, f32[512,256]{1,0:T(8,128)S(1)}, u32[]{:S(2)}, u32[]{:S(2)}) collective-permute-start(f32[512,256]{1,0:T(8,128)S(1)} %get-tuple-element.46.refs_0_.rest_2_), channel_id=1, source_target_pairs={{0,4},{4,0},{8,12},{12,8},{1,5},{5,1},{9,13},{13,9},{2,6},{6,2},{1... | collective-permute-start | bytes 1572872 | tf_op jit(solution)/shard_map/ppermute | solution.py:554
  13.1 1.2 %copy-done = bf16[2,4,256,256]{3,2,1,0:T(8,128)(2,1)S(1)} copy-done((bf16[2,4,256,256]{3,2,1,0:T(8,128)(2,1)S(1)}, bf16[2,4,256,256]{3,2,1,0:T(8,128)(2,1)}, u32[]{:S(2)}) %copy-start) | copy-done | bytes 1048600
  14.3 0.7 %dft.10.own_m = f32[1024,256]{1,0:T(8,128)S(1)} custom-call(s32[1]{0:T(128)} %bitcast.pos_ref, bf16[2,4,256,256]{3,2,1,0:T(8,128)(2,1)S(1)} %copy-done, f32[512,256]{1,0:T(8,128)S(1)} %get-tuple-element.46.refs_0_.rest_2_), custom_call_target="tpu_custom_call" | custom-call | flops 402653184 | bytes 1572864 | tf_op jit(solution)/shard_map/dft/pallas_call | solution.py:153
  15.0 0.0 copy-start.1
  15.0 0.0 copy-start.5
  15.1 0.7 %dft.9.own_g = f32[1024,256]{1,0:T(8,128)S(1)} custom-call(s32[1]{0:T(128)} %bitcast.pos_ref, bf16[2,4,256,256]{3,2,1,0:T(8,128)(2,1)S(1)} %copy-done, f32[512,256]{1,0:T(8,128)S(1)} %mul.3.gated_ref.refs_0_.rest_1_), custom_call_target="tpu_custom_call" | custom-call | flops 402653184 | bytes 1572864 | tf_op jit(solution)/shard_map/dft/pallas_call | solution.py:153
  15.8 0.0 collective-permute-done.2.refs_0_.gated_ref
  15.8 5.5 %collective-permute-done.3.refs_0_.refs_1_.gated_ref = f32[512,256]{1,0:T(8,128)S(1)} collective-permute-done((f32[512,256]{1,0:T(8,128)S(1)}, f32[512,256]{1,0:T(8,128)S(1)}, u32[]{:S(2)}, u32[]{:S(2)}) %collective-permute-start.3) | collective-permute-done | bytes 524320 | tf_op jit(solution)/shard_map/ppermute | solution.py:554
  21.3 0.7 collective-permute-start.5
  22.0 1.3 %collective-permute-start.6 = (f32[512,256]{1,0:T(8,128)S(1)}, f32[512,256]{1,0:T(8,128)S(1)}, u32[]{:S(2)}, u32[]{:S(2)}) collective-permute-start(f32[512,256]{1,0:T(8,128)S(1)} %collective-permute-done.2.refs_0_.gated_ref), channel_id=1, source_target_pairs={{4,0},{8,12},{5,1},{9,13},{6,2},{10,14},{7,3},{11,15},{20,16},{24,... | collective-permute-start | bytes 1572872 | tf_op jit(solution)/shard_map/ppermute | solution.py:554
  23.3 0.7 %dft.12.next_g = f32[1024,256]{1,0:T(8,128)S(1)} custom-call(s32[1]{0:T(128)} %bitcast.pos_ref, bf16[2,4,256,256]{3,2,1,0:T(8,128)(2,1)S(1)} %copy-done, f32[512,256]{1,0:T(8,128)S(1)} %collective-permute-done.2.refs_0_.gated_ref, f32[512,256]{1,0:T(8,128)S(1)} %collective-permute-done.3.refs_0_.refs_1_.gated_ref), custom_call_target="tpu_custom_call" | custom-call | flops 402653184 | bytes 1572864 | tf_op jit(solution)/shard_map/dft/pallas_call | solution.py:153
  24.0 0.7 %dft.11.outer_g = f32[1024,256]{1,0:T(8,128)S(1)} custom-call(s32[1]{0:T(128)} %bitcast.pos_ref, bf16[2,4,256,256]{3,2,1,0:T(8,128)(2,1)S(1)} %copy-done, f32[512,256]{1,0:T(8,128)S(1)} %collective-permute-done.3.refs_0_.refs_1_.gated_ref), custom_call_target="tpu_custom_call" | custom-call | flops 402653184 | bytes 1572864 | tf_op jit(solution)/shard_map/dft/pallas_call | solution.py:153
  24.7 6.1 %taps.1.win_near.win_far.win_own.win_outer.win_next.win_two.win_ref = f32[7,1024,256]{2,1,0:T(8,128)S(1)} custom-call(bf16[2,4,256,256]{3,2,1,0:T(8,128)(2,1)S(1)} %copy-done.1, f32[4096,256]{1,0:T(8,128)S(1)} %copy-done.5), custom_call_target="tpu_custom_call" | custom-call | flops 3221225472 | bytes 12582912 | tf_op jit(solution)/shard_map/taps/pallas_call | solution.py:191
  30.9 1.7 %collective-permute-done.1.refs_0_.refs_1_.mixed_ref = f32[512,256]{1,0:T(8,128)S(1)} collective-permute-done((f32[512,256]{1,0:T(8,128)S(1)}, f32[512,256]{1,0:T(8,128)S(1)}, u32[]{:S(2)}, u32[]{:S(2)}) %collective-permute-start.1) | collective-permute-done | bytes 524320 | tf_op jit(solution)/shard_map/ppermute | solution.py:554
  32.5 0.7 %dft.13.outer_m = f32[1024,256]{1,0:T(8,128)S(1)} custom-call(s32[1]{0:T(128)} %bitcast.pos_ref, bf16[2,4,256,256]{3,2,1,0:T(8,128)(2,1)S(1)} %copy-done.1, f32[512,256]{1,0:T(8,128)S(1)} %collective-permute-done.1.refs_0_.refs_1_.mixed_ref), custom_call_target="tpu_custom_call" | custom-call | flops 402653184 | bytes 1572864 | tf_op jit(solution)/shard_map/dft/pallas_call | solution.py:153
  33.2 0.8 %dft.14.next_ref.next_m = f32[1024,256]{1,0:T(8,128)S(1)} custom-call(s32[1]{0:T(128)} %bitcast.pos_ref, bf16[2,4,256,256]{3,2,1,0:T(8,128)(2,1)S(1)} %copy-done.1, f32[512,256]{1,0:T(8,128)S(1)} %collective-permute-done.refs_0_.mixed_ref, f32[512,256]{1,0:T(8,128)S(1)} %collective-permute-done.1.refs_0_.refs_1_.mixed_ref), custom_call_target="tpu_custom_call" | custom-call | flops 402653184 | bytes 1572864 | tf_op jit(solution)/shard_map/dft/pallas_call | solution.py:153
  34.0 0.7 %collective-permute-start.4 = (f32[512,256]{1,0:T(8,128)S(1)}, f32[512,256]{1,0:T(8,128)S(1)}, u32[]{:S(2)}, u32[]{:S(2)}) collective-permute-start(f32[512,256]{1,0:T(8,128)S(1)} %collective-permute-done.1.refs_0_.refs_1_.mixed_ref), channel_id=1, source_target_pairs={{4,8},{8,4},{5,9},{9,5},{6,10},{10,6},{7,11},{11,7},{20,24},{24,20... | collective-permute-start | bytes 1572872 | tf_op jit(solution)/shard_map/ppermute | solution.py:554
  34.7 0.1 sums.3.near_sums
  34.8 0.1 sums.2.side_ref
  34.9 0.3 ahead.1
  35.3 1.3 %collective-permute-start.7 = (f32[512,256]{1,0:T(8,128)S(1)}, f32[512,256]{1,0:T(8,128)S(1)}, u32[]{:S(2)}, u32[]{:S(2)}) collective-permute-start(f32[512,256]{1,0:T(8,128)S(1)} %collective-permute-done.5.refs_0_.gated_ref), channel_id=1, source_target_pairs={{4,0},{8,12},{5,1},{9,13},{6,2},{10,14},{7,3},{11,15},{20,16},{24,... | collective-permute-start | bytes 1572872 | tf_op jit(solution)/shard_map/ppermute | solution.py:554
  36.6 6.0 %collective-permute-done.6.refs_1_ = f32[512,256]{1,0:T(8,128)S(1)} collective-permute-done((f32[512,256]{1,0:T(8,128)S(1)}, f32[512,256]{1,0:T(8,128)S(1)}, u32[]{:S(2)}, u32[]{:S(2)}) %collective-permute-start.6) | collective-permute-done | bytes 524320 | tf_op jit(solution)/shard_map/ppermute | solution.py:554
  42.6 0.7 %dft.15.two_g = f32[1024,256]{1,0:T(8,128)S(1)} custom-call(s32[1]{0:T(128)} %bitcast.pos_ref, bf16[2,4,256,256]{3,2,1,0:T(8,128)(2,1)S(1)} %copy-done.1, f32[512,256]{1,0:T(8,128)S(1)} %collective-permute-done.5.refs_0_.gated_ref, f32[512,256]{1,0:T(8,128)S(1)} %collective-permute-done.6.refs_1_), custom_call_target="tpu_custom_call" | custom-call | flops 402653184 | bytes 1572864 | tf_op jit(solution)/shard_map/dft/pallas_call | solution.py:153
  43.3 0.0 copy-start.2
  43.3 2.2 %early.1.acc_ref = f32[4,1024,256]{2,1,0:T(8,128)S(1)} custom-call(s32[1]{0:T(128)} %bitcast.pos_ref, f32[7,1024,256]{2,1,0:T(8,128)S(1)} %taps.1.win_near.win_far.win_own.win_outer.win_next.win_two.win_ref, f32[7,1024,256]{2,1,0:T(8,128)S(1)} %taps.1.win_near.win_far.win_own.win_outer.win_next.win_two.win_ref, ...), custom_call_target="tpu_custom_call" | custom-call | flops 26214400 | bytes 15728640 | tf_op jit(solution)/shard_map/early/pallas_call | solution.py:396
  45.6 1.4 %partial.2.made_ref = f32[520,128]{1,0:T(8,128)S(1)} custom-call(bf16[2,4,256,256]{3,2,1,0:T(8,128)(2,1)S(1)} %copy-done.1, bf16[2,4,256,256]{3,2,1,0:T(8,128)(2,1)S(1)} %copy-done.2, f32[1024,256]{1,0:T(8,128)S(1)} %get-tuple-element.65.near_ref, f32[1024,256]{1,0:T(8,128)S(1)} %get-tuple-element.66.win_ref, ...), custom_call_target="tpu_custom_call" | custom-call | flops 402653184 | bytes 1572864 | tf_op jit(solution)/shard_map/partial/pallas_call | solution.py:277
  46.9 0.0 copy-start.7
  47.0 0.0 copy-start.9
  47.0 1.4 %collective-permute-start.9 = (f32[520,128]{1,0:T(8,128)S(1)}, f32[520,128]{1,0:T(8,128)S(1)}, u32[]{:S(2)}, u32[]{:S(2)}) collective-permute-start(f32[520,128]{1,0:T(8,128)S(1)} %partial.2.made_ref), channel_id=1, source_target_pairs={{4,0},{8,12},{5,1},{9,13},{6,2},{10,14},{7,3},{11,15},{20,16},{24,... | collective-permute-start | bytes 798728 | tf_op jit(solution)/shard_map/ppermute | solution.py:554
  48.4 1.4 %partial.3.made_ref = f32[520,128]{1,0:T(8,128)S(1)} custom-call(bf16[2,4,256,256]{3,2,1,0:T(8,128)(2,1)S(1)} %copy-done.1, bf16[2,4,256,256]{3,2,1,0:T(8,128)(2,1)S(1)} %copy-done.2, f32[1024,256]{1,0:T(8,128)S(1)} %get-tuple-element.65.near_ref, f32[1024,256]{1,0:T(8,128)S(1)} %get-tuple-element.66.win_ref, ...), custom_call_target="tpu_custom_call" | custom-call | flops 402653184 | bytes 1572864 | tf_op jit(solution)/shard_map/partial/pallas_call | solution.py:277
  49.8 1.3 %collective-permute-start.8 = (f32[520,128]{1,0:T(8,128)S(1)}, f32[520,128]{1,0:T(8,128)S(1)}, u32[]{:S(2)}, u32[]{:S(2)}) collective-permute-start(f32[520,128]{1,0:T(8,128)S(1)} %partial.3.made_ref), channel_id=1, source_target_pairs={{4,0},{8,12},{5,1},{9,13},{6,2},{10,14},{7,3},{11,15},{20,16},{24,... | collective-permute-start | bytes 798728 | tf_op jit(solution)/shard_map/ppermute | solution.py:554
  51.1 0.7 %dft.17.rest_0_ = f32[1024,256]{1,0:T(8,128)S(1)} custom-call(s32[1]{0:T(128)} %bitcast.pos_ref, bf16[2,4,256,256]{3,2,1,0:T(8,128)(2,1)S(1)} %copy-done.1, f32[512,256]{1,0:T(8,128)S(1)} %collective-permute-done.4.x_ref.refs_0_), custom_call_target="tpu_custom_call" | custom-call | flops 402653184 | bytes 1572864 | tf_op jit(solution)/shard_map/dft/pallas_call | solution.py:153
  51.8 3.5 %collective-permute-done.7.refs_0_ = f32[512,256]{1,0:T(8,128)S(1)} collective-permute-done((f32[512,256]{1,0:T(8,128)S(1)}, f32[512,256]{1,0:T(8,128)S(1)}, u32[]{:S(2)}, u32[]{:S(2)}) %collective-permute-start.7) | collective-permute-done | bytes 524320 | tf_op jit(solution)/shard_map/ppermute | solution.py:554
  55.3 0.7 %dft.16.three_g = f32[1024,256]{1,0:T(8,128)S(1)} custom-call(s32[1]{0:T(128)} %bitcast.pos_ref, bf16[2,4,256,256]{3,2,1,0:T(8,128)(2,1)S(1)} %copy-done.1, f32[512,256]{1,0:T(8,128)S(1)} %collective-permute-done.7.refs_0_), custom_call_target="tpu_custom_call" | custom-call | flops 402653184 | bytes 1572864 | tf_op jit(solution)/shard_map/dft/pallas_call | solution.py:153
  56.0 0.0 copy-start.3
  56.0 0.0 copy-start.4
  56.0 6.0 %late.1 = (f32[512,256]{1,0:T(8,128)}, f32[1024,256]{1,0:T(8,128)}, f32[512,256]{1,0:T(8,128)S(1)}) custom-call(s32[1]{0:T(128)} %bitcast.pos_ref, bf16[2,4,256,256]{3,2,1,0:T(8,128)(2,1)S(1)} %copy-done.2, f32[4,1024,256]{2,1,0:T(8,128)S(1)} %early.1.acc_ref, f32[7,1024,256]{2,1,0:T(8,128)S(1)} %taps.1.win_near.win_far.win_own.win_outer.win_next.win_two.win_ref, ...), custom_call_target="tpu_custom_call" | custom-call | flops 1610612736 | bytes 13107200 | tf_op jit(solution)/shard_map/late/pallas_call | solution.py:493
  62.1 2.2 %collective-permute-done.9.sent_ref = f32[520,128]{1,0:T(8,128)S(1)} collective-permute-done((f32[520,128]{1,0:T(8,128)S(1)}, f32[520,128]{1,0:T(8,128)S(1)}, u32[]{:S(2)}, u32[]{:S(2)}) %collective-permute-start.9) | collective-permute-done | bytes 266272 | tf_op jit(solution)/shard_map/ppermute | solution.py:554
  64.3 0.9 %finish.2 = (f32[512,256]{1,0:T(8,128)}, f32[512,256]{1,0:T(8,128)}, f32[1,256]{1,0:T(1,128)}) custom-call(f32[512,256]{1,0:T(8,128)S(1)} %get-tuple-element.71.back_ref, f32[512,256]{1,0:T(8,128)S(1)} %copy-done.3, f32[512,256]{1,0:T(8,128)S(1)} %copy-done.4, f32[520,128]{1,0:T(8,128)S(1)} %partial.2.made_ref, ...), custom_call_target="tpu_custom_call" | custom-call | flops 196608 | bytes 1572864 | tf_op jit(solution)/shard_map/finish/pallas_call | solution.py:540
  65.2 3.0 %collective-permute-done.8.sent_ref = f32[520,128]{1,0:T(8,128)S(1)} collective-permute-done((f32[520,128]{1,0:T(8,128)S(1)}, f32[520,128]{1,0:T(8,128)S(1)}, u32[]{:S(2)}, u32[]{:S(2)}) %collective-permute-start.8) | collective-permute-done | bytes 266272 | tf_op jit(solution)/shard_map/ppermute | solution.py:554
  68.2 0.9 %finish.3 = (f32[512,256]{1,0:T(8,128)}, f32[512,256]{1,0:T(8,128)}, f32[1,256]{1,0:T(1,128)}) custom-call(f32[512,256]{1,0:T(8,128)S(1)} %get-tuple-element.71.back_ref, f32[512,256]{1,0:T(8,128)S(1)} %copy-done.3, f32[512,256]{1,0:T(8,128)S(1)} %copy-done.4, ...), custom_call_target="tpu_custom_call", output_to_operand_aliasing={{0}: (7, {}), {1}: (8, {}), {2}: (9, {})} | custom-call | flops 196608 | bytes 1572864 | tf_op jit(solution)/shard_map/finish/pallas_call | solution.py:540
  (13 shorter events, 0.0 us)
Async XLA Ops:
  1.9 13.9 %collective-permute-start.2 = (f32[512,256]{1,0:T(8,128)S(1)}, f32[512,256]{1,0:T(8,128)S(1)}, u32[]{:S(2)}, u32[]{:S(2)}) collective-permute-start(f32[512,256]{1,0:T(8,128)S(1)} %mul.3.gated_ref.refs_0_.rest_1_), channel_id=1, source_target_pairs={{4,8},{8,4},{5,9},{9,5},{6,10},{10,6},{7,11},{11,7},{20,24},{24,20... | collective-permute-start | bytes 1572872 | tf_op jit(solution)/shard_map/ppermute | solution.py:554
  2.6 18.7 %collective-permute-start.3 = (f32[512,256]{1,0:T(8,128)S(1)}, f32[512,256]{1,0:T(8,128)S(1)}, u32[]{:S(2)}, u32[]{:S(2)}) collective-permute-start(f32[512,256]{1,0:T(8,128)S(1)} %mul.3.gated_ref.refs_0_.rest_1_), channel_id=1, source_target_pairs={{0,4},{4,0},{8,12},{12,8},{1,5},{5,1},{9,13},{13,9},{2,6},{6,2},{1... | collective-permute-start | bytes 1572872 | tf_op jit(solution)/shard_map/ppermute | solution.py:554
  8.5 1.0 %copy-start.6 = (f32[512,256]{1,0:T(8,128)S(1)}, f32[512,256]{1,0:T(8,128)}, u32[]{:S(2)}) copy-start(f32[512,256]{1,0:T(8,128)} %rest_4_.1) | copy-start | bytes 1572868
  9.5 1.0 %copy-start.8 = (f32[512,256]{1,0:T(8,128)S(1)}, f32[512,256]{1,0:T(8,128)}, u32[]{:S(2)}) copy-start(f32[512,256]{1,0:T(8,128)} %query_ref.1) | copy-start | bytes 1572868
  10.6 20.2 %collective-permute-start = (f32[512,256]{1,0:T(8,128)S(1)}, f32[512,256]{1,0:T(8,128)S(1)}, u32[]{:S(2)}, u32[]{:S(2)}) collective-permute-start(f32[512,256]{1,0:T(8,128)S(1)} %get-tuple-element.46.refs_0_.rest_2_), channel_id=1, source_target_pairs={{4,8},{8,4},{5,9},{9,5},{6,10},{10,6},{7,11},{11,7},{20,24},{24,20... | collective-permute-start | bytes 1572872 | tf_op jit(solution)/shard_map/ppermute | solution.py:554
  11.3 21.2 %collective-permute-start.1 = (f32[512,256]{1,0:T(8,128)S(1)}, f32[512,256]{1,0:T(8,128)S(1)}, u32[]{:S(2)}, u32[]{:S(2)}) collective-permute-start(f32[512,256]{1,0:T(8,128)S(1)} %get-tuple-element.46.refs_0_.rest_2_), channel_id=1, source_target_pairs={{0,4},{4,0},{8,12},{12,8},{1,5},{5,1},{9,13},{13,9},{2,6},{6,2},{1... | collective-permute-start | bytes 1572872 | tf_op jit(solution)/shard_map/ppermute | solution.py:554
  13.1 1.2 %copy-start = (bf16[2,4,256,256]{3,2,1,0:T(8,128)(2,1)S(1)}, bf16[2,4,256,256]{3,2,1,0:T(8,128)(2,1)}, u32[]{:S(2)}) copy-start(bf16[2,4,256,256]{3,2,1,0:T(8,128)(2,1)} %constant.9.clone.table_ref) | copy-start | bytes 3145732
  15.0 9.7 %copy-start.1 = (bf16[2,4,256,256]{3,2,1,0:T(8,128)(2,1)S(1)}, bf16[2,4,256,256]{3,2,1,0:T(8,128)(2,1)}, u32[]{:S(2)}) copy-start(bf16[2,4,256,256]{3,2,1,0:T(8,128)(2,1)} %constant.9.clone.table_ref) | copy-start | bytes 3145732
  15.0 9.7 %copy-start.5 = (f32[4096,256]{1,0:T(8,128)S(1)}, f32[4096,256]{1,0:T(8,128)}, u32[]{:S(2)}) copy-start(f32[4096,256]{1,0:T(8,128)} %x_ref) | copy-start | bytes 12582916
  21.3 14.0 %collective-permute-start.5 = (f32[512,256]{1,0:T(8,128)S(1)}, f32[512,256]{1,0:T(8,128)S(1)}, u32[]{:S(2)}, u32[]{:S(2)}) collective-permute-start(f32[512,256]{1,0:T(8,128)S(1)} %collective-permute-done.3.refs_0_.refs_1_.gated_ref), channel_id=1, source_target_pairs={{4,8},{8,4},{5,9},{9,5},{6,10},{10,6},{7,11},{11,7},{20,24},{24,20... | collective-permute-start | bytes 1572872 | tf_op jit(solution)/shard_map/ppermute | solution.py:554
  22.0 20.6 %collective-permute-start.6 = (f32[512,256]{1,0:T(8,128)S(1)}, f32[512,256]{1,0:T(8,128)S(1)}, u32[]{:S(2)}, u32[]{:S(2)}) collective-permute-start(f32[512,256]{1,0:T(8,128)S(1)} %collective-permute-done.2.refs_0_.gated_ref), channel_id=1, source_target_pairs={{4,0},{8,12},{5,1},{9,13},{6,2},{10,14},{7,3},{11,15},{20,16},{24,... | collective-permute-start | bytes 1572872 | tf_op jit(solution)/shard_map/ppermute | solution.py:554
  34.0 11.5 %collective-permute-start.4 = (f32[512,256]{1,0:T(8,128)S(1)}, f32[512,256]{1,0:T(8,128)S(1)}, u32[]{:S(2)}, u32[]{:S(2)}) collective-permute-start(f32[512,256]{1,0:T(8,128)S(1)} %collective-permute-done.1.refs_0_.refs_1_.mixed_ref), channel_id=1, source_target_pairs={{4,8},{8,4},{5,9},{9,5},{6,10},{10,6},{7,11},{11,7},{20,24},{24,20... | collective-permute-start | bytes 1572872 | tf_op jit(solution)/shard_map/ppermute | solution.py:554
  35.3 20.0 %collective-permute-start.7 = (f32[512,256]{1,0:T(8,128)S(1)}, f32[512,256]{1,0:T(8,128)S(1)}, u32[]{:S(2)}, u32[]{:S(2)}) collective-permute-start(f32[512,256]{1,0:T(8,128)S(1)} %collective-permute-done.5.refs_0_.gated_ref), channel_id=1, source_target_pairs={{4,0},{8,12},{5,1},{9,13},{6,2},{10,14},{7,3},{11,15},{20,16},{24,... | collective-permute-start | bytes 1572872 | tf_op jit(solution)/shard_map/ppermute | solution.py:554
  43.3 2.2 %copy-start.2 = (bf16[2,4,256,256]{3,2,1,0:T(8,128)(2,1)S(1)}, bf16[2,4,256,256]{3,2,1,0:T(8,128)(2,1)}, u32[]{:S(2)}) copy-start(bf16[2,4,256,256]{3,2,1,0:T(8,128)(2,1)} %constant.10.clone.inverse_ref) | copy-start | bytes 3145732
  46.9 9.1 %copy-start.7 = (f32[512,256]{1,0:T(8,128)S(1)}, f32[512,256]{1,0:T(8,128)}, u32[]{:S(2)}) copy-start(f32[512,256]{1,0:T(8,128)} %rest_4_.1) | copy-start | bytes 1572868
  47.0 9.1 %copy-start.9 = (f32[256]{0:T(256)S(1)}, f32[256]{0:T(256)}, u32[]{:S(2)}) copy-start(f32[256]{0:T(256)} %param.12) | copy-start | bytes 3076
  47.0 17.3 %collective-permute-start.9 = (f32[520,128]{1,0:T(8,128)S(1)}, f32[520,128]{1,0:T(8,128)S(1)}, u32[]{:S(2)}, u32[]{:S(2)}) collective-permute-start(f32[520,128]{1,0:T(8,128)S(1)} %partial.2.made_ref), channel_id=1, source_target_pairs={{4,0},{8,12},{5,1},{9,13},{6,2},{10,14},{7,3},{11,15},{20,16},{24,... | collective-permute-start | bytes 798728 | tf_op jit(solution)/shard_map/ppermute | solution.py:554
  49.8 18.4 %collective-permute-start.8 = (f32[520,128]{1,0:T(8,128)S(1)}, f32[520,128]{1,0:T(8,128)S(1)}, u32[]{:S(2)}, u32[]{:S(2)}) collective-permute-start(f32[520,128]{1,0:T(8,128)S(1)} %partial.3.made_ref), channel_id=1, source_target_pairs={{4,0},{8,12},{5,1},{9,13},{6,2},{10,14},{7,3},{11,15},{20,16},{24,... | collective-permute-start | bytes 798728 | tf_op jit(solution)/shard_map/ppermute | solution.py:554
  56.0 8.3 %copy-start.3 = (f32[512,256]{1,0:T(8,128)S(1)}, f32[512,256]{1,0:T(8,128)}, u32[]{:S(2)}) copy-start(f32[512,256]{1,0:T(8,128)} %key_ref.3) | copy-start | bytes 1572868
  56.0 8.3 %copy-start.4 = (f32[512,256]{1,0:T(8,128)S(1)}, f32[512,256]{1,0:T(8,128)}, u32[]{:S(2)}) copy-start(f32[512,256]{1,0:T(8,128)} %values_ref.3) | copy-start | bytes 1572868

commit v15 on v13

--- a/solution.py
+++ b/solution.py
@@ -503,13 +503,15 @@
     )(pos, inverse, acc, windows, three_g, two_g, own_m, outer_m, next_m, two_m, gated, mixed, skip, upstream)
 
 
-def finish_kernel(back_ref, key_ref, values_ref, made_ref, sent_ref, own_ref, side_ref, *rest):
+def finish_kernel(half, back_ref, key_ref, values_ref, made_ref, sent_ref, own_ref, side_ref, *rest):
     key_out, value_out, skip_out = rest[-3:]
     seg = back_ref.shape[0]
-    back = back_ref[...] + sent_ref[:seg, :]
-    key_out[...] = back * values_ref[...]
-    value_out[...] = back * key_ref[...]
-    total = (own_ref[...] + side_ref[...]) + (made_ref[seg:, :] + sent_ref[seg:, :])
+    width = sent_ref.shape[1]
+    lanes = slice(half * width, (half + 1) * width)
+    back = back_ref[:, lanes] + sent_ref[:seg, :]
+    key_out[...] = back * values_ref[:, lanes]
+    value_out[...] = back * key_ref[:, lanes]
+    total = (own_ref[:, lanes] + side_ref[:, lanes]) + (made_ref[seg:, :] + sent_ref[seg:, :])
     skip_out[...] = jnp.sum(total, axis=0, keepdims=True)
 
 
@@ -522,9 +524,12 @@
 
     held = pl.BlockSpec(memory_space=pl.ANY)
     return pl.pallas_call(
-        finish_kernel,
+        functools.partial(finish_kernel, half),
         grid=(1,),
-        in_specs=[lanes(seg)] * 3 + [whole_spec((seg + 8, width))] * 2 + [lanes(8)] * 2 + [held] * len(before),
+        in_specs=[whole_spec((seg, full))] * 3
+        + [whole_spec((seg + 8, width))] * 2
+        + [whole_spec((8, full))] * 2
+        + [held] * len(before),
         out_specs=[lanes(seg), lanes(seg), lanes(1)],
         out_shape=[f32(seg, full), f32(seg, full), f32(1, full)],
         input_output_aliases={7 + i: i for i in range(len(before))},

time: 69.4 us -> 69.4 us (level)
  no operation moved by 1% of the time
where the time goes in v15:
time: 69.4 us; the launch traced here: 68.9 us
  Pallas kernels  25.4 us (37%)
  waiting for transfers between devices  22.3 us (32%)
  starting transfers between devices  15.7 us (23%)
  local copies, waits for them, and re-layouts  3.35 us (5%)
  other arithmetic  1.27 us (2%)
  between operations  0.93 us (1%)
    ppermute x10, waiting for transfers between devices, send(): return lax.ppermute(x, 'ctx', list(pairs))  22.3 us
    ppermute x10, starting transfers between devices, send(): return lax.ppermute(x, 'ctx', list(pairs))  15.7 us
    pallas_call x9, Pallas kernels, dft(): pl.pallas_call(functools.partial(dft_kernel, choose), grid_spec=pltpu.Pre...  6.47 us
    pallas_call x1, Pallas kernels, late(): pl.pallas_call(late_kernel, grid_spec=pltpu.PrefetchScalarGridSpec(num_sc...  6.03 us
    pallas_call x1, Pallas kernels, taps_spectra(): pl.pallas_call(taps_kernel, grid=(blocks,), in_specs=[whole_spec(table.sh...  5.95 us
    unnamed x20, local copies, waits for them, and re-layouts  3.35 us
    pallas_call x2, Pallas kernels, back_partial(): pl.pallas_call(partial_kernel, grid_spec=pltpu.PrefetchScalarGridSpec(num...  2.73 us
    pallas_call x1, Pallas kernels, early(): pl.pallas_call(early_kernel, grid_spec=pltpu.PrefetchScalarGridSpec(num_s...  2.2 us
  transfers between devices with their start and end apart: 10, of which 6 were waited for; matrix products, arithmetic and copies ran while one was open for 0% of the time, Pallas kernels for 36%

profile of v15, /device:TPU:0, one launch (start us, length us, event | category | flops | bytes accessed | tf_op | source)
XLA Modules:
  0.0 68.9 jit_solution(1708757390060556765)
XLA Ops:
  0.6 1.3 %mul.3.gated_ref.refs_0_.rest_1_ = f32[512,256]{1,0:T(8,128)S(1)} multiply(f32[512,256]{1,0:T(8,128)} %key_ref.3, f32[512,256]{1,0:T(8,128)} %values_ref.3) | non-fusion elementwise | flops 131072 | bytes 1572864 | tf_op jit(solution)/shard_map/mul | solution.py:565
  1.9 0.7 %collective-permute-start.2 = (f32[512,256]{1,0:T(8,128)S(1)}, f32[512,256]{1,0:T(8,128)S(1)}, u32[]{:S(2)}, u32[]{:S(2)}) collective-permute-start(f32[512,256]{1,0:T(8,128)S(1)} %mul.3.gated_ref.refs_0_.rest_1_), channel_id=1, source_target_pairs={{4,8},{8,4},{5,9},{9,5},{6,10},{10,6},{7,11},{11,7},{20,24},{24,20... | collective-permute-start | bytes 1572872 | tf_op jit(solution)/shard_map/ppermute | solution.py:543
  2.6 5.9 %collective-permute-start.3 = (f32[512,256]{1,0:T(8,128)S(1)}, f32[512,256]{1,0:T(8,128)S(1)}, u32[]{:S(2)}, u32[]{:S(2)}) collective-permute-start(f32[512,256]{1,0:T(8,128)S(1)} %mul.3.gated_ref.refs_0_.rest_1_), channel_id=1, source_target_pairs={{0,4},{4,0},{8,12},{12,8},{1,5},{5,1},{9,13},{13,9},{2,6},{6,2},{1... | collective-permute-start | bytes 1572872 | tf_op jit(solution)/shard_map/ppermute | solution.py:543
  8.5 1.0 %copy-done.6 = f32[512,256]{1,0:T(8,128)S(1)} copy-done((f32[512,256]{1,0:T(8,128)S(1)}, f32[512,256]{1,0:T(8,128)}, u32[]{:S(2)}) %copy-start.6) | copy-done | bytes 524312
  9.5 1.0 %copy-done.8 = f32[512,256]{1,0:T(8,128)S(1)} copy-done((f32[512,256]{1,0:T(8,128)S(1)}, f32[512,256]{1,0:T(8,128)}, u32[]{:S(2)}) %copy-start.8) | copy-done | bytes 524312
  10.6 0.1 mix.1
  10.6 0.7 %collective-permute-start = (f32[512,256]{1,0:T(8,128)S(1)}, f32[512,256]{1,0:T(8,128)S(1)}, u32[]{:S(2)}, u32[]{:S(2)}) collective-permute-start(f32[512,256]{1,0:T(8,128)S(1)} %get-tuple-element.44.refs_0_.rest_2_), channel_id=1, source_target_pairs={{4,8},{8,4},{5,9},{9,5},{6,10},{10,6},{7,11},{11,7},{20,24},{24,20... | collective-permute-start | bytes 1572872 | tf_op jit(solution)/shard_map/ppermute | solution.py:543
  11.3 1.7 %collective-permute-start.1 = (f32[512,256]{1,0:T(8,128)S(1)}, f32[512,256]{1,0:T(8,128)S(1)}, u32[]{:S(2)}, u32[]{:S(2)}) collective-permute-start(f32[512,256]{1,0:T(8,128)S(1)} %get-tuple-element.44.refs_0_.rest_2_), channel_id=1, source_target_pairs={{0,4},{4,0},{8,12},{12,8},{1,5},{5,1},{9,13},{13,9},{2,6},{6,2},{1... | collective-permute-start | bytes 1572872 | tf_op jit(solution)/shard_map/ppermute | solution.py:543
  13.1 1.2 %copy-done = bf16[2,4,256,256]{3,2,1,0:T(8,128)(2,1)S(1)} copy-done((bf16[2,4,256,256]{3,2,1,0:T(8,128)(2,1)S(1)}, bf16[2,4,256,256]{3,2,1,0:T(8,128)(2,1)}, u32[]{:S(2)}) %copy-start) | copy-done | bytes 1048600
  14.3 0.7 %dft.10.own_m = f32[1024,256]{1,0:T(8,128)S(1)} custom-call(s32[1]{0:T(128)} %bitcast.pos_ref, bf16[2,4,256,256]{3,2,1,0:T(8,128)(2,1)S(1)} %copy-done, f32[512,256]{1,0:T(8,128)S(1)} %get-tuple-element.44.refs_0_.rest_2_), custom_call_target="tpu_custom_call" | custom-call | flops 402653184 | bytes 1572864 | tf_op jit(solution)/shard_map/dft/pallas_call | solution.py:153
  15.0 0.0 copy-start.1
  15.0 0.0 copy-start.5
  15.1 0.7 %dft.9.own_g = f32[1024,256]{1,0:T(8,128)S(1)} custom-call(s32[1]{0:T(128)} %bitcast.pos_ref, bf16[2,4,256,256]{3,2,1,0:T(8,128)(2,1)S(1)} %copy-done, f32[512,256]{1,0:T(8,128)S(1)} %mul.3.gated_ref.refs_0_.rest_1_), custom_call_target="tpu_custom_call" | custom-call | flops 402653184 | bytes 1572864 | tf_op jit(solution)/shard_map/dft/pallas_call | solution.py:153
  15.8 0.0 collective-permute-done.2.refs_0_.gated_ref
  15.8 5.5 %collective-permute-done.3.refs_0_.refs_1_.gated_ref = f32[512,256]{1,0:T(8,128)S(1)} collective-permute-done((f32[512,256]{1,0:T(8,128)S(1)}, f32[512,256]{1,0:T(8,128)S(1)}, u32[]{:S(2)}, u32[]{:S(2)}) %collective-permute-start.3) | collective-permute-done | bytes 524320 | tf_op jit(solution)/shard_map/ppermute | solution.py:543
  21.3 0.7 collective-permute-start.5
  22.0 1.3 %collective-permute-start.6 = (f32[512,256]{1,0:T(8,128)S(1)}, f32[512,256]{1,0:T(8,128)S(1)}, u32[]{:S(2)}, u32[]{:S(2)}) collective-permute-start(f32[512,256]{1,0:T(8,128)S(1)} %collective-permute-done.2.refs_0_.gated_ref), channel_id=1, source_target_pairs={{4,0},{8,12},{5,1},{9,13},{6,2},{10,14},{7,3},{11,15},{20,16},{24,... | collective-permute-start | bytes 1572872 | tf_op jit(solution)/shard_map/ppermute | solution.py:543
  23.3 0.7 %dft.12.next_g = f32[1024,256]{1,0:T(8,128)S(1)} custom-call(s32[1]{0:T(128)} %bitcast.pos_ref, bf16[2,4,256,256]{3,2,1,0:T(8,128)(2,1)S(1)} %copy-done, f32[512,256]{1,0:T(8,128)S(1)} %collective-permute-done.2.refs_0_.gated_ref, f32[512,256]{1,0:T(8,128)S(1)} %collective-permute-done.3.refs_0_.refs_1_.gated_ref), custom_call_target="tpu_custom_call" | custom-call | flops 402653184 | bytes 1572864 | tf_op jit(solution)/shard_map/dft/pallas_call | solution.py:153
  24.0 0.7 %dft.11.outer_g = f32[1024,256]{1,0:T(8,128)S(1)} custom-call(s32[1]{0:T(128)} %bitcast.pos_ref, bf16[2,4,256,256]{3,2,1,0:T(8,128)(2,1)S(1)} %copy-done, f32[512,256]{1,0:T(8,128)S(1)} %collective-permute-done.3.refs_0_.refs_1_.gated_ref), custom_call_target="tpu_custom_call" | custom-call | flops 402653184 | bytes 1572864 | tf_op jit(solution)/shard_map/dft/pallas_call | solution.py:153
  24.7 5.9 %taps.1.win_own.win_outer.win_next.win_two.win_near.win_far.win_ref = f32[7,1024,256]{2,1,0:T(8,128)S(1)} custom-call(bf16[2,4,256,256]{3,2,1,0:T(8,128)(2,1)S(1)} %copy-done.1, f32[4096,256]{1,0:T(8,128)S(1)} %copy-done.5), custom_call_target="tpu_custom_call" | custom-call | flops 3221225472 | bytes 12582912 | tf_op jit(solution)/shard_map/taps/pallas_call | solution.py:191
  30.7 1.8 %collective-permute-done.1.refs_0_.refs_1_.mixed_ref = f32[512,256]{1,0:T(8,128)S(1)} collective-permute-done((f32[512,256]{1,0:T(8,128)S(1)}, f32[512,256]{1,0:T(8,128)S(1)}, u32[]{:S(2)}, u32[]{:S(2)}) %collective-permute-start.1) | collective-permute-done | bytes 524320 | tf_op jit(solution)/shard_map/ppermute | solution.py:543
  32.5 0.7 %dft.13.outer_m = f32[1024,256]{1,0:T(8,128)S(1)} custom-call(s32[1]{0:T(128)} %bitcast.pos_ref, bf16[2,4,256,256]{3,2,1,0:T(8,128)(2,1)S(1)} %copy-done.1, f32[512,256]{1,0:T(8,128)S(1)} %collective-permute-done.1.refs_0_.refs_1_.mixed_ref), custom_call_target="tpu_custom_call" | custom-call | flops 402653184 | bytes 1572864 | tf_op jit(solution)/shard_map/dft/pallas_call | solution.py:153
  33.2 0.7 %dft.14.next_m.next_ref = f32[1024,256]{1,0:T(8,128)S(1)} custom-call(s32[1]{0:T(128)} %bitcast.pos_ref, bf16[2,4,256,256]{3,2,1,0:T(8,128)(2,1)S(1)} %copy-done.1, f32[512,256]{1,0:T(8,128)S(1)} %collective-permute-done.refs_0_.mixed_ref, f32[512,256]{1,0:T(8,128)S(1)} %collective-permute-done.1.refs_0_.refs_1_.mixed_ref), custom_call_target="tpu_custom_call" | custom-call | flops 402653184 | bytes 1572864 | tf_op jit(solution)/shard_map/dft/pallas_call | solution.py:153
  34.0 0.7 %collective-permute-start.4 = (f32[512,256]{1,0:T(8,128)S(1)}, f32[512,256]{1,0:T(8,128)S(1)}, u32[]{:S(2)}, u32[]{:S(2)}) collective-permute-start(f32[512,256]{1,0:T(8,128)S(1)} %collective-permute-done.1.refs_0_.refs_1_.mixed_ref), channel_id=1, source_target_pairs={{4,8},{8,4},{5,9},{9,5},{6,10},{10,6},{7,11},{11,7},{20,24},{24,20... | collective-permute-start | bytes 1572872 | tf_op jit(solution)/shard_map/ppermute | solution.py:543
  34.7 0.1 sums.3.near_sums
  34.8 0.1 sums.2.side_ref
  34.9 0.0 collective-permute-done.5.refs_0_.gated_ref
  34.9 1.3 %collective-permute-start.7 = (f32[512,256]{1,0:T(8,128)S(1)}, f32[512,256]{1,0:T(8,128)S(1)}, u32[]{:S(2)}, u32[]{:S(2)}) collective-permute-start(f32[512,256]{1,0:T(8,128)S(1)} %collective-permute-done.5.refs_0_.gated_ref), channel_id=1, source_target_pairs={{4,0},{8,12},{5,1},{9,13},{6,2},{10,14},{7,3},{11,15},{20,16},{24,... | collective-permute-start | bytes 1572872 | tf_op jit(solution)/shard_map/ppermute | solution.py:543
  36.2 6.4 %collective-permute-done.6.refs_1_ = f32[512,256]{1,0:T(8,128)S(1)} collective-permute-done((f32[512,256]{1,0:T(8,128)S(1)}, f32[512,256]{1,0:T(8,128)S(1)}, u32[]{:S(2)}, u32[]{:S(2)}) %collective-permute-start.6) | collective-permute-done | bytes 524320 | tf_op jit(solution)/shard_map/ppermute | solution.py:543
  42.6 0.7 %dft.15.two_g = f32[1024,256]{1,0:T(8,128)S(1)} custom-call(s32[1]{0:T(128)} %bitcast.pos_ref, bf16[2,4,256,256]{3,2,1,0:T(8,128)(2,1)S(1)} %copy-done.1, f32[512,256]{1,0:T(8,128)S(1)} %collective-permute-done.5.refs_0_.gated_ref, f32[512,256]{1,0:T(8,128)S(1)} %collective-permute-done.6.refs_1_), custom_call_target="tpu_custom_call" | custom-call | flops 402653184 | bytes 1572864 | tf_op jit(solution)/shard_map/dft/pallas_call | solution.py:153
  43.3 0.0 copy-start.2
  43.3 2.2 %early.1.acc_ref = f32[4,1024,256]{2,1,0:T(8,128)S(1)} custom-call(s32[1]{0:T(128)} %bitcast.pos_ref, f32[7,1024,256]{2,1,0:T(8,128)S(1)} %taps.1.win_own.win_outer.win_next.win_two.win_near.win_far.win_ref, f32[7,1024,256]{2,1,0:T(8,128)S(1)} %taps.1.win_own.win_outer.win_next.win_two.win_near.win_far.win_ref, ...), custom_call_target="tpu_custom_call" | custom-call | flops 26214400 | bytes 15728640 | tf_op jit(solution)/shard_map/early/pallas_call | solution.py:380
  45.6 1.4 %partial.2.made_ref = f32[520,128]{1,0:T(8,128)S(1)} custom-call(s32[1]{0:T(128)} %bitcast.pos_ref, bf16[2,4,256,256]{3,2,1,0:T(8,128)(2,1)S(1)} %copy-done.1, bf16[2,4,256,256]{3,2,1,0:T(8,128)(2,1)S(1)} %copy-done.2, f32[7,1024,256]{2,1,0:T(8,128)S(1)} %taps.1.win_own.win_outer.win_next.win_two.win_near.win_far.win_ref, ...), custom_call_target="tpu_custom_call" | custom-call | flops 402653184 | bytes 1572864 | tf_op jit(solution)/shard_map/partial/pallas_call | solution.py:249
  46.9 1.3 %collective-permute-start.9 = (f32[520,128]{1,0:T(8,128)S(1)}, f32[520,128]{1,0:T(8,128)S(1)}, u32[]{:S(2)}, u32[]{:S(2)}) collective-permute-start(f32[520,128]{1,0:T(8,128)S(1)} %partial.2.made_ref), channel_id=1, source_target_pairs={{4,0},{8,12},{5,1},{9,13},{6,2},{10,14},{7,3},{11,15},{20,16},{24,... | collective-permute-start | bytes 798728 | tf_op jit(solution)/shard_map/ppermute | solution.py:543
  48.2 1.4 %partial.3.made_ref = f32[520,128]{1,0:T(8,128)S(1)} custom-call(s32[1]{0:T(128)} %bitcast.pos_ref, bf16[2,4,256,256]{3,2,1,0:T(8,128)(2,1)S(1)} %copy-done.1, bf16[2,4,256,256]{3,2,1,0:T(8,128)(2,1)S(1)} %copy-done.2, f32[7,1024,256]{2,1,0:T(8,128)S(1)} %taps.1.win_own.win_outer.win_next.win_two.win_near.win_far.win_ref, ...), custom_call_target="tpu_custom_call" | custom-call | flops 402653184 | bytes 1572864 | tf_op jit(solution)/shard_map/partial/pallas_call | solution.py:249
  49.6 0.0 copy-start.7
  49.6 0.0 copy-start.9
  49.6 1.4 %collective-permute-start.8 = (f32[520,128]{1,0:T(8,128)S(1)}, f32[520,128]{1,0:T(8,128)S(1)}, u32[]{:S(2)}, u32[]{:S(2)}) collective-permute-start(f32[520,128]{1,0:T(8,128)S(1)} %partial.3.made_ref), channel_id=1, source_target_pairs={{4,0},{8,12},{5,1},{9,13},{6,2},{10,14},{7,3},{11,15},{20,16},{24,... | collective-permute-start | bytes 798728 | tf_op jit(solution)/shard_map/ppermute | solution.py:543
  51.1 0.7 %dft.17.rest_0_ = f32[1024,256]{1,0:T(8,128)S(1)} custom-call(s32[1]{0:T(128)} %bitcast.pos_ref, bf16[2,4,256,256]{3,2,1,0:T(8,128)(2,1)S(1)} %copy-done.1, f32[512,256]{1,0:T(8,128)S(1)} %collective-permute-done.4.x_ref.refs_0_), custom_call_target="tpu_custom_call" | custom-call | flops 402653184 | bytes 1572864 | tf_op jit(solution)/shard_map/dft/pallas_call | solution.py:153
  51.8 3.5 %collective-permute-done.7.refs_0_ = f32[512,256]{1,0:T(8,128)S(1)} collective-permute-done((f32[512,256]{1,0:T(8,128)S(1)}, f32[512,256]{1,0:T(8,128)S(1)}, u32[]{:S(2)}, u32[]{:S(2)}) %collective-permute-start.7) | collective-permute-done | bytes 524320 | tf_op jit(solution)/shard_map/ppermute | solution.py:543
  55.3 0.7 %dft.16.three_g = f32[1024,256]{1,0:T(8,128)S(1)} custom-call(s32[1]{0:T(128)} %bitcast.pos_ref, bf16[2,4,256,256]{3,2,1,0:T(8,128)(2,1)S(1)} %copy-done.1, f32[512,256]{1,0:T(8,128)S(1)} %collective-permute-done.7.refs_0_), custom_call_target="tpu_custom_call" | custom-call | flops 402653184 | bytes 1572864 | tf_op jit(solution)/shard_map/dft/pallas_call | solution.py:153
  56.0 0.0 copy-start.3
  56.0 0.0 copy-start.4
  56.0 6.0 %late.1 = (f32[512,256]{1,0:T(8,128)}, f32[1024,256]{1,0:T(8,128)}, f32[512,256]{1,0:T(8,128)S(1)}) custom-call(s32[1]{0:T(128)} %bitcast.pos_ref, bf16[2,4,256,256]{3,2,1,0:T(8,128)(2,1)S(1)} %copy-done.2, f32[4,1024,256]{2,1,0:T(8,128)S(1)} %early.1.acc_ref, f32[7,1024,256]{2,1,0:T(8,128)S(1)} %taps.1.win_own.win_outer.win_next.win_two.win_near.win_far.win_ref, ...), custom_call_target="tpu_custom_call" | custom-call | flops 1610612736 | bytes 13107200 | tf_op jit(solution)/shard_map/late/pallas_call | solution.py:477
  62.1 2.1 %collective-permute-done.9.sent_ref = f32[520,128]{1,0:T(8,128)S(1)} collective-permute-done((f32[520,128]{1,0:T(8,128)S(1)}, f32[520,128]{1,0:T(8,128)S(1)}, u32[]{:S(2)}, u32[]{:S(2)}) %collective-permute-start.9) | collective-permute-done | bytes 266272 | tf_op jit(solution)/shard_map/ppermute | solution.py:543
  64.2 0.9 %finish.2 = (f32[512,256]{1,0:T(8,128)}, f32[512,256]{1,0:T(8,128)}, f32[1,256]{1,0:T(1,128)}) custom-call(f32[512,256]{1,0:T(8,128)S(1)} %get-tuple-element.67.back_ref, f32[512,256]{1,0:T(8,128)S(1)} %copy-done.3, f32[512,256]{1,0:T(8,128)S(1)} %copy-done.4, f32[520,128]{1,0:T(8,128)S(1)} %partial.2.made_ref, ...), custom_call_target="tpu_custom_call" | custom-call | flops 196608 | bytes 1572864 | tf_op jit(solution)/shard_map/finish/pallas_call | solution.py:526
  65.0 3.0 %collective-permute-done.8.sent_ref = f32[520,128]{1,0:T(8,128)S(1)} collective-permute-done((f32[520,128]{1,0:T(8,128)S(1)}, f32[520,128]{1,0:T(8,128)S(1)}, u32[]{:S(2)}, u32[]{:S(2)}) %collective-permute-start.8) | collective-permute-done | bytes 266272 | tf_op jit(solution)/shard_map/ppermute | solution.py:543
  68.1 0.9 %finish.3 = (f32[512,256]{1,0:T(8,128)}, f32[512,256]{1,0:T(8,128)}, f32[1,256]{1,0:T(1,128)}) custom-call(f32[512,256]{1,0:T(8,128)S(1)} %get-tuple-element.67.back_ref, f32[512,256]{1,0:T(8,128)S(1)} %copy-done.3, f32[512,256]{1,0:T(8,128)S(1)} %copy-done.4, ...), custom_call_target="tpu_custom_call", output_to_operand_aliasing={{0}: (7, {}), {1}: (8, {}), {2}: (9, {})} | custom-call | flops 196608 | bytes 1572864 | tf_op jit(solution)/shard_map/finish/pallas_call | solution.py:526
  (12 shorter events, 0.0 us)
Async XLA Ops:
  1.9 13.9 %collective-permute-start.2 = (f32[512,256]{1,0:T(8,128)S(1)}, f32[512,256]{1,0:T(8,128)S(1)}, u32[]{:S(2)}, u32[]{:S(2)}) collective-permute-start(f32[512,256]{1,0:T(8,128)S(1)} %mul.3.gated_ref.refs_0_.rest_1_), channel_id=1, source_target_pairs={{4,8},{8,4},{5,9},{9,5},{6,10},{10,6},{7,11},{11,7},{20,24},{24,20... | collective-permute-start | bytes 1572872 | tf_op jit(solution)/shard_map/ppermute | solution.py:543
  2.6 18.7 %collective-permute-start.3 = (f32[512,256]{1,0:T(8,128)S(1)}, f32[512,256]{1,0:T(8,128)S(1)}, u32[]{:S(2)}, u32[]{:S(2)}) collective-permute-start(f32[512,256]{1,0:T(8,128)S(1)} %mul.3.gated_ref.refs_0_.rest_1_), channel_id=1, source_target_pairs={{0,4},{4,0},{8,12},{12,8},{1,5},{5,1},{9,13},{13,9},{2,6},{6,2},{1... | collective-permute-start | bytes 1572872 | tf_op jit(solution)/shard_map/ppermute | solution.py:543
  8.5 1.0 %copy-start.6 = (f32[512,256]{1,0:T(8,128)S(1)}, f32[512,256]{1,0:T(8,128)}, u32[]{:S(2)}) copy-start(f32[512,256]{1,0:T(8,128)} %rest_4_.1) | copy-start | bytes 1572868
  9.5 1.0 %copy-start.8 = (f32[512,256]{1,0:T(8,128)S(1)}, f32[512,256]{1,0:T(8,128)}, u32[]{:S(2)}) copy-start(f32[512,256]{1,0:T(8,128)} %query_ref.1) | copy-start | bytes 1572868
  10.6 20.1 %collective-permute-start = (f32[512,256]{1,0:T(8,128)S(1)}, f32[512,256]{1,0:T(8,128)S(1)}, u32[]{:S(2)}, u32[]{:S(2)}) collective-permute-start(f32[512,256]{1,0:T(8,128)S(1)} %get-tuple-element.44.refs_0_.rest_2_), channel_id=1, source_target_pairs={{4,8},{8,4},{5,9},{9,5},{6,10},{10,6},{7,11},{11,7},{20,24},{24,20... | collective-permute-start | bytes 1572872 | tf_op jit(solution)/shard_map/ppermute | solution.py:543
  11.3 21.2 %collective-permute-start.1 = (f32[512,256]{1,0:T(8,128)S(1)}, f32[512,256]{1,0:T(8,128)S(1)}, u32[]{:S(2)}, u32[]{:S(2)}) collective-permute-start(f32[512,256]{1,0:T(8,128)S(1)} %get-tuple-element.44.refs_0_.rest_2_), channel_id=1, source_target_pairs={{0,4},{4,0},{8,12},{12,8},{1,5},{5,1},{9,13},{13,9},{2,6},{6,2},{1... | collective-permute-start | bytes 1572872 | tf_op jit(solution)/shard_map/ppermute | solution.py:543
  13.1 1.2 %copy-start = (bf16[2,4,256,256]{3,2,1,0:T(8,128)(2,1)S(1)}, bf16[2,4,256,256]{3,2,1,0:T(8,128)(2,1)}, u32[]{:S(2)}) copy-start(bf16[2,4,256,256]{3,2,1,0:T(8,128)(2,1)} %constant.9.clone.table_ref) | copy-start | bytes 3145732
  15.0 9.7 %copy-start.1 = (bf16[2,4,256,256]{3,2,1,0:T(8,128)(2,1)S(1)}, bf16[2,4,256,256]{3,2,1,0:T(8,128)(2,1)}, u32[]{:S(2)}) copy-start(bf16[2,4,256,256]{3,2,1,0:T(8,128)(2,1)} %constant.9.clone.table_ref) | copy-start | bytes 3145732
  15.0 9.7 %copy-start.5 = (f32[4096,256]{1,0:T(8,128)S(1)}, f32[4096,256]{1,0:T(8,128)}, u32[]{:S(2)}) copy-start(f32[4096,256]{1,0:T(8,128)} %x_ref) | copy-start | bytes 12582916
  21.3 13.6 %collective-permute-start.5 = (f32[512,256]{1,0:T(8,128)S(1)}, f32[512,256]{1,0:T(8,128)S(1)}, u32[]{:S(2)}, u32[]{:S(2)}) collective-permute-start(f32[512,256]{1,0:T(8,128)S(1)} %collective-permute-done.3.refs_0_.refs_1_.gated_ref), channel_id=1, source_target_pairs={{4,8},{8,4},{5,9},{9,5},{6,10},{10,6},{7,11},{11,7},{20,24},{24,20... | collective-permute-start | bytes 1572872 | tf_op jit(solution)/shard_map/ppermute | solution.py:543
  22.0 20.6 %collective-permute-start.6 = (f32[512,256]{1,0:T(8,128)S(1)}, f32[512,256]{1,0:T(8,128)S(1)}, u32[]{:S(2)}, u32[]{:S(2)}) collective-permute-start(f32[512,256]{1,0:T(8,128)S(1)} %collective-permute-done.2.refs_0_.gated_ref), channel_id=1, source_target_pairs={{4,0},{8,12},{5,1},{9,13},{6,2},{10,14},{7,3},{11,15},{20,16},{24,... | collective-permute-start | bytes 1572872 | tf_op jit(solution)/shard_map/ppermute | solution.py:543
  34.0 11.6 %collective-permute-start.4 = (f32[512,256]{1,0:T(8,128)S(1)}, f32[512,256]{1,0:T(8,128)S(1)}, u32[]{:S(2)}, u32[]{:S(2)}) collective-permute-start(f32[512,256]{1,0:T(8,128)S(1)} %collective-permute-done.1.refs_0_.refs_1_.mixed_ref), channel_id=1, source_target_pairs={{4,8},{8,4},{5,9},{9,5},{6,10},{10,6},{7,11},{11,7},{20,24},{24,20... | collective-permute-start | bytes 1572872 | tf_op jit(solution)/shard_map/ppermute | solution.py:543
  34.9 20.4 %collective-permute-start.7 = (f32[512,256]{1,0:T(8,128)S(1)}, f32[512,256]{1,0:T(8,128)S(1)}, u32[]{:S(2)}, u32[]{:S(2)}) collective-permute-start(f32[512,256]{1,0:T(8,128)S(1)} %collective-permute-done.5.refs_0_.gated_ref), channel_id=1, source_target_pairs={{4,0},{8,12},{5,1},{9,13},{6,2},{10,14},{7,3},{11,15},{20,16},{24,... | collective-permute-start | bytes 1572872 | tf_op jit(solution)/shard_map/ppermute | solution.py:543
  43.3 2.2 %copy-start.2 = (bf16[2,4,256,256]{3,2,1,0:T(8,128)(2,1)S(1)}, bf16[2,4,256,256]{3,2,1,0:T(8,128)(2,1)}, u32[]{:S(2)}) copy-start(bf16[2,4,256,256]{3,2,1,0:T(8,128)(2,1)} %constant.10.clone.inverse_ref) | copy-start | bytes 3145732
  46.9 17.2 %collective-permute-start.9 = (f32[520,128]{1,0:T(8,128)S(1)}, f32[520,128]{1,0:T(8,128)S(1)}, u32[]{:S(2)}, u32[]{:S(2)}) collective-permute-start(f32[520,128]{1,0:T(8,128)S(1)} %partial.2.made_ref), channel_id=1, source_target_pairs={{4,0},{8,12},{5,1},{9,13},{6,2},{10,14},{7,3},{11,15},{20,16},{24,... | collective-permute-start | bytes 798728 | tf_op jit(solution)/shard_map/ppermute | solution.py:543
  49.6 6.4 %copy-start.7 = (f32[512,256]{1,0:T(8,128)S(1)}, f32[512,256]{1,0:T(8,128)}, u32[]{:S(2)}) copy-start(f32[512,256]{1,0:T(8,128)} %rest_4_.1) | copy-start | bytes 1572868
  49.6 6.4 %copy-start.9 = (f32[256]{0:T(256)S(1)}, f32[256]{0:T(256)}, u32[]{:S(2)}) copy-start(f32[256]{0:T(256)} %param.12) | copy-start | bytes 3076
  49.6 18.4 %collective-permute-start.8 = (f32[520,128]{1,0:T(8,128)S(1)}, f32[520,128]{1,0:T(8,128)S(1)}, u32[]{:S(2)}, u32[]{:S(2)}) collective-permute-start(f32[520,128]{1,0:T(8,128)S(1)} %partial.3.made_ref), channel_id=1, source_target_pairs={{4,0},{8,12},{5,1},{9,13},{6,2},{10,14},{7,3},{11,15},{20,16},{24,... | collective-permute-start | bytes 798728 | tf_op jit(solution)/shard_map/ppermute | solution.py:543
  56.0 8.1 %copy-start.3 = (f32[512,256]{1,0:T(8,128)S(1)}, f32[512,256]{1,0:T(8,128)}, u32[]{:S(2)}) copy-start(f32[512,256]{1,0:T(8,128)} %key_ref.3) | copy-start | bytes 1572868
  56.0 8.1 %copy-start.4 = (f32[512,256]{1,0:T(8,128)S(1)}, f32[512,256]{1,0:T(8,128)}, u32[]{:S(2)}) copy-start(f32[512,256]{1,0:T(8,128)} %values_ref.3) | copy-start | bytes 1572868

commit v16 on v15

--- a/solution.py
+++ b/solution.py
@@ -573,7 +573,7 @@
     outer_g = dft(pos, table, seg, side, choose=True)
     next_g = dft(pos, table, seg, over, side, choose=True)
     windows = taps_spectra(table, filter_taps, seg)
-    over_x, side_x, windows, outer_g, next_g = after((over_x, side_x, windows, outer_g, next_g))
+    side_x, over_x, windows, outer_g, next_g = after((side_x, over_x, windows, outer_g, next_g))
 
     outer_m = dft(pos, table, seg, side_x, choose=True)
     next_m = dft(pos, table, seg, over_x, side_x, choose=True)

time: 69.4 us -> 69.4 us (level)
  starting transfers between devices: 15.7 us -> 14 us
  waiting for transfers between devices: 22.3 us -> 23.9 us
    ppermute x10, starting transfers between devices: 15.7 us -> 14 us  [send(): return lax.ppermute(x, 'ctx', list(pairs))]
    ppermute x10, waiting for transfers between devices: 22.3 us -> 23.9 us  [send(): return lax.ppermute(x, 'ctx', list(pairs))]
where the time goes in v16:
time: 69.4 us; the launch traced here: 68.9 us
  Pallas kernels  25.4 us (37%)
  waiting for transfers between devices  23.9 us (34%)
  starting transfers between devices  14 us (20%)
  local copies, waits for them, and re-layouts  3.35 us (5%)
  other arithmetic  1.27 us (2%)
  between operations  0.94 us (1%)
    ppermute x10, waiting for transfers between devices, send(): return lax.ppermute(x, 'ctx', list(pairs))  23.9 us
    ppermute x10, starting transfers between devices, send(): return lax.ppermute(x, 'ctx', list(pairs))  14 us
    pallas_call x9, Pallas kernels, dft(): pl.pallas_call(functools.partial(dft_kernel, choose), grid_spec=pltpu.Pre...  6.48 us
    pallas_call x1, Pallas kernels, late(): pl.pallas_call(late_kernel, grid_spec=pltpu.PrefetchScalarGridSpec(num_sc...  6.03 us
    pallas_call x1, Pallas kernels, taps_spectra(): pl.pallas_call(taps_kernel, grid=(blocks,), in_specs=[whole_spec(table.sh...  5.95 us
    unnamed x20, local copies, waits for them, and re-layouts  3.35 us
    pallas_call x2, Pallas kernels, back_partial(): pl.pallas_call(partial_kernel, grid_spec=pltpu.PrefetchScalarGridSpec(num...  2.73 us
    pallas_call x1, Pallas kernels, early(): pl.pallas_call(early_kernel, grid_spec=pltpu.PrefetchScalarGridSpec(num_s...  2.2 us
  transfers between devices with their start and end apart: 10, of which 6 were waited for; matrix products, arithmetic and copies ran while one was open for 0% of the time, Pallas kernels for 36%

profile of v16, /device:TPU:0, one launch (start us, length us, event | category | flops | bytes accessed | tf_op | source)
XLA Modules:
  0.0 68.9 jit_solution(4626110666085544159)
XLA Ops:
  0.6 1.3 %mul.3.gated_ref.refs_0_.rest_1_ = f32[512,256]{1,0:T(8,128)S(1)} multiply(f32[512,256]{1,0:T(8,128)} %key_ref.3, f32[512,256]{1,0:T(8,128)} %values_ref.3) | non-fusion elementwise | flops 131072 | bytes 1572864 | tf_op jit(solution)/shard_map/mul | solution.py:565
  1.9 0.7 %collective-permute-start.2 = (f32[512,256]{1,0:T(8,128)S(1)}, f32[512,256]{1,0:T(8,128)S(1)}, u32[]{:S(2)}, u32[]{:S(2)}) collective-permute-start(f32[512,256]{1,0:T(8,128)S(1)} %mul.3.gated_ref.refs_0_.rest_1_), channel_id=1, source_target_pairs={{4,8},{8,4},{5,9},{9,5},{6,10},{10,6},{7,11},{11,7},{20,24},{24,20... | collective-permute-start | bytes 1572872 | tf_op jit(solution)/shard_map/ppermute | solution.py:543
  2.6 5.9 %collective-permute-start.3 = (f32[512,256]{1,0:T(8,128)S(1)}, f32[512,256]{1,0:T(8,128)S(1)}, u32[]{:S(2)}, u32[]{:S(2)}) collective-permute-start(f32[512,256]{1,0:T(8,128)S(1)} %mul.3.gated_ref.refs_0_.rest_1_), channel_id=1, source_target_pairs={{0,4},{4,0},{8,12},{12,8},{1,5},{5,1},{9,13},{13,9},{2,6},{6,2},{1... | collective-permute-start | bytes 1572872 | tf_op jit(solution)/shard_map/ppermute | solution.py:543
  8.5 1.0 %copy-done.6 = f32[512,256]{1,0:T(8,128)S(1)} copy-done((f32[512,256]{1,0:T(8,128)S(1)}, f32[512,256]{1,0:T(8,128)}, u32[]{:S(2)}) %copy-start.6) | copy-done | bytes 524312
  9.5 1.0 %copy-done.8 = f32[512,256]{1,0:T(8,128)S(1)} copy-done((f32[512,256]{1,0:T(8,128)S(1)}, f32[512,256]{1,0:T(8,128)}, u32[]{:S(2)}) %copy-start.8) | copy-done | bytes 524312
  10.6 0.1 mix.1
  10.6 0.1 collective-permute-start
  10.7 0.7 %collective-permute-start.1 = (f32[512,256]{1,0:T(8,128)S(1)}, f32[512,256]{1,0:T(8,128)S(1)}, u32[]{:S(2)}, u32[]{:S(2)}) collective-permute-start(f32[512,256]{1,0:T(8,128)S(1)} %get-tuple-element.44.refs_0_.rest_2_), channel_id=1, source_target_pairs={{4,8},{8,4},{5,9},{9,5},{6,10},{10,6},{7,11},{11,7},{20,24},{24,20... | collective-permute-start | bytes 1572872 | tf_op jit(solution)/shard_map/ppermute | solution.py:543
  11.4 0.0 copy-start
  11.4 1.2 %copy-done = bf16[2,4,256,256]{3,2,1,0:T(8,128)(2,1)S(1)} copy-done((bf16[2,4,256,256]{3,2,1,0:T(8,128)(2,1)S(1)}, bf16[2,4,256,256]{3,2,1,0:T(8,128)(2,1)}, u32[]{:S(2)}) %copy-start) | copy-done | bytes 1048600
  12.7 0.7 %dft.10.own_m = f32[1024,256]{1,0:T(8,128)S(1)} custom-call(s32[1]{0:T(128)} %bitcast.pos_ref, bf16[2,4,256,256]{3,2,1,0:T(8,128)(2,1)S(1)} %copy-done, f32[512,256]{1,0:T(8,128)S(1)} %get-tuple-element.44.refs_0_.rest_2_), custom_call_target="tpu_custom_call" | custom-call | flops 402653184 | bytes 1572864 | tf_op jit(solution)/shard_map/dft/pallas_call | solution.py:153
  13.4 0.0 copy-start.1
  13.4 0.0 copy-start.5
  13.4 0.7 %dft.9.own_g = f32[1024,256]{1,0:T(8,128)S(1)} custom-call(s32[1]{0:T(128)} %bitcast.pos_ref, bf16[2,4,256,256]{3,2,1,0:T(8,128)(2,1)S(1)} %copy-done, f32[512,256]{1,0:T(8,128)S(1)} %mul.3.gated_ref.refs_0_.rest_1_), custom_call_target="tpu_custom_call" | custom-call | flops 402653184 | bytes 1572864 | tf_op jit(solution)/shard_map/dft/pallas_call | solution.py:153
  14.1 0.0 collective-permute-done.2.refs_0_.gated_ref
  14.1 7.1 %collective-permute-done.3.refs_0_.refs_1_.gated_ref = f32[512,256]{1,0:T(8,128)S(1)} collective-permute-done((f32[512,256]{1,0:T(8,128)S(1)}, f32[512,256]{1,0:T(8,128)S(1)}, u32[]{:S(2)}, u32[]{:S(2)}) %collective-permute-start.3) | collective-permute-done | bytes 524320 | tf_op jit(solution)/shard_map/ppermute | solution.py:543
  21.3 0.7 collective-permute-start.5
  22.0 1.3 %collective-permute-start.6 = (f32[512,256]{1,0:T(8,128)S(1)}, f32[512,256]{1,0:T(8,128)S(1)}, u32[]{:S(2)}, u32[]{:S(2)}) collective-permute-start(f32[512,256]{1,0:T(8,128)S(1)} %collective-permute-done.2.refs_0_.gated_ref), channel_id=1, source_target_pairs={{4,0},{8,12},{5,1},{9,13},{6,2},{10,14},{7,3},{11,15},{20,16},{24,... | collective-permute-start | bytes 1572872 | tf_op jit(solution)/shard_map/ppermute | solution.py:543
  23.3 0.7 %dft.12.next_g = f32[1024,256]{1,0:T(8,128)S(1)} custom-call(s32[1]{0:T(128)} %bitcast.pos_ref, bf16[2,4,256,256]{3,2,1,0:T(8,128)(2,1)S(1)} %copy-done, f32[512,256]{1,0:T(8,128)S(1)} %collective-permute-done.2.refs_0_.gated_ref, f32[512,256]{1,0:T(8,128)S(1)} %collective-permute-done.3.refs_0_.refs_1_.gated_ref), custom_call_target="tpu_custom_call" | custom-call | flops 402653184 | bytes 1572864 | tf_op jit(solution)/shard_map/dft/pallas_call | solution.py:153
  24.0 0.7 %dft.11.outer_g = f32[1024,256]{1,0:T(8,128)S(1)} custom-call(s32[1]{0:T(128)} %bitcast.pos_ref, bf16[2,4,256,256]{3,2,1,0:T(8,128)(2,1)S(1)} %copy-done, f32[512,256]{1,0:T(8,128)S(1)} %collective-permute-done.3.refs_0_.refs_1_.gated_ref), custom_call_target="tpu_custom_call" | custom-call | flops 402653184 | bytes 1572864 | tf_op jit(solution)/shard_map/dft/pallas_call | solution.py:153
  24.7 5.9 %taps.1.win_own.win_outer.win_next.win_two.win_near.win_far.win_ref = f32[7,1024,256]{2,1,0:T(8,128)S(1)} custom-call(bf16[2,4,256,256]{3,2,1,0:T(8,128)(2,1)S(1)} %copy-done.1, f32[4096,256]{1,0:T(8,128)S(1)} %copy-done.5), custom_call_target="tpu_custom_call" | custom-call | flops 3221225472 | bytes 12582912 | tf_op jit(solution)/shard_map/taps/pallas_call | solution.py:191
  30.7 1.8 %collective-permute-done.refs_0_.refs_1_.mixed_ref = f32[512,256]{1,0:T(8,128)S(1)} collective-permute-done((f32[512,256]{1,0:T(8,128)S(1)}, f32[512,256]{1,0:T(8,128)S(1)}, u32[]{:S(2)}, u32[]{:S(2)}) %collective-permute-start) | collective-permute-done | bytes 524320 | tf_op jit(solution)/shard_map/ppermute | solution.py:543
  32.5 0.7 %dft.13.outer_m = f32[1024,256]{1,0:T(8,128)S(1)} custom-call(s32[1]{0:T(128)} %bitcast.pos_ref, bf16[2,4,256,256]{3,2,1,0:T(8,128)(2,1)S(1)} %copy-done.1, f32[512,256]{1,0:T(8,128)S(1)} %collective-permute-done.refs_0_.refs_1_.mixed_ref), custom_call_target="tpu_custom_call" | custom-call | flops 402653184 | bytes 1572864 | tf_op jit(solution)/shard_map/dft/pallas_call | solution.py:153
  33.2 0.7 %dft.14.next_m.next_ref = f32[1024,256]{1,0:T(8,128)S(1)} custom-call(s32[1]{0:T(128)} %bitcast.pos_ref, bf16[2,4,256,256]{3,2,1,0:T(8,128)(2,1)S(1)} %copy-done.1, f32[512,256]{1,0:T(8,128)S(1)} %collective-permute-done.1.refs_0_.mixed_ref, f32[512,256]{1,0:T(8,128)S(1)} %collective-permute-done.refs_0_.refs_1_.mixed_ref), custom_call_target="tpu_custom_call" | custom-call | flops 402653184 | bytes 1572864 | tf_op jit(solution)/shard_map/dft/pallas_call | solution.py:153
  34.0 0.7 %collective-permute-start.4 = (f32[512,256]{1,0:T(8,128)S(1)}, f32[512,256]{1,0:T(8,128)S(1)}, u32[]{:S(2)}, u32[]{:S(2)}) collective-permute-start(f32[512,256]{1,0:T(8,128)S(1)} %collective-permute-done.refs_0_.refs_1_.mixed_ref), channel_id=1, source_target_pairs={{4,8},{8,4},{5,9},{9,5},{6,10},{10,6},{7,11},{11,7},{20,24},{24,20... | collective-permute-start | bytes 1572872 | tf_op jit(solution)/shard_map/ppermute | solution.py:543
  34.7 0.1 sums.3.near_sums
  34.8 0.1 sums.2.side_ref
  34.9 1.3 %collective-permute-start.7 = (f32[512,256]{1,0:T(8,128)S(1)}, f32[512,256]{1,0:T(8,128)S(1)}, u32[]{:S(2)}, u32[]{:S(2)}) collective-permute-start(f32[512,256]{1,0:T(8,128)S(1)} %collective-permute-done.5.refs_0_.gated_ref), channel_id=1, source_target_pairs={{4,0},{8,12},{5,1},{9,13},{6,2},{10,14},{7,3},{11,15},{20,16},{24,... | collective-permute-start | bytes 1572872 | tf_op jit(solution)/shard_map/ppermute | solution.py:543
  36.2 6.4 %collective-permute-done.6.refs_1_ = f32[512,256]{1,0:T(8,128)S(1)} collective-permute-done((f32[512,256]{1,0:T(8,128)S(1)}, f32[512,256]{1,0:T(8,128)S(1)}, u32[]{:S(2)}, u32[]{:S(2)}) %collective-permute-start.6) | collective-permute-done | bytes 524320 | tf_op jit(solution)/shard_map/ppermute | solution.py:543
  42.6 0.7 %dft.15.two_g = f32[1024,256]{1,0:T(8,128)S(1)} custom-call(s32[1]{0:T(128)} %bitcast.pos_ref, bf16[2,4,256,256]{3,2,1,0:T(8,128)(2,1)S(1)} %copy-done.1, f32[512,256]{1,0:T(8,128)S(1)} %collective-permute-done.5.refs_0_.gated_ref, f32[512,256]{1,0:T(8,128)S(1)} %collective-permute-done.6.refs_1_), custom_call_target="tpu_custom_call" | custom-call | flops 402653184 | bytes 1572864 | tf_op jit(solution)/shard_map/dft/pallas_call | solution.py:153
  43.3 0.0 copy-start.2
  43.3 2.2 %early.1.acc_ref = f32[4,1024,256]{2,1,0:T(8,128)S(1)} custom-call(s32[1]{0:T(128)} %bitcast.pos_ref, f32[7,1024,256]{2,1,0:T(8,128)S(1)} %taps.1.win_own.win_outer.win_next.win_two.win_near.win_far.win_ref, f32[7,1024,256]{2,1,0:T(8,128)S(1)} %taps.1.win_own.win_outer.win_next.win_two.win_near.win_far.win_ref, ...), custom_call_target="tpu_custom_call" | custom-call | flops 26214400 | bytes 15728640 | tf_op jit(solution)/shard_map/early/pallas_call | solution.py:380
  45.6 1.4 %partial.2.made_ref = f32[520,128]{1,0:T(8,128)S(1)} custom-call(s32[1]{0:T(128)} %bitcast.pos_ref, bf16[2,4,256,256]{3,2,1,0:T(8,128)(2,1)S(1)} %copy-done.1, bf16[2,4,256,256]{3,2,1,0:T(8,128)(2,1)S(1)} %copy-done.2, f32[7,1024,256]{2,1,0:T(8,128)S(1)} %taps.1.win_own.win_outer.win_next.win_two.win_near.win_far.win_ref, ...), custom_call_target="tpu_custom_call" | custom-call | flops 402653184 | bytes 1572864 | tf_op jit(solution)/shard_map/partial/pallas_call | solution.py:249
  46.9 1.3 %collective-permute-start.9 = (f32[520,128]{1,0:T(8,128)S(1)}, f32[520,128]{1,0:T(8,128)S(1)}, u32[]{:S(2)}, u32[]{:S(2)}) collective-permute-start(f32[520,128]{1,0:T(8,128)S(1)} %partial.2.made_ref), channel_id=1, source_target_pairs={{4,0},{8,12},{5,1},{9,13},{6,2},{10,14},{7,3},{11,15},{20,16},{24,... | collective-permute-start | bytes 798728 | tf_op jit(solution)/shard_map/ppermute | solution.py:543
  48.2 1.4 %partial.3.made_ref = f32[520,128]{1,0:T(8,128)S(1)} custom-call(s32[1]{0:T(128)} %bitcast.pos_ref, bf16[2,4,256,256]{3,2,1,0:T(8,128)(2,1)S(1)} %copy-done.1, bf16[2,4,256,256]{3,2,1,0:T(8,128)(2,1)S(1)} %copy-done.2, f32[7,1024,256]{2,1,0:T(8,128)S(1)} %taps.1.win_own.win_outer.win_next.win_two.win_near.win_far.win_ref, ...), custom_call_target="tpu_custom_call" | custom-call | flops 402653184 | bytes 1572864 | tf_op jit(solution)/shard_map/partial/pallas_call | solution.py:249
  49.6 0.0 copy-start.7
  49.6 0.0 copy-start.9
  49.6 1.4 %collective-permute-start.8 = (f32[520,128]{1,0:T(8,128)S(1)}, f32[520,128]{1,0:T(8,128)S(1)}, u32[]{:S(2)}, u32[]{:S(2)}) collective-permute-start(f32[520,128]{1,0:T(8,128)S(1)} %partial.3.made_ref), channel_id=1, source_target_pairs={{4,0},{8,12},{5,1},{9,13},{6,2},{10,14},{7,3},{11,15},{20,16},{24,... | collective-permute-start | bytes 798728 | tf_op jit(solution)/shard_map/ppermute | solution.py:543
  51.1 0.7 %dft.17.rest_0_ = f32[1024,256]{1,0:T(8,128)S(1)} custom-call(s32[1]{0:T(128)} %bitcast.pos_ref, bf16[2,4,256,256]{3,2,1,0:T(8,128)(2,1)S(1)} %copy-done.1, f32[512,256]{1,0:T(8,128)S(1)} %collective-permute-done.4.x_ref.refs_0_), custom_call_target="tpu_custom_call" | custom-call | flops 402653184 | bytes 1572864 | tf_op jit(solution)/shard_map/dft/pallas_call | solution.py:153
  51.8 3.5 %collective-permute-done.7.refs_0_ = f32[512,256]{1,0:T(8,128)S(1)} collective-permute-done((f32[512,256]{1,0:T(8,128)S(1)}, f32[512,256]{1,0:T(8,128)S(1)}, u32[]{:S(2)}, u32[]{:S(2)}) %collective-permute-start.7) | collective-permute-done | bytes 524320 | tf_op jit(solution)/shard_map/ppermute | solution.py:543
  55.3 0.7 %dft.16.three_g = f32[1024,256]{1,0:T(8,128)S(1)} custom-call(s32[1]{0:T(128)} %bitcast.pos_ref, bf16[2,4,256,256]{3,2,1,0:T(8,128)(2,1)S(1)} %copy-done.1, f32[512,256]{1,0:T(8,128)S(1)} %collective-permute-done.7.refs_0_), custom_call_target="tpu_custom_call" | custom-call | flops 402653184 | bytes 1572864 | tf_op jit(solution)/shard_map/dft/pallas_call | solution.py:153
  56.0 0.0 copy-start.3
  56.0 0.0 copy-start.4
  56.0 6.0 %late.1 = (f32[512,256]{1,0:T(8,128)}, f32[1024,256]{1,0:T(8,128)}, f32[512,256]{1,0:T(8,128)S(1)}) custom-call(s32[1]{0:T(128)} %bitcast.pos_ref, bf16[2,4,256,256]{3,2,1,0:T(8,128)(2,1)S(1)} %copy-done.2, f32[4,1024,256]{2,1,0:T(8,128)S(1)} %early.1.acc_ref, f32[7,1024,256]{2,1,0:T(8,128)S(1)} %taps.1.win_own.win_outer.win_next.win_two.win_near.win_far.win_ref, ...), custom_call_target="tpu_custom_call" | custom-call | flops 1610612736 | bytes 13107200 | tf_op jit(solution)/shard_map/late/pallas_call | solution.py:477
  62.1 2.1 %collective-permute-done.9.sent_ref = f32[520,128]{1,0:T(8,128)S(1)} collective-permute-done((f32[520,128]{1,0:T(8,128)S(1)}, f32[520,128]{1,0:T(8,128)S(1)}, u32[]{:S(2)}, u32[]{:S(2)}) %collective-permute-start.9) | collective-permute-done | bytes 266272 | tf_op jit(solution)/shard_map/ppermute | solution.py:543
  64.2 0.9 %finish.2 = (f32[512,256]{1,0:T(8,128)}, f32[512,256]{1,0:T(8,128)}, f32[1,256]{1,0:T(1,128)}) custom-call(f32[512,256]{1,0:T(8,128)S(1)} %get-tuple-element.67.back_ref, f32[512,256]{1,0:T(8,128)S(1)} %copy-done.3, f32[512,256]{1,0:T(8,128)S(1)} %copy-done.4, f32[520,128]{1,0:T(8,128)S(1)} %partial.2.made_ref, ...), custom_call_target="tpu_custom_call" | custom-call | flops 196608 | bytes 1572864 | tf_op jit(solution)/shard_map/finish/pallas_call | solution.py:526
  65.0 3.0 %collective-permute-done.8.sent_ref = f32[520,128]{1,0:T(8,128)S(1)} collective-permute-done((f32[520,128]{1,0:T(8,128)S(1)}, f32[520,128]{1,0:T(8,128)S(1)}, u32[]{:S(2)}, u32[]{:S(2)}) %collective-permute-start.8) | collective-permute-done | bytes 266272 | tf_op jit(solution)/shard_map/ppermute | solution.py:543
  68.1 0.9 %finish.3 = (f32[512,256]{1,0:T(8,128)}, f32[512,256]{1,0:T(8,128)}, f32[1,256]{1,0:T(1,128)}) custom-call(f32[512,256]{1,0:T(8,128)S(1)} %get-tuple-element.67.back_ref, f32[512,256]{1,0:T(8,128)S(1)} %copy-done.3, f32[512,256]{1,0:T(8,128)S(1)} %copy-done.4, ...), custom_call_target="tpu_custom_call", output_to_operand_aliasing={{0}: (7, {}), {1}: (8, {}), {2}: (9, {})} | custom-call | flops 196608 | bytes 1572864 | tf_op jit(solution)/shard_map/finish/pallas_call | solution.py:526
  (12 shorter events, 0.0 us)
Async XLA Ops:
  1.9 12.2 %collective-permute-start.2 = (f32[512,256]{1,0:T(8,128)S(1)}, f32[512,256]{1,0:T(8,128)S(1)}, u32[]{:S(2)}, u32[]{:S(2)}) collective-permute-start(f32[512,256]{1,0:T(8,128)S(1)} %mul.3.gated_ref.refs_0_.rest_1_), channel_id=1, source_target_pairs={{4,8},{8,4},{5,9},{9,5},{6,10},{10,6},{7,11},{11,7},{20,24},{24,20... | collective-permute-start | bytes 1572872 | tf_op jit(solution)/shard_map/ppermute | solution.py:543
  2.6 18.7 %collective-permute-start.3 = (f32[512,256]{1,0:T(8,128)S(1)}, f32[512,256]{1,0:T(8,128)S(1)}, u32[]{:S(2)}, u32[]{:S(2)}) collective-permute-start(f32[512,256]{1,0:T(8,128)S(1)} %mul.3.gated_ref.refs_0_.rest_1_), channel_id=1, source_target_pairs={{0,4},{4,0},{8,12},{12,8},{1,5},{5,1},{9,13},{13,9},{2,6},{6,2},{1... | collective-permute-start | bytes 1572872 | tf_op jit(solution)/shard_map/ppermute | solution.py:543
  8.5 1.0 %copy-start.6 = (f32[512,256]{1,0:T(8,128)S(1)}, f32[512,256]{1,0:T(8,128)}, u32[]{:S(2)}) copy-start(f32[512,256]{1,0:T(8,128)} %rest_4_.1) | copy-start | bytes 1572868
  9.5 1.0 %copy-start.8 = (f32[512,256]{1,0:T(8,128)S(1)}, f32[512,256]{1,0:T(8,128)}, u32[]{:S(2)}) copy-start(f32[512,256]{1,0:T(8,128)} %query_ref.1) | copy-start | bytes 1572868
  10.6 21.9 %collective-permute-start = (f32[512,256]{1,0:T(8,128)S(1)}, f32[512,256]{1,0:T(8,128)S(1)}, u32[]{:S(2)}, u32[]{:S(2)}) collective-permute-start(f32[512,256]{1,0:T(8,128)S(1)} %get-tuple-element.44.refs_0_.rest_2_), channel_id=1, source_target_pairs={{0,4},{4,0},{8,12},{12,8},{1,5},{5,1},{9,13},{13,9},{2,6},{6,2},{1... | collective-permute-start | bytes 1572872 | tf_op jit(solution)/shard_map/ppermute | solution.py:543
  10.7 21.8 %collective-permute-start.1 = (f32[512,256]{1,0:T(8,128)S(1)}, f32[512,256]{1,0:T(8,128)S(1)}, u32[]{:S(2)}, u32[]{:S(2)}) collective-permute-start(f32[512,256]{1,0:T(8,128)S(1)} %get-tuple-element.44.refs_0_.rest_2_), channel_id=1, source_target_pairs={{4,8},{8,4},{5,9},{9,5},{6,10},{10,6},{7,11},{11,7},{20,24},{24,20... | collective-permute-start | bytes 1572872 | tf_op jit(solution)/shard_map/ppermute | solution.py:543
  11.4 1.2 %copy-start = (bf16[2,4,256,256]{3,2,1,0:T(8,128)(2,1)S(1)}, bf16[2,4,256,256]{3,2,1,0:T(8,128)(2,1)}, u32[]{:S(2)}) copy-start(bf16[2,4,256,256]{3,2,1,0:T(8,128)(2,1)} %constant.9.clone.table_ref) | copy-start | bytes 3145732
  13.4 11.4 %copy-start.1 = (bf16[2,4,256,256]{3,2,1,0:T(8,128)(2,1)S(1)}, bf16[2,4,256,256]{3,2,1,0:T(8,128)(2,1)}, u32[]{:S(2)}) copy-start(bf16[2,4,256,256]{3,2,1,0:T(8,128)(2,1)} %constant.9.clone.table_ref) | copy-start | bytes 3145732
  13.4 11.4 %copy-start.5 = (f32[4096,256]{1,0:T(8,128)S(1)}, f32[4096,256]{1,0:T(8,128)}, u32[]{:S(2)}) copy-start(f32[4096,256]{1,0:T(8,128)} %x_ref) | copy-start | bytes 12582916
  21.3 13.6 %collective-permute-start.5 = (f32[512,256]{1,0:T(8,128)S(1)}, f32[512,256]{1,0:T(8,128)S(1)}, u32[]{:S(2)}, u32[]{:S(2)}) collective-permute-start(f32[512,256]{1,0:T(8,128)S(1)} %collective-permute-done.3.refs_0_.refs_1_.gated_ref), channel_id=1, source_target_pairs={{4,8},{8,4},{5,9},{9,5},{6,10},{10,6},{7,11},{11,7},{20,24},{24,20... | collective-permute-start | bytes 1572872 | tf_op jit(solution)/shard_map/ppermute | solution.py:543
  22.0 20.6 %collective-permute-start.6 = (f32[512,256]{1,0:T(8,128)S(1)}, f32[512,256]{1,0:T(8,128)S(1)}, u32[]{:S(2)}, u32[]{:S(2)}) collective-permute-start(f32[512,256]{1,0:T(8,128)S(1)} %collective-permute-done.2.refs_0_.gated_ref), channel_id=1, source_target_pairs={{4,0},{8,12},{5,1},{9,13},{6,2},{10,14},{7,3},{11,15},{20,16},{24,... | collective-permute-start | bytes 1572872 | tf_op jit(solution)/shard_map/ppermute | solution.py:543
  34.0 11.6 %collective-permute-start.4 = (f32[512,256]{1,0:T(8,128)S(1)}, f32[512,256]{1,0:T(8,128)S(1)}, u32[]{:S(2)}, u32[]{:S(2)}) collective-permute-start(f32[512,256]{1,0:T(8,128)S(1)} %collective-permute-done.refs_0_.refs_1_.mixed_ref), channel_id=1, source_target_pairs={{4,8},{8,4},{5,9},{9,5},{6,10},{10,6},{7,11},{11,7},{20,24},{24,20... | collective-permute-start | bytes 1572872 | tf_op jit(solution)/shard_map/ppermute | solution.py:543
  34.9 20.3 %collective-permute-start.7 = (f32[512,256]{1,0:T(8,128)S(1)}, f32[512,256]{1,0:T(8,128)S(1)}, u32[]{:S(2)}, u32[]{:S(2)}) collective-permute-start(f32[512,256]{1,0:T(8,128)S(1)} %collective-permute-done.5.refs_0_.gated_ref), channel_id=1, source_target_pairs={{4,0},{8,12},{5,1},{9,13},{6,2},{10,14},{7,3},{11,15},{20,16},{24,... | collective-permute-start | bytes 1572872 | tf_op jit(solution)/shard_map/ppermute | solution.py:543
  43.3 2.2 %copy-start.2 = (bf16[2,4,256,256]{3,2,1,0:T(8,128)(2,1)S(1)}, bf16[2,4,256,256]{3,2,1,0:T(8,128)(2,1)}, u32[]{:S(2)}) copy-start(bf16[2,4,256,256]{3,2,1,0:T(8,128)(2,1)} %constant.10.clone.inverse_ref) | copy-start | bytes 3145732
  46.9 17.2 %collective-permute-start.9 = (f32[520,128]{1,0:T(8,128)S(1)}, f32[520,128]{1,0:T(8,128)S(1)}, u32[]{:S(2)}, u32[]{:S(2)}) collective-permute-start(f32[520,128]{1,0:T(8,128)S(1)} %partial.2.made_ref), channel_id=1, source_target_pairs={{4,0},{8,12},{5,1},{9,13},{6,2},{10,14},{7,3},{11,15},{20,16},{24,... | collective-permute-start | bytes 798728 | tf_op jit(solution)/shard_map/ppermute | solution.py:543
  49.6 6.4 %copy-start.7 = (f32[512,256]{1,0:T(8,128)S(1)}, f32[512,256]{1,0:T(8,128)}, u32[]{:S(2)}) copy-start(f32[512,256]{1,0:T(8,128)} %rest_4_.1) | copy-start | bytes 1572868
  49.6 6.4 %copy-start.9 = (f32[256]{0:T(256)S(1)}, f32[256]{0:T(256)}, u32[]{:S(2)}) copy-start(f32[256]{0:T(256)} %param.12) | copy-start | bytes 3076
  49.6 18.4 %collective-permute-start.8 = (f32[520,128]{1,0:T(8,128)S(1)}, f32[520,128]{1,0:T(8,128)S(1)}, u32[]{:S(2)}, u32[]{:S(2)}) collective-permute-start(f32[520,128]{1,0:T(8,128)S(1)} %partial.3.made_ref), channel_id=1, source_target_pairs={{4,0},{8,12},{5,1},{9,13},{6,2},{10,14},{7,3},{11,15},{20,16},{24,... | collective-permute-start | bytes 798728 | tf_op jit(solution)/shard_map/ppermute | solution.py:543
  56.0 8.1 %copy-start.3 = (f32[512,256]{1,0:T(8,128)S(1)}, f32[512,256]{1,0:T(8,128)}, u32[]{:S(2)}) copy-start(f32[512,256]{1,0:T(8,128)} %key_ref.3) | copy-start | bytes 1572868
  56.0 8.1 %copy-start.4 = (f32[512,256]{1,0:T(8,128)S(1)}, f32[512,256]{1,0:T(8,128)}, u32[]{:S(2)}) copy-start(f32[512,256]{1,0:T(8,128)} %values_ref.3) | copy-start | bytes 1572868

commit v17 on v15

--- a/solution.py
+++ b/solution.py
@@ -503,15 +503,14 @@
     )(pos, inverse, acc, windows, three_g, two_g, own_m, outer_m, next_m, two_m, gated, mixed, skip, upstream)
 
 
-def finish_kernel(half, back_ref, key_ref, values_ref, made_ref, sent_ref, own_ref, side_ref, *rest):
+def finish_kernel(half, back_ref, key_ref, values_ref, sent_ref, made_sums, sent_sums, own_ref, side_ref, *rest):
     key_out, value_out, skip_out = rest[-3:]
-    seg = back_ref.shape[0]
     width = sent_ref.shape[1]
     lanes = slice(half * width, (half + 1) * width)
-    back = back_ref[:, lanes] + sent_ref[:seg, :]
+    back = back_ref[:, lanes] + sent_ref[...]
     key_out[...] = back * values_ref[:, lanes]
     value_out[...] = back * key_ref[:, lanes]
-    total = (own_ref[:, lanes] + side_ref[:, lanes]) + (made_ref[seg:, :] + sent_ref[seg:, :])
+    total = (own_ref[:, lanes] + side_ref[:, lanes]) + (made_sums[...] + sent_sums[...])
     skip_out[...] = jnp.sum(total, axis=0, keepdims=True)
 
 
@@ -519,24 +518,24 @@
     seg, full = back.shape
     width = full // 2
 
-    def lanes(rows):
-        return pl.BlockSpec((rows, width), lambda i: (0, half))
-
+    rows = seg // 2
+    block = pl.BlockSpec((rows, width), lambda i: (i, half))
+    below = pl.BlockSpec((8, width), lambda i: (seg // 8, 0))
     held = pl.BlockSpec(memory_space=pl.ANY)
     return pl.pallas_call(
         functools.partial(finish_kernel, half),
-        grid=(1,),
-        in_specs=[whole_spec((seg, full))] * 3
-        + [whole_spec((seg + 8, width))] * 2
+        grid=(seg // rows,),
+        in_specs=[pl.BlockSpec((rows, full), lambda i: (i, 0))] * 3
+        + [pl.BlockSpec((rows, width), lambda i: (i, 0)), below, below]
         + [whole_spec((8, full))] * 2
         + [held] * len(before),
-        out_specs=[lanes(seg), lanes(seg), lanes(1)],
+        out_specs=[block, block, pl.BlockSpec((1, width), lambda i: (0, half))],
         out_shape=[f32(seg, full), f32(seg, full), f32(1, full)],
-        input_output_aliases={7 + i: i for i in range(len(before))},
+        input_output_aliases={8 + i: i for i in range(len(before))},
         compiler_params=params(12),
         cost_estimate=cost(3 * seg * width, 24 * seg * width),
         name="finish",
-    )(back, key_gate, values, made, sent, own_sums, side_sums, *before)
+    )(back, key_gate, values, sent, made, sent, own_sums, side_sums, *before)
 
 
 def send(x, *pairs):

time: 69.4 us -> 69.3 us (level)
  no operation moved by 1% of the time
where the time goes in v17:
time: 69.3 us; the launch traced here: 68.9 us
  Pallas kernels  25.4 us (37%)
  waiting for transfers between devices  22.3 us (32%)
  starting transfers between devices  15.7 us (23%)
  local copies, waits for them, and re-layouts  3.35 us (5%)
  other arithmetic  1.27 us (2%)
  between operations  0.93 us (1%)
    ppermute x10, waiting for transfers between devices, send(): return lax.ppermute(x, 'ctx', list(pairs))  22.3 us
    ppermute x10, starting transfers between devices, send(): return lax.ppermute(x, 'ctx', list(pairs))  15.7 us
    pallas_call x9, Pallas kernels, dft(): pl.pallas_call(functools.partial(dft_kernel, choose), grid_spec=pltpu.Pre...  6.47 us
    pallas_call x1, Pallas kernels, late(): pl.pallas_call(late_kernel, grid_spec=pltpu.PrefetchScalarGridSpec(num_sc...  6.03 us
    pallas_call x1, Pallas kernels, taps_spectra(): pl.pallas_call(taps_kernel, grid=(blocks,), in_specs=[whole_spec(table.sh...  5.95 us
    unnamed x20, local copies, waits for them, and re-layouts  3.35 us
    pallas_call x2, Pallas kernels, back_partial(): pl.pallas_call(partial_kernel, grid_spec=pltpu.PrefetchScalarGridSpec(num...  2.73 us
    pallas_call x1, Pallas kernels, early(): pl.pallas_call(early_kernel, grid_spec=pltpu.PrefetchScalarGridSpec(num_s...  2.2 us
  transfers between devices with their start and end apart: 10, of which 6 were waited for; matrix products, arithmetic and copies ran while one was open for 0% of the time, Pallas kernels for 36%

profile of v17, /device:TPU:0, one launch (start us, length us, event | category | flops | bytes accessed | tf_op | source)
XLA Modules:
  0.0 68.9 jit_solution(4817210739504470737)
XLA Ops:
  0.6 1.3 %mul.3.gated_ref.refs_0_.rest_1_ = f32[512,256]{1,0:T(8,128)S(1)} multiply(f32[512,256]{1,0:T(8,128)} %key_ref.3, f32[512,256]{1,0:T(8,128)} %values_ref.3) | non-fusion elementwise | flops 131072 | bytes 1572864 | tf_op jit(solution)/shard_map/mul | solution.py:564
  1.9 0.7 %collective-permute-start.2 = (f32[512,256]{1,0:T(8,128)S(1)}, f32[512,256]{1,0:T(8,128)S(1)}, u32[]{:S(2)}, u32[]{:S(2)}) collective-permute-start(f32[512,256]{1,0:T(8,128)S(1)} %mul.3.gated_ref.refs_0_.rest_1_), channel_id=1, source_target_pairs={{4,8},{8,4},{5,9},{9,5},{6,10},{10,6},{7,11},{11,7},{20,24},{24,20... | collective-permute-start | bytes 1572872 | tf_op jit(solution)/shard_map/ppermute | solution.py:542
  2.6 5.9 %collective-permute-start.3 = (f32[512,256]{1,0:T(8,128)S(1)}, f32[512,256]{1,0:T(8,128)S(1)}, u32[]{:S(2)}, u32[]{:S(2)}) collective-permute-start(f32[512,256]{1,0:T(8,128)S(1)} %mul.3.gated_ref.refs_0_.rest_1_), channel_id=1, source_target_pairs={{0,4},{4,0},{8,12},{12,8},{1,5},{5,1},{9,13},{13,9},{2,6},{6,2},{1... | collective-permute-start | bytes 1572872 | tf_op jit(solution)/shard_map/ppermute | solution.py:542
  8.5 1.0 %copy-done.6 = f32[512,256]{1,0:T(8,128)S(1)} copy-done((f32[512,256]{1,0:T(8,128)S(1)}, f32[512,256]{1,0:T(8,128)}, u32[]{:S(2)}) %copy-start.6) | copy-done | bytes 524312
  9.5 1.0 %copy-done.8 = f32[512,256]{1,0:T(8,128)S(1)} copy-done((f32[512,256]{1,0:T(8,128)S(1)}, f32[512,256]{1,0:T(8,128)}, u32[]{:S(2)}) %copy-start.8) | copy-done | bytes 524312
  10.6 0.1 mix.1
  10.6 0.7 %collective-permute-start = (f32[512,256]{1,0:T(8,128)S(1)}, f32[512,256]{1,0:T(8,128)S(1)}, u32[]{:S(2)}, u32[]{:S(2)}) collective-permute-start(f32[512,256]{1,0:T(8,128)S(1)} %get-tuple-element.44.refs_0_.rest_2_), channel_id=1, source_target_pairs={{4,8},{8,4},{5,9},{9,5},{6,10},{10,6},{7,11},{11,7},{20,24},{24,20... | collective-permute-start | bytes 1572872 | tf_op jit(solution)/shard_map/ppermute | solution.py:542
  11.3 1.7 %collective-permute-start.1 = (f32[512,256]{1,0:T(8,128)S(1)}, f32[512,256]{1,0:T(8,128)S(1)}, u32[]{:S(2)}, u32[]{:S(2)}) collective-permute-start(f32[512,256]{1,0:T(8,128)S(1)} %get-tuple-element.44.refs_0_.rest_2_), channel_id=1, source_target_pairs={{0,4},{4,0},{8,12},{12,8},{1,5},{5,1},{9,13},{13,9},{2,6},{6,2},{1... | collective-permute-start | bytes 1572872 | tf_op jit(solution)/shard_map/ppermute | solution.py:542
  13.1 1.2 %copy-done = bf16[2,4,256,256]{3,2,1,0:T(8,128)(2,1)S(1)} copy-done((bf16[2,4,256,256]{3,2,1,0:T(8,128)(2,1)S(1)}, bf16[2,4,256,256]{3,2,1,0:T(8,128)(2,1)}, u32[]{:S(2)}) %copy-start) | copy-done | bytes 1048600
  14.3 0.7 %dft.10.own_m = f32[1024,256]{1,0:T(8,128)S(1)} custom-call(s32[1]{0:T(128)} %bitcast.pos_ref, bf16[2,4,256,256]{3,2,1,0:T(8,128)(2,1)S(1)} %copy-done, f32[512,256]{1,0:T(8,128)S(1)} %get-tuple-element.44.refs_0_.rest_2_), custom_call_target="tpu_custom_call" | custom-call | flops 402653184 | bytes 1572864 | tf_op jit(solution)/shard_map/dft/pallas_call | solution.py:153
  15.0 0.0 copy-start.1
  15.0 0.0 copy-start.5
  15.1 0.7 %dft.9.own_g = f32[1024,256]{1,0:T(8,128)S(1)} custom-call(s32[1]{0:T(128)} %bitcast.pos_ref, bf16[2,4,256,256]{3,2,1,0:T(8,128)(2,1)S(1)} %copy-done, f32[512,256]{1,0:T(8,128)S(1)} %mul.3.gated_ref.refs_0_.rest_1_), custom_call_target="tpu_custom_call" | custom-call | flops 402653184 | bytes 1572864 | tf_op jit(solution)/shard_map/dft/pallas_call | solution.py:153
  15.8 5.5 %collective-permute-done.3.refs_0_.refs_1_.gated_ref = f32[512,256]{1,0:T(8,128)S(1)} collective-permute-done((f32[512,256]{1,0:T(8,128)S(1)}, f32[512,256]{1,0:T(8,128)S(1)}, u32[]{:S(2)}, u32[]{:S(2)}) %collective-permute-start.3) | collective-permute-done | bytes 524320 | tf_op jit(solution)/shard_map/ppermute | solution.py:542
  21.3 0.7 collective-permute-start.5
  22.0 1.3 %collective-permute-start.6 = (f32[512,256]{1,0:T(8,128)S(1)}, f32[512,256]{1,0:T(8,128)S(1)}, u32[]{:S(2)}, u32[]{:S(2)}) collective-permute-start(f32[512,256]{1,0:T(8,128)S(1)} %collective-permute-done.2.refs_0_.gated_ref), channel_id=1, source_target_pairs={{4,0},{8,12},{5,1},{9,13},{6,2},{10,14},{7,3},{11,15},{20,16},{24,... | collective-permute-start | bytes 1572872 | tf_op jit(solution)/shard_map/ppermute | solution.py:542
  23.3 0.7 %dft.12.next_g = f32[1024,256]{1,0:T(8,128)S(1)} custom-call(s32[1]{0:T(128)} %bitcast.pos_ref, bf16[2,4,256,256]{3,2,1,0:T(8,128)(2,1)S(1)} %copy-done, f32[512,256]{1,0:T(8,128)S(1)} %collective-permute-done.2.refs_0_.gated_ref, f32[512,256]{1,0:T(8,128)S(1)} %collective-permute-done.3.refs_0_.refs_1_.gated_ref), custom_call_target="tpu_custom_call" | custom-call | flops 402653184 | bytes 1572864 | tf_op jit(solution)/shard_map/dft/pallas_call | solution.py:153
  24.0 0.7 %dft.11.outer_g = f32[1024,256]{1,0:T(8,128)S(1)} custom-call(s32[1]{0:T(128)} %bitcast.pos_ref, bf16[2,4,256,256]{3,2,1,0:T(8,128)(2,1)S(1)} %copy-done, f32[512,256]{1,0:T(8,128)S(1)} %collective-permute-done.3.refs_0_.refs_1_.gated_ref), custom_call_target="tpu_custom_call" | custom-call | flops 402653184 | bytes 1572864 | tf_op jit(solution)/shard_map/dft/pallas_call | solution.py:153
  24.7 5.9 %taps.1.win_own.win_outer.win_next.win_two.win_near.win_far.win_ref = f32[7,1024,256]{2,1,0:T(8,128)S(1)} custom-call(bf16[2,4,256,256]{3,2,1,0:T(8,128)(2,1)S(1)} %copy-done.1, f32[4096,256]{1,0:T(8,128)S(1)} %copy-done.5), custom_call_target="tpu_custom_call" | custom-call | flops 3221225472 | bytes 12582912 | tf_op jit(solution)/shard_map/taps/pallas_call | solution.py:191
  30.7 0.0 collective-permute-done.refs_0_.mixed_ref
  30.7 1.8 %collective-permute-done.1.refs_0_.refs_1_.mixed_ref = f32[512,256]{1,0:T(8,128)S(1)} collective-permute-done((f32[512,256]{1,0:T(8,128)S(1)}, f32[512,256]{1,0:T(8,128)S(1)}, u32[]{:S(2)}, u32[]{:S(2)}) %collective-permute-start.1) | collective-permute-done | bytes 524320 | tf_op jit(solution)/shard_map/ppermute | solution.py:542
  32.5 0.7 %dft.13.outer_m = f32[1024,256]{1,0:T(8,128)S(1)} custom-call(s32[1]{0:T(128)} %bitcast.pos_ref, bf16[2,4,256,256]{3,2,1,0:T(8,128)(2,1)S(1)} %copy-done.1, f32[512,256]{1,0:T(8,128)S(1)} %collective-permute-done.1.refs_0_.refs_1_.mixed_ref), custom_call_target="tpu_custom_call" | custom-call | flops 402653184 | bytes 1572864 | tf_op jit(solution)/shard_map/dft/pallas_call | solution.py:153
  33.2 0.7 %dft.14.next_m.next_ref = f32[1024,256]{1,0:T(8,128)S(1)} custom-call(s32[1]{0:T(128)} %bitcast.pos_ref, bf16[2,4,256,256]{3,2,1,0:T(8,128)(2,1)S(1)} %copy-done.1, f32[512,256]{1,0:T(8,128)S(1)} %collective-permute-done.refs_0_.mixed_ref, f32[512,256]{1,0:T(8,128)S(1)} %collective-permute-done.1.refs_0_.refs_1_.mixed_ref), custom_call_target="tpu_custom_call" | custom-call | flops 402653184 | bytes 1572864 | tf_op jit(solution)/shard_map/dft/pallas_call | solution.py:153
  34.0 0.7 %collective-permute-start.4 = (f32[512,256]{1,0:T(8,128)S(1)}, f32[512,256]{1,0:T(8,128)S(1)}, u32[]{:S(2)}, u32[]{:S(2)}) collective-permute-start(f32[512,256]{1,0:T(8,128)S(1)} %collective-permute-done.1.refs_0_.refs_1_.mixed_ref), channel_id=1, source_target_pairs={{4,8},{8,4},{5,9},{9,5},{6,10},{10,6},{7,11},{11,7},{20,24},{24,20... | collective-permute-start | bytes 1572872 | tf_op jit(solution)/shard_map/ppermute | solution.py:542
  34.7 0.1 sums.3.near_sums
  34.8 0.1 sums.2.side_ref
  34.9 1.3 %collective-permute-start.7 = (f32[512,256]{1,0:T(8,128)S(1)}, f32[512,256]{1,0:T(8,128)S(1)}, u32[]{:S(2)}, u32[]{:S(2)}) collective-permute-start(f32[512,256]{1,0:T(8,128)S(1)} %collective-permute-done.5.refs_0_.gated_ref), channel_id=1, source_target_pairs={{4,0},{8,12},{5,1},{9,13},{6,2},{10,14},{7,3},{11,15},{20,16},{24,... | collective-permute-start | bytes 1572872 | tf_op jit(solution)/shard_map/ppermute | solution.py:542
  36.2 6.4 %collective-permute-done.6.refs_1_ = f32[512,256]{1,0:T(8,128)S(1)} collective-permute-done((f32[512,256]{1,0:T(8,128)S(1)}, f32[512,256]{1,0:T(8,128)S(1)}, u32[]{:S(2)}, u32[]{:S(2)}) %collective-permute-start.6) | collective-permute-done | bytes 524320 | tf_op jit(solution)/shard_map/ppermute | solution.py:542
  42.6 0.7 %dft.15.two_g = f32[1024,256]{1,0:T(8,128)S(1)} custom-call(s32[1]{0:T(128)} %bitcast.pos_ref, bf16[2,4,256,256]{3,2,1,0:T(8,128)(2,1)S(1)} %copy-done.1, f32[512,256]{1,0:T(8,128)S(1)} %collective-permute-done.5.refs_0_.gated_ref, f32[512,256]{1,0:T(8,128)S(1)} %collective-permute-done.6.refs_1_), custom_call_target="tpu_custom_call" | custom-call | flops 402653184 | bytes 1572864 | tf_op jit(solution)/shard_map/dft/pallas_call | solution.py:153
  43.3 0.0 copy-start.2
  43.3 2.2 %early.1.acc_ref = f32[4,1024,256]{2,1,0:T(8,128)S(1)} custom-call(s32[1]{0:T(128)} %bitcast.pos_ref, f32[7,1024,256]{2,1,0:T(8,128)S(1)} %taps.1.win_own.win_outer.win_next.win_two.win_near.win_far.win_ref, f32[7,1024,256]{2,1,0:T(8,128)S(1)} %taps.1.win_own.win_outer.win_next.win_two.win_near.win_far.win_ref, ...), custom_call_target="tpu_custom_call" | custom-call | flops 26214400 | bytes 15728640 | tf_op jit(solution)/shard_map/early/pallas_call | solution.py:380
  45.6 0.0 collective-permute-done.4.x_ref.refs_0_
  45.6 1.4 %partial.2.made_sums = f32[520,128]{1,0:T(8,128)S(1)} custom-call(s32[1]{0:T(128)} %bitcast.pos_ref, bf16[2,4,256,256]{3,2,1,0:T(8,128)(2,1)S(1)} %copy-done.1, bf16[2,4,256,256]{3,2,1,0:T(8,128)(2,1)S(1)} %copy-done.2, f32[7,1024,256]{2,1,0:T(8,128)S(1)} %taps.1.win_own.win_outer.win_next.win_two.win_near.win_far.win_ref, ...), custom_call_target="tpu_custom_call" | custom-call | flops 402653184 | bytes 1572864 | tf_op jit(solution)/shard_map/partial/pallas_call | solution.py:249
  46.9 1.3 %collective-permute-start.9 = (f32[520,128]{1,0:T(8,128)S(1)}, f32[520,128]{1,0:T(8,128)S(1)}, u32[]{:S(2)}, u32[]{:S(2)}) collective-permute-start(f32[520,128]{1,0:T(8,128)S(1)} %partial.2.made_sums), channel_id=1, source_target_pairs={{4,0},{8,12},{5,1},{9,13},{6,2},{10,14},{7,3},{11,15},{20,16},{24,... | collective-permute-start | bytes 798728 | tf_op jit(solution)/shard_map/ppermute | solution.py:542
  48.2 1.4 %partial.3.made_sums = f32[520,128]{1,0:T(8,128)S(1)} custom-call(s32[1]{0:T(128)} %bitcast.pos_ref, bf16[2,4,256,256]{3,2,1,0:T(8,128)(2,1)S(1)} %copy-done.1, bf16[2,4,256,256]{3,2,1,0:T(8,128)(2,1)S(1)} %copy-done.2, f32[7,1024,256]{2,1,0:T(8,128)S(1)} %taps.1.win_own.win_outer.win_next.win_two.win_near.win_far.win_ref, ...), custom_call_target="tpu_custom_call" | custom-call | flops 402653184 | bytes 1572864 | tf_op jit(solution)/shard_map/partial/pallas_call | solution.py:249
  49.6 0.0 copy-start.7
  49.6 0.0 copy-start.9
  49.6 1.4 %collective-permute-start.8 = (f32[520,128]{1,0:T(8,128)S(1)}, f32[520,128]{1,0:T(8,128)S(1)}, u32[]{:S(2)}, u32[]{:S(2)}) collective-permute-start(f32[520,128]{1,0:T(8,128)S(1)} %partial.3.made_sums), channel_id=1, source_target_pairs={{4,0},{8,12},{5,1},{9,13},{6,2},{10,14},{7,3},{11,15},{20,16},{24,... | collective-permute-start | bytes 798728 | tf_op jit(solution)/shard_map/ppermute | solution.py:542
  51.1 0.7 %dft.17.rest_0_ = f32[1024,256]{1,0:T(8,128)S(1)} custom-call(s32[1]{0:T(128)} %bitcast.pos_ref, bf16[2,4,256,256]{3,2,1,0:T(8,128)(2,1)S(1)} %copy-done.1, f32[512,256]{1,0:T(8,128)S(1)} %collective-permute-done.4.x_ref.refs_0_), custom_call_target="tpu_custom_call" | custom-call | flops 402653184 | bytes 1572864 | tf_op jit(solution)/shard_map/dft/pallas_call | solution.py:153
  51.8 3.5 %collective-permute-done.7.refs_0_ = f32[512,256]{1,0:T(8,128)S(1)} collective-permute-done((f32[512,256]{1,0:T(8,128)S(1)}, f32[512,256]{1,0:T(8,128)S(1)}, u32[]{:S(2)}, u32[]{:S(2)}) %collective-permute-start.7) | collective-permute-done | bytes 524320 | tf_op jit(solution)/shard_map/ppermute | solution.py:542
  55.3 0.7 %dft.16.three_g = f32[1024,256]{1,0:T(8,128)S(1)} custom-call(s32[1]{0:T(128)} %bitcast.pos_ref, bf16[2,4,256,256]{3,2,1,0:T(8,128)(2,1)S(1)} %copy-done.1, f32[512,256]{1,0:T(8,128)S(1)} %collective-permute-done.7.refs_0_), custom_call_target="tpu_custom_call" | custom-call | flops 402653184 | bytes 1572864 | tf_op jit(solution)/shard_map/dft/pallas_call | solution.py:153
  56.0 0.0 copy-start.3
  56.0 0.0 copy-start.4
  56.0 6.0 %late.1 = (f32[512,256]{1,0:T(8,128)}, f32[1024,256]{1,0:T(8,128)}, f32[512,256]{1,0:T(8,128)S(1)}) custom-call(s32[1]{0:T(128)} %bitcast.pos_ref, bf16[2,4,256,256]{3,2,1,0:T(8,128)(2,1)S(1)} %copy-done.2, f32[4,1024,256]{2,1,0:T(8,128)S(1)} %early.1.acc_ref, f32[7,1024,256]{2,1,0:T(8,128)S(1)} %taps.1.win_own.win_outer.win_next.win_two.win_near.win_far.win_ref, ...), custom_call_target="tpu_custom_call" | custom-call | flops 1610612736 | bytes 13107200 | tf_op jit(solution)/shard_map/late/pallas_call | solution.py:477
  62.1 2.1 %collective-permute-done.9.sent_ref.sent_sums = f32[520,128]{1,0:T(8,128)S(1)} collective-permute-done((f32[520,128]{1,0:T(8,128)S(1)}, f32[520,128]{1,0:T(8,128)S(1)}, u32[]{:S(2)}, u32[]{:S(2)}) %collective-permute-start.9) | collective-permute-done | bytes 266272 | tf_op jit(solution)/shard_map/ppermute | solution.py:542
  64.2 0.8 %finish.2 = (f32[512,256]{1,0:T(8,128)}, f32[512,256]{1,0:T(8,128)}, f32[1,256]{1,0:T(1,128)}) custom-call(f32[512,256]{1,0:T(8,128)S(1)} %get-tuple-element.67.back_ref, f32[512,256]{1,0:T(8,128)S(1)} %copy-done.3, f32[512,256]{1,0:T(8,128)S(1)} %copy-done.4, f32[520,128]{1,0:T(8,128)S(1)} %collective-permute-done.9.sent_ref.sent_sums, ...), custom_call_target="tpu_custom_call" | custom-call | flops 196608 | bytes 1572864 | tf_op jit(solution)/shard_map/finish/pallas_call | solution.py:525
  65.0 3.1 %collective-permute-done.8.sent_ref.sent_sums = f32[520,128]{1,0:T(8,128)S(1)} collective-permute-done((f32[520,128]{1,0:T(8,128)S(1)}, f32[520,128]{1,0:T(8,128)S(1)}, u32[]{:S(2)}, u32[]{:S(2)}) %collective-permute-start.8) | collective-permute-done | bytes 266272 | tf_op jit(solution)/shard_map/ppermute | solution.py:542
  68.1 0.8 %finish.3 = (f32[512,256]{1,0:T(8,128)}, f32[512,256]{1,0:T(8,128)}, f32[1,256]{1,0:T(1,128)}) custom-call(f32[512,256]{1,0:T(8,128)S(1)} %get-tuple-element.67.back_ref, f32[512,256]{1,0:T(8,128)S(1)} %copy-done.3, f32[512,256]{1,0:T(8,128)S(1)} %copy-done.4, ...), custom_call_target="tpu_custom_call", output_to_operand_aliasing={{0}: (8, {}), {1}: (9, {}), {2}: (10, {})} | custom-call | flops 196608 | bytes 1572864 | tf_op jit(solution)/shard_map/finish/pallas_call | solution.py:525
  (12 shorter events, 0.0 us)
Async XLA Ops:
  1.9 13.9 %collective-permute-start.2 = (f32[512,256]{1,0:T(8,128)S(1)}, f32[512,256]{1,0:T(8,128)S(1)}, u32[]{:S(2)}, u32[]{:S(2)}) collective-permute-start(f32[512,256]{1,0:T(8,128)S(1)} %mul.3.gated_ref.refs_0_.rest_1_), channel_id=1, source_target_pairs={{4,8},{8,4},{5,9},{9,5},{6,10},{10,6},{7,11},{11,7},{20,24},{24,20... | collective-permute-start | bytes 1572872 | tf_op jit(solution)/shard_map/ppermute | solution.py:542
  2.6 18.7 %collective-permute-start.3 = (f32[512,256]{1,0:T(8,128)S(1)}, f32[512,256]{1,0:T(8,128)S(1)}, u32[]{:S(2)}, u32[]{:S(2)}) collective-permute-start(f32[512,256]{1,0:T(8,128)S(1)} %mul.3.gated_ref.refs_0_.rest_1_), channel_id=1, source_target_pairs={{0,4},{4,0},{8,12},{12,8},{1,5},{5,1},{9,13},{13,9},{2,6},{6,2},{1... | collective-permute-start | bytes 1572872 | tf_op jit(solution)/shard_map/ppermute | solution.py:542
  8.5 1.0 %copy-start.6 = (f32[512,256]{1,0:T(8,128)S(1)}, f32[512,256]{1,0:T(8,128)}, u32[]{:S(2)}) copy-start(f32[512,256]{1,0:T(8,128)} %rest_4_.1) | copy-start | bytes 1572868
  9.5 1.0 %copy-start.8 = (f32[512,256]{1,0:T(8,128)S(1)}, f32[512,256]{1,0:T(8,128)}, u32[]{:S(2)}) copy-start(f32[512,256]{1,0:T(8,128)} %query_ref.1) | copy-start | bytes 1572868
  10.6 20.1 %collective-permute-start = (f32[512,256]{1,0:T(8,128)S(1)}, f32[512,256]{1,0:T(8,128)S(1)}, u32[]{:S(2)}, u32[]{:S(2)}) collective-permute-start(f32[512,256]{1,0:T(8,128)S(1)} %get-tuple-element.44.refs_0_.rest_2_), channel_id=1, source_target_pairs={{4,8},{8,4},{5,9},{9,5},{6,10},{10,6},{7,11},{11,7},{20,24},{24,20... | collective-permute-start | bytes 1572872 | tf_op jit(solution)/shard_map/ppermute | solution.py:542
  11.3 21.2 %collective-permute-start.1 = (f32[512,256]{1,0:T(8,128)S(1)}, f32[512,256]{1,0:T(8,128)S(1)}, u32[]{:S(2)}, u32[]{:S(2)}) collective-permute-start(f32[512,256]{1,0:T(8,128)S(1)} %get-tuple-element.44.refs_0_.rest_2_), channel_id=1, source_target_pairs={{0,4},{4,0},{8,12},{12,8},{1,5},{5,1},{9,13},{13,9},{2,6},{6,2},{1... | collective-permute-start | bytes 1572872 | tf_op jit(solution)/shard_map/ppermute | solution.py:542
  13.1 1.2 %copy-start = (bf16[2,4,256,256]{3,2,1,0:T(8,128)(2,1)S(1)}, bf16[2,4,256,256]{3,2,1,0:T(8,128)(2,1)}, u32[]{:S(2)}) copy-start(bf16[2,4,256,256]{3,2,1,0:T(8,128)(2,1)} %constant.9.clone.table_ref) | copy-start | bytes 3145732
  15.0 9.7 %copy-start.1 = (bf16[2,4,256,256]{3,2,1,0:T(8,128)(2,1)S(1)}, bf16[2,4,256,256]{3,2,1,0:T(8,128)(2,1)}, u32[]{:S(2)}) copy-start(bf16[2,4,256,256]{3,2,1,0:T(8,128)(2,1)} %constant.9.clone.table_ref) | copy-start | bytes 3145732
  15.0 9.7 %copy-start.5 = (f32[4096,256]{1,0:T(8,128)S(1)}, f32[4096,256]{1,0:T(8,128)}, u32[]{:S(2)}) copy-start(f32[4096,256]{1,0:T(8,128)} %x_ref) | copy-start | bytes 12582916
  21.3 13.6 %collective-permute-start.5 = (f32[512,256]{1,0:T(8,128)S(1)}, f32[512,256]{1,0:T(8,128)S(1)}, u32[]{:S(2)}, u32[]{:S(2)}) collective-permute-start(f32[512,256]{1,0:T(8,128)S(1)} %collective-permute-done.3.refs_0_.refs_1_.gated_ref), channel_id=1, source_target_pairs={{4,8},{8,4},{5,9},{9,5},{6,10},{10,6},{7,11},{11,7},{20,24},{24,20... | collective-permute-start | bytes 1572872 | tf_op jit(solution)/shard_map/ppermute | solution.py:542
  22.0 20.6 %collective-permute-start.6 = (f32[512,256]{1,0:T(8,128)S(1)}, f32[512,256]{1,0:T(8,128)S(1)}, u32[]{:S(2)}, u32[]{:S(2)}) collective-permute-start(f32[512,256]{1,0:T(8,128)S(1)} %collective-permute-done.2.refs_0_.gated_ref), channel_id=1, source_target_pairs={{4,0},{8,12},{5,1},{9,13},{6,2},{10,14},{7,3},{11,15},{20,16},{24,... | collective-permute-start | bytes 1572872 | tf_op jit(solution)/shard_map/ppermute | solution.py:542
  34.0 11.6 %collective-permute-start.4 = (f32[512,256]{1,0:T(8,128)S(1)}, f32[512,256]{1,0:T(8,128)S(1)}, u32[]{:S(2)}, u32[]{:S(2)}) collective-permute-start(f32[512,256]{1,0:T(8,128)S(1)} %collective-permute-done.1.refs_0_.refs_1_.mixed_ref), channel_id=1, source_target_pairs={{4,8},{8,4},{5,9},{9,5},{6,10},{10,6},{7,11},{11,7},{20,24},{24,20... | collective-permute-start | bytes 1572872 | tf_op jit(solution)/shard_map/ppermute | solution.py:542
  34.9 20.4 %collective-permute-start.7 = (f32[512,256]{1,0:T(8,128)S(1)}, f32[512,256]{1,0:T(8,128)S(1)}, u32[]{:S(2)}, u32[]{:S(2)}) collective-permute-start(f32[512,256]{1,0:T(8,128)S(1)} %collective-permute-done.5.refs_0_.gated_ref), channel_id=1, source_target_pairs={{4,0},{8,12},{5,1},{9,13},{6,2},{10,14},{7,3},{11,15},{20,16},{24,... | collective-permute-start | bytes 1572872 | tf_op jit(solution)/shard_map/ppermute | solution.py:542
  43.3 2.2 %copy-start.2 = (bf16[2,4,256,256]{3,2,1,0:T(8,128)(2,1)S(1)}, bf16[2,4,256,256]{3,2,1,0:T(8,128)(2,1)}, u32[]{:S(2)}) copy-start(bf16[2,4,256,256]{3,2,1,0:T(8,128)(2,1)} %constant.10.clone.inverse_ref) | copy-start | bytes 3145732
  46.9 17.2 %collective-permute-start.9 = (f32[520,128]{1,0:T(8,128)S(1)}, f32[520,128]{1,0:T(8,128)S(1)}, u32[]{:S(2)}, u32[]{:S(2)}) collective-permute-start(f32[520,128]{1,0:T(8,128)S(1)} %partial.2.made_sums), channel_id=1, source_target_pairs={{4,0},{8,12},{5,1},{9,13},{6,2},{10,14},{7,3},{11,15},{20,16},{24,... | collective-permute-start | bytes 798728 | tf_op jit(solution)/shard_map/ppermute | solution.py:542
  49.6 6.4 %copy-start.7 = (f32[512,256]{1,0:T(8,128)S(1)}, f32[512,256]{1,0:T(8,128)}, u32[]{:S(2)}) copy-start(f32[512,256]{1,0:T(8,128)} %rest_4_.1) | copy-start | bytes 1572868
  49.6 6.4 %copy-start.9 = (f32[256]{0:T(256)S(1)}, f32[256]{0:T(256)}, u32[]{:S(2)}) copy-start(f32[256]{0:T(256)} %param.12) | copy-start | bytes 3076
  49.6 18.4 %collective-permute-start.8 = (f32[520,128]{1,0:T(8,128)S(1)}, f32[520,128]{1,0:T(8,128)S(1)}, u32[]{:S(2)}, u32[]{:S(2)}) collective-permute-start(f32[520,128]{1,0:T(8,128)S(1)} %partial.3.made_sums), channel_id=1, source_target_pairs={{4,0},{8,12},{5,1},{9,13},{6,2},{10,14},{7,3},{11,15},{20,16},{24,... | collective-permute-start | bytes 798728 | tf_op jit(solution)/shard_map/ppermute | solution.py:542
  56.0 8.1 %copy-start.3 = (f32[512,256]{1,0:T(8,128)S(1)}, f32[512,256]{1,0:T(8,128)}, u32[]{:S(2)}) copy-start(f32[512,256]{1,0:T(8,128)} %key_ref.3) | copy-start | bytes 1572868
  56.0 8.1 %copy-start.4 = (f32[512,256]{1,0:T(8,128)S(1)}, f32[512,256]{1,0:T(8,128)}, u32[]{:S(2)}) copy-start(f32[512,256]{1,0:T(8,128)} %values_ref.3) | copy-start | bytes 1572868
